TPU v7x, 32 devices: a whole 2x2x4 slice. The times are simulated.
32 devices in a mesh: aux: 4 (over x, core), orb: 8 (over z, y).
Axes of the slice: x: 2, y: 2, z: 4, core: 2. Of those that a mesh axis runs over, the one named last changes fastest.
Arguments:
- raw_ints: bfloat16 [4, 8, 1024, 1536], P(None, 'orb', 'aux'), may hold values from -0.625 to 0.625
- fit_inverse: bfloat16 [32, 1024, 1024], P(('aux', 'orb')), may hold values from -0.1875 to 0.1875
- pair_orbs: int32 [512, 2], P(('aux', 'orb')), may hold values from 0 to 7, all different within a row; in each aligned block of 16 rows (0 to 15, 16 to 31, ...) at most 8 rows name the same one
- pno_coef: bfloat16 [512, 2, 32, 1536], P(('aux', 'orb')), may hold values from -0.15625 to 0.15625
- pno_energy: float32 [512, 2, 32], P(('aux', 'orb')), may hold values from 0.3 to 6
- occ_energy: float32 [32], replicated, may hold values from -1.5 to -0.3
- fit_offset: int32 [32], replicated, may hold values from 0 to 255
Outputs:
- amplitude: float32 [512, 1024], P(('aux', 'orb'))
- energy: float32 [512], P(('aux', 'orb'))
Inputs may be any that keep to these rules, and one draw needn't show every extreme that they name: `pair_orbs`: each entry is an orbital's index within the pair's region; the two entries of a row differ; among the rows of one device no orbital is named more than 8 times.
All inputs are finite; a program needn't handle non-finite values.
Results may differ from a plain program's by a relative error of at most 0.0057.
Values may be sent and summed in bfloat16 or wider, within the bound.
No kernel may reach another device: no remote copies, remote signals or barrier semaphores. Data moves between devices by JAX's collectives and lax.ppermute only.
A program may use at most 64 MiB of HBM per device.

v0:
```python
import jax
import jax.numpy as jnp
from jax import lax
from jax.sharding import PartitionSpec as P


def align_rows(shifted_in, begin_at):
    return lax.dynamic_slice_in_dim(shifted_in, begin_at, shifted_in.shape[1] * 2 // 3, 1)


def on_device(raw_ints, fit_inverse, pair_orbs, pno_coef, pno_energy, occ_energy, fit_offset):
    orb_count = lax.axis_size("orb")
    region = lax.axis_index("aux")
    inverse = fit_inverse[0]
    gathered = lax.all_to_all(raw_ints, "aux", split_axis=0, concat_axis=2, tiled=True)
    fitted = jnp.dot(inverse, gathered[0, 0], preferred_element_type=jnp.float32).astype(
        jnp.bfloat16
    )
    fit_rows = fitted.shape[0]
    pair_count = pair_orbs.shape[0]
    pno_count = pno_coef.shape[2]
    dom_count = pno_coef.shape[3]
    side_count = 2 * pair_count
    capacity = max(2, 4 * pair_count // orb_count)
    slot_count = orb_count * capacity
    side_orbs = pair_orbs.reshape(side_count)
    matches = side_orbs[:, None] == side_orbs[None, :]
    sequence = jnp.arange(side_count, dtype=jnp.int32)
    earlier = sequence[None, :] < sequence[:, None]
    position = jnp.sum(jnp.where(matches & earlier, 1, 0), axis=1)
    slot_index = side_orbs * capacity + position
    placing = jnp.where(
        slot_index[None, :] == jnp.arange(slot_count, dtype=jnp.int32)[:, None], 1.0, 0.0
    ).astype(jnp.bfloat16)
    outgoing = jnp.dot(
        placing,
        pno_coef.reshape(side_count, pno_count * dom_count),
        preferred_element_type=jnp.float32,
    ).astype(jnp.bfloat16)
    outgoing = outgoing.reshape(orb_count, capacity, pno_count, dom_count)
    projected = jnp.einsum(
        "scpd,fd->scpf",
        lax.all_to_all(outgoing, "orb", split_axis=0, concat_axis=0, tiled=True),
        fitted,
        preferred_element_type=jnp.float32,
    ).astype(jnp.bfloat16)
    returned = lax.all_to_all(projected, "orb", split_axis=0, concat_axis=0, tiled=True)
    side_blocks = jnp.dot(
        placing.T,
        returned.reshape(slot_count, pno_count * fit_rows),
        preferred_element_type=jnp.float32,
    ).astype(jnp.bfloat16)
    side_blocks = side_blocks.reshape(pair_count, 2, pno_count, fit_rows)
    orb_total = occ_energy.shape[0]
    global_orb = region * orb_count + pair_orbs
    selector = global_orb[:, :, None] == jnp.arange(orb_total, dtype=jnp.int32)[None, None, :]
    offsets = jnp.sum(jnp.where(selector, fit_offset[None, None, :], 0), axis=2)
    occupied = jnp.sum(jnp.where(selector, occ_energy[None, None, :], 0.0), axis=2)
    margin = fit_rows // 4
    shift_rows = offsets[:, 0] - offsets[:, 1]
    padded = jnp.pad(side_blocks[:, 1], ((0, 0), (0, 0), (margin, margin)))
    aligned = jax.vmap(align_rows)(padded, margin + shift_rows)
    coupling = jnp.einsum(
        "npr,nqr->npq", side_blocks[:, 0], aligned, preferred_element_type=jnp.float32
    )
    denominator = (
        pno_energy[:, 0, :, None]
        + pno_energy[:, 1, None, :]
        - occupied[:, 0, None, None]
        - occupied[:, 1, None, None]
    )
    amplitude = -coupling / denominator
    energy = jnp.sum(coupling * (2.0 * amplitude - jnp.swapaxes(amplitude, 1, 2)), axis=(1, 2))
    return (amplitude.reshape(pair_count, pno_count * pno_count), energy)


def solution(mesh):
    return jax.shard_map(
        on_device,
        mesh=mesh,
        in_specs=(
            P(None, "orb", "aux", None),
            P(("aux", "orb"), None, None),
            P(("aux", "orb"), None),
            P(("aux", "orb"), None, None, None),
            P(("aux", "orb"), None, None),
            P(),
            P(),
        ),
        out_specs=(P(("aux", "orb"), None), P(("aux", "orb"))),
        check_vma=False,
    )
```

profile of v0, /device:TPU:0, one launch (start us, length us, event | category | flops | bytes accessed | tf_op | source)
XLA Modules:
  0.0 369.7 jit_solution(10046944388487365889)
XLA Ops:
  0.7 4.8 %all-to-all-start.1 = ((bf16[4,1,256,1536]{3,2,1,0:T(8,128)(2,1)}), bf16[4,1,256,1536]{3,2,1,0:T(8,128)(2,1)}, u32[]{:S(2)}, u32[]{:S(2)}) async-start(bf16[4,1,256,1536]{3,2,1,0:T(8,128)(2,1)} %param.7), calls=%async_computation.1 | async-start | bytes 6291456 | tf_op jit(solution)/shard_map/all_to_all | solution.py:15
  5.7 3.6 copy.29
  9.5 1.8 convolution_convert_fusion
  11.3 4.9 %copy.22 = bf16[8,8,32,1536]{3,2,1,0:T(8,128)(2,1)} copy(bf16[8,8,32,1536]{3,1,2,0:T(8,128)(2,1)S(1)} %bitcast.59) | data formatting | bytes 12582912 | tf_op jit(solution)/shard_map/reshape | solution.py:40
  16.2 26.9 %all-to-all-done.1 = bf16[4,1,256,1536]{3,2,1,0:T(8,128)(2,1)} async-done(((bf16[4,1,256,1536]{3,2,1,0:T(8,128)(2,1)}), bf16[4,1,256,1536]{3,2,1,0:T(8,128)(2,1)}, u32[]{:S(2)}, u32[]{:S(2)}) %all-to-all-start.1) | async-done | bytes 3145760 | tf_op jit(solution)/shard_map/all_to_all | solution.py:15
  43.1 144.9 %all_to_all.19 = bf16[8,8,32,1536]{3,2,1,0:T(8,128)(2,1)} all-to-all(bf16[8,8,32,1536]{3,2,1,0:T(8,128)(2,1)} %copy.22), channel_id=1, replica_groups=mesh['aux'=4,'orb'=8] {'orb'}, dimensions={0} | all-to-all | bytes 12582912 | tf_op jit(solution)/shard_map/all_to_all | solution.py:43
  188.0 15.3 %convolution_convert_fusion.3 = bf16[8,8,32,1024]{3,2,1,0:T(8,128)(2,1)} fusion(bf16[8,8,32,1536]{3,2,1,0:T(8,128)(2,1)} %all_to_all.19, bf16[1024,1536]{1,0:T(8,128)(2,1)} %bitcast.2, bf16[1,1024,1024]{2,1,0:T(8,128)(2,1)S(1)} %copy-done), kind=kOutput, calls=%fused_computation.6 | convolution fusion | flops 9667346432 | bytes 15728640 | tf_op jit(solution)/shard_map/scpd,fd->scpf/dot_general | solution.py:41
  203.3 4.9 %all-to-all-start.2 = ((bf16[8,8,32,1024]{3,2,1,0:T(8,128)(2,1)}), bf16[8,8,32,1024]{3,2,1,0:T(8,128)(2,1)}, u32[]{:S(2)}, u32[]{:S(2)}) async-start(bf16[8,8,32,1024]{3,2,1,0:T(8,128)(2,1)} %convolution_convert_fusion.3), calls=%async_computation.2 | async-start | bytes 8388608 | tf_op jit(solution)/shard_map/all_to_all | solution.py:47
  208.6 91.6 %all-to-all-done.2 = bf16[8,8,32,1024]{3,2,1,0:T(8,128)(2,1)} async-done(((bf16[8,8,32,1024]{3,2,1,0:T(8,128)(2,1)}), bf16[8,8,32,1024]{3,2,1,0:T(8,128)(2,1)}, u32[]{:S(2)}, u32[]{:S(2)}) %all-to-all-start.2) | async-done | bytes 4194336 | tf_op jit(solution)/shard_map/all_to_all | solution.py:47
  300.3 4.6 %copy.30 = bf16[8,8,32,1024]{3,1,2,0:T(8,128)(2,1)S(1)} copy(bf16[8,8,32,1024]{3,2,1,0:T(8,128)(2,1)} %all-to-all-done.2) | data formatting | bytes 8388608
  305.7 1.2 copy.31
  306.8 1.3 copy-done.1
  308.2 1.3 pad.5
  309.6 56.3 %while.1 = (s32[]{:T(128)}, bf16[16,32,1536]{2,1,0:T(8,128)(2,1)}, s32[16,3]{0,1:T(4,128)S(1)}, bf16[16,32,1024]{2,1,0:T(8,128)(2,1)}, s32[]{:T(128)}) while((s32[]{:T(128)}, bf16[16,32,1536]{2,1,0:T(8,128)(2,1)}, s32[16,3]{0,1:T(4,128)S(1)}, bf16[16,32,1024]{2,1,0:T(8,128)(2,1)}, s32[]{:T(128)}) %tuple.26), condition=%wide.while_cond, body=%wide.while_body.sunk | while | flops 2 | bytes 132713 | solution.py:8
  310.2 2.9 dynamic-slice_dynamic-update-slice_fusion.2
  313.7 2.9 dynamic-slice_dynamic-update-slice_fusion.2
  317.2 2.9 dynamic-slice_dynamic-update-slice_fusion.2
  320.8 2.9 dynamic-slice_dynamic-update-slice_fusion.2
  324.3 2.9 dynamic-slice_dynamic-update-slice_fusion.2
  327.8 2.9 dynamic-slice_dynamic-update-slice_fusion.2
  331.3 2.9 dynamic-slice_dynamic-update-slice_fusion.2
  334.8 2.9 dynamic-slice_dynamic-update-slice_fusion.2
  338.4 2.9 dynamic-slice_dynamic-update-slice_fusion.2
  341.9 2.9 dynamic-slice_dynamic-update-slice_fusion.2
  345.4 2.9 dynamic-slice_dynamic-update-slice_fusion.2
  348.9 2.9 dynamic-slice_dynamic-update-slice_fusion.2
  352.4 2.9 dynamic-slice_dynamic-update-slice_fusion.2
  356.0 2.9 dynamic-slice_dynamic-update-slice_fusion.2
  359.5 2.9 dynamic-slice_dynamic-update-slice_fusion.2
  363.0 2.9 dynamic-slice_dynamic-update-slice_fusion.2
  365.9 1.9 fusion.2
  368.0 0.9 multiply_reduce_fusion
  (61 shorter events, 12.9 us)
Async XLA Ops:
  0.6 187.4 %copy-start = (bf16[1,1024,1024]{2,1,0:T(8,128)(2,1)S(1)}, bf16[1,1024,1024]{2,1,0:T(8,128)(2,1)}, u32[]{:S(2)}) copy-start(bf16[1,1024,1024]{2,1,0:T(8,128)(2,1)} %param.8) | copy-start | bytes 6291460
  0.6 4.8 %copy-start.3 = (s32[16,2]{0,1:T(2,128)S(1)}, s32[16,2]{0,1:T(2,128)}, u32[]{:S(2)}) copy-start(s32[16,2]{0,1:T(2,128)} %param.9) | copy-start | bytes 388
  0.7 42.5 %all-to-all-start.1 = ((bf16[4,1,256,1536]{3,2,1,0:T(8,128)(2,1)}), bf16[4,1,256,1536]{3,2,1,0:T(8,128)(2,1)}, u32[]{:S(2)}, u32[]{:S(2)}) async-start(bf16[4,1,256,1536]{3,2,1,0:T(8,128)(2,1)} %param.7), calls=%async_computation.1 | async-start | bytes 6291456 | tf_op jit(solution)/shard_map/all_to_all | solution.py:15
  203.3 4.9 %copy-start.4 = (s32[32]{0:T(128)S(1)}, s32[32]{0:T(128)}, u32[]{:S(2)}) copy-start(s32[32]{0:T(128)} %param.13) | copy-start | bytes 388
  203.3 5.1 %copy-start.5 = (f32[32]{0:T(128)S(1)}, f32[32]{0:T(128)}, u32[]{:S(2)}) copy-start(f32[32]{0:T(128)} %param.12) | copy-start | bytes 388
  203.3 5.3 %copy-start.2 = (f32[16,2,32]{2,1,0:T(2,128)S(1)}, f32[16,2,32]{2,1,0:T(2,128)}, u32[]{:S(2)}) copy-start(f32[16,2,32]{2,1,0:T(2,128)} %param.11) | copy-start | bytes 12292
  203.3 97.0 %all-to-all-start.2 = ((bf16[8,8,32,1024]{3,2,1,0:T(8,128)(2,1)}), bf16[8,8,32,1024]{3,2,1,0:T(8,128)(2,1)}, u32[]{:S(2)}, u32[]{:S(2)}) async-start(bf16[8,8,32,1024]{3,2,1,0:T(8,128)(2,1)} %convolution_convert_fusion.3), calls=%async_computation.2 | async-start | bytes 8388608 | tf_op jit(solution)/shard_map/all_to_all | solution.py:47
  306.8 1.3 copy-start.1
where the time goes:
time: 371 us; the launch traced here: 370 us
  blocking collectives  145 us (39%)
  waiting for transfers between devices  119 us (32%)
  local copies, waits for them, and re-layouts  74.5 us (20%)
  matrix products  19.8 us (5%)
  starting transfers between devices  9.69 us (3%)
    all_to_all x1, blocking collectives, on_device(): lax.all_to_all(outgoing, 'orb', split_axis=0, concat_axis=0, tiled=True)  145 us
    all_to_all x1, waiting for transfers between devices, on_device(): lax.all_to_all(projected, 'orb', split_axis=0, concat_axis=0, tiled=True)  91.6 us
    gather x48, local copies, waits for them, and re-layouts  56.3 us
    all_to_all x1, waiting for transfers between devices, on_device(): lax.all_to_all(raw_ints, 'aux', split_axis=0, concat_axis=2, tiled=True)  26.9 us
    dot_general x1, matrix products, on_device(): jnp.einsum('scpd,fd->scpf', lax.all_to_all(outgoing, 'orb', split_axis=0,...  15.3 us
    unnamed x17, local copies, waits for them, and re-layouts  10.9 us
  transfers between devices with their start and end apart: 2, of which 2 were waited for; matrix products, arithmetic and copies ran while one was open for 3% of the time, Pallas kernels for 0%

commit v1 on v0

v1 whole, which is shorter than its diff:
```python
import functools

import jax
import jax.numpy as jnp
from jax import lax
from jax.experimental import pallas as pl
from jax.experimental.pallas import tpu as pltpu
from jax.sharding import PartitionSpec as P

LAST = 128
SMEM = pl.BlockSpec(memory_space=pltpu.SMEM)
VMEM = pl.BlockSpec(memory_space=pltpu.VMEM)
ANY = pl.BlockSpec(memory_space=pl.ANY)


def copy(source, target, sem):
    return pltpu.make_async_copy(source, target, sem)


def pack_kernel(group, capacity, orbs, place, coef, *refs):
    outs, (held, count, holder, load_sem, store_sem) = refs[:-5], refs[-5:]
    load = copy(coef, held, load_sem)
    load.start()

    def clear(i, carry):
        holder[i] = 0
        return carry

    def clear_count(i, carry):
        count[i] = 0
        return carry

    def assign(s, carry):
        orb = orbs[s]
        at = count[orb]
        holder[orb * capacity + at] = s
        count[orb] = at + 1
        return carry

    lax.fori_loop(0, 2 * group * capacity, clear, 0)
    lax.fori_loop(0, 2 * group, clear_count, 0)
    lax.fori_loop(0, held.shape[0], assign, 0)
    load.wait()
    for mask, out in enumerate(outs):
        for kind in range(2):
            orb = place[1] ^ (mask + kind * group)

            def send(k, carry, orb=orb, kind=kind, out=out, sem=store_sem.at[mask]):
                copy(held.at[holder[orb * capacity + k]], out.at[kind * capacity + k], sem).start()
                return carry

            lax.fori_loop(0, capacity, send, 0)
    for mask, out in enumerate(outs):
        copy(held.at[pl.ds(0, 2 * capacity)], out, store_sem.at[mask]).wait()


def pack(orbs, place, coef, group, capacity):
    side_count, pno_count, dom_count = coef.shape
    block = jax.ShapeDtypeStruct((2 * capacity, pno_count, dom_count), coef.dtype)
    return pl.pallas_call(
        functools.partial(pack_kernel, group, capacity),
        out_shape=(block,) * group,
        in_specs=[SMEM, SMEM, ANY],
        out_specs=(ANY,) * group,
        scratch_shapes=[
            pltpu.VMEM(coef.shape, coef.dtype),
            pltpu.SMEM((2 * group,), jnp.int32),
            pltpu.SMEM((2 * group * capacity,), jnp.int32),
            pltpu.SemaphoreType.DMA,
            pltpu.SemaphoreType.DMA((group,)),
        ],
        cost_estimate=pl.CostEstimate(
            flops=0, transcendentals=0, bytes_accessed=6 * side_count * pno_count * dom_count
        ),
        name="pack",
    )(orbs, place, coef)


def project_kernel(group, capacity, kind, pieces, *refs):
    inner = group // 2
    count = group + len(pieces)
    blocks, parts = refs[:group], refs[group:count]
    outs, (left, right, made, left_sem, right_sem, out_sem) = refs[-6 - inner : -6], refs[-6:]
    row_count = right.shape[0]
    _, pno_count, dom_count = left.shape
    lines = 2 * capacity
    for part, (row, column, width) in zip(parts, pieces):
        copy(
            part.at[pl.ds(row, row_count)], right.at[:, pl.ds(column, width)], right_sem
        ).start()
    for i in range(inner):
        for j in range(2):
            copy(
                blocks[i + j * inner].at[pl.ds(kind * capacity, capacity)],
                left.at[pl.ds(i * lines + j * capacity, capacity)],
                left_sem.at[i],
            ).start()
    copy(right, right, right_sem).wait()
    step = row_count if row_count <= 512 else 256
    for i in range(inner):
        mine = left.at[pl.ds(i * lines, lines)]
        copy(mine, mine, left_sem.at[i]).wait()

        def tile(t, carry, i=i, mine=mine):
            at = t * step if isinstance(t, int) else pl.multiple_of(t * step, step)
            product = lax.dot_general(
                mine[...].reshape(lines * pno_count, dom_count),
                right[pl.ds(at, step), :],
                (((1,), (1,)), ((), ())),
                preferred_element_type=jnp.float32,
            )
            made[i, :, :, pl.ds(at, step)] = product.astype(made.dtype).reshape(
                lines, pno_count, step
            )
            return carry

        if row_count == step:
            tile(0, 0)
        else:
            lax.fori_loop(0, row_count // step, tile, 0)
        copy(made.at[i], outs[i], out_sem).start()
    for i in range(inner):
        copy(made.at[i], outs[i], out_sem).wait()


def project(blocks, kind, parts, pieces, row_count, tokens):
    group = len(blocks)
    inner = group // 2
    slots, pno_count, dom_count = blocks[0].shape
    capacity = slots // 2
    dtype = blocks[0].dtype
    out = jax.ShapeDtypeStruct((slots, pno_count, row_count), dtype)
    return pl.pallas_call(
        functools.partial(project_kernel, group, capacity, kind, tuple(pieces)),
        out_shape=(out,) * inner,
        in_specs=[ANY] * (group + len(parts) + len(tokens)),
        out_specs=(ANY,) * inner,
        scratch_shapes=[
            pltpu.VMEM((group * capacity, pno_count, dom_count), dtype),
            pltpu.VMEM((row_count, dom_count), dtype),
            pltpu.VMEM((inner, slots, pno_count, row_count), dtype),
            pltpu.SemaphoreType.DMA((inner,)),
            pltpu.SemaphoreType.DMA,
            pltpu.SemaphoreType.DMA,
        ],
        compiler_params=pltpu.CompilerParams(vmem_limit_bytes=24 << 20),
        cost_estimate=pl.CostEstimate(
            flops=2 * group * capacity * pno_count * dom_count * row_count,
            transcendentals=0,
            bytes_accessed=2 * group * capacity * pno_count * dom_count,
        ),
    )(*blocks, *parts, *tokens)


def gather_sides(near, far, spans, slots, held, sem):
    inner = len(near)
    low, width = spans[0][0], sum(size for _, size in spans)
    for i in range(inner):
        copy(
            near[i].at[pl.ds(0, slots), :, pl.ds(low, width)],
            held.at[pl.ds(i * slots, slots)],
            sem,
        ).start()
        for c, (begin, size) in enumerate(spans):
            copy(
                far[c * inner + i].at[pl.ds(0, slots)],
                held.at[pl.ds((inner + i) * slots, slots), :, pl.ds(begin - low, size)],
                sem,
            ).start()


def overlap(first, second, limits, low):
    if low < limits[2]:
        lane = lax.broadcasted_iota(jnp.int32, (1, second.shape[1]), 1) + low
        apart = (lane < limits[0]) != (lane < limits[1])
        second = second * jnp.where(apart, 0.0, 1.0).astype(second.dtype)
    return lax.dot_general(
        first, second, (((1,), (1,)), ((), ())), preferred_element_type=jnp.float32
    )


def relay_kernel(inner, spans, margin, rows, offsets, before, *refs):
    near, far = refs[:inner], refs[inner : 2 * inner]
    sent, coupling, held, sem = refs[-4:]
    low = spans[0][0]
    pair_count = sent.shape[0]
    gather_sides(near, far, spans, near[0].shape[0], held, sem)
    copy(held, held, sem).wait()

    def choose(n, carry):
        sent[n] = held[jnp.maximum(jnp.maximum(rows[1, 2 * n], rows[1, 2 * n + 1]), 0)]
        return carry

    lax.fori_loop(0, pair_count, choose, 0, unroll=4)
    for h in range(2):

        def one_pair(n, carry, h=h):
            first, second = rows[h, 2 * n], rows[h, 2 * n + 1]
            product = overlap(
                held[jnp.maximum(first, 0)],
                held[jnp.maximum(second, 0)],
                (offsets[h, 2 * n], offsets[h, 2 * n + 1], margin),
                low,
            )
            product = jnp.where((first >= 0) & (second >= 0), product, 0.0)
            coupling[h, n] = product if low == 0 else product + before[h, n]
            return carry

        lax.fori_loop(0, pair_count, one_pair, 0, unroll=4)


def relay(rows, offsets, before, near, far, span, margin, tokens):
    inner = len(near)
    slots, pno_count, _ = near[0].shape
    pair_count = rows.shape[1] // 2
    return pl.pallas_call(
        functools.partial(relay_kernel, inner, (span,), margin),
        out_shape=(
            jax.ShapeDtypeStruct((pair_count, pno_count, span[1]), near[0].dtype),
            jax.ShapeDtypeStruct((2, pair_count, pno_count, pno_count), jnp.float32),
        ),
        in_specs=[SMEM, SMEM, VMEM] + [ANY] * (len(near) + len(far) + len(tokens)),
        out_specs=(VMEM, VMEM),
        scratch_shapes=[
            pltpu.VMEM((2 * inner * slots, pno_count, span[1]), near[0].dtype),
            pltpu.SemaphoreType.DMA,
        ],
        compiler_params=pltpu.CompilerParams(vmem_limit_bytes=24 << 20),
    )(rows, offsets, before, *near, *far, *tokens)


def mixed_pairs(inner, spans, margin, rows, offsets, near, far, others, held, sem, write):
    low = spans[0][0]
    slots = near[0].shape[0] // 2
    pair_count = others[0].shape[0]
    at = 2 * inner * slots
    gather_sides(near, far, spans, slots, held, sem)
    for other, (begin, size) in zip(others, spans):
        copy(
            other, held.at[pl.ds(at, pair_count), :, pl.ds(begin - low, size)], sem
        ).start()
    copy(held, held, sem).wait()

    def one_pair(n, carry):
        first, second = rows[0, 2 * n], rows[0, 2 * n + 1]
        product = overlap(
            held[jnp.where(first >= 0, first, at + n)],
            held[jnp.where(second >= 0, second, at + n)],
            (offsets[0, 2 * n], offsets[0, 2 * n + 1], margin),
            low,
        )
        write(n, jnp.where((first >= 0) != (second >= 0), product, 0.0))
        return carry

    lax.fori_loop(0, pair_count, one_pair, 0, unroll=4)


def mixed_kernel(inner, spans, margin, rows, offsets, *refs):
    near, refs = refs[:inner], refs[inner:]
    far, refs = refs[: inner * len(spans)], refs[inner * len(spans) :]
    others = refs[: len(spans)]
    coupling, held, sem = refs[-3:]

    def write(n, product):
        coupling[n] = product

    mixed_pairs(inner, spans, margin, rows, offsets, near, far, others, held, sem, write)


def finish_kernel(inner, spans, margin, rows, offsets, here, there, before, denominator, *refs):
    near, refs = refs[:inner], refs[inner:]
    far, refs = refs[: inner * len(spans)], refs[inner * len(spans) :]
    others = refs[: len(spans)]
    amplitude, energy, coupling, held, sem = refs[-5:]

    def write(n, product):
        coupling[n] = product

    mixed_pairs(inner, spans, margin, rows, offsets, near, far, others, held, sem, write)
    total = coupling[...] + before[...] + here[0] + there[...]
    result = -total / denominator[...]
    amplitude[...] = result
    parts = total * (2.0 * result - jnp.swapaxes(result, 1, 2))
    energy[...] = jnp.sum(jnp.sum(parts, axis=1), axis=1, keepdims=True)


def mixed(rows, offsets, near, far, others, spans, margin, tokens, finals):
    inner = len(near)
    slots, pno_count, _ = near[0].shape
    pair_count = rows.shape[1] // 2
    width = sum(size for _, size in spans)
    square = jax.ShapeDtypeStruct((pair_count, pno_count, pno_count), jnp.float32)
    line = jax.ShapeDtypeStruct((pair_count, 1), jnp.float32)
    scratch = [
        pltpu.VMEM((inner * slots + pair_count, pno_count, width), near[0].dtype),
        pltpu.SemaphoreType.DMA,
    ]
    if finals:
        scratch = [pltpu.VMEM(square.shape, jnp.float32)] + scratch
    return pl.pallas_call(
        functools.partial(
            finish_kernel if finals else mixed_kernel, inner, tuple(spans), margin
        ),
        out_shape=(square, line) if finals else square,
        in_specs=[SMEM] * 2
        + [VMEM] * len(finals)
        + [ANY] * (len(near) + len(far) + len(others) + len(tokens)),
        out_specs=(VMEM, VMEM) if finals else VMEM,
        scratch_shapes=scratch,
        compiler_params=pltpu.CompilerParams(vmem_limit_bytes=24 << 20),
    )(rows, offsets, *finals, *near, *far, *others, *tokens)


def slots_of(orbs):
    sequence = jnp.arange(orbs.shape[1], dtype=jnp.int32)
    same = orbs[:, :, None] == orbs[:, None, :]
    earlier = sequence[None, None, :] < sequence[None, :, None]
    return jnp.sum(jnp.where(same & earlier, 1, 0), axis=2).astype(jnp.int32)


def chunk_spans(fit_rows):
    sizes, start = [], 0
    body = (fit_rows - LAST) // 128
    for c in range(3):
        sizes.append(128 * (body // 3 + (1 if c < body % 3 else 0)))
    spans = []
    for size in sizes + [LAST]:
        spans.append((start, size))
        start += size
    return spans


def on_device(raw_ints, fit_inverse, pair_orbs, pno_coef, pno_energy, occ_energy, fit_offset):
    orb_count = lax.axis_size("orb")
    region, me = lax.axis_index("aux"), lax.axis_index("orb")
    group = orb_count // 2
    inner = group // 2
    pair_count = pair_orbs.shape[0]
    pno_count, dom_count = pno_coef.shape[2:]
    side_count = 2 * pair_count
    capacity = max(2, 4 * pair_count // orb_count)
    fit_rows = fit_inverse.shape[1]
    margin = fit_rows // 4

    def across(array, mask):
        return lax.ppermute(array, "orb", [(i, i ^ mask) for i in range(orb_count)])

    own_orbs = pair_orbs.reshape(side_count)
    place = jnp.stack([region, me]).astype(jnp.int32)
    half = dom_count // 2
    raw_parts = []
    for k in range(2):
        part = lax.all_to_all(
            raw_ints[:, :, :, k * half : (k + 1) * half],
            "aux",
            split_axis=0,
            concat_axis=2,
            tiled=True,
        )
        raw_parts.append(part[0, 0])
    packed = pack(
        own_orbs, place, pno_coef.reshape(side_count, pno_count, dom_count), group, capacity
    )
    blocks = [packed[0]]
    for m in range(1, group):
        blocks.append(across(packed[m], m))
    own_offset = fit_offset[region * orb_count + me]
    turned = lax.optimization_barrier(jnp.roll(fit_inverse[0], own_offset, axis=0))
    orbs = jnp.stack([own_orbs, across(own_orbs, inner)])
    differs = orbs ^ me
    line = jnp.where((differs & group) != 0, inner, 0) + (differs & (inner - 1))
    home = jnp.arange(2, dtype=jnp.int32)[:, None]
    position = slots_of(orbs)
    there = (differs & inner) != 0
    rows = jnp.where(there, -1, line * 2 * capacity + home * capacity + position)
    rows_home = jnp.where(there, -1, line * capacity + position)
    orb_total = occ_energy.shape[0]
    global_orb = region * orb_count + orbs
    selector = global_orb[:, :, None] == jnp.arange(orb_total, dtype=jnp.int32)[None, None, :]
    offsets = jnp.sum(jnp.where(selector, fit_offset[None, None, :], 0), axis=2)
    occupied = jnp.sum(jnp.where(selector[0], occ_energy[None, :], 0.0), axis=1)
    occupied = occupied.reshape(pair_count, 2)
    denominator = (
        pno_energy[:, 0, :, None]
        + pno_energy[:, 1, None, :]
        - occupied[:, 0, None, None]
        - occupied[:, 1, None, None]
    )
    spans = chunk_spans(fit_rows)
    fitted, mirrored = [], []
    for k in range(2):
        fitted.append(
            jnp.dot(turned, raw_parts[k], preferred_element_type=jnp.float32).astype(jnp.bfloat16)
        )
        if k == 0:
            mirrored.append(across(fitted[0], group))
        else:
            for begin, size in spans:
                mirrored.append(across(fitted[1][begin : begin + size], group))

    def hop(outs):
        return [outs[0]] + [across(outs[i], i) for i in range(1, inner)]

    near = project(blocks, 0, fitted, [(0, 0, half), (0, half, half)], fit_rows, [])
    near = hop(near)
    far, others, tokens = [], [], []
    here = jnp.zeros((8, 128), jnp.float32)
    body = None
    for c, span in enumerate(spans):
        final = c == len(spans) - 1
        parts = project(
            blocks,
            1,
            [mirrored[0], mirrored[1 + c]],
            [(span[0], 0, half), (0, half, half)],
            span[1],
            tokens,
        )
        if final:
            body = mixed(
                rows_home,
                offsets,
                near,
                far[0] + far[1],
                others[:2],
                spans[:2],
                margin,
                [parts[0]],
                [],
            )
        far.append(hop(parts))
        sent, here = relay(rows, offsets, here, near, far[c], span, margin, [body] if final else [])
        tokens = [here]
        others.append(across(sent, inner))
    amplitude, energy = mixed(
        rows_home,
        offsets,
        near,
        far[2] + far[3],
        others[2:],
        spans[2:],
        margin,
        [],
        [here, across(here[1], inner), body, denominator],
    )
    return (amplitude.reshape(pair_count, pno_count * pno_count), energy.reshape(pair_count))


def solution(mesh):
    return jax.shard_map(
        on_device,
        mesh=mesh,
        in_specs=(
            P(None, "orb", "aux", None),
            P(("aux", "orb"), None, None),
            P(("aux", "orb"), None),
            P(("aux", "orb"), None, None, None),
            P(("aux", "orb"), None, None),
            P(),
            P(),
        ),
        out_specs=(P(("aux", "orb"), None), P(("aux", "orb"))),
        check_vma=False,
    )
```

time: 371 us -> 264 us (0.71)
  blocking collectives: 145 us -> 0 us
  local copies, waits for them, and re-layouts: 74.5 us -> 18.5 us
  Pallas kernels: 0 us -> 42.9 us
  waiting for transfers between devices: 119 us -> 151 us
  starting transfers between devices: 9.69 us -> 35.5 us
  matrix products: 19.8 us -> 6.92 us
  other arithmetic: 1.52 us -> 5.72 us
    all_to_all x1 -> x0, blocking collectives: 145 us -> none  [on_device(): lax.all_to_all(outgoing, 'orb', split_axis=0, concat_axis=0, tiled=True)]
    ppermute x0 -> x19, waiting for transfers between devices: none -> 132 us  [across(): return lax.ppermute(array, 'orb', [(i, i ^ mask) for i in range(orb_count)])]
    all_to_all x2, waiting for transfers between devices: 119 us -> 19.4 us  [on_device(): lax.all_to_all(raw_ints[:, :, :, k * half:(k + 1) * half], 'aux', split_a...]
    gather x48 -> x0, local copies, waits for them, and re-layouts: 56.3 us -> none
    pallas_call x0 -> x12, Pallas kernels: none -> 42.9 us  [the longest x5 22 us: project(): pl.pallas_call(functools.partial(project_kernel, group, capacity, kind, t...]
    ppermute x0 -> x19, starting transfers between devices: none -> 26.8 us  [across(): return lax.ppermute(array, 'orb', [(i, i ^ mask) for i in range(orb_count)])]
    dot_general x4 -> x2, matrix products: 19.8 us -> 6.92 us  [on_device(): jnp.dot(turned, raw_parts[k], preferred_element_type=jnp.float32)]
    slice x0 -> x5, local copies, waits for them, and re-layouts: none -> 7.96 us  [the longest x1 3.87 us: on_device(): raw_ints[:, :, :, k * half:(k + 1) * half]]
  transfers between devices with their start and end apart: 2 -> 21, of which waited for: 2 -> 10; matrix products, arithmetic and copies ran while one was open for 3% -> 7% of each run, Pallas kernels for 0% -> 14%
where the time goes in v1:
time: 264 us; the launch traced here: 263 us
  waiting for transfers between devices  151 us (57%)
  Pallas kernels  42.9 us (16%)
  starting transfers between devices  35.5 us (13%)
  local copies, waits for them, and re-layouts  18.5 us (7%)
  matrix products  6.92 us (3%)
  other arithmetic  5.72 us (2%)
  between operations  2.73 us (1%)
    ppermute x19, waiting for transfers between devices, across(): return lax.ppermute(array, 'orb', [(i, i ^ mask) for i in range(orb_count)])  132 us
    ppermute x19, starting transfers between devices, across(): return lax.ppermute(array, 'orb', [(i, i ^ mask) for i in range(orb_count)])  26.8 us
    pallas_call x5, Pallas kernels, project(): pl.pallas_call(functools.partial(project_kernel, group, capacity, kind, t...  22 us
    all_to_all x2, waiting for transfers between devices, on_device(): lax.all_to_all(raw_ints[:, :, :, k * half:(k + 1) * half], 'aux', split_a...  19.4 us
    pallas_call x4, Pallas kernels, relay(): pl.pallas_call(functools.partial(relay_kernel, inner, (span,), margin), o...  10.6 us
    all_to_all x2, starting transfers between devices, on_device(): lax.all_to_all(raw_ints[:, :, :, k * half:(k + 1) * half], 'aux', split_a...  8.71 us
    unnamed x55, local copies, waits for them, and re-layouts  7.24 us
    dot_general x2, matrix products, on_device(): jnp.dot(turned, raw_parts[k], preferred_element_type=jnp.float32)  6.92 us
  transfers between devices with their start and end apart: 21, of which 10 were waited for; matrix products, arithmetic and copies ran while one was open for 7% of the time, Pallas kernels for 14%

profile of v1, /device:TPU:0, one launch (start us, length us, event | category | flops | bytes accessed | tf_op | source)
XLA Modules:
  0.0 263.4 jit_solution(3456082482031158816)
XLA Ops:
  0.6 3.9 %fusion.2 = (bf16[4,1,256,768]{3,2,1,0:T(8,128)(2,1)}, bf16[4,1,256,768]{3,2,1,0:T(8,128)(2,1)}) fusion(bf16[4,1,256,1536]{3,2,1,0:T(8,128)(2,1)} %param.7), kind=kLoop, calls=%fused_computation.24 | loop fusion | bytes 6291456 | tf_op jit(solution)/shard_map/slice | solution.py:354
  4.5 4.4 %all-to-all-start = ((bf16[4,1,256,768]{3,2,1,0:T(8,128)(2,1)}), bf16[4,1,256,768]{3,2,1,0:T(8,128)(2,1)S(1)}, u32[]{:S(2)}, u32[]{:S(2)}) async-start(bf16[4,1,256,768]{3,2,1,0:T(8,128)(2,1)} %get-tuple-element.53), calls=%async_computation | async-start | bytes 3145728 | tf_op jit(solution)/shard_map/all_to_all | solution.py:353
  9.6 19.4 %all-to-all-done = bf16[4,1,256,768]{3,2,1,0:T(8,128)(2,1)S(1)} async-done(((bf16[4,1,256,768]{3,2,1,0:T(8,128)(2,1)}), bf16[4,1,256,768]{3,2,1,0:T(8,128)(2,1)S(1)}, u32[]{:S(2)}, u32[]{:S(2)}) %all-to-all-start) | async-done | bytes 1572896 | tf_op jit(solution)/shard_map/all_to_all | solution.py:353
  30.1 4.3 %all-to-all-start.1 = ((bf16[4,1,256,768]{3,2,1,0:T(8,128)(2,1)}), bf16[4,1,256,768]{3,2,1,0:T(8,128)(2,1)}, u32[]{:S(2)}, u32[]{:S(2)}) async-start(bf16[4,1,256,768]{3,2,1,0:T(8,128)(2,1)} %get-tuple-element.52), calls=%async_computation.1 | async-start | bytes 3145728 | tf_op jit(solution)/shard_map/all_to_all | solution.py:353
  35.0 5.3 %pack.1 = (bf16[16,32,1536]{2,1,0:T(8,128)(2,1)}, bf16[16,32,1536]{2,1,0:T(8,128)(2,1)}, bf16[16,32,1536]{2,1,0:T(8,128)(2,1)}, bf16[16,32,1536]{2,1,0:T(8,128)(2,1)}) custom-call(s32[32]{0:T(128)} %reshape.71.orbs, s32[2]{0:T(128)} %pad_add_fusion.1.place, bf16[32,32,1536]{2,1,0:T(8,128)(2,1)} %bitcast.20), custom_call_target="tpu_custom_call" | custom-call | bytes 9437184 | tf_op jit(solution)/shard_map/pack/pallas_call | solution.py:60
  40.3 2.4 collective-permute-start.1
  46.5 3.7 %fusion = bf16[1024,1024]{1,0:T(8,128)(2,1)S(1)} fusion(s32[]{:T(128)S(6)} %select_n.46, bf16[1024,1024]{1,0:T(8,128)(2,1)} %bitcast.21), kind=kLoop, calls=%fused_computation.2 | loop fusion | flops 4194304 | bytes 4194308 | tf_op jit(solution)/shard_map/jit(_roll_dynamic)/concatenate | solution.py:368
  50.2 3.0 %convolution_convert_fusion.1.refs_4_ = bf16[1024,768]{1,0:T(8,128)(2,1)} fusion(bf16[1024,1024]{1,0:T(8,128)(2,1)S(1)} %fusion, bf16[1024,768]{1,0:T(8,128)(2,1)S(1)} %bitcast.22), kind=kOutput, calls=%fused_computation.4 | convolution fusion | flops 1611399168 | bytes 5242880 | tf_op jit(solution)/shard_map/dot_general | solution.py:393
  53.2 3.0 %collective-permute-start.5 = (bf16[1024,768]{1,0:T(8,128)(2,1)}, bf16[1024,768]{1,0:T(8,128)(2,1)}, u32[]{:S(2)}, u32[]{:S(2)}) collective-permute-start(bf16[1024,768]{1,0:T(8,128)(2,1)} %convolution_convert_fusion.1.refs_4_), channel_id=1, source_target_pairs={{0,4},{1,5},{2,6},{3,7},{4,0},{5,1},{6,2},{7,3},{8,12},{9,13},{10,... | collective-permute-start | bytes 4718600 | tf_op jit(solution)/shard_map/ppermute | solution.py:346
  57.8 3.9 %convolution_convert_fusion.refs_5_ = bf16[1024,768]{1,0:T(8,128)(2,1)S(1)} fusion(bf16[1024,1024]{1,0:T(8,128)(2,1)} %copy-done.17, bf16[1024,768]{1,0:T(8,128)(2,1)} %bitcast.7), kind=kOutput, calls=%fused_computation.3 | convolution fusion | flops 1611399168 | bytes 5242880 | tf_op jit(solution)/shard_map/dot_general | solution.py:393
  62.7 15.2 %collective-permute-done.1.refs_1_ = bf16[16,32,1536]{2,1,0:T(8,128)(2,1)S(1)} collective-permute-done((bf16[16,32,1536]{2,1,0:T(8,128)(2,1)}, bf16[16,32,1536]{2,1,0:T(8,128)(2,1)S(1)}, u32[]{:S(2)}, u32[]{:S(2)}) %collective-permute-start.1) | collective-permute-done | bytes 1572896 | tf_op jit(solution)/shard_map/ppermute | solution.py:346
  77.9 2.8 %collective-permute-start.6 = (bf16[384,768]{1,0:T(8,128)(2,1)}, bf16[384,768]{1,0:T(8,128)(2,1)S(1)}, u32[]{:S(2)}, u32[]{:S(2)}) collective-permute-start(bf16[384,768]{1,0:T(8,128)(2,1)} %slice.48), channel_id=1, source_target_pairs={{0,4},{1,5},{2,6},{3,7},{4,0},{5,1},{6,2},{7,3},{8,12},{9,13},{10,... | collective-permute-start | bytes 1769480 | tf_op jit(solution)/shard_map/ppermute | solution.py:346
  80.7 45.9 %collective-permute-done.2.refs_2_ = bf16[16,32,1536]{2,1,0:T(8,128)(2,1)} collective-permute-done((bf16[16,32,1536]{2,1,0:T(8,128)(2,1)}, bf16[16,32,1536]{2,1,0:T(8,128)(2,1)}, u32[]{:S(2)}, u32[]{:S(2)}) %collective-permute-start.2) | collective-permute-done | bytes 1572896 | tf_op jit(solution)/shard_map/ppermute | solution.py:346
  126.6 32.7 %collective-permute-done.3.refs_3_ = bf16[16,32,1536]{2,1,0:T(8,128)(2,1)} collective-permute-done((bf16[16,32,1536]{2,1,0:T(8,128)(2,1)}, bf16[16,32,1536]{2,1,0:T(8,128)(2,1)}, u32[]{:S(2)}, u32[]{:S(2)}) %collective-permute-start.3) | collective-permute-done | bytes 1572896 | tf_op jit(solution)/shard_map/ppermute | solution.py:346
  159.3 7.6 %shard_map.86 = (bf16[16,32,1024]{2,1,0:T(8,128)(2,1)S(1)}, bf16[16,32,1024]{2,1,0:T(8,128)(2,1)}) custom-call(bf16[16,32,1536]{2,1,0:T(8,128)(2,1)S(1)} %copy-done, bf16[16,32,1536]{2,1,0:T(8,128)(2,1)S(1)} %collective-permute-done.1.refs_1_, bf16[16,32,1536]{2,1,0:T(8,128)(2,1)} %collective-permute-done.2.refs_2_, ...), custom_call_target="tpu_custom_call" | custom-call | flops 3221225472 | bytes 3145728 | tf_op jit(solution)/shard_map/pallas_call | solution.py:133
  174.2 3.7 %shard_map.87 = (bf16[16,32,384]{2,1,0:T(8,128)(2,1)S(1)}, bf16[16,32,384]{2,1,0:T(8,128)(2,1)S(1)}) custom-call(bf16[16,32,1536]{2,1,0:T(8,128)(2,1)S(1)} %copy-done.1, bf16[16,32,1536]{2,1,0:T(8,128)(2,1)S(1)} %copy-done.3, bf16[16,32,1536]{2,1,0:T(8,128)(2,1)} %collective-permute-done.2.refs_2_, bf16[16,32,1536]{2,1,0:T(8,128)(2,1)} %collective-permute-done.3.refs_3_, ...), custom_call_target="tpu_custom_call" | custom-call | flops 1207959552 | bytes 3145728 | tf_op jit(solution)/shard_map/pallas_call | solution.py:133
  181.0 12.2 %collective-permute-done.4.refs_1_ = bf16[16,32,1024]{2,1,0:T(8,128)(2,1)S(1)} collective-permute-done((bf16[16,32,1024]{2,1,0:T(8,128)(2,1)}, bf16[16,32,1024]{2,1,0:T(8,128)(2,1)S(1)}, u32[]{:S(2)}, u32[]{:S(2)}) %collective-permute-start.4) | collective-permute-done | bytes 1048608 | tf_op jit(solution)/shard_map/ppermute | solution.py:346
  193.2 7.0 %collective-permute-done.7.refs_3_ = bf16[16,32,384]{2,1,0:T(8,128)(2,1)S(1)} collective-permute-done((bf16[16,32,384]{2,1,0:T(8,128)(2,1)S(1)}, bf16[16,32,384]{2,1,0:T(8,128)(2,1)S(1)}, u32[]{:S(2)}, u32[]{:S(2)}) %collective-permute-start.7) | collective-permute-done | bytes 393248 | tf_op jit(solution)/shard_map/ppermute | solution.py:346
  200.3 3.2 %shard_map.88 = (bf16[16,32,384]{2,1,0:T(8,128)(2,1)}, f32[2,16,32,32]{3,2,1,0:T(8,128)S(1)}) custom-call(s32[2,32]{1,0:T(2,128)S(1)} %get-tuple-element.58.rows, s32[2,32]{1,0:T(2,128)S(1)} %select_reduce_fusion.offsets, f32[8,128]{1,0:T(8,128)S(1)} %broadcast_in_dim.55.before, bf16[16,32,1024]{2,1,0:T(8,128)(2,1)S(1)} %get-tuple-element.30.refs_0_, ...), custom_call_target="tpu_custom_call" | custom-call | tf_op jit(solution)/shard_map/pallas_call | solution.py:216
  203.5 3.3 %shard_map.89 = (bf16[16,32,256]{2,1,0:T(8,128)(2,1)S(1)}, bf16[16,32,256]{2,1,0:T(8,128)(2,1)S(1)}) custom-call(bf16[16,32,1536]{2,1,0:T(8,128)(2,1)S(1)} %copy-done.1, bf16[16,32,1536]{2,1,0:T(8,128)(2,1)S(1)} %copy-done.4, bf16[16,32,1536]{2,1,0:T(8,128)(2,1)} %collective-permute-done.2.refs_2_, bf16[16,32,1536]{2,1,0:T(8,128)(2,1)} %collective-permute-done.3.refs_3_, ...), custom_call_target="tpu_custom_call" | custom-call | flops 805306368 | bytes 3145728 | tf_op jit(solution)/shard_map/pallas_call | solution.py:133
  208.3 5.6 %collective-permute-done.9.refs_3_.refs_5_ = bf16[16,32,256]{2,1,0:T(8,128)(2,1)S(1)} collective-permute-done((bf16[16,32,256]{2,1,0:T(8,128)(2,1)S(1)}, bf16[16,32,256]{2,1,0:T(8,128)(2,1)S(1)}, u32[]{:S(2)}, u32[]{:S(2)}) %collective-permute-start.9) | collective-permute-done | bytes 262176 | tf_op jit(solution)/shard_map/ppermute | solution.py:346
  213.8 2.6 shard_map.90
  216.5 3.3 %shard_map.91 = (bf16[16,32,256]{2,1,0:T(8,128)(2,1)S(1)}, bf16[16,32,256]{2,1,0:T(8,128)(2,1)S(1)}) custom-call(bf16[16,32,1536]{2,1,0:T(8,128)(2,1)S(1)} %copy-done.1, bf16[16,32,1536]{2,1,0:T(8,128)(2,1)S(1)} %copy-done.4, bf16[16,32,1536]{2,1,0:T(8,128)(2,1)} %collective-permute-done.2.refs_2_, bf16[16,32,1536]{2,1,0:T(8,128)(2,1)} %collective-permute-done.3.refs_3_, ...), custom_call_target="tpu_custom_call" | custom-call | flops 805306368 | bytes 3145728 | tf_op jit(solution)/shard_map/pallas_call | solution.py:133
  223.4 3.4 %collective-permute-start.14 = (bf16[16,32,384]{2,1,0:T(8,128)(2,1)}, bf16[16,32,384]{2,1,0:T(8,128)(2,1)}, u32[]{:S(2)}, u32[]{:S(2)}) collective-permute-start(bf16[16,32,384]{2,1,0:T(8,128)(2,1)} %get-tuple-element.43), channel_id=1, source_target_pairs={{0,2},{1,3},{2,0},{3,1},{4,6},{5,7},{6,4},{7,5},{8,10},{9,11},{10,... | collective-permute-start | bytes 1179656 | tf_op jit(solution)/shard_map/ppermute | solution.py:346
  226.9 2.0 shard_map.92
  229.7 2.3 collective-permute-done.12.refs_5_
  232.0 4.0 %shard_map.93 = (bf16[16,32,128]{2,1,0:T(8,128)(2,1)S(1)}, bf16[16,32,128]{2,1,0:T(8,128)(2,1)}) custom-call(bf16[16,32,1536]{2,1,0:T(8,128)(2,1)S(1)} %copy-done.1, bf16[16,32,1536]{2,1,0:T(8,128)(2,1)S(1)} %copy-done.4, bf16[16,32,1536]{2,1,0:T(8,128)(2,1)} %collective-permute-done.2.refs_2_, bf16[16,32,1536]{2,1,0:T(8,128)(2,1)} %collective-permute-done.3.refs_3_, ...), custom_call_target="tpu_custom_call" | custom-call | flops 402653184 | bytes 3145728 | tf_op jit(solution)/shard_map/pallas_call | solution.py:133
  239.1 5.3 %collective-permute-done.15.refs_7_ = bf16[16,32,256]{2,1,0:T(8,128)(2,1)} collective-permute-done((bf16[16,32,256]{2,1,0:T(8,128)(2,1)}, bf16[16,32,256]{2,1,0:T(8,128)(2,1)}, u32[]{:S(2)}, u32[]{:S(2)}) %collective-permute-start.15) | collective-permute-done | bytes 262176 | tf_op jit(solution)/shard_map/ppermute | solution.py:346
  246.3 2.5 shard_map.94.refs_4_.before
  248.9 2.9 %shard_map.95 = (bf16[16,32,128]{2,1,0:T(8,128)(2,1)S(1)}, f32[2,16,32,32]{3,2,1,0:T(8,128)S(1)}) custom-call(s32[2,32]{1,0:T(2,128)S(1)} %get-tuple-element.58.rows, s32[2,32]{1,0:T(2,128)S(1)} %select_reduce_fusion.offsets, f32[2,16,32,32]{3,2,1,0:T(8,128)S(1)} %get-tuple-element.40.refs_6_.before, bf16[16,32,1024]{2,1,0:T(8,128)(2,1)S(1)} %get-tuple-element.30.refs_0_, ...), custom_call_target="tpu_custom_call" | custom-call | tf_op jit(solution)/shard_map/pallas_call | solution.py:216
  254.1 5.5 %collective-permute-done.16.there = f32[16,32,32]{2,1,0:T(8,128)S(1)} collective-permute-done((f32[16,32,32]{2,1,0:T(8,128)S(1)}, f32[16,32,32]{2,1,0:T(8,128)S(1)}, u32[]{:S(2)}, u32[]{:S(2)}) %collective-permute-start.16) | collective-permute-done | bytes 65568 | tf_op jit(solution)/shard_map/ppermute | solution.py:346
  259.6 2.4 shard_map.96
  (104 shorter events, 32.0 us)
Async XLA Ops:
  4.5 24.4 %all-to-all-start = ((bf16[4,1,256,768]{3,2,1,0:T(8,128)(2,1)}), bf16[4,1,256,768]{3,2,1,0:T(8,128)(2,1)S(1)}, u32[]{:S(2)}, u32[]{:S(2)}) async-start(bf16[4,1,256,768]{3,2,1,0:T(8,128)(2,1)} %get-tuple-element.53), calls=%async_computation | async-start | bytes 3145728 | tf_op jit(solution)/shard_map/all_to_all | solution.py:353
  30.1 27.7 %all-to-all-start.1 = ((bf16[4,1,256,768]{3,2,1,0:T(8,128)(2,1)}), bf16[4,1,256,768]{3,2,1,0:T(8,128)(2,1)}, u32[]{:S(2)}, u32[]{:S(2)}) async-start(bf16[4,1,256,768]{3,2,1,0:T(8,128)(2,1)} %get-tuple-element.52), calls=%async_computation.1 | async-start | bytes 3145728 | tf_op jit(solution)/shard_map/all_to_all | solution.py:353
  35.0 9.2 %copy-start.25 = (s32[32]{0:T(128)S(1)}, s32[32]{0:T(128)}, u32[]{:S(2)}) copy-start(s32[32]{0:T(128)} %param.13) | copy-start | bytes 388
  40.3 37.6 %collective-permute-start.1 = (bf16[16,32,1536]{2,1,0:T(8,128)(2,1)}, bf16[16,32,1536]{2,1,0:T(8,128)(2,1)S(1)}, u32[]{:S(2)}, u32[]{:S(2)}) collective-permute-start(bf16[16,32,1536]{2,1,0:T(8,128)(2,1)} %get-tuple-element.27), channel_id=1, source_target_pairs={{0,1},{1,0},{2,3},{3,2},{4,5},{5,4},{6,7},{7,6},{8,9},{9,8},{10,11... | collective-permute-start | bytes 4718600 | tf_op jit(solution)/shard_map/ppermute | solution.py:346
  42.7 83.9 %collective-permute-start.2 = (bf16[16,32,1536]{2,1,0:T(8,128)(2,1)}, bf16[16,32,1536]{2,1,0:T(8,128)(2,1)}, u32[]{:S(2)}, u32[]{:S(2)}) collective-permute-start(bf16[16,32,1536]{2,1,0:T(8,128)(2,1)} %get-tuple-element.28), channel_id=1, source_target_pairs={{0,2},{1,3},{2,0},{3,1},{4,6},{5,7},{6,4},{7,5},{8,10},{9,11},{10,... | collective-permute-start | bytes 4718600 | tf_op jit(solution)/shard_map/ppermute | solution.py:346
  44.2 115.1 %collective-permute-start.3 = (bf16[16,32,1536]{2,1,0:T(8,128)(2,1)}, bf16[16,32,1536]{2,1,0:T(8,128)(2,1)}, u32[]{:S(2)}, u32[]{:S(2)}) collective-permute-start(bf16[16,32,1536]{2,1,0:T(8,128)(2,1)} %get-tuple-element.29), channel_id=1, source_target_pairs={{0,3},{1,2},{2,1},{3,0},{4,7},{5,6},{6,5},{7,4},{8,11},{9,10},{10,... | collective-permute-start | bytes 4718600 | tf_op jit(solution)/shard_map/ppermute | solution.py:346
  50.2 6.0 %copy-start.23 = (s32[32]{0:T(128)S(1)}, s32[32]{0:T(128)}, u32[]{:S(2)}) copy-start(s32[32]{0:T(128)} %reshape.71.orbs) | copy-start | bytes 388
  53.2 118.5 %collective-permute-start.5 = (bf16[1024,768]{1,0:T(8,128)(2,1)}, bf16[1024,768]{1,0:T(8,128)(2,1)}, u32[]{:S(2)}, u32[]{:S(2)}) collective-permute-start(bf16[1024,768]{1,0:T(8,128)(2,1)} %convolution_convert_fusion.1.refs_4_), channel_id=1, source_target_pairs={{0,4},{1,5},{2,6},{3,7},{4,0},{5,1},{6,2},{7,3},{8,12},{9,13},{10,... | collective-permute-start | bytes 4718600 | tf_op jit(solution)/shard_map/ppermute | solution.py:346
  56.2 112.5 %collective-permute-start = (s32[32]{0:T(128)S(1)}, s32[32]{0:T(128)S(1)}, u32[]{:S(2)}, u32[]{:S(2)}) collective-permute-start(s32[32]{0:T(128)S(1)} %copy-done.23), channel_id=1, source_target_pairs={{0,2},{1,3},{2,0},{3,1},{4,6},{5,7},{6,4},{7,5},{8,10},{9,11},{10,... | collective-permute-start | bytes 392 | tf_op jit(solution)/shard_map/ppermute | solution.py:346
  57.8 101.5 %copy-start = (bf16[16,32,1536]{2,1,0:T(8,128)(2,1)S(1)}, bf16[16,32,1536]{2,1,0:T(8,128)(2,1)}, u32[]{:S(2)}) copy-start(bf16[16,32,1536]{2,1,0:T(8,128)(2,1)} %get-tuple-element.26.refs_0_) | copy-start | bytes 4718596
  61.7 105.2 %copy-start.5 = (bf16[1024,768]{1,0:T(8,128)(2,1)}, bf16[1024,768]{1,0:T(8,128)(2,1)S(1)}, u32[]{:S(2)}) copy-start(bf16[1024,768]{1,0:T(8,128)(2,1)S(1)} %convolution_convert_fusion.refs_5_) | copy-start | bytes 4718596
  77.9 89.0 %copy-start.2 = (bf16[16,32,1536]{2,1,0:T(8,128)(2,1)}, bf16[16,32,1536]{2,1,0:T(8,128)(2,1)S(1)}, u32[]{:S(2)}) copy-start(bf16[16,32,1536]{2,1,0:T(8,128)(2,1)S(1)} %collective-permute-done.1.refs_1_) | copy-start | bytes 4718596
  77.9 93.0 %collective-permute-start.6 = (bf16[384,768]{1,0:T(8,128)(2,1)}, bf16[384,768]{1,0:T(8,128)(2,1)S(1)}, u32[]{:S(2)}, u32[]{:S(2)}) collective-permute-start(bf16[384,768]{1,0:T(8,128)(2,1)} %slice.48), channel_id=1, source_target_pairs={{0,4},{1,5},{2,6},{3,7},{4,0},{5,1},{6,2},{7,3},{8,12},{9,13},{10,... | collective-permute-start | bytes 1769480 | tf_op jit(solution)/shard_map/ppermute | solution.py:346
  166.9 26.3 %collective-permute-start.4 = (bf16[16,32,1024]{2,1,0:T(8,128)(2,1)}, bf16[16,32,1024]{2,1,0:T(8,128)(2,1)S(1)}, u32[]{:S(2)}, u32[]{:S(2)}) collective-permute-start(bf16[16,32,1024]{2,1,0:T(8,128)(2,1)} %get-tuple-element.31), channel_id=1, source_target_pairs={{0,1},{1,0},{2,3},{3,2},{4,5},{5,4},{6,7},{7,6},{8,9},{9,8},{10,11... | collective-permute-start | bytes 3145736 | tf_op jit(solution)/shard_map/ppermute | solution.py:346
  170.1 33.4 %collective-permute-start.8 = (bf16[256,768]{1,0:T(8,128)(2,1)S(1)}, bf16[256,768]{1,0:T(8,128)(2,1)S(1)}, u32[]{:S(2)}, u32[]{:S(2)}) collective-permute-start(bf16[256,768]{1,0:T(8,128)(2,1)S(1)} %get-tuple-element.55), channel_id=1, source_target_pairs={{0,4},{1,5},{2,6},{3,7},{4,0},{5,1},{6,2},{7,3},{8,12},{9,13},{10,... | collective-permute-start | bytes 1179656 | tf_op jit(solution)/shard_map/ppermute | solution.py:346
  177.9 25.5 %copy-start.4 = (bf16[16,32,1536]{2,1,0:T(8,128)(2,1)S(1)}, bf16[16,32,1536]{2,1,0:T(8,128)(2,1)}, u32[]{:S(2)}) copy-start(bf16[16,32,1536]{2,1,0:T(8,128)(2,1)} %copy-done.2) | copy-start | bytes 4718596
  177.9 22.3 %collective-permute-start.7 = (bf16[16,32,384]{2,1,0:T(8,128)(2,1)S(1)}, bf16[16,32,384]{2,1,0:T(8,128)(2,1)S(1)}, u32[]{:S(2)}, u32[]{:S(2)}) collective-permute-start(bf16[16,32,384]{2,1,0:T(8,128)(2,1)S(1)} %get-tuple-element.33), channel_id=1, source_target_pairs={{0,1},{1,0},{2,3},{3,2},{4,5},{5,4},{6,7},{7,6},{8,9},{9,8},{10,11... | collective-permute-start | bytes 1179656 | tf_op jit(solution)/shard_map/ppermute | solution.py:346
  179.8 36.7 %collective-permute-start.10 = (bf16[256,768]{1,0:T(8,128)(2,1)S(1)}, bf16[256,768]{1,0:T(8,128)(2,1)S(1)}, u32[]{:S(2)}, u32[]{:S(2)}) collective-permute-start(bf16[256,768]{1,0:T(8,128)(2,1)S(1)} %get-tuple-element.54), channel_id=1, source_target_pairs={{0,4},{1,5},{2,6},{3,7},{4,0},{5,1},{6,2},{7,3},{8,12},{9,13},{10,... | collective-permute-start | bytes 1179656 | tf_op jit(solution)/shard_map/ppermute | solution.py:346
  206.8 9.6 %copy-start.10 = (bf16[16,32,256]{2,1,0:T(8,128)(2,1)}, bf16[16,32,256]{2,1,0:T(8,128)(2,1)S(1)}, u32[]{:S(2)}) copy-start(bf16[16,32,256]{2,1,0:T(8,128)(2,1)S(1)} %get-tuple-element.35.refs_2_.refs_4_) | copy-start | bytes 786436
  206.8 7.0 %collective-permute-start.9 = (bf16[16,32,256]{2,1,0:T(8,128)(2,1)S(1)}, bf16[16,32,256]{2,1,0:T(8,128)(2,1)S(1)}, u32[]{:S(2)}, u32[]{:S(2)}) collective-permute-start(bf16[16,32,256]{2,1,0:T(8,128)(2,1)S(1)} %get-tuple-element.36), channel_id=1, source_target_pairs={{0,1},{1,0},{2,3},{3,2},{4,5},{5,4},{6,7},{7,6},{8,9},{9,8},{10,11... | collective-permute-start | bytes 786440 | tf_op jit(solution)/shard_map/ppermute | solution.py:346
  219.8 9.1 %copy-start.6 = (bf16[16,32,256]{2,1,0:T(8,128)(2,1)}, bf16[16,32,256]{2,1,0:T(8,128)(2,1)S(1)}, u32[]{:S(2)}) copy-start(bf16[16,32,256]{2,1,0:T(8,128)(2,1)S(1)} %get-tuple-element.38.refs_2_) | copy-start | bytes 786436
  219.8 7.1 %collective-permute-start.11 = (bf16[16,32,256]{2,1,0:T(8,128)(2,1)S(1)}, bf16[16,32,256]{2,1,0:T(8,128)(2,1)S(1)}, u32[]{:S(2)}, u32[]{:S(2)}) collective-permute-start(bf16[16,32,256]{2,1,0:T(8,128)(2,1)S(1)} %get-tuple-element.39), channel_id=1, source_target_pairs={{0,1},{1,0},{2,3},{3,2},{4,5},{5,4},{6,7},{7,6},{8,9},{9,8},{10,11... | collective-permute-start | bytes 786440 | tf_op jit(solution)/shard_map/ppermute | solution.py:346
  222.6 9.4 %collective-permute-start.12 = (bf16[128,768]{1,0:T(8,128)(2,1)S(1)}, bf16[128,768]{1,0:T(8,128)(2,1)S(1)}, u32[]{:S(2)}, u32[]{:S(2)}) collective-permute-start(bf16[128,768]{1,0:T(8,128)(2,1)S(1)} %slice.51), channel_id=1, source_target_pairs={{0,4},{1,5},{2,6},{3,7},{4,0},{5,1},{6,2},{7,3},{8,12},{9,13},{10,... | collective-permute-start | bytes 589832 | tf_op jit(solution)/shard_map/ppermute | solution.py:346
  223.4 15.6 %collective-permute-start.14 = (bf16[16,32,384]{2,1,0:T(8,128)(2,1)}, bf16[16,32,384]{2,1,0:T(8,128)(2,1)}, u32[]{:S(2)}, u32[]{:S(2)}) collective-permute-start(bf16[16,32,384]{2,1,0:T(8,128)(2,1)} %get-tuple-element.43), channel_id=1, source_target_pairs={{0,2},{1,3},{2,0},{3,1},{4,6},{5,7},{6,4},{7,5},{8,10},{9,11},{10,... | collective-permute-start | bytes 1179656 | tf_op jit(solution)/shard_map/ppermute | solution.py:346
  226.8 17.6 %collective-permute-start.15 = (bf16[16,32,256]{2,1,0:T(8,128)(2,1)}, bf16[16,32,256]{2,1,0:T(8,128)(2,1)}, u32[]{:S(2)}, u32[]{:S(2)}) collective-permute-start(bf16[16,32,256]{2,1,0:T(8,128)(2,1)} %get-tuple-element.44), channel_id=1, source_target_pairs={{0,2},{1,3},{2,0},{3,1},{4,6},{5,7},{6,4},{7,5},{8,10},{9,11},{10,... | collective-permute-start | bytes 786440 | tf_op jit(solution)/shard_map/ppermute | solution.py:346
  232.0 5.2 %copy-start.26 = (f32[32]{0:T(128)S(1)}, f32[32]{0:T(128)}, u32[]{:S(2)}) copy-start(f32[32]{0:T(128)} %param.12) | copy-start | bytes 388
  236.0 12.9 %collective-permute-start.13 = (bf16[16,32,128]{2,1,0:T(8,128)(2,1)}, bf16[16,32,128]{2,1,0:T(8,128)(2,1)}, u32[]{:S(2)}, u32[]{:S(2)}) collective-permute-start(bf16[16,32,128]{2,1,0:T(8,128)(2,1)} %get-tuple-element.42), channel_id=1, source_target_pairs={{0,1},{1,0},{2,3},{3,2},{4,5},{5,4},{6,7},{7,6},{8,9},{9,8},{10,11... | collective-permute-start | bytes 393224 | tf_op jit(solution)/shard_map/ppermute | solution.py:346
  239.0 20.6 %collective-permute-start.17 = (bf16[16,32,256]{2,1,0:T(8,128)(2,1)}, bf16[16,32,256]{2,1,0:T(8,128)(2,1)S(1)}, u32[]{:S(2)}, u32[]{:S(2)}) collective-permute-start(bf16[16,32,256]{2,1,0:T(8,128)(2,1)} %copy-done.16), channel_id=1, source_target_pairs={{0,2},{1,3},{2,0},{3,1},{4,6},{5,7},{6,4},{7,5},{8,10},{9,11},{10,... | collective-permute-start | bytes 786440 | tf_op jit(solution)/shard_map/ppermute | solution.py:346
  248.8 10.8 %copy-start.7 = (bf16[16,32,256]{2,1,0:T(8,128)(2,1)S(1)}, bf16[16,32,256]{2,1,0:T(8,128)(2,1)}, u32[]{:S(2)}) copy-start(bf16[16,32,256]{2,1,0:T(8,128)(2,1)} %copy-done.6) | copy-start | bytes 786436
  248.9 10.8 %copy-start.9 = (bf16[16,32,256]{2,1,0:T(8,128)(2,1)S(1)}, bf16[16,32,256]{2,1,0:T(8,128)(2,1)}, u32[]{:S(2)}) copy-start(bf16[16,32,256]{2,1,0:T(8,128)(2,1)} %copy-done.8) | copy-start | bytes 786436
  251.8 7.8 %collective-permute-start.18 = (bf16[16,32,128]{2,1,0:T(8,128)(2,1)S(1)}, bf16[16,32,128]{2,1,0:T(8,128)(2,1)S(1)}, u32[]{:S(2)}, u32[]{:S(2)}) collective-permute-start(bf16[16,32,128]{2,1,0:T(8,128)(2,1)S(1)} %get-tuple-element.47), channel_id=1, source_target_pairs={{0,2},{1,3},{2,0},{3,1},{4,6},{5,7},{6,4},{7,5},{8,10},{9,11},{10,... | collective-permute-start | bytes 393224 | tf_op jit(solution)/shard_map/ppermute | solution.py:346
  252.8 6.8 %collective-permute-start.16 = (f32[16,32,32]{2,1,0:T(8,128)S(1)}, f32[16,32,32]{2,1,0:T(8,128)S(1)}, u32[]{:S(2)}, u32[]{:S(2)}) collective-permute-start(f32[16,32,32]{2,1,0:T(8,128)S(1)} %slice_bitcast_fusion), channel_id=1, source_target_pairs={{0,2},{1,3},{2,0},{3,1},{4,6},{5,7},{6,4},{7,5},{8,10},{9,11},{10,... | collective-permute-start | bytes 196616 | tf_op jit(solution)/shard_map/ppermute | solution.py:346
  (16 other events, 40.6 us)

commit v2 on v1

--- a/solution.py
+++ b/solution.py
@@ -7,7 +7,6 @@
 from jax.experimental.pallas import tpu as pltpu
 from jax.sharding import PartitionSpec as P
 
-LAST = 128
 SMEM = pl.BlockSpec(memory_space=pltpu.SMEM)
 VMEM = pl.BlockSpec(memory_space=pltpu.VMEM)
 ANY = pl.BlockSpec(memory_space=pl.ANY)
@@ -319,15 +318,8 @@
 
 
 def chunk_spans(fit_rows):
-    sizes, start = [], 0
-    body = (fit_rows - LAST) // 128
-    for c in range(3):
-        sizes.append(128 * (body // 3 + (1 if c < body % 3 else 0)))
-    spans = []
-    for size in sizes + [LAST]:
-        spans.append((start, size))
-        start += size
-    return spans
+    sizes = (fit_rows // 2, 3 * fit_rows // 8, fit_rows // 8)
+    return [(sum(sizes[:c]), size) for c, size in enumerate(sizes)]
 
 
 def on_device(raw_ints, fit_inverse, pair_orbs, pno_coef, pno_energy, occ_energy, fit_offset):
@@ -346,27 +338,32 @@
         return lax.ppermute(array, "orb", [(i, i ^ mask) for i in range(orb_count)])
 
     own_orbs = pair_orbs.reshape(side_count)
+    mate_orbs = across(own_orbs, inner)
     place = jnp.stack([region, me]).astype(jnp.int32)
     half = dom_count // 2
-    raw_parts = []
-    for k in range(2):
+
+    def exchange(array, k):
         part = lax.all_to_all(
-            raw_ints[:, :, :, k * half : (k + 1) * half],
+            array[:, :, :, k * half : (k + 1) * half],
             "aux",
             split_axis=0,
             concat_axis=2,
             tiled=True,
         )
-        raw_parts.append(part[0, 0])
+        return part[0, 0]
+
+    raw_parts = [exchange(raw_ints, 0)]
     packed = pack(
         own_orbs, place, pno_coef.reshape(side_count, pno_count, dom_count), group, capacity
     )
+    later, packed = lax.optimization_barrier((raw_ints, packed))
+    raw_parts.append(exchange(later, 1))
     blocks = [packed[0]]
     for m in range(1, group):
         blocks.append(across(packed[m], m))
     own_offset = fit_offset[region * orb_count + me]
     turned = lax.optimization_barrier(jnp.roll(fit_inverse[0], own_offset, axis=0))
-    orbs = jnp.stack([own_orbs, across(own_orbs, inner)])
+    orbs = jnp.stack([own_orbs, mate_orbs])
     differs = orbs ^ me
     line = jnp.where((differs & group) != 0, inner, 0) + (differs & (inner - 1))
     home = jnp.arange(2, dtype=jnp.int32)[:, None]
@@ -401,47 +398,52 @@
     def hop(outs):
         return [outs[0]] + [across(outs[i], i) for i in range(1, inner)]
 
-    near = project(blocks, 0, fitted, [(0, 0, half), (0, half, half)], fit_rows, [])
-    near = hop(near)
-    far, others, tokens = [], [], []
-    here = jnp.zeros((8, 128), jnp.float32)
-    body = None
-    for c, span in enumerate(spans):
-        final = c == len(spans) - 1
+    def project_far(c, tokens):
+        begin, size = spans[c]
         parts = project(
             blocks,
             1,
             [mirrored[0], mirrored[1 + c]],
-            [(span[0], 0, half), (0, half, half)],
-            span[1],
+            [(begin, 0, half), (0, half, half)],
+            size,
             tokens,
         )
-        if final:
-            body = mixed(
-                rows_home,
-                offsets,
-                near,
-                far[0] + far[1],
-                others[:2],
-                spans[:2],
-                margin,
-                [parts[0]],
-                [],
-            )
-        far.append(hop(parts))
-        sent, here = relay(rows, offsets, here, near, far[c], span, margin, [body] if final else [])
-        tokens = [here]
-        others.append(across(sent, inner))
+        return hop(parts)
+
+    def pass_on(c, before, tokens):
+        sent, here = relay(rows, offsets, before, near, far[c], spans[c], margin, tokens)
+        return across(sent, inner), here
+
+    near = project(
+        blocks,
+        0,
+        fitted,
+        [(0, 0, half), (0, half, half)],
+        fit_rows,
+        [denominator, rows, rows_home, offsets],
+    )
+    near = hop(near)
+    far, others = [None] * 3, [None] * 3
+    far[0] = project_far(0, [])
+    others[0], here = pass_on(0, jnp.zeros((8, 128), jnp.float32), [])
+    far[1] = project_far(1, [here])
+    far[2] = project_far(2, [far[1][0]])
+    others[1], here = pass_on(1, here, [far[2][0]])
+    others[2], here = pass_on(2, here, [])
+    there = across(here[1], inner)
+    body = mixed(
+        rows_home, offsets, near, far[0] + far[1], others[:2], spans[:2], margin, [here], []
+    )
     amplitude, energy = mixed(
         rows_home,
         offsets,
         near,
-        far[2] + far[3],
+        far[2],
         others[2:],
         spans[2:],
         margin,
         [],
-        [here, across(here[1], inner), body, denominator],
+        [here, there, body, denominator],
     )
     return (amplitude.reshape(pair_count, pno_count * pno_count), energy.reshape(pair_count))
 

time: 264 us -> 222 us (0.84)
  waiting for transfers between devices: 151 us -> 133 us
  local copies, waits for them, and re-layouts: 18.5 us -> 6.06 us
  Pallas kernels: 42.9 us -> 32.2 us
  starting transfers between devices: 35.5 us -> 31 us
    ppermute x19 -> x16, waiting for transfers between devices: 132 us -> 122 us  [across(): return lax.ppermute(array, 'orb', [(i, i ^ mask) for i in range(orb_count)])]
    all_to_all x2, waiting for transfers between devices: 19.4 us -> 11.5 us  [exchange(): lax.all_to_all(array[:, :, :, k * half:(k + 1) * half], 'aux', split_axis...]
    unnamed x55 -> x15, local copies, waits for them, and re-layouts: 7.24 us -> 0.12 us
    pallas_call x5 -> x4, Pallas kernels: 22 us -> 16.4 us  [project(): pl.pallas_call(functools.partial(project_kernel, group, capacity, kind, t...]
    ppermute x19 -> x16, starting transfers between devices: 26.8 us -> 22 us  [across(): return lax.ppermute(array, 'orb', [(i, i ^ mask) for i in range(orb_count)])]
    pallas_call x4 -> x3, Pallas kernels: 10.6 us -> 7.04 us  [relay(): pl.pallas_call(functools.partial(relay_kernel, inner, (span,), margin), o...]
    slice x3, local copies, waits for them, and re-layouts: 3.14 us -> 0.11 us  [on_device(): mirrored.append(across(fitted[1][begin:begin + size], group))]
  transfers between devices with their start and end apart: 21 -> 18, of which waited for: 10 -> 10; matrix products, arithmetic and copies ran while one was open for 7% -> 8% of each run, Pallas kernels for 14% -> 12%
where the time goes in v2:
time: 222 us; the launch traced here: 221 us
  waiting for transfers between devices  133 us (60%)
  Pallas kernels  32.2 us (15%)
  starting transfers between devices  31 us (14%)
  matrix products  8.93 us (4%)
  other arithmetic  7.11 us (3%)
  local copies, waits for them, and re-layouts  6.06 us (3%)
  between operations  2.88 us (1%)
    ppermute x16, waiting for transfers between devices, across(): return lax.ppermute(array, 'orb', [(i, i ^ mask) for i in range(orb_count)])  122 us
    ppermute x16, starting transfers between devices, across(): return lax.ppermute(array, 'orb', [(i, i ^ mask) for i in range(orb_count)])  22 us
    pallas_call x4, Pallas kernels, project(): pl.pallas_call(functools.partial(project_kernel, group, capacity, kind, t...  16.4 us
    all_to_all x2, waiting for transfers between devices, exchange(): lax.all_to_all(array[:, :, :, k * half:(k + 1) * half], 'aux', split_axis...  11.5 us
    all_to_all x2, starting transfers between devices, exchange(): lax.all_to_all(array[:, :, :, k * half:(k + 1) * half], 'aux', split_axis...  9.05 us
    dot_general x2, matrix products, on_device(): jnp.dot(turned, raw_parts[k], preferred_element_type=jnp.float32)  8.93 us
    pallas_call x3, Pallas kernels, relay(): pl.pallas_call(functools.partial(relay_kernel, inner, (span,), margin), o...  7.04 us
    pallas_call x1, Pallas kernels, pack(): pl.pallas_call(functools.partial(pack_kernel, group, capacity), out_shape...  5.35 us
  transfers between devices with their start and end apart: 18, of which 10 were waited for; matrix products, arithmetic and copies ran while one was open for 8% of the time, Pallas kernels for 12%

profile of v2, /device:TPU:0, one launch (start us, length us, event | category | flops | bytes accessed | tf_op | source)
XLA Modules:
  0.0 221.4 jit_solution(16466775900863743330)
XLA Ops:
  0.6 2.8 %slice.33 = bf16[4,1,256,768]{3,2,1,0:T(8,128)(2,1)} slice(bf16[4,1,256,1536]{3,2,1,0:T(8,128)(2,1)} %param.7), slice={[0:4], [0:1], [0:256], [0:768]} | slice | bytes 3145728 | tf_op jit(solution)/shard_map/slice | solution.py:347
  3.4 4.5 %all-to-all-start = ((bf16[4,1,256,768]{3,2,1,0:T(8,128)(2,1)}), bf16[4,1,256,768]{3,2,1,0:T(8,128)(2,1)}, u32[]{:S(2)}, u32[]{:S(2)}) async-start(bf16[4,1,256,768]{3,2,1,0:T(8,128)(2,1)} %slice.33), calls=%async_computation | async-start | bytes 3145728 | tf_op jit(solution)/shard_map/all_to_all | solution.py:346
  8.1 3.1 %collective-permute-start = (s32[32]{0:T(128)S(1)}, s32[32]{0:T(128)S(1)}, u32[]{:S(2)}, u32[]{:S(2)}) collective-permute-start(s32[32]{0:T(128)S(1)} %reshape.71.orbs), channel_id=1, source_target_pairs={{0,2},{1,3},{2,0},{3,1},{4,6},{5,7},{6,4},{7,5},{8,10},{9,11},{10,... | collective-permute-start | bytes 392 | tf_op jit(solution)/shard_map/ppermute | solution.py:338
  11.8 5.4 %pack.1 = (bf16[16,32,1536]{2,1,0:T(8,128)(2,1)}, bf16[16,32,1536]{2,1,0:T(8,128)(2,1)}, bf16[16,32,1536]{2,1,0:T(8,128)(2,1)}, bf16[16,32,1536]{2,1,0:T(8,128)(2,1)}) custom-call(s32[32]{0:T(128)} %copy-done.3, s32[2]{0:T(128)} %pad_add_fusion.1.place, bf16[32,32,1536]{2,1,0:T(8,128)(2,1)} %bitcast.20), custom_call_target="tpu_custom_call" | custom-call | bytes 9437184 | tf_op jit(solution)/shard_map/pack/pallas_call | solution.py:59
  17.2 1.6 collective-permute-start.1
  23.4 5.1 %fusion = bf16[1024,1024]{1,0:T(8,128)(2,1)} fusion(s32[]{:T(128)S(6)} %select_n.46, bf16[1024,1024]{1,0:T(8,128)(2,1)} %bitcast.21), kind=kLoop, calls=%fused_computation.2 | loop fusion | flops 4194304 | bytes 4194308 | tf_op jit(solution)/shard_map/jit(_roll_dynamic)/concatenate | solution.py:365
  30.0 4.6 %all-to-all-start.1 = ((bf16[4,1,256,768]{3,2,1,0:T(8,128)(2,1)}), bf16[4,1,256,768]{3,2,1,0:T(8,128)(2,1)}, u32[]{:S(2)}, u32[]{:S(2)}) async-start(bf16[4,1,256,768]{3,2,1,0:T(8,128)(2,1)} %slice.34), calls=%async_computation.1 | async-start | bytes 3145728 | tf_op jit(solution)/shard_map/all_to_all | solution.py:346
  34.9 5.1 %convolution_convert_fusion.1.refs_4_ = bf16[1024,768]{1,0:T(8,128)(2,1)} fusion(bf16[1024,1024]{1,0:T(8,128)(2,1)} %fusion, bf16[1024,768]{1,0:T(8,128)(2,1)} %bitcast.6), kind=kOutput, calls=%fused_computation.4 | convolution fusion | flops 1611399168 | bytes 5242880 | tf_op jit(solution)/shard_map/dot_general | solution.py:390
  40.0 2.6 %collective-permute-start.5 = (bf16[1024,768]{1,0:T(8,128)(2,1)}, bf16[1024,768]{1,0:T(8,128)(2,1)}, u32[]{:S(2)}, u32[]{:S(2)}) collective-permute-start(bf16[1024,768]{1,0:T(8,128)(2,1)} %convolution_convert_fusion.1.refs_4_), channel_id=1, source_target_pairs={{0,4},{1,5},{2,6},{3,7},{4,0},{5,1},{6,2},{7,3},{8,12},{9,13},{10,... | collective-permute-start | bytes 4718600 | tf_op jit(solution)/shard_map/ppermute | solution.py:338
  43.0 11.5 %all-to-all-done.1 = bf16[4,1,256,768]{3,2,1,0:T(8,128)(2,1)} async-done(((bf16[4,1,256,768]{3,2,1,0:T(8,128)(2,1)}), bf16[4,1,256,768]{3,2,1,0:T(8,128)(2,1)}, u32[]{:S(2)}, u32[]{:S(2)}) %all-to-all-start.1) | async-done | bytes 1572896 | tf_op jit(solution)/shard_map/all_to_all | solution.py:346
  54.5 3.8 %convolution_convert_fusion.refs_5_ = bf16[1024,768]{1,0:T(8,128)(2,1)S(1)} fusion(bf16[1024,1024]{1,0:T(8,128)(2,1)} %fusion, bf16[1024,768]{1,0:T(8,128)(2,1)} %bitcast.7), kind=kOutput, calls=%fused_computation.3 | convolution fusion | flops 1611399168 | bytes 5242880 | tf_op jit(solution)/shard_map/dot_general | solution.py:390
  58.4 2.6 %collective-permute-start.6 = (bf16[512,768]{1,0:T(8,128)(2,1)S(1)}, bf16[512,768]{1,0:T(8,128)(2,1)S(1)}, u32[]{:S(2)}, u32[]{:S(2)}) collective-permute-start(bf16[512,768]{1,0:T(8,128)(2,1)S(1)} %slice.47), channel_id=1, source_target_pairs={{0,4},{1,5},{2,6},{3,7},{4,0},{5,1},{6,2},{7,3},{8,12},{9,13},{10,... | collective-permute-start | bytes 2359304 | tf_op jit(solution)/shard_map/ppermute | solution.py:338
  61.2 41.9 %collective-permute-done.2.refs_2_ = bf16[16,32,1536]{2,1,0:T(8,128)(2,1)S(1)} collective-permute-done((bf16[16,32,1536]{2,1,0:T(8,128)(2,1)}, bf16[16,32,1536]{2,1,0:T(8,128)(2,1)S(1)}, u32[]{:S(2)}, u32[]{:S(2)}) %collective-permute-start.2) | collective-permute-done | bytes 1572896 | tf_op jit(solution)/shard_map/ppermute | solution.py:338
  103.1 31.6 %collective-permute-done.3.refs_3_ = bf16[16,32,1536]{2,1,0:T(8,128)(2,1)} collective-permute-done((bf16[16,32,1536]{2,1,0:T(8,128)(2,1)}, bf16[16,32,1536]{2,1,0:T(8,128)(2,1)}, u32[]{:S(2)}, u32[]{:S(2)}) %collective-permute-start.3) | collective-permute-done | bytes 1572896 | tf_op jit(solution)/shard_map/ppermute | solution.py:338
  134.8 6.5 %shard_map.86 = (bf16[16,32,1024]{2,1,0:T(8,128)(2,1)S(1)}, bf16[16,32,1024]{2,1,0:T(8,128)(2,1)S(1)}) custom-call(bf16[16,32,1536]{2,1,0:T(8,128)(2,1)S(1)} %copy-done, bf16[16,32,1536]{2,1,0:T(8,128)(2,1)S(1)} %collective-permute-done.1.refs_1_, bf16[16,32,1536]{2,1,0:T(8,128)(2,1)S(1)} %collective-permute-done.2.refs_2_, ...), custom_call_target="tpu_custom_call" | custom-call | flops 3221225472 | bytes 3145728 | tf_op jit(solution)/shard_map/pallas_call | solution.py:132
  141.3 2.6 %collective-permute-start.4 = (bf16[16,32,1024]{2,1,0:T(8,128)(2,1)S(1)}, bf16[16,32,1024]{2,1,0:T(8,128)(2,1)S(1)}, u32[]{:S(2)}, u32[]{:S(2)}) collective-permute-start(bf16[16,32,1024]{2,1,0:T(8,128)(2,1)S(1)} %get-tuple-element.37), channel_id=1, source_target_pairs={{0,1},{1,0},{2,3},{3,2},{4,5},{5,4},{6,7},{7,6},{8,9},{9,8},{10,11... | collective-permute-start | bytes 3145736 | tf_op jit(solution)/shard_map/ppermute | solution.py:338
  144.0 14.5 %collective-permute-done.6.refs_5_ = bf16[512,768]{1,0:T(8,128)(2,1)S(1)} collective-permute-done((bf16[512,768]{1,0:T(8,128)(2,1)S(1)}, bf16[512,768]{1,0:T(8,128)(2,1)S(1)}, u32[]{:S(2)}, u32[]{:S(2)}) %collective-permute-start.6) | collective-permute-done | bytes 786464 | tf_op jit(solution)/shard_map/ppermute | solution.py:338
  158.5 3.3 %shard_map.87 = (bf16[16,32,512]{2,1,0:T(8,128)(2,1)S(1)}, bf16[16,32,512]{2,1,0:T(8,128)(2,1)S(1)}) custom-call(bf16[16,32,1536]{2,1,0:T(8,128)(2,1)S(1)} %copy-done, bf16[16,32,1536]{2,1,0:T(8,128)(2,1)S(1)} %collective-permute-done.1.refs_1_, bf16[16,32,1536]{2,1,0:T(8,128)(2,1)S(1)} %collective-permute-done.2.refs_2_, ...), custom_call_target="tpu_custom_call" | custom-call | flops 1610612736 | bytes 3145728 | tf_op jit(solution)/shard_map/pallas_call | solution.py:132
  161.8 1.6 collective-permute-start.7
  163.4 4.5 %collective-permute-done.4.refs_1_ = bf16[16,32,1024]{2,1,0:T(8,128)(2,1)S(1)} collective-permute-done((bf16[16,32,1024]{2,1,0:T(8,128)(2,1)S(1)}, bf16[16,32,1024]{2,1,0:T(8,128)(2,1)S(1)}, u32[]{:S(2)}, u32[]{:S(2)}) %collective-permute-start.4) | collective-permute-done | bytes 1048608 | tf_op jit(solution)/shard_map/ppermute | solution.py:338
  167.9 9.6 %collective-permute-done.7.refs_3_ = bf16[16,32,512]{2,1,0:T(8,128)(2,1)S(1)} collective-permute-done((bf16[16,32,512]{2,1,0:T(8,128)(2,1)S(1)}, bf16[16,32,512]{2,1,0:T(8,128)(2,1)S(1)}, u32[]{:S(2)}, u32[]{:S(2)}) %collective-permute-start.7) | collective-permute-done | bytes 524320 | tf_op jit(solution)/shard_map/ppermute | solution.py:338
  177.5 2.3 %shard_map.88 = (bf16[16,32,512]{2,1,0:T(8,128)(2,1)S(1)}, f32[2,16,32,32]{3,2,1,0:T(8,128)S(1)}) custom-call(s32[2,32]{1,0:T(2,128)S(1)} %get-tuple-element.56.refs_7_.rows, s32[2,32]{1,0:T(2,128)S(1)} %select_reduce_fusion.refs_9_.offsets, f32[8,128]{1,0:T(8,128)S(1)} %broadcast_in_dim.55.before, bf16[16,32,1024]{2,1,0:T(8,128)(2,1)S(1)} %get-tuple-element.36.refs_0_, ...), custom_call_target="tpu_custom_call" | custom-call | tf_op jit(solution)/shard_map/pallas_call | solution.py:215
  179.8 3.5 %shard_map.89 = (bf16[16,32,384]{2,1,0:T(8,128)(2,1)S(1)}, bf16[16,32,384]{2,1,0:T(8,128)(2,1)S(1)}) custom-call(bf16[16,32,1536]{2,1,0:T(8,128)(2,1)S(1)} %copy-done, bf16[16,32,1536]{2,1,0:T(8,128)(2,1)S(1)} %collective-permute-done.1.refs_1_, bf16[16,32,1536]{2,1,0:T(8,128)(2,1)S(1)} %collective-permute-done.2.refs_2_, ...), custom_call_target="tpu_custom_call" | custom-call | flops 1207959552 | bytes 3145728 | tf_op jit(solution)/shard_map/pallas_call | solution.py:132
  183.3 1.8 collective-permute-start.9
  185.5 7.8 %collective-permute-done.10.refs_5_ = bf16[128,768]{1,0:T(8,128)(2,1)S(1)} collective-permute-done((bf16[128,768]{1,0:T(8,128)(2,1)S(1)}, bf16[128,768]{1,0:T(8,128)(2,1)S(1)}, u32[]{:S(2)}, u32[]{:S(2)}) %collective-permute-start.10) | collective-permute-done | bytes 196640 | tf_op jit(solution)/shard_map/ppermute | solution.py:338
  193.3 3.2 %shard_map.90 = (bf16[16,32,128]{2,1,0:T(8,128)(2,1)S(1)}, bf16[16,32,128]{2,1,0:T(8,128)(2,1)S(1)}) custom-call(bf16[16,32,1536]{2,1,0:T(8,128)(2,1)S(1)} %copy-done, bf16[16,32,1536]{2,1,0:T(8,128)(2,1)S(1)} %collective-permute-done.1.refs_1_, bf16[16,32,1536]{2,1,0:T(8,128)(2,1)S(1)} %collective-permute-done.2.refs_2_, ...), custom_call_target="tpu_custom_call" | custom-call | flops 402653184 | bytes 3145728 | tf_op jit(solution)/shard_map/pallas_call | solution.py:132
  197.9 2.5 %shard_map.91 = (bf16[16,32,384]{2,1,0:T(8,128)(2,1)S(1)}, f32[2,16,32,32]{3,2,1,0:T(8,128)S(1)}) custom-call(s32[2,32]{1,0:T(2,128)S(1)} %get-tuple-element.56.refs_7_.rows, s32[2,32]{1,0:T(2,128)S(1)} %select_reduce_fusion.refs_9_.offsets, f32[2,16,32,32]{3,2,1,0:T(8,128)S(1)} %get-tuple-element.40.refs_6_.before, ...), custom_call_target="tpu_custom_call" | custom-call | tf_op jit(solution)/shard_map/pallas_call | solution.py:215
  201.6 2.2 shard_map.92
  206.0 6.5 %collective-permute-done.14.refs_7_ = bf16[16,32,384]{2,1,0:T(8,128)(2,1)S(1)} collective-permute-done((bf16[16,32,384]{2,1,0:T(8,128)(2,1)S(1)}, bf16[16,32,384]{2,1,0:T(8,128)(2,1)S(1)}, u32[]{:S(2)}, u32[]{:S(2)}) %collective-permute-start.14) | collective-permute-done | bytes 393248 | tf_op jit(solution)/shard_map/ppermute | solution.py:338
  212.4 1.7 shard_map.93.before
  214.1 4.2 %collective-permute-done.12.there = f32[16,32,32]{2,1,0:T(8,128)S(1)} collective-permute-done((f32[16,32,32]{2,1,0:T(8,128)S(1)}, f32[16,32,32]{2,1,0:T(8,128)S(1)}, u32[]{:S(2)}, u32[]{:S(2)}) %collective-permute-start.12) | collective-permute-done | bytes 65568 | tf_op jit(solution)/shard_map/ppermute | solution.py:338
  218.3 1.7 shard_map.94
  (57 shorter events, 12.4 us)
Async XLA Ops:
  3.4 4.5 %copy-start.4 = (s32[16,2]{0,1:T(2,128)S(1)}, s32[16,2]{0,1:T(2,128)}, u32[]{:S(2)}) copy-start(s32[16,2]{0,1:T(2,128)} %param.9) | copy-start | bytes 388
  3.4 26.6 %all-to-all-start = ((bf16[4,1,256,768]{3,2,1,0:T(8,128)(2,1)}), bf16[4,1,256,768]{3,2,1,0:T(8,128)(2,1)}, u32[]{:S(2)}, u32[]{:S(2)}) async-start(bf16[4,1,256,768]{3,2,1,0:T(8,128)(2,1)} %slice.33), calls=%async_computation | async-start | bytes 3145728 | tf_op jit(solution)/shard_map/all_to_all | solution.py:346
  8.1 3.7 %copy-start.3 = (s32[32]{0:T(128)}, s32[32]{0:T(128)S(1)}, u32[]{:S(2)}) copy-start(s32[32]{0:T(128)S(1)} %reshape.71.orbs) | copy-start | bytes 388
  8.1 21.7 %collective-permute-start = (s32[32]{0:T(128)S(1)}, s32[32]{0:T(128)S(1)}, u32[]{:S(2)}, u32[]{:S(2)}) collective-permute-start(s32[32]{0:T(128)S(1)} %reshape.71.orbs), channel_id=1, source_target_pairs={{0,2},{1,3},{2,0},{3,1},{4,6},{5,7},{6,4},{7,5},{8,10},{9,11},{10,... | collective-permute-start | bytes 392 | tf_op jit(solution)/shard_map/ppermute | solution.py:338
  11.8 8.9 %copy-start.6 = (s32[32]{0:T(128)S(1)}, s32[32]{0:T(128)}, u32[]{:S(2)}) copy-start(s32[32]{0:T(128)} %param.13) | copy-start | bytes 388
  17.2 44.1 %collective-permute-start.1 = (bf16[16,32,1536]{2,1,0:T(8,128)(2,1)}, bf16[16,32,1536]{2,1,0:T(8,128)(2,1)S(1)}, u32[]{:S(2)}, u32[]{:S(2)}) collective-permute-start(bf16[16,32,1536]{2,1,0:T(8,128)(2,1)} %get-tuple-element.32), channel_id=1, source_target_pairs={{0,1},{1,0},{2,3},{3,2},{4,5},{5,4},{6,7},{7,6},{8,9},{9,8},{10,11... | collective-permute-start | bytes 4718600 | tf_op jit(solution)/shard_map/ppermute | solution.py:338
  18.7 84.4 %collective-permute-start.2 = (bf16[16,32,1536]{2,1,0:T(8,128)(2,1)}, bf16[16,32,1536]{2,1,0:T(8,128)(2,1)S(1)}, u32[]{:S(2)}, u32[]{:S(2)}) collective-permute-start(bf16[16,32,1536]{2,1,0:T(8,128)(2,1)} %get-tuple-element.33), channel_id=1, source_target_pairs={{0,2},{1,3},{2,0},{3,1},{4,6},{5,7},{6,4},{7,5},{8,10},{9,11},{10,... | collective-permute-start | bytes 4718600 | tf_op jit(solution)/shard_map/ppermute | solution.py:338
  19.2 115.6 %collective-permute-start.3 = (bf16[16,32,1536]{2,1,0:T(8,128)(2,1)}, bf16[16,32,1536]{2,1,0:T(8,128)(2,1)}, u32[]{:S(2)}, u32[]{:S(2)}) collective-permute-start(bf16[16,32,1536]{2,1,0:T(8,128)(2,1)} %get-tuple-element.34), channel_id=1, source_target_pairs={{0,3},{1,2},{2,1},{3,0},{4,7},{5,6},{6,5},{7,4},{8,11},{9,10},{10,... | collective-permute-start | bytes 4718600 | tf_op jit(solution)/shard_map/ppermute | solution.py:338
  23.3 5.1 %copy-start.2 = (f32[16,2,32]{2,1,0:T(2,128)S(1)}, f32[16,2,32]{2,1,0:T(2,128)}, u32[]{:S(2)}) copy-start(f32[16,2,32]{2,1,0:T(2,128)} %param.11) | copy-start | bytes 12292
  23.4 5.2 %copy-start.1 = (bf16[4,1,256,1536]{3,2,1,0:T(8,128)(2,1)S(1)}, bf16[4,1,256,1536]{3,2,1,0:T(8,128)(2,1)}, u32[]{:S(2)}) copy-start(bf16[4,1,256,1536]{3,2,1,0:T(8,128)(2,1)} %param.7) | copy-start | bytes 9437188
  30.0 4.7 %copy-start.5 = (f32[32]{0:T(128)S(1)}, f32[32]{0:T(128)}, u32[]{:S(2)}) copy-start(f32[32]{0:T(128)} %param.12) | copy-start | bytes 388
  30.0 24.5 %all-to-all-start.1 = ((bf16[4,1,256,768]{3,2,1,0:T(8,128)(2,1)}), bf16[4,1,256,768]{3,2,1,0:T(8,128)(2,1)}, u32[]{:S(2)}, u32[]{:S(2)}) async-start(bf16[4,1,256,768]{3,2,1,0:T(8,128)(2,1)} %slice.34), calls=%async_computation.1 | async-start | bytes 3145728 | tf_op jit(solution)/shard_map/all_to_all | solution.py:346
  40.0 118.5 %collective-permute-start.5 = (bf16[1024,768]{1,0:T(8,128)(2,1)}, bf16[1024,768]{1,0:T(8,128)(2,1)}, u32[]{:S(2)}, u32[]{:S(2)}) collective-permute-start(bf16[1024,768]{1,0:T(8,128)(2,1)} %convolution_convert_fusion.1.refs_4_), channel_id=1, source_target_pairs={{0,4},{1,5},{2,6},{3,7},{4,0},{5,1},{6,2},{7,3},{8,12},{9,13},{10,... | collective-permute-start | bytes 4718600 | tf_op jit(solution)/shard_map/ppermute | solution.py:338
  58.3 76.5 %copy-start = (bf16[16,32,1536]{2,1,0:T(8,128)(2,1)S(1)}, bf16[16,32,1536]{2,1,0:T(8,128)(2,1)}, u32[]{:S(2)}) copy-start(bf16[16,32,1536]{2,1,0:T(8,128)(2,1)} %get-tuple-element.31.refs_0_) | copy-start | bytes 4718596
  58.4 100.1 %collective-permute-start.6 = (bf16[512,768]{1,0:T(8,128)(2,1)S(1)}, bf16[512,768]{1,0:T(8,128)(2,1)S(1)}, u32[]{:S(2)}, u32[]{:S(2)}) collective-permute-start(bf16[512,768]{1,0:T(8,128)(2,1)S(1)} %slice.47), channel_id=1, source_target_pairs={{0,4},{1,5},{2,6},{3,7},{4,0},{5,1},{6,2},{7,3},{8,12},{9,13},{10,... | collective-permute-start | bytes 2359304 | tf_op jit(solution)/shard_map/ppermute | solution.py:338
  141.3 26.6 %collective-permute-start.4 = (bf16[16,32,1024]{2,1,0:T(8,128)(2,1)S(1)}, bf16[16,32,1024]{2,1,0:T(8,128)(2,1)S(1)}, u32[]{:S(2)}, u32[]{:S(2)}) collective-permute-start(bf16[16,32,1024]{2,1,0:T(8,128)(2,1)S(1)} %get-tuple-element.37), channel_id=1, source_target_pairs={{0,1},{1,0},{2,3},{3,2},{4,5},{5,4},{6,7},{7,6},{8,9},{9,8},{10,11... | collective-permute-start | bytes 3145736 | tf_op jit(solution)/shard_map/ppermute | solution.py:338
  143.9 35.9 %collective-permute-start.8 = (bf16[384,768]{1,0:T(8,128)(2,1)S(1)}, bf16[384,768]{1,0:T(8,128)(2,1)S(1)}, u32[]{:S(2)}, u32[]{:S(2)}) collective-permute-start(bf16[384,768]{1,0:T(8,128)(2,1)S(1)} %slice.48), channel_id=1, source_target_pairs={{0,4},{1,5},{2,6},{3,7},{4,0},{5,1},{6,2},{7,3},{8,12},{9,13},{10,... | collective-permute-start | bytes 1769480 | tf_op jit(solution)/shard_map/ppermute | solution.py:338
  161.8 15.7 %collective-permute-start.7 = (bf16[16,32,512]{2,1,0:T(8,128)(2,1)S(1)}, bf16[16,32,512]{2,1,0:T(8,128)(2,1)S(1)}, u32[]{:S(2)}, u32[]{:S(2)}) collective-permute-start(bf16[16,32,512]{2,1,0:T(8,128)(2,1)S(1)} %get-tuple-element.39), channel_id=1, source_target_pairs={{0,1},{1,0},{2,3},{3,2},{4,5},{5,4},{6,7},{7,6},{8,9},{9,8},{10,11... | collective-permute-start | bytes 1572872 | tf_op jit(solution)/shard_map/ppermute | solution.py:338
  183.3 14.6 %collective-permute-start.9 = (bf16[16,32,384]{2,1,0:T(8,128)(2,1)S(1)}, bf16[16,32,384]{2,1,0:T(8,128)(2,1)S(1)}, u32[]{:S(2)}, u32[]{:S(2)}) collective-permute-start(bf16[16,32,384]{2,1,0:T(8,128)(2,1)S(1)} %get-tuple-element.42), channel_id=1, source_target_pairs={{0,1},{1,0},{2,3},{3,2},{4,5},{5,4},{6,7},{7,6},{8,9},{9,8},{10,11... | collective-permute-start | bytes 1179656 | tf_op jit(solution)/shard_map/ppermute | solution.py:338
  185.1 8.2 %collective-permute-start.10 = (bf16[128,768]{1,0:T(8,128)(2,1)S(1)}, bf16[128,768]{1,0:T(8,128)(2,1)S(1)}, u32[]{:S(2)}, u32[]{:S(2)}) collective-permute-start(bf16[128,768]{1,0:T(8,128)(2,1)S(1)} %slice.49), channel_id=1, source_target_pairs={{0,4},{1,5},{2,6},{3,7},{4,0},{5,1},{6,2},{7,3},{8,12},{9,13},{10,... | collective-permute-start | bytes 589832 | tf_op jit(solution)/shard_map/ppermute | solution.py:338
  185.2 20.8 %collective-permute-start.13 = (bf16[16,32,512]{2,1,0:T(8,128)(2,1)S(1)}, bf16[16,32,512]{2,1,0:T(8,128)(2,1)S(1)}, u32[]{:S(2)}, u32[]{:S(2)}) collective-permute-start(bf16[16,32,512]{2,1,0:T(8,128)(2,1)S(1)} %get-tuple-element.47), channel_id=1, source_target_pairs={{0,2},{1,3},{2,0},{3,1},{4,6},{5,7},{6,4},{7,5},{8,10},{9,11},{10,... | collective-permute-start | bytes 1572872 | tf_op jit(solution)/shard_map/ppermute | solution.py:338
  196.5 5.0 %collective-permute-start.11 = (bf16[16,32,128]{2,1,0:T(8,128)(2,1)S(1)}, bf16[16,32,128]{2,1,0:T(8,128)(2,1)S(1)}, u32[]{:S(2)}, u32[]{:S(2)}) collective-permute-start(bf16[16,32,128]{2,1,0:T(8,128)(2,1)S(1)} %get-tuple-element.45), channel_id=1, source_target_pairs={{0,1},{1,0},{2,3},{3,2},{4,5},{5,4},{6,7},{7,6},{8,9},{9,8},{10,11... | collective-permute-start | bytes 393224 | tf_op jit(solution)/shard_map/ppermute | solution.py:338
  200.4 12.1 %collective-permute-start.14 = (bf16[16,32,384]{2,1,0:T(8,128)(2,1)S(1)}, bf16[16,32,384]{2,1,0:T(8,128)(2,1)S(1)}, u32[]{:S(2)}, u32[]{:S(2)}) collective-permute-start(bf16[16,32,384]{2,1,0:T(8,128)(2,1)S(1)} %get-tuple-element.48), channel_id=1, source_target_pairs={{0,2},{1,3},{2,0},{3,1},{4,6},{5,7},{6,4},{7,5},{8,10},{9,11},{10,... | collective-permute-start | bytes 1179656 | tf_op jit(solution)/shard_map/ppermute | solution.py:338
  203.8 14.5 %collective-permute-start.15 = (bf16[16,32,128]{2,1,0:T(8,128)(2,1)S(1)}, bf16[16,32,128]{2,1,0:T(8,128)(2,1)S(1)}, u32[]{:S(2)}, u32[]{:S(2)}) collective-permute-start(bf16[16,32,128]{2,1,0:T(8,128)(2,1)S(1)} %get-tuple-element.49), channel_id=1, source_target_pairs={{0,2},{1,3},{2,0},{3,1},{4,6},{5,7},{6,4},{7,5},{8,10},{9,11},{10,... | collective-permute-start | bytes 393224 | tf_op jit(solution)/shard_map/ppermute | solution.py:338
  204.8 13.5 %collective-permute-start.12 = (f32[16,32,32]{2,1,0:T(8,128)S(1)}, f32[16,32,32]{2,1,0:T(8,128)S(1)}, u32[]{:S(2)}, u32[]{:S(2)}) collective-permute-start(f32[16,32,32]{2,1,0:T(8,128)S(1)} %slice_bitcast_fusion), channel_id=1, source_target_pairs={{0,2},{1,3},{2,0},{3,1},{4,6},{5,7},{6,4},{7,5},{8,10},{9,11},{10,... | collective-permute-start | bytes 196616 | tf_op jit(solution)/shard_map/ppermute | solution.py:338

commit v3 on v2

--- a/solution.py
+++ b/solution.py
@@ -42,7 +42,7 @@
     load.wait()
     for mask, out in enumerate(outs):
         for kind in range(2):
-            orb = place[1] ^ (mask + kind * group)
+            orb = place[1] ^ mask ^ (kind * (group + group // 2))
 
             def send(k, carry, orb=orb, kind=kind, out=out, sem=store_sem.at[mask]):
                 copy(held.at[holder[orb * capacity + k]], out.at[kind * capacity + k], sem).start()
@@ -75,18 +75,23 @@
     )(orbs, place, coef)
 
 
-def project_kernel(group, capacity, kind, pieces, *refs):
+def project_kernel(group, capacity, kind, pieces, place, *refs):
     inner = group // 2
-    count = group + len(pieces)
-    blocks, parts = refs[:group], refs[group:count]
+    blocks, parts = refs[:group], refs[group : group + len(pieces)]
     outs, (left, right, made, left_sem, right_sem, out_sem) = refs[-6 - inner : -6], refs[-6:]
     row_count = right.shape[0]
     _, pno_count, dom_count = left.shape
     lines = 2 * capacity
-    for part, (row, column, width) in zip(parts, pieces):
-        copy(
-            part.at[pl.ds(row, row_count)], right.at[:, pl.ds(column, width)], right_sem
-        ).start()
+    plane = place[1] // inner
+    at_end = (plane == 0) | (plane == 3)
+    for part, (row, column, width, end) in zip(parts, pieces):
+
+        @pl.when(at_end == end if kind else plane >= 0)
+        def _(part=part, row=row, column=column, width=width):
+            copy(
+                part.at[pl.ds(row, row_count)], right.at[:, pl.ds(column, width)], right_sem
+            ).start()
+
     for i in range(inner):
         for j in range(2):
             copy(
@@ -122,7 +127,7 @@
         copy(made.at[i], outs[i], out_sem).wait()
 
 
-def project(blocks, kind, parts, pieces, row_count, tokens):
+def project(place, blocks, kind, parts, pieces, row_count, tokens):
     group = len(blocks)
     inner = group // 2
     slots, pno_count, dom_count = blocks[0].shape
@@ -132,7 +137,7 @@
     return pl.pallas_call(
         functools.partial(project_kernel, group, capacity, kind, tuple(pieces)),
         out_shape=(out,) * inner,
-        in_specs=[ANY] * (group + len(parts) + len(tokens)),
+        in_specs=[SMEM] + [ANY] * (group + len(parts) + len(tokens)),
         out_specs=(ANY,) * inner,
         scratch_shapes=[
             pltpu.VMEM((group * capacity, pno_count, dom_count), dtype),
@@ -148,7 +153,7 @@
             transcendentals=0,
             bytes_accessed=2 * group * capacity * pno_count * dom_count,
         ),
-    )(*blocks, *parts, *tokens)
+    )(place, *blocks, *parts, *tokens)
 
 
 def gather_sides(near, far, spans, slots, held, sem):
@@ -365,10 +370,11 @@
     turned = lax.optimization_barrier(jnp.roll(fit_inverse[0], own_offset, axis=0))
     orbs = jnp.stack([own_orbs, mate_orbs])
     differs = orbs ^ me
-    line = jnp.where((differs & group) != 0, inner, 0) + (differs & (inner - 1))
+    other_half = (differs & group) != 0
+    line = jnp.where(other_half, inner, 0) + (differs & (inner - 1))
     home = jnp.arange(2, dtype=jnp.int32)[:, None]
     position = slots_of(orbs)
-    there = (differs & inner) != 0
+    there = ((differs & inner) != 0) != other_half
     rows = jnp.where(there, -1, line * 2 * capacity + home * capacity + position)
     rows_home = jnp.where(there, -1, line * capacity + position)
     orb_total = occ_energy.shape[0]
@@ -384,16 +390,18 @@
         - occupied[:, 1, None, None]
     )
     spans = chunk_spans(fit_rows)
+    reverse = group + inner
+    ends = [(i, i ^ reverse) for i in range(orb_count) if i // inner in (0, 3)]
+    middles = [(i, i ^ reverse) for i in range(orb_count) if i // inner in (1, 2)]
     fitted, mirrored = [], []
     for k in range(2):
         fitted.append(
             jnp.dot(turned, raw_parts[k], preferred_element_type=jnp.float32).astype(jnp.bfloat16)
         )
-        if k == 0:
-            mirrored.append(across(fitted[0], group))
-        else:
-            for begin, size in spans:
-                mirrored.append(across(fitted[1][begin : begin + size], group))
+        mirrored.append(lax.ppermute(fitted[k], "orb", middles))
+    for begin, size in spans:
+        chunk = jnp.concatenate([part[begin : begin + size] for part in fitted], axis=1)
+        mirrored.append(lax.ppermute(chunk, "orb", ends))
 
     def hop(outs):
         return [outs[0]] + [across(outs[i], i) for i in range(1, inner)]
@@ -401,10 +409,11 @@
     def project_far(c, tokens):
         begin, size = spans[c]
         parts = project(
+            place,
             blocks,
             1,
-            [mirrored[0], mirrored[1 + c]],
-            [(begin, 0, half), (0, half, half)],
+            [mirrored[0], mirrored[1], mirrored[2 + c]],
+            [(begin, 0, half, False), (begin, half, half, False), (0, 0, dom_count, True)],
             size,
             tokens,
         )
@@ -415,16 +424,17 @@
         return across(sent, inner), here
 
     near = project(
+        place,
         blocks,
         0,
         fitted,
-        [(0, 0, half), (0, half, half)],
+        [(0, 0, half, False), (0, half, half, False)],
         fit_rows,
-        [denominator, rows, rows_home, offsets],
+        [denominator],
     )
     near = hop(near)
     far, others = [None] * 3, [None] * 3
-    far[0] = project_far(0, [])
+    far[0] = project_far(0, [rows, rows_home, offsets])
     others[0], here = pass_on(0, jnp.zeros((8, 128), jnp.float32), [])
     far[1] = project_far(1, [here])
     far[2] = project_far(2, [far[1][0]])

time: 222 us -> 242 us (1.090)
  starting transfers between devices: 31 us -> 110 us
  waiting for transfers between devices: 133 us -> 60.8 us
  local copies, waits for them, and re-layouts: 6.06 us -> 14.8 us
    ppermute x16 -> x12, waiting for transfers between devices: 122 us -> 22.4 us  [across(): return lax.ppermute(array, 'orb', [(i, i ^ mask) for i in range(orb_count)])]
    ppermute x0 -> x5, starting transfers between devices: none -> 51.3 us  [the longest x3 47.5 us: on_device(): mirrored.append(lax.ppermute(chunk, 'orb', ends))]
    ppermute x16 -> x12, starting transfers between devices: 22 us -> 49.7 us  [across(): return lax.ppermute(array, 'orb', [(i, i ^ mask) for i in range(orb_count)])]
    ppermute x0 -> x5, waiting for transfers between devices: none -> 27.7 us  [the longest x3 27.7 us: on_device(): mirrored.append(lax.ppermute(chunk, 'orb', ends))]
    slice x3 -> x6, local copies, waits for them, and re-layouts: 0.11 us -> 7.53 us  [on_device(): part[begin:begin + size]]
  transfers between devices with their start and end apart: 18 -> 19, of which waited for: 10 -> 5; matrix products, arithmetic and copies ran while one was open for 8% -> 12% of each run, Pallas kernels for 12% -> 13%
where the time goes in v3:
time: 242 us; the launch traced here: 241 us
  starting transfers between devices  110 us (45%)
  waiting for transfers between devices  60.8 us (25%)
  Pallas kernels  34.2 us (14%)
  local copies, waits for them, and re-layouts  14.8 us (6%)
  matrix products  9.99 us (4%)
  other arithmetic  8.42 us (3%)
  between operations  2.92 us (1%)
    ppermute x12, starting transfers between devices, across(): return lax.ppermute(array, 'orb', [(i, i ^ mask) for i in range(orb_count)])  49.7 us
    ppermute x3, starting transfers between devices, on_device(): mirrored.append(lax.ppermute(chunk, 'orb', ends))  47.5 us
    ppermute x3, waiting for transfers between devices, on_device(): mirrored.append(lax.ppermute(chunk, 'orb', ends))  27.7 us
    ppermute x12, waiting for transfers between devices, across(): return lax.ppermute(array, 'orb', [(i, i ^ mask) for i in range(orb_count)])  22.4 us
    pallas_call x4, Pallas kernels, project(): pl.pallas_call(functools.partial(project_kernel, group, capacity, kind, t...  18.3 us
    all_to_all x2, waiting for transfers between devices, exchange(): lax.all_to_all(array[:, :, :, k * half:(k + 1) * half], 'aux', split_axis...  10.7 us
    dot_general x2, matrix products, on_device(): jnp.dot(turned, raw_parts[k], preferred_element_type=jnp.float32)  9.99 us
    all_to_all x2, starting transfers between devices, exchange(): lax.all_to_all(array[:, :, :, k * half:(k + 1) * half], 'aux', split_axis...  8.97 us
  transfers between devices with their start and end apart: 19, of which 5 were waited for; matrix products, arithmetic and copies ran while one was open for 12% of the time, Pallas kernels for 13%

profile of v3, /device:TPU:0, one launch (start us, length us, event | category | flops | bytes accessed | tf_op | source)
XLA Modules:
  0.0 241.1 jit_solution(6261929721575116558)
XLA Ops:
  0.6 2.7 %slice.42 = bf16[4,1,256,768]{3,2,1,0:T(8,128)(2,1)} slice(bf16[4,1,256,1536]{3,2,1,0:T(8,128)(2,1)} %param.7), slice={[0:4], [0:1], [0:256], [0:768]} | slice | bytes 3145728 | tf_op jit(solution)/shard_map/slice | solution.py:352
  3.3 4.5 %all-to-all-start = ((bf16[4,1,256,768]{3,2,1,0:T(8,128)(2,1)}), bf16[4,1,256,768]{3,2,1,0:T(8,128)(2,1)}, u32[]{:S(2)}, u32[]{:S(2)}) async-start(bf16[4,1,256,768]{3,2,1,0:T(8,128)(2,1)} %slice.42), calls=%async_computation | async-start | bytes 3145728 | tf_op jit(solution)/shard_map/all_to_all | solution.py:351
  8.0 3.1 %collective-permute-start = (s32[32]{0:T(128)S(1)}, s32[32]{0:T(128)S(1)}, u32[]{:S(2)}, u32[]{:S(2)}) collective-permute-start(s32[32]{0:T(128)S(1)} %reshape.71.orbs), channel_id=1, source_target_pairs={{0,2},{1,3},{2,0},{3,1},{4,6},{5,7},{6,4},{7,5},{8,10},{9,11},{10,... | collective-permute-start | bytes 392 | tf_op jit(solution)/shard_map/ppermute | solution.py:343
  11.7 5.4 %pack.1 = (bf16[16,32,1536]{2,1,0:T(8,128)(2,1)}, bf16[16,32,1536]{2,1,0:T(8,128)(2,1)}, bf16[16,32,1536]{2,1,0:T(8,128)(2,1)}, bf16[16,32,1536]{2,1,0:T(8,128)(2,1)}) custom-call(s32[32]{0:T(128)} %copy-done.4, s32[2]{0:T(128)} %pad_add_fusion.1.place, bf16[32,32,1536]{2,1,0:T(8,128)(2,1)} %bitcast.20), custom_call_target="tpu_custom_call" | custom-call | bytes 9437184 | tf_op jit(solution)/shard_map/pack/pallas_call | solution.py:59
  23.2 2.7 %slice.43 = bf16[4,1,256,768]{3,2,1,0:T(8,128)(2,1)} slice(bf16[4,1,256,1536]{3,2,1,0:T(8,128)(2,1)} %param.7), slice={[0:4], [0:1], [0:256], [768:1536]} | slice | bytes 3145728 | tf_op jit(solution)/shard_map/slice | solution.py:352
  25.9 5.0 %fusion = bf16[1024,1024]{1,0:T(8,128)(2,1)} fusion(s32[]{:T(128)S(6)} %select_n.46, bf16[1024,1024]{1,0:T(8,128)(2,1)} %bitcast.21), kind=kLoop, calls=%fused_computation.2 | loop fusion | flops 4194304 | bytes 4194308 | tf_op jit(solution)/shard_map/jit(_roll_dynamic)/concatenate | solution.py:370
  30.9 4.5 %all-to-all-start.1 = ((bf16[4,1,256,768]{3,2,1,0:T(8,128)(2,1)}), bf16[4,1,256,768]{3,2,1,0:T(8,128)(2,1)}, u32[]{:S(2)}, u32[]{:S(2)}) async-start(bf16[4,1,256,768]{3,2,1,0:T(8,128)(2,1)} %slice.43), calls=%async_computation.1 | async-start | bytes 3145728 | tf_op jit(solution)/shard_map/all_to_all | solution.py:351
  35.8 5.0 %convolution_convert_fusion.1.refs_4_ = bf16[1024,768]{1,0:T(8,128)(2,1)} fusion(bf16[1024,1024]{1,0:T(8,128)(2,1)} %fusion, bf16[1024,768]{1,0:T(8,128)(2,1)} %bitcast.6), kind=kOutput, calls=%fused_computation.4 | convolution fusion | flops 1611399168 | bytes 5242880 | tf_op jit(solution)/shard_map/dot_general | solution.py:399
  40.8 2.1 slice.59
  42.8 1.9 collective-permute-start.5
  44.7 10.7 %all-to-all-done.1 = bf16[4,1,256,768]{3,2,1,0:T(8,128)(2,1)} async-done(((bf16[4,1,256,768]{3,2,1,0:T(8,128)(2,1)}), bf16[4,1,256,768]{3,2,1,0:T(8,128)(2,1)}, u32[]{:S(2)}, u32[]{:S(2)}) %all-to-all-start.1) | async-done | bytes 1572896 | tf_op jit(solution)/shard_map/all_to_all | solution.py:351
  55.5 5.0 %convolution_convert_fusion.refs_5_ = bf16[1024,768]{1,0:T(8,128)(2,1)} fusion(bf16[1024,1024]{1,0:T(8,128)(2,1)} %fusion, bf16[1024,768]{1,0:T(8,128)(2,1)} %bitcast.7), kind=kOutput, calls=%fused_computation.3 | convolution fusion | flops 1611399168 | bytes 5242880 | tf_op jit(solution)/shard_map/dot_general | solution.py:399
  61.7 1.8 collective-permute-start.6
  64.8 4.4 %collective-permute-start.7 = (bf16[512,1536]{1,0:T(8,128)(2,1)}, bf16[512,1536]{1,0:T(8,128)(2,1)}, u32[]{:S(2)}, u32[]{:S(2)}) collective-permute-start(bf16[512,1536]{1,0:T(8,128)(2,1)} %pad_maximum_fusion), channel_id=1, source_target_pairs={{0,6},{1,7},{6,0},{7,1},{8,14},{9,15},{14,8},{15,9},{16,22},{17,23... | collective-permute-start | bytes 4718600 | tf_op jit(solution)/shard_map/ppermute | solution.py:404
  72.3 3.3 %collective-permute-start.9 = (bf16[384,1536]{1,0:T(8,128)(2,1)S(1)}, bf16[384,1536]{1,0:T(8,128)(2,1)S(1)}, u32[]{:S(2)}, u32[]{:S(2)}) collective-permute-start(bf16[384,1536]{1,0:T(8,128)(2,1)S(1)} %pad_maximum_fusion.1), channel_id=1, source_target_pairs={{0,6},{1,7},{6,0},{7,1},{8,14},{9,15},{14,8},{15,9},{16,22},{17,23... | collective-permute-start | bytes 3538952 | tf_op jit(solution)/shard_map/ppermute | solution.py:404
  75.6 13.3 %collective-permute-done.3.refs_3_ = bf16[16,32,1536]{2,1,0:T(8,128)(2,1)} collective-permute-done((bf16[16,32,1536]{2,1,0:T(8,128)(2,1)}, bf16[16,32,1536]{2,1,0:T(8,128)(2,1)}, u32[]{:S(2)}, u32[]{:S(2)}) %collective-permute-start.3) | collective-permute-done | bytes 1572896 | tf_op jit(solution)/shard_map/ppermute | solution.py:343
  88.9 7.5 %shard_map.86 = (bf16[16,32,1024]{2,1,0:T(8,128)(2,1)S(1)}, bf16[16,32,1024]{2,1,0:T(8,128)(2,1)S(1)}) custom-call(s32[2]{0:T(128)S(1)} %copy-done.1, bf16[16,32,1536]{2,1,0:T(8,128)(2,1)S(1)} %copy-done, bf16[16,32,1536]{2,1,0:T(8,128)(2,1)S(1)} %collective-permute-done.1.refs_1_, bf16[16,32,1536]{2,1,0:T(8,128)(2,1)S(1)} %collective-permute-done.2.refs_2_, ...), custom_call_target="tpu_custom_call" | custom-call | flops 3221225472 | bytes 3145728 | tf_op jit(solution)/shard_map/pallas_call | solution.py:137
  98.1 27.7 %collective-permute-done.7.refs_6_ = bf16[512,1536]{1,0:T(8,128)(2,1)} collective-permute-done((bf16[512,1536]{1,0:T(8,128)(2,1)}, bf16[512,1536]{1,0:T(8,128)(2,1)}, u32[]{:S(2)}, u32[]{:S(2)}) %collective-permute-start.7) | collective-permute-done | bytes 1572896 | tf_op jit(solution)/shard_map/ppermute | solution.py:404
  125.8 4.1 %shard_map.87 = (bf16[16,32,512]{2,1,0:T(8,128)(2,1)S(1)}, bf16[16,32,512]{2,1,0:T(8,128)(2,1)S(1)}) custom-call(s32[2]{0:T(128)S(1)} %copy-done.1, bf16[16,32,1536]{2,1,0:T(8,128)(2,1)S(1)} %copy-done, bf16[16,32,1536]{2,1,0:T(8,128)(2,1)S(1)} %collective-permute-done.1.refs_1_, bf16[16,32,1536]{2,1,0:T(8,128)(2,1)S(1)} %collective-permute-done.2.refs_2_, ...), custom_call_target="tpu_custom_call" | custom-call | flops 1610612736 | bytes 3145728 | tf_op jit(solution)/shard_map/pallas_call | solution.py:137
  132.4 39.9 %collective-permute-start.11 = (bf16[128,1536]{1,0:T(8,128)(2,1)S(1)}, bf16[128,1536]{1,0:T(8,128)(2,1)S(1)}, u32[]{:S(2)}, u32[]{:S(2)}) collective-permute-start(bf16[128,1536]{1,0:T(8,128)(2,1)S(1)} %pad_maximum_fusion.2), channel_id=1, source_target_pairs={{0,6},{1,7},{6,0},{7,1},{8,14},{9,15},{14,8},{15,9},{16,22},{17,23... | collective-permute-start | bytes 1179656 | tf_op jit(solution)/shard_map/ppermute | solution.py:404
  172.4 2.3 shard_map.88
  174.7 3.4 %shard_map.89 = (bf16[16,32,384]{2,1,0:T(8,128)(2,1)S(1)}, bf16[16,32,384]{2,1,0:T(8,128)(2,1)S(1)}) custom-call(s32[2]{0:T(128)S(1)} %copy-done.1, bf16[16,32,1536]{2,1,0:T(8,128)(2,1)S(1)} %copy-done, bf16[16,32,1536]{2,1,0:T(8,128)(2,1)S(1)} %collective-permute-done.1.refs_1_, bf16[16,32,1536]{2,1,0:T(8,128)(2,1)S(1)} %collective-permute-done.2.refs_2_, ...), custom_call_target="tpu_custom_call" | custom-call | flops 1207959552 | bytes 3145728 | tf_op jit(solution)/shard_map/pallas_call | solution.py:137
  178.1 1.7 collective-permute-start.10
  179.8 30.5 %collective-permute-start.14 = (bf16[16,32,512]{2,1,0:T(8,128)(2,1)S(1)}, bf16[16,32,512]{2,1,0:T(8,128)(2,1)S(1)}, u32[]{:S(2)}, u32[]{:S(2)}) collective-permute-start(bf16[16,32,512]{2,1,0:T(8,128)(2,1)S(1)} %get-tuple-element.47), channel_id=1, source_target_pairs={{0,2},{1,3},{2,0},{3,1},{4,6},{5,7},{6,4},{7,5},{8,10},{9,11},{10,... | collective-permute-start | bytes 1572872 | tf_op jit(solution)/shard_map/ppermute | solution.py:343
  210.3 3.4 %shard_map.90 = (bf16[16,32,128]{2,1,0:T(8,128)(2,1)S(1)}, bf16[16,32,128]{2,1,0:T(8,128)(2,1)S(1)}) custom-call(s32[2]{0:T(128)S(1)} %copy-done.1, bf16[16,32,1536]{2,1,0:T(8,128)(2,1)S(1)} %copy-done, bf16[16,32,1536]{2,1,0:T(8,128)(2,1)S(1)} %collective-permute-done.1.refs_1_, bf16[16,32,1536]{2,1,0:T(8,128)(2,1)S(1)} %collective-permute-done.2.refs_2_, ...), custom_call_target="tpu_custom_call" | custom-call | flops 402653184 | bytes 3145728 | tf_op jit(solution)/shard_map/pallas_call | solution.py:137
  214.2 2.5 %shard_map.91 = (bf16[16,32,384]{2,1,0:T(8,128)(2,1)S(1)}, f32[2,16,32,32]{3,2,1,0:T(8,128)S(1)}) custom-call(s32[2,32]{1,0:T(2,128)S(1)} %get-tuple-element.56.refs_7_.rows, s32[2,32]{1,0:T(2,128)S(1)} %select_reduce_fusion.refs_9_.offsets, f32[2,16,32,32]{3,2,1,0:T(8,128)S(1)} %get-tuple-element.40.refs_7_.before, ...), custom_call_target="tpu_custom_call" | custom-call | tf_op jit(solution)/shard_map/pallas_call | solution.py:220
  216.8 6.0 %collective-permute-start.15 = (bf16[16,32,384]{2,1,0:T(8,128)(2,1)S(1)}, bf16[16,32,384]{2,1,0:T(8,128)(2,1)S(1)}, u32[]{:S(2)}, u32[]{:S(2)}) collective-permute-start(bf16[16,32,384]{2,1,0:T(8,128)(2,1)S(1)} %get-tuple-element.48), channel_id=1, source_target_pairs={{0,2},{1,3},{2,0},{3,1},{4,6},{5,7},{6,4},{7,5},{8,10},{9,11},{10,... | collective-permute-start | bytes 1179656 | tf_op jit(solution)/shard_map/ppermute | solution.py:343
  222.8 2.2 shard_map.92
  225.1 2.1 collective-permute-start.13
  227.2 5.6 %collective-permute-done.15.refs_7_ = bf16[16,32,384]{2,1,0:T(8,128)(2,1)S(1)} collective-permute-done((bf16[16,32,384]{2,1,0:T(8,128)(2,1)S(1)}, bf16[16,32,384]{2,1,0:T(8,128)(2,1)S(1)}, u32[]{:S(2)}, u32[]{:S(2)}) %collective-permute-start.15) | collective-permute-done | bytes 393248 | tf_op jit(solution)/shard_map/ppermute | solution.py:343
  234.4 3.5 %collective-permute-done.13.there = f32[16,32,32]{2,1,0:T(8,128)S(1)} collective-permute-done((f32[16,32,32]{2,1,0:T(8,128)S(1)}, f32[16,32,32]{2,1,0:T(8,128)S(1)}, u32[]{:S(2)}, u32[]{:S(2)}) %collective-permute-start.13) | collective-permute-done | bytes 65568 | tf_op jit(solution)/shard_map/ppermute | solution.py:343
  237.9 1.8 shard_map.94
  (67 shorter events, 18.9 us)
Async XLA Ops:
  3.3 4.5 %copy-start.5 = (s32[16,2]{0,1:T(2,128)S(1)}, s32[16,2]{0,1:T(2,128)}, u32[]{:S(2)}) copy-start(s32[16,2]{0,1:T(2,128)} %param.9) | copy-start | bytes 388
  3.3 27.6 %all-to-all-start = ((bf16[4,1,256,768]{3,2,1,0:T(8,128)(2,1)}), bf16[4,1,256,768]{3,2,1,0:T(8,128)(2,1)}, u32[]{:S(2)}, u32[]{:S(2)}) async-start(bf16[4,1,256,768]{3,2,1,0:T(8,128)(2,1)} %slice.42), calls=%async_computation | async-start | bytes 3145728 | tf_op jit(solution)/shard_map/all_to_all | solution.py:351
  8.0 3.8 %copy-start.4 = (s32[32]{0:T(128)}, s32[32]{0:T(128)S(1)}, u32[]{:S(2)}) copy-start(s32[32]{0:T(128)S(1)} %reshape.71.orbs) | copy-start | bytes 388
  8.0 27.5 %collective-permute-start = (s32[32]{0:T(128)S(1)}, s32[32]{0:T(128)S(1)}, u32[]{:S(2)}, u32[]{:S(2)}) collective-permute-start(s32[32]{0:T(128)S(1)} %reshape.71.orbs), channel_id=1, source_target_pairs={{0,2},{1,3},{2,0},{3,1},{4,6},{5,7},{6,4},{7,5},{8,10},{9,11},{10,... | collective-permute-start | bytes 392 | tf_op jit(solution)/shard_map/ppermute | solution.py:343
  11.7 9.0 %copy-start.7 = (s32[32]{0:T(128)S(1)}, s32[32]{0:T(128)}, u32[]{:S(2)}) copy-start(s32[32]{0:T(128)} %param.13) | copy-start | bytes 388
  17.1 47.7 %collective-permute-start.1 = (bf16[16,32,1536]{2,1,0:T(8,128)(2,1)}, bf16[16,32,1536]{2,1,0:T(8,128)(2,1)S(1)}, u32[]{:S(2)}, u32[]{:S(2)}) collective-permute-start(bf16[16,32,1536]{2,1,0:T(8,128)(2,1)} %get-tuple-element.32), channel_id=1, source_target_pairs={{0,1},{1,0},{2,3},{3,2},{4,5},{5,4},{6,7},{7,6},{8,9},{9,8},{10,11... | collective-permute-start | bytes 4718600 | tf_op jit(solution)/shard_map/ppermute | solution.py:343
  18.7 53.6 %collective-permute-start.2 = (bf16[16,32,1536]{2,1,0:T(8,128)(2,1)}, bf16[16,32,1536]{2,1,0:T(8,128)(2,1)S(1)}, u32[]{:S(2)}, u32[]{:S(2)}) collective-permute-start(bf16[16,32,1536]{2,1,0:T(8,128)(2,1)} %get-tuple-element.33), channel_id=1, source_target_pairs={{0,2},{1,3},{2,0},{3,1},{4,6},{5,7},{6,4},{7,5},{8,10},{9,11},{10,... | collective-permute-start | bytes 4718600 | tf_op jit(solution)/shard_map/ppermute | solution.py:343
  19.2 69.7 %collective-permute-start.3 = (bf16[16,32,1536]{2,1,0:T(8,128)(2,1)}, bf16[16,32,1536]{2,1,0:T(8,128)(2,1)}, u32[]{:S(2)}, u32[]{:S(2)}) collective-permute-start(bf16[16,32,1536]{2,1,0:T(8,128)(2,1)} %get-tuple-element.34), channel_id=1, source_target_pairs={{0,3},{1,2},{2,1},{3,0},{4,7},{5,6},{6,5},{7,4},{8,11},{9,10},{10,... | collective-permute-start | bytes 4718600 | tf_op jit(solution)/shard_map/ppermute | solution.py:343
  30.9 4.5 %copy-start.3 = (f32[16,2,32]{2,1,0:T(2,128)S(1)}, f32[16,2,32]{2,1,0:T(2,128)}, u32[]{:S(2)}) copy-start(f32[16,2,32]{2,1,0:T(2,128)} %param.11) | copy-start | bytes 12292
  30.9 24.6 %all-to-all-start.1 = ((bf16[4,1,256,768]{3,2,1,0:T(8,128)(2,1)}), bf16[4,1,256,768]{3,2,1,0:T(8,128)(2,1)}, u32[]{:S(2)}, u32[]{:S(2)}) async-start(bf16[4,1,256,768]{3,2,1,0:T(8,128)(2,1)} %slice.43), calls=%async_computation.1 | async-start | bytes 3145728 | tf_op jit(solution)/shard_map/all_to_all | solution.py:351
  42.8 55.3 %collective-permute-start.5 = (bf16[1024,768]{1,0:T(8,128)(2,1)}, bf16[1024,768]{1,0:T(8,128)(2,1)}, u32[]{:S(2)}, u32[]{:S(2)}) collective-permute-start(bf16[1024,768]{1,0:T(8,128)(2,1)} %convolution_convert_fusion.1.refs_4_), channel_id=1, source_target_pairs={{2,4},{3,5},{4,2},{5,3},{10,12},{11,13},{12,10},{13,11},{18,20},{1... | collective-permute-start | bytes 4718600 | tf_op jit(solution)/shard_map/ppermute | solution.py:401
  60.4 3.1 %copy-start.2 = (bf16[512,768]{1,0:T(8,128)(2,1)S(1)}, bf16[512,768]{1,0:T(8,128)(2,1)}, u32[]{:S(2)}) copy-start(bf16[512,768]{1,0:T(8,128)(2,1)} %slice.59) | copy-start | bytes 2359300
  61.7 7.6 %copy-start.6 = (f32[32]{0:T(128)S(1)}, f32[32]{0:T(128)}, u32[]{:S(2)}) copy-start(f32[32]{0:T(128)} %param.12) | copy-start | bytes 388
  61.7 64.1 %collective-permute-start.6 = (bf16[1024,768]{1,0:T(8,128)(2,1)}, bf16[1024,768]{1,0:T(8,128)(2,1)}, u32[]{:S(2)}, u32[]{:S(2)}) collective-permute-start(bf16[1024,768]{1,0:T(8,128)(2,1)} %convolution_convert_fusion.refs_5_), channel_id=1, source_target_pairs={{2,4},{3,5},{4,2},{5,3},{10,12},{11,13},{12,10},{13,11},{18,20},{1... | collective-permute-start | bytes 4718600 | tf_op jit(solution)/shard_map/ppermute | solution.py:401
  64.8 61.0 %collective-permute-start.7 = (bf16[512,1536]{1,0:T(8,128)(2,1)}, bf16[512,1536]{1,0:T(8,128)(2,1)}, u32[]{:S(2)}, u32[]{:S(2)}) collective-permute-start(bf16[512,1536]{1,0:T(8,128)(2,1)} %pad_maximum_fusion), channel_id=1, source_target_pairs={{0,6},{1,7},{6,0},{7,1},{8,14},{9,15},{14,8},{15,9},{16,22},{17,23... | collective-permute-start | bytes 4718600 | tf_op jit(solution)/shard_map/ppermute | solution.py:404
  71.0 17.9 %copy-start = (bf16[16,32,1536]{2,1,0:T(8,128)(2,1)S(1)}, bf16[16,32,1536]{2,1,0:T(8,128)(2,1)}, u32[]{:S(2)}) copy-start(bf16[16,32,1536]{2,1,0:T(8,128)(2,1)} %get-tuple-element.31.refs_0_) | copy-start | bytes 4718596
  71.0 17.9 %copy-start.1 = (s32[2]{0:T(128)S(1)}, s32[2]{0:T(128)}, u32[]{:S(2)}) copy-start(s32[2]{0:T(128)} %pad_add_fusion.1.place) | copy-start | bytes 28
  72.3 102.4 %collective-permute-start.9 = (bf16[384,1536]{1,0:T(8,128)(2,1)S(1)}, bf16[384,1536]{1,0:T(8,128)(2,1)S(1)}, u32[]{:S(2)}, u32[]{:S(2)}) collective-permute-start(bf16[384,1536]{1,0:T(8,128)(2,1)S(1)} %pad_maximum_fusion.1), channel_id=1, source_target_pairs={{0,6},{1,7},{6,0},{7,1},{8,14},{9,15},{14,8},{15,9},{16,22},{17,23... | collective-permute-start | bytes 3538952 | tf_op jit(solution)/shard_map/ppermute | solution.py:404
  96.4 76.0 %collective-permute-start.4 = (bf16[16,32,1024]{2,1,0:T(8,128)(2,1)S(1)}, bf16[16,32,1024]{2,1,0:T(8,128)(2,1)S(1)}, u32[]{:S(2)}, u32[]{:S(2)}) collective-permute-start(bf16[16,32,1024]{2,1,0:T(8,128)(2,1)S(1)} %get-tuple-element.37), channel_id=1, source_target_pairs={{0,1},{1,0},{2,3},{3,2},{4,5},{5,4},{6,7},{7,6},{8,9},{9,8},{10,11... | collective-permute-start | bytes 3145736 | tf_op jit(solution)/shard_map/ppermute | solution.py:343
  129.9 42.4 %collective-permute-start.8 = (bf16[16,32,512]{2,1,0:T(8,128)(2,1)S(1)}, bf16[16,32,512]{2,1,0:T(8,128)(2,1)S(1)}, u32[]{:S(2)}, u32[]{:S(2)}) collective-permute-start(bf16[16,32,512]{2,1,0:T(8,128)(2,1)S(1)} %get-tuple-element.39), channel_id=1, source_target_pairs={{0,1},{1,0},{2,3},{3,2},{4,5},{5,4},{6,7},{7,6},{8,9},{9,8},{10,11... | collective-permute-start | bytes 1572872 | tf_op jit(solution)/shard_map/ppermute | solution.py:343
  132.4 77.8 %collective-permute-start.11 = (bf16[128,1536]{1,0:T(8,128)(2,1)S(1)}, bf16[128,1536]{1,0:T(8,128)(2,1)S(1)}, u32[]{:S(2)}, u32[]{:S(2)}) collective-permute-start(bf16[128,1536]{1,0:T(8,128)(2,1)S(1)} %pad_maximum_fusion.2), channel_id=1, source_target_pairs={{0,6},{1,7},{6,0},{7,1},{8,14},{9,15},{14,8},{15,9},{16,22},{17,23... | collective-permute-start | bytes 1179656 | tf_op jit(solution)/shard_map/ppermute | solution.py:404
  178.1 36.1 %collective-permute-start.10 = (bf16[16,32,384]{2,1,0:T(8,128)(2,1)S(1)}, bf16[16,32,384]{2,1,0:T(8,128)(2,1)S(1)}, u32[]{:S(2)}, u32[]{:S(2)}) collective-permute-start(bf16[16,32,384]{2,1,0:T(8,128)(2,1)S(1)} %get-tuple-element.42), channel_id=1, source_target_pairs={{0,1},{1,0},{2,3},{3,2},{4,5},{5,4},{6,7},{7,6},{8,9},{9,8},{10,11... | collective-permute-start | bytes 1179656 | tf_op jit(solution)/shard_map/ppermute | solution.py:343
  179.8 47.4 %collective-permute-start.14 = (bf16[16,32,512]{2,1,0:T(8,128)(2,1)S(1)}, bf16[16,32,512]{2,1,0:T(8,128)(2,1)S(1)}, u32[]{:S(2)}, u32[]{:S(2)}) collective-permute-start(bf16[16,32,512]{2,1,0:T(8,128)(2,1)S(1)} %get-tuple-element.47), channel_id=1, source_target_pairs={{0,2},{1,3},{2,0},{3,1},{4,6},{5,7},{6,4},{7,5},{8,10},{9,11},{10,... | collective-permute-start | bytes 1572872 | tf_op jit(solution)/shard_map/ppermute | solution.py:343
  213.6 9.1 %collective-permute-start.12 = (bf16[16,32,128]{2,1,0:T(8,128)(2,1)S(1)}, bf16[16,32,128]{2,1,0:T(8,128)(2,1)S(1)}, u32[]{:S(2)}, u32[]{:S(2)}) collective-permute-start(bf16[16,32,128]{2,1,0:T(8,128)(2,1)S(1)} %get-tuple-element.45), channel_id=1, source_target_pairs={{0,1},{1,0},{2,3},{3,2},{4,5},{5,4},{6,7},{7,6},{8,9},{9,8},{10,11... | collective-permute-start | bytes 393224 | tf_op jit(solution)/shard_map/ppermute | solution.py:343
  216.8 16.0 %collective-permute-start.15 = (bf16[16,32,384]{2,1,0:T(8,128)(2,1)S(1)}, bf16[16,32,384]{2,1,0:T(8,128)(2,1)S(1)}, u32[]{:S(2)}, u32[]{:S(2)}) collective-permute-start(bf16[16,32,384]{2,1,0:T(8,128)(2,1)S(1)} %get-tuple-element.48), channel_id=1, source_target_pairs={{0,2},{1,3},{2,0},{3,1},{4,6},{5,7},{6,4},{7,5},{8,10},{9,11},{10,... | collective-permute-start | bytes 1179656 | tf_op jit(solution)/shard_map/ppermute | solution.py:343
  225.0 12.9 %collective-permute-start.16 = (bf16[16,32,128]{2,1,0:T(8,128)(2,1)S(1)}, bf16[16,32,128]{2,1,0:T(8,128)(2,1)S(1)}, u32[]{:S(2)}, u32[]{:S(2)}) collective-permute-start(bf16[16,32,128]{2,1,0:T(8,128)(2,1)S(1)} %get-tuple-element.49), channel_id=1, source_target_pairs={{0,2},{1,3},{2,0},{3,1},{4,6},{5,7},{6,4},{7,5},{8,10},{9,11},{10,... | collective-permute-start | bytes 393224 | tf_op jit(solution)/shard_map/ppermute | solution.py:343
  225.1 12.8 %collective-permute-start.13 = (f32[16,32,32]{2,1,0:T(8,128)S(1)}, f32[16,32,32]{2,1,0:T(8,128)S(1)}, u32[]{:S(2)}, u32[]{:S(2)}) collective-permute-start(f32[16,32,32]{2,1,0:T(8,128)S(1)} %slice_bitcast_fusion), channel_id=1, source_target_pairs={{0,2},{1,3},{2,0},{3,1},{4,6},{5,7},{6,4},{7,5},{8,10},{9,11},{10,... | collective-permute-start | bytes 196616 | tf_op jit(solution)/shard_map/ppermute | solution.py:343

commit v4 on v3

--- a/solution.py
+++ b/solution.py
@@ -343,7 +343,6 @@
         return lax.ppermute(array, "orb", [(i, i ^ mask) for i in range(orb_count)])
 
     own_orbs = pair_orbs.reshape(side_count)
-    mate_orbs = across(own_orbs, inner)
     place = jnp.stack([region, me]).astype(jnp.int32)
     half = dom_count // 2
 
@@ -361,28 +360,19 @@
     packed = pack(
         own_orbs, place, pno_coef.reshape(side_count, pno_count, dom_count), group, capacity
     )
-    later, packed = lax.optimization_barrier((raw_ints, packed))
-    raw_parts.append(exchange(later, 1))
     blocks = [packed[0]]
     for m in range(1, group):
         blocks.append(across(packed[m], m))
     own_offset = fit_offset[region * orb_count + me]
-    turned = lax.optimization_barrier(jnp.roll(fit_inverse[0], own_offset, axis=0))
-    orbs = jnp.stack([own_orbs, mate_orbs])
-    differs = orbs ^ me
-    other_half = (differs & group) != 0
-    line = jnp.where(other_half, inner, 0) + (differs & (inner - 1))
-    home = jnp.arange(2, dtype=jnp.int32)[:, None]
-    position = slots_of(orbs)
-    there = ((differs & inner) != 0) != other_half
-    rows = jnp.where(there, -1, line * 2 * capacity + home * capacity + position)
-    rows_home = jnp.where(there, -1, line * capacity + position)
+    turned = jnp.roll(fit_inverse[0], own_offset, axis=0)
+    mate_orbs = across(own_orbs, inner)
     orb_total = occ_energy.shape[0]
-    global_orb = region * orb_count + orbs
-    selector = global_orb[:, :, None] == jnp.arange(orb_total, dtype=jnp.int32)[None, None, :]
-    offsets = jnp.sum(jnp.where(selector, fit_offset[None, None, :], 0), axis=2)
-    occupied = jnp.sum(jnp.where(selector[0], occ_energy[None, :], 0.0), axis=1)
-    occupied = occupied.reshape(pair_count, 2)
+
+    def pick(values, chosen):
+        selector = (region * orb_count + chosen)[:, None] == jnp.arange(orb_total, dtype=jnp.int32)
+        return jnp.sum(jnp.where(selector, values[None, :], 0), axis=1)
+
+    occupied = pick(occ_energy, own_orbs).reshape(pair_count, 2)
     denominator = (
         pno_energy[:, 0, :, None]
         + pno_energy[:, 1, None, :]
@@ -399,6 +389,9 @@
             jnp.dot(turned, raw_parts[k], preferred_element_type=jnp.float32).astype(jnp.bfloat16)
         )
         mirrored.append(lax.ppermute(fitted[k], "orb", middles))
+        if k == 0:
+            later, fitted[0] = lax.optimization_barrier((raw_ints, fitted[0]))
+            raw_parts.append(exchange(later, 1))
     for begin, size in spans:
         chunk = jnp.concatenate([part[begin : begin + size] for part in fitted], axis=1)
         mirrored.append(lax.ppermute(chunk, "orb", ends))
@@ -432,7 +425,18 @@
         fit_rows,
         [denominator],
     )
+    mate_orbs, *near = lax.optimization_barrier((mate_orbs, *near))
     near = hop(near)
+    orbs = jnp.stack([own_orbs, mate_orbs])
+    differs = orbs ^ me
+    other_half = (differs & group) != 0
+    line = jnp.where(other_half, inner, 0) + (differs & (inner - 1))
+    home = jnp.arange(2, dtype=jnp.int32)[:, None]
+    position = slots_of(orbs)
+    there = ((differs & inner) != 0) != other_half
+    rows = jnp.where(there, -1, line * 2 * capacity + home * capacity + position)
+    rows_home = jnp.where(there, -1, line * capacity + position)
+    offsets = pick(fit_offset, orbs.reshape(2 * side_count)).reshape(2, side_count)
     far, others = [None] * 3, [None] * 3
     far[0] = project_far(0, [rows, rows_home, offsets])
     others[0], here = pass_on(0, jnp.zeros((8, 128), jnp.float32), [])

time: 242 us -> 237 us (0.979)
  starting transfers between devices: 110 us -> 87.8 us
  waiting for transfers between devices: 60.8 us -> 77.8 us
  other arithmetic: 8.42 us -> 4.36 us
  Pallas kernels: 34.2 us -> 37.1 us
    ppermute x12, starting transfers between devices: 49.7 us -> 15.4 us  [across(): return lax.ppermute(array, 'orb', [(i, i ^ mask) for i in range(orb_count)])]
    ppermute x12, waiting for transfers between devices: 22.4 us -> 54.4 us  [across(): return lax.ppermute(array, 'orb', [(i, i ^ mask) for i in range(orb_count)])]
    ppermute x3, waiting for transfers between devices: 27.7 us -> 0.01 us  [on_device(): mirrored.append(lax.ppermute(chunk, 'orb', ends))]
    all_to_all x2, waiting for transfers between devices: 10.7 us -> 23.3 us  [exchange(): lax.all_to_all(array[:, :, :, k * half:(k + 1) * half], 'aux', split_axis...]
    ppermute x3, starting transfers between devices: 47.5 us -> 59.6 us  [on_device(): mirrored.append(lax.ppermute(chunk, 'orb', ends))]
    concatenate x1 -> x0, other arithmetic: 4.95 us -> none  [on_device(): jnp.roll(fit_inverse[0], own_offset, axis=0)]
    pallas_call x4, Pallas kernels: 18.3 us -> 21.4 us  [project(): pl.pallas_call(functools.partial(project_kernel, group, capacity, kind, t...]
    unnamed x17 -> x29, local copies, waits for them, and re-layouts: 0.12 us -> 2.94 us
  transfers between devices with their start and end apart: 19 -> 19, of which waited for: 5 -> 9; matrix products, arithmetic and copies ran while one was open for 12% -> 7% of each run, Pallas kernels for 13% -> 15%
where the time goes in v4:
time: 237 us
  starting transfers between devices  87.8 us (37%)
  waiting for transfers between devices  77.8 us (33%)
  Pallas kernels  37.1 us (16%)
  local copies, waits for them, and re-layouts  15.1 us (6%)
  matrix products  11.5 us (5%)
  other arithmetic  4.36 us (2%)
  between operations  2.96 us (1%)
    ppermute x3, starting transfers between devices, on_device(): mirrored.append(lax.ppermute(chunk, 'orb', ends))  59.6 us
    ppermute x12, waiting for transfers between devices, across(): return lax.ppermute(array, 'orb', [(i, i ^ mask) for i in range(orb_count)])  54.4 us
    all_to_all x2, waiting for transfers between devices, exchange(): lax.all_to_all(array[:, :, :, k * half:(k + 1) * half], 'aux', split_axis...  23.3 us
    pallas_call x4, Pallas kernels, project(): pl.pallas_call(functools.partial(project_kernel, group, capacity, kind, t...  21.4 us
    ppermute x12, starting transfers between devices, across(): return lax.ppermute(array, 'orb', [(i, i ^ mask) for i in range(orb_count)])  15.4 us
    dot_general x2, matrix products, on_device(): jnp.dot(turned, raw_parts[k], preferred_element_type=jnp.float32)  11.5 us
    all_to_all x2, starting transfers between devices, exchange(): lax.all_to_all(array[:, :, :, k * half:(k + 1) * half], 'aux', split_axis...  8.88 us
    pallas_call x3, Pallas kernels, relay(): pl.pallas_call(functools.partial(relay_kernel, inner, (span,), margin), o...  7.04 us
  transfers between devices with their start and end apart: 19, of which 9 were waited for; matrix products, arithmetic and copies ran while one was open for 7% of the time, Pallas kernels for 15%

profile of v4, /device:TPU:0, one launch (start us, length us, event | category | flops | bytes accessed | tf_op | source)
XLA Modules:
  0.0 236.6 jit_solution(8213070250556970512)
XLA Ops:
  0.6 2.7 %slice.39 = bf16[4,1,256,768]{3,2,1,0:T(8,128)(2,1)} slice(bf16[4,1,256,1536]{3,2,1,0:T(8,128)(2,1)} %param.7), slice={[0:4], [0:1], [0:256], [0:768]} | slice | bytes 3145728 | tf_op jit(solution)/shard_map/slice | solution.py:351
  3.3 4.4 %all-to-all-start = ((bf16[4,1,256,768]{3,2,1,0:T(8,128)(2,1)}), bf16[4,1,256,768]{3,2,1,0:T(8,128)(2,1)S(1)}, u32[]{:S(2)}, u32[]{:S(2)}) async-start(bf16[4,1,256,768]{3,2,1,0:T(8,128)(2,1)} %slice.39), calls=%async_computation | async-start | bytes 3145728 | tf_op jit(solution)/shard_map/all_to_all | solution.py:350
  10.2 17.5 %all-to-all-done = bf16[4,1,256,768]{3,2,1,0:T(8,128)(2,1)S(1)} async-done(((bf16[4,1,256,768]{3,2,1,0:T(8,128)(2,1)}), bf16[4,1,256,768]{3,2,1,0:T(8,128)(2,1)S(1)}, u32[]{:S(2)}, u32[]{:S(2)}) %all-to-all-start) | async-done | bytes 1572896 | tf_op jit(solution)/shard_map/all_to_all | solution.py:350
  27.7 5.6 %convolution_convert_fusion.1.refs_4_ = bf16[1024,768]{1,0:T(8,128)(2,1)} fusion(bf16[1024,768]{1,0:T(8,128)(2,1)S(1)} %bitcast.15, s32[]{:T(128)S(6)} %select_n.41, bf16[1024,1024]{1,0:T(8,128)(2,1)} %bitcast.20), kind=kOutput, calls=%fused_computation.4 | convolution fusion | flops 1615593472 | bytes 5242884 | tf_op jit(solution)/shard_map/dot_general | solution.py:389
  34.6 4.5 %all-to-all-start.1 = ((bf16[4,1,256,768]{3,2,1,0:T(8,128)(2,1)}), bf16[4,1,256,768]{3,2,1,0:T(8,128)(2,1)}, u32[]{:S(2)}, u32[]{:S(2)}) async-start(bf16[4,1,256,768]{3,2,1,0:T(8,128)(2,1)} %slice.40), calls=%async_computation.1 | async-start | bytes 3145728 | tf_op jit(solution)/shard_map/all_to_all | solution.py:350
  40.4 5.3 %pack.1 = (bf16[16,32,1536]{2,1,0:T(8,128)(2,1)}, bf16[16,32,1536]{2,1,0:T(8,128)(2,1)}, bf16[16,32,1536]{2,1,0:T(8,128)(2,1)}, bf16[16,32,1536]{2,1,0:T(8,128)(2,1)}) custom-call(s32[32]{0:T(128)} %reshape.70.orbs, s32[2]{0:T(128)} %pad_add_fusion.1.place, bf16[32,32,1536]{2,1,0:T(8,128)(2,1)} %bitcast.14), custom_call_target="tpu_custom_call" | custom-call | bytes 9437184 | tf_op jit(solution)/shard_map/pack/pallas_call | solution.py:59
  45.8 2.4 %collective-permute-start.1 = (bf16[16,32,1536]{2,1,0:T(8,128)(2,1)}, bf16[16,32,1536]{2,1,0:T(8,128)(2,1)S(1)}, u32[]{:S(2)}, u32[]{:S(2)}) collective-permute-start(bf16[16,32,1536]{2,1,0:T(8,128)(2,1)} %get-tuple-element.28), channel_id=1, source_target_pairs={{0,1},{1,0},{2,3},{3,2},{4,5},{5,4},{6,7},{7,6},{8,9},{9,8},{10,11... | collective-permute-start | bytes 4718600 | tf_op jit(solution)/shard_map/ppermute | solution.py:343
  48.2 1.6 collective-permute-start.2
  50.3 1.9 collective-permute-start.5
  53.4 5.8 %all-to-all-done.1 = bf16[4,1,256,768]{3,2,1,0:T(8,128)(2,1)} async-done(((bf16[4,1,256,768]{3,2,1,0:T(8,128)(2,1)}), bf16[4,1,256,768]{3,2,1,0:T(8,128)(2,1)}, u32[]{:S(2)}, u32[]{:S(2)}) %all-to-all-start.1) | async-done | bytes 1572896 | tf_op jit(solution)/shard_map/all_to_all | solution.py:350
  59.2 5.9 %convolution_convert_fusion.refs_5_ = bf16[1024,768]{1,0:T(8,128)(2,1)} fusion(bf16[1024,768]{1,0:T(8,128)(2,1)} %bitcast.6, s32[]{:T(128)S(6)} %select_n.41, bf16[1024,1024]{1,0:T(8,128)(2,1)} %bitcast.21), kind=kOutput, calls=%fused_computation.3 | convolution fusion | flops 1615593472 | bytes 5242884 | tf_op jit(solution)/shard_map/dot_general | solution.py:389
  66.4 2.1 collective-permute-start.6
  69.7 13.7 %collective-permute-done.1.refs_1_ = bf16[16,32,1536]{2,1,0:T(8,128)(2,1)S(1)} collective-permute-done((bf16[16,32,1536]{2,1,0:T(8,128)(2,1)}, bf16[16,32,1536]{2,1,0:T(8,128)(2,1)S(1)}, u32[]{:S(2)}, u32[]{:S(2)}) %collective-permute-start.1) | collective-permute-done | bytes 1572896 | tf_op jit(solution)/shard_map/ppermute | solution.py:343
  83.4 5.7 %collective-permute-start.7 = (bf16[512,1536]{1,0:T(8,128)(2,1)}, bf16[512,1536]{1,0:T(8,128)(2,1)}, u32[]{:S(2)}, u32[]{:S(2)}) collective-permute-start(bf16[512,1536]{1,0:T(8,128)(2,1)} %pad_maximum_fusion), channel_id=1, source_target_pairs={{0,6},{1,7},{6,0},{7,1},{8,14},{9,15},{14,8},{15,9},{16,22},{17,23... | collective-permute-start | bytes 4718600 | tf_op jit(solution)/shard_map/ppermute | solution.py:397
  91.7 26.9 %collective-permute-done.3.refs_3_ = bf16[16,32,1536]{2,1,0:T(8,128)(2,1)} collective-permute-done((bf16[16,32,1536]{2,1,0:T(8,128)(2,1)}, bf16[16,32,1536]{2,1,0:T(8,128)(2,1)}, u32[]{:S(2)}, u32[]{:S(2)}) %collective-permute-start.3) | collective-permute-done | bytes 1572896 | tf_op jit(solution)/shard_map/ppermute | solution.py:343
  118.6 51.9 %collective-permute-start.9 = (bf16[384,1536]{1,0:T(8,128)(2,1)}, bf16[384,1536]{1,0:T(8,128)(2,1)}, u32[]{:S(2)}, u32[]{:S(2)}) collective-permute-start(bf16[384,1536]{1,0:T(8,128)(2,1)} %pad_maximum_fusion.1), channel_id=1, source_target_pairs={{0,6},{1,7},{6,0},{7,1},{8,14},{9,15},{14,8},{15,9},{16,22},{17,23... | collective-permute-start | bytes 3538952 | tf_op jit(solution)/shard_map/ppermute | solution.py:397
  170.5 8.3 %shard_map.86 = (bf16[16,32,1024]{2,1,0:T(8,128)(2,1)S(1)}, bf16[16,32,1024]{2,1,0:T(8,128)(2,1)}) custom-call(s32[2]{0:T(128)S(1)} %copy-done.7, bf16[16,32,1536]{2,1,0:T(8,128)(2,1)S(1)} %copy-done, bf16[16,32,1536]{2,1,0:T(8,128)(2,1)S(1)} %collective-permute-done.1.refs_1_, bf16[16,32,1536]{2,1,0:T(8,128)(2,1)} %collective-permute-done.2.refs_2_, ...), custom_call_target="tpu_custom_call" | custom-call | flops 3221225472 | bytes 3145728 | tf_op jit(solution)/shard_map/pallas_call | solution.py:137
  178.8 1.6 collective-permute-start.4
  183.8 4.3 %shard_map.87 = (bf16[16,32,512]{2,1,0:T(8,128)(2,1)S(1)}, bf16[16,32,512]{2,1,0:T(8,128)(2,1)S(1)}) custom-call(s32[2]{0:T(128)S(1)} %copy-done.7, bf16[16,32,1536]{2,1,0:T(8,128)(2,1)S(1)} %copy-done.1, bf16[16,32,1536]{2,1,0:T(8,128)(2,1)S(1)} %copy-done.4, bf16[16,32,1536]{2,1,0:T(8,128)(2,1)} %collective-permute-done.2.refs_2_, ...), custom_call_target="tpu_custom_call" | custom-call | flops 1610612736 | bytes 3145728 | tf_op jit(solution)/shard_map/pallas_call | solution.py:137
  190.7 1.9 collective-permute-start.11
  192.7 2.5 %collective-permute-done.4.refs_1_ = bf16[16,32,1024]{2,1,0:T(8,128)(2,1)S(1)} collective-permute-done((bf16[16,32,1024]{2,1,0:T(8,128)(2,1)}, bf16[16,32,1024]{2,1,0:T(8,128)(2,1)S(1)}, u32[]{:S(2)}, u32[]{:S(2)}) %collective-permute-start.4) | collective-permute-done | bytes 1048608 | tf_op jit(solution)/shard_map/ppermute | solution.py:343
  195.2 6.7 %collective-permute-done.8.refs_3_ = bf16[16,32,512]{2,1,0:T(8,128)(2,1)S(1)} collective-permute-done((bf16[16,32,512]{2,1,0:T(8,128)(2,1)S(1)}, bf16[16,32,512]{2,1,0:T(8,128)(2,1)S(1)}, u32[]{:S(2)}, u32[]{:S(2)}) %collective-permute-start.8) | collective-permute-done | bytes 524320 | tf_op jit(solution)/shard_map/ppermute | solution.py:343
  201.9 2.3 shard_map.88
  204.3 4.5 %shard_map.89 = (bf16[16,32,384]{2,1,0:T(8,128)(2,1)S(1)}, bf16[16,32,384]{2,1,0:T(8,128)(2,1)S(1)}) custom-call(s32[2]{0:T(128)S(1)} %copy-done.7, bf16[16,32,1536]{2,1,0:T(8,128)(2,1)S(1)} %copy-done.2, bf16[16,32,1536]{2,1,0:T(8,128)(2,1)S(1)} %copy-done.5, bf16[16,32,1536]{2,1,0:T(8,128)(2,1)} %collective-permute-done.2.refs_2_, ...), custom_call_target="tpu_custom_call" | custom-call | flops 1207959552 | bytes 3145728 | tf_op jit(solution)/shard_map/pallas_call | solution.py:137
  209.3 4.7 %collective-permute-start.14 = (bf16[16,32,512]{2,1,0:T(8,128)(2,1)S(1)}, bf16[16,32,512]{2,1,0:T(8,128)(2,1)S(1)}, u32[]{:S(2)}, u32[]{:S(2)}) collective-permute-start(bf16[16,32,512]{2,1,0:T(8,128)(2,1)S(1)} %get-tuple-element.47), channel_id=1, source_target_pairs={{0,2},{1,3},{2,0},{3,1},{4,6},{5,7},{6,4},{7,5},{8,10},{9,11},{10,... | collective-permute-start | bytes 1572872 | tf_op jit(solution)/shard_map/ppermute | solution.py:343
  214.0 4.4 %shard_map.90 = (bf16[16,32,128]{2,1,0:T(8,128)(2,1)S(1)}, bf16[16,32,128]{2,1,0:T(8,128)(2,1)S(1)}) custom-call(s32[2]{0:T(128)S(1)} %copy-done.7, bf16[16,32,1536]{2,1,0:T(8,128)(2,1)S(1)} %copy-done.2, bf16[16,32,1536]{2,1,0:T(8,128)(2,1)S(1)} %copy-done.5, bf16[16,32,1536]{2,1,0:T(8,128)(2,1)} %collective-permute-done.2.refs_2_, ...), custom_call_target="tpu_custom_call" | custom-call | flops 402653184 | bytes 3145728 | tf_op jit(solution)/shard_map/pallas_call | solution.py:137
  218.9 2.5 %shard_map.91 = (bf16[16,32,384]{2,1,0:T(8,128)(2,1)S(1)}, f32[2,16,32,32]{3,2,1,0:T(8,128)S(1)}) custom-call(s32[2,32]{1,0:T(2,128)S(1)} %get-tuple-element.56.refs_7_.rows, s32[2,32]{1,0:T(2,128)S(1)} %reshape.73.refs_9_.offsets, f32[2,16,32,32]{3,2,1,0:T(8,128)S(1)} %get-tuple-element.40.refs_7_.before, ...), custom_call_target="tpu_custom_call" | custom-call | tf_op jit(solution)/shard_map/pallas_call | solution.py:220
  223.4 2.2 shard_map.92
  225.8 2.0 collective-permute-start.13
  229.3 1.7 shard_map.93.before
  231.0 2.5 %collective-permute-done.13.there = f32[16,32,32]{2,1,0:T(8,128)S(1)} collective-permute-done((f32[16,32,32]{2,1,0:T(8,128)S(1)}, f32[16,32,32]{2,1,0:T(8,128)S(1)}, u32[]{:S(2)}, u32[]{:S(2)}) %collective-permute-start.13) | collective-permute-done | bytes 65568 | tf_op jit(solution)/shard_map/ppermute | solution.py:343
  233.5 1.7 shard_map.94
  (80 shorter events, 22.0 us)
Async XLA Ops:
  3.3 4.4 %copy-start.13 = (s32[32]{0:T(128)S(1)}, s32[32]{0:T(128)}, u32[]{:S(2)}) copy-start(s32[32]{0:T(128)} %param.13) | copy-start | bytes 388
  3.3 24.4 %all-to-all-start = ((bf16[4,1,256,768]{3,2,1,0:T(8,128)(2,1)}), bf16[4,1,256,768]{3,2,1,0:T(8,128)(2,1)S(1)}, u32[]{:S(2)}, u32[]{:S(2)}) async-start(bf16[4,1,256,768]{3,2,1,0:T(8,128)(2,1)} %slice.39), calls=%async_computation | async-start | bytes 3145728 | tf_op jit(solution)/shard_map/all_to_all | solution.py:350
  27.7 5.6 %copy-start.8 = (bf16[4,1,256,1536]{3,2,1,0:T(8,128)(2,1)S(1)}, bf16[4,1,256,1536]{3,2,1,0:T(8,128)(2,1)}, u32[]{:S(2)}) copy-start(bf16[4,1,256,1536]{3,2,1,0:T(8,128)(2,1)} %param.7) | copy-start | bytes 9437188
  34.6 4.5 %copy-start.11 = (s32[16,2]{0,1:T(2,128)S(1)}, s32[16,2]{0,1:T(2,128)}, u32[]{:S(2)}) copy-start(s32[16,2]{0,1:T(2,128)} %param.9) | copy-start | bytes 388
  34.6 24.6 %all-to-all-start.1 = ((bf16[4,1,256,768]{3,2,1,0:T(8,128)(2,1)}), bf16[4,1,256,768]{3,2,1,0:T(8,128)(2,1)}, u32[]{:S(2)}, u32[]{:S(2)}) async-start(bf16[4,1,256,768]{3,2,1,0:T(8,128)(2,1)} %slice.40), calls=%async_computation.1 | async-start | bytes 3145728 | tf_op jit(solution)/shard_map/all_to_all | solution.py:350
  39.1 10.6 %copy-start.12 = (f32[32]{0:T(128)S(1)}, f32[32]{0:T(128)}, u32[]{:S(2)}) copy-start(f32[32]{0:T(128)} %param.12) | copy-start | bytes 388
  39.8 9.9 %copy-start.10 = (s32[32]{0:T(128)S(1)}, s32[32]{0:T(128)}, u32[]{:S(2)}) copy-start(s32[32]{0:T(128)} %reshape.70.orbs) | copy-start | bytes 388
  45.8 37.6 %collective-permute-start.1 = (bf16[16,32,1536]{2,1,0:T(8,128)(2,1)}, bf16[16,32,1536]{2,1,0:T(8,128)(2,1)S(1)}, u32[]{:S(2)}, u32[]{:S(2)}) collective-permute-start(bf16[16,32,1536]{2,1,0:T(8,128)(2,1)} %get-tuple-element.28), channel_id=1, source_target_pairs={{0,1},{1,0},{2,3},{3,2},{4,5},{5,4},{6,7},{7,6},{8,9},{9,8},{10,11... | collective-permute-start | bytes 4718600 | tf_op jit(solution)/shard_map/ppermute | solution.py:343
  48.2 43.5 %collective-permute-start.2 = (bf16[16,32,1536]{2,1,0:T(8,128)(2,1)}, bf16[16,32,1536]{2,1,0:T(8,128)(2,1)}, u32[]{:S(2)}, u32[]{:S(2)}) collective-permute-start(bf16[16,32,1536]{2,1,0:T(8,128)(2,1)} %get-tuple-element.29), channel_id=1, source_target_pairs={{0,2},{1,3},{2,0},{3,1},{4,6},{5,7},{6,4},{7,5},{8,10},{9,11},{10,... | collective-permute-start | bytes 4718600 | tf_op jit(solution)/shard_map/ppermute | solution.py:343
  49.7 68.8 %collective-permute-start.3 = (bf16[16,32,1536]{2,1,0:T(8,128)(2,1)}, bf16[16,32,1536]{2,1,0:T(8,128)(2,1)}, u32[]{:S(2)}, u32[]{:S(2)}) collective-permute-start(bf16[16,32,1536]{2,1,0:T(8,128)(2,1)} %get-tuple-element.30), channel_id=1, source_target_pairs={{0,3},{1,2},{2,1},{3,0},{4,7},{5,6},{6,5},{7,4},{8,11},{9,10},{10,... | collective-permute-start | bytes 4718600 | tf_op jit(solution)/shard_map/ppermute | solution.py:343
  50.3 130.6 %collective-permute-start.5 = (bf16[1024,768]{1,0:T(8,128)(2,1)}, bf16[1024,768]{1,0:T(8,128)(2,1)}, u32[]{:S(2)}, u32[]{:S(2)}) collective-permute-start(bf16[1024,768]{1,0:T(8,128)(2,1)} %convolution_convert_fusion.1.refs_4_), channel_id=1, source_target_pairs={{2,4},{3,5},{4,2},{5,3},{10,12},{11,13},{12,10},{13,11},{18,20},{1... | collective-permute-start | bytes 4718600 | tf_op jit(solution)/shard_map/ppermute | solution.py:391
  65.1 23.9 %copy-start.9 = (f32[16,2,32]{2,1,0:T(2,128)S(1)}, f32[16,2,32]{2,1,0:T(2,128)}, u32[]{:S(2)}) copy-start(f32[16,2,32]{2,1,0:T(2,128)} %param.11) | copy-start | bytes 12292
  66.3 22.9 %copy-start.6 = (bf16[1024,768]{1,0:T(8,128)(2,1)S(1)}, bf16[1024,768]{1,0:T(8,128)(2,1)}, u32[]{:S(2)}) copy-start(bf16[1024,768]{1,0:T(8,128)(2,1)} %convolution_convert_fusion.1.refs_4_) | copy-start | bytes 4718596
  66.4 114.6 %collective-permute-start.6 = (bf16[1024,768]{1,0:T(8,128)(2,1)}, bf16[1024,768]{1,0:T(8,128)(2,1)}, u32[]{:S(2)}, u32[]{:S(2)}) collective-permute-start(bf16[1024,768]{1,0:T(8,128)(2,1)} %convolution_convert_fusion.refs_5_), channel_id=1, source_target_pairs={{2,4},{3,5},{4,2},{5,3},{10,12},{11,13},{12,10},{13,11},{18,20},{1... | collective-permute-start | bytes 4718600 | tf_op jit(solution)/shard_map/ppermute | solution.py:391
  83.4 87.1 %copy-start.3 = (bf16[16,32,1536]{2,1,0:T(8,128)(2,1)}, bf16[16,32,1536]{2,1,0:T(8,128)(2,1)S(1)}, u32[]{:S(2)}) copy-start(bf16[16,32,1536]{2,1,0:T(8,128)(2,1)S(1)} %collective-permute-done.1.refs_1_) | copy-start | bytes 4718596
  83.4 97.6 %collective-permute-start.7 = (bf16[512,1536]{1,0:T(8,128)(2,1)}, bf16[512,1536]{1,0:T(8,128)(2,1)}, u32[]{:S(2)}, u32[]{:S(2)}) collective-permute-start(bf16[512,1536]{1,0:T(8,128)(2,1)} %pad_maximum_fusion), channel_id=1, source_target_pairs={{0,6},{1,7},{6,0},{7,1},{8,14},{9,15},{14,8},{15,9},{16,22},{17,23... | collective-permute-start | bytes 4718600 | tf_op jit(solution)/shard_map/ppermute | solution.py:397
  89.3 81.2 %copy-start = (bf16[16,32,1536]{2,1,0:T(8,128)(2,1)S(1)}, bf16[16,32,1536]{2,1,0:T(8,128)(2,1)}, u32[]{:S(2)}) copy-start(bf16[16,32,1536]{2,1,0:T(8,128)(2,1)} %get-tuple-element.27.refs_0_) | copy-start | bytes 4718596
  89.3 81.2 %copy-start.7 = (s32[2]{0:T(128)S(1)}, s32[2]{0:T(128)}, u32[]{:S(2)}) copy-start(s32[2]{0:T(128)} %pad_add_fusion.1.place) | copy-start | bytes 28
  91.7 87.1 %collective-permute-start = (s32[32]{0:T(128)S(1)}, s32[32]{0:T(128)S(1)}, u32[]{:S(2)}, u32[]{:S(2)}) collective-permute-start(s32[32]{0:T(128)S(1)} %copy-done.10), channel_id=1, source_target_pairs={{0,2},{1,3},{2,0},{3,1},{4,6},{5,7},{6,4},{7,5},{8,10},{9,11},{10,... | collective-permute-start | bytes 392 | tf_op jit(solution)/shard_map/ppermute | solution.py:343
  118.6 85.7 %collective-permute-start.9 = (bf16[384,1536]{1,0:T(8,128)(2,1)}, bf16[384,1536]{1,0:T(8,128)(2,1)}, u32[]{:S(2)}, u32[]{:S(2)}) collective-permute-start(bf16[384,1536]{1,0:T(8,128)(2,1)} %pad_maximum_fusion.1), channel_id=1, source_target_pairs={{0,6},{1,7},{6,0},{7,1},{8,14},{9,15},{14,8},{15,9},{16,22},{17,23... | collective-permute-start | bytes 3538952 | tf_op jit(solution)/shard_map/ppermute | solution.py:397
  178.8 16.4 %collective-permute-start.4 = (bf16[16,32,1024]{2,1,0:T(8,128)(2,1)}, bf16[16,32,1024]{2,1,0:T(8,128)(2,1)S(1)}, u32[]{:S(2)}, u32[]{:S(2)}) collective-permute-start(bf16[16,32,1024]{2,1,0:T(8,128)(2,1)} %get-tuple-element.37), channel_id=1, source_target_pairs={{0,1},{1,0},{2,3},{3,2},{4,5},{5,4},{6,7},{7,6},{8,9},{9,8},{10,11... | collective-permute-start | bytes 3145736 | tf_op jit(solution)/shard_map/ppermute | solution.py:343
  181.0 1.4 copy-start.1
  188.1 13.9 %collective-permute-start.8 = (bf16[16,32,512]{2,1,0:T(8,128)(2,1)S(1)}, bf16[16,32,512]{2,1,0:T(8,128)(2,1)S(1)}, u32[]{:S(2)}, u32[]{:S(2)}) collective-permute-start(bf16[16,32,512]{2,1,0:T(8,128)(2,1)S(1)} %get-tuple-element.39), channel_id=1, source_target_pairs={{0,1},{1,0},{2,3},{3,2},{4,5},{5,4},{6,7},{7,6},{8,9},{9,8},{10,11... | collective-permute-start | bytes 1572872 | tf_op jit(solution)/shard_map/ppermute | solution.py:343
  189.6 14.7 %copy-start.2 = (bf16[16,32,1536]{2,1,0:T(8,128)(2,1)S(1)}, bf16[16,32,1536]{2,1,0:T(8,128)(2,1)}, u32[]{:S(2)}) copy-start(bf16[16,32,1536]{2,1,0:T(8,128)(2,1)} %get-tuple-element.27.refs_0_) | copy-start | bytes 4718596
  189.6 14.7 %copy-start.5 = (bf16[16,32,1536]{2,1,0:T(8,128)(2,1)S(1)}, bf16[16,32,1536]{2,1,0:T(8,128)(2,1)}, u32[]{:S(2)}) copy-start(bf16[16,32,1536]{2,1,0:T(8,128)(2,1)} %copy-done.3) | copy-start | bytes 4718596
  190.7 23.3 %collective-permute-start.11 = (bf16[128,1536]{1,0:T(8,128)(2,1)S(1)}, bf16[128,1536]{1,0:T(8,128)(2,1)S(1)}, u32[]{:S(2)}, u32[]{:S(2)}) collective-permute-start(bf16[128,1536]{1,0:T(8,128)(2,1)S(1)} %pad_maximum_fusion.2), channel_id=1, source_target_pairs={{0,6},{1,7},{6,0},{7,1},{8,14},{9,15},{14,8},{15,9},{16,22},{17,23... | collective-permute-start | bytes 1179656 | tf_op jit(solution)/shard_map/ppermute | solution.py:397
  208.8 10.1 %collective-permute-start.10 = (bf16[16,32,384]{2,1,0:T(8,128)(2,1)S(1)}, bf16[16,32,384]{2,1,0:T(8,128)(2,1)S(1)}, u32[]{:S(2)}, u32[]{:S(2)}) collective-permute-start(bf16[16,32,384]{2,1,0:T(8,128)(2,1)S(1)} %get-tuple-element.42), channel_id=1, source_target_pairs={{0,1},{1,0},{2,3},{3,2},{4,5},{5,4},{6,7},{7,6},{8,9},{9,8},{10,11... | collective-permute-start | bytes 1179656 | tf_op jit(solution)/shard_map/ppermute | solution.py:343
  209.3 18.5 %collective-permute-start.14 = (bf16[16,32,512]{2,1,0:T(8,128)(2,1)S(1)}, bf16[16,32,512]{2,1,0:T(8,128)(2,1)S(1)}, u32[]{:S(2)}, u32[]{:S(2)}) collective-permute-start(bf16[16,32,512]{2,1,0:T(8,128)(2,1)S(1)} %get-tuple-element.47), channel_id=1, source_target_pairs={{0,2},{1,3},{2,0},{3,1},{4,6},{5,7},{6,4},{7,5},{8,10},{9,11},{10,... | collective-permute-start | bytes 1572872 | tf_op jit(solution)/shard_map/ppermute | solution.py:343
  218.4 5.0 %collective-permute-start.12 = (bf16[16,32,128]{2,1,0:T(8,128)(2,1)S(1)}, bf16[16,32,128]{2,1,0:T(8,128)(2,1)S(1)}, u32[]{:S(2)}, u32[]{:S(2)}) collective-permute-start(bf16[16,32,128]{2,1,0:T(8,128)(2,1)S(1)} %get-tuple-element.45), channel_id=1, source_target_pairs={{0,1},{1,0},{2,3},{3,2},{4,5},{5,4},{6,7},{7,6},{8,9},{9,8},{10,11... | collective-permute-start | bytes 393224 | tf_op jit(solution)/shard_map/ppermute | solution.py:343
  221.4 7.8 %collective-permute-start.15 = (bf16[16,32,384]{2,1,0:T(8,128)(2,1)S(1)}, bf16[16,32,384]{2,1,0:T(8,128)(2,1)S(1)}, u32[]{:S(2)}, u32[]{:S(2)}) collective-permute-start(bf16[16,32,384]{2,1,0:T(8,128)(2,1)S(1)} %get-tuple-element.48), channel_id=1, source_target_pairs={{0,2},{1,3},{2,0},{3,1},{4,6},{5,7},{6,4},{7,5},{8,10},{9,11},{10,... | collective-permute-start | bytes 1179656 | tf_op jit(solution)/shard_map/ppermute | solution.py:343
  225.6 7.9 %collective-permute-start.16 = (bf16[16,32,128]{2,1,0:T(8,128)(2,1)S(1)}, bf16[16,32,128]{2,1,0:T(8,128)(2,1)S(1)}, u32[]{:S(2)}, u32[]{:S(2)}) collective-permute-start(bf16[16,32,128]{2,1,0:T(8,128)(2,1)S(1)} %get-tuple-element.49), channel_id=1, source_target_pairs={{0,2},{1,3},{2,0},{3,1},{4,6},{5,7},{6,4},{7,5},{8,10},{9,11},{10,... | collective-permute-start | bytes 393224 | tf_op jit(solution)/shard_map/ppermute | solution.py:343
  225.8 7.7 %collective-permute-start.13 = (f32[16,32,32]{2,1,0:T(8,128)S(1)}, f32[16,32,32]{2,1,0:T(8,128)S(1)}, u32[]{:S(2)}, u32[]{:S(2)}) collective-permute-start(f32[16,32,32]{2,1,0:T(8,128)S(1)} %slice_bitcast_fusion), channel_id=1, source_target_pairs={{0,2},{1,3},{2,0},{3,1},{4,6},{5,7},{6,4},{7,5},{8,10},{9,11},{10,... | collective-permute-start | bytes 196616 | tf_op jit(solution)/shard_map/ppermute | solution.py:343
  (1 other events, 1.4 us)

commit v5 on v4

--- a/solution.py
+++ b/solution.py
@@ -86,7 +86,7 @@
     at_end = (plane == 0) | (plane == 3)
     for part, (row, column, width, end) in zip(parts, pieces):
 
-        @pl.when(at_end == end if kind else plane >= 0)
+        @pl.when((plane >= 0) if end is None else (at_end == end))
         def _(part=part, row=row, column=column, width=width):
             copy(
                 part.at[pl.ds(row, row_count)], right.at[:, pl.ds(column, width)], right_sem
@@ -383,18 +383,19 @@
     reverse = group + inner
     ends = [(i, i ^ reverse) for i in range(orb_count) if i // inner in (0, 3)]
     middles = [(i, i ^ reverse) for i in range(orb_count) if i // inner in (1, 2)]
-    fitted, mirrored = [], []
+    fitted = []
     for k in range(2):
         fitted.append(
             jnp.dot(turned, raw_parts[k], preferred_element_type=jnp.float32).astype(jnp.bfloat16)
         )
-        mirrored.append(lax.ppermute(fitted[k], "orb", middles))
         if k == 0:
+            from_middle = lax.ppermute(fitted[0], "orb", middles)
+            from_end = lax.ppermute(fitted[0], "orb", ends)
             later, fitted[0] = lax.optimization_barrier((raw_ints, fitted[0]))
             raw_parts.append(exchange(later, 1))
+    mirrored = []
     for begin, size in spans:
-        chunk = jnp.concatenate([part[begin : begin + size] for part in fitted], axis=1)
-        mirrored.append(lax.ppermute(chunk, "orb", ends))
+        mirrored.append(across(fitted[1][begin : begin + size], reverse))
 
     def hop(outs):
         return [outs[0]] + [across(outs[i], i) for i in range(1, inner)]
@@ -405,8 +406,8 @@
             place,
             blocks,
             1,
-            [mirrored[0], mirrored[1], mirrored[2 + c]],
-            [(begin, 0, half, False), (begin, half, half, False), (0, 0, dom_count, True)],
+            [from_middle, from_end, mirrored[c]],
+            [(begin, 0, half, False), (begin, 0, half, True), (0, half, half, None)],
             size,
             tokens,
         )
@@ -421,7 +422,7 @@
         blocks,
         0,
         fitted,
-        [(0, 0, half, False), (0, half, half, False)],
+        [(0, 0, half, None), (0, half, half, None)],
         fit_rows,
         [denominator],
     )

time: 237 us -> 264 us (1.11)
  starting transfers between devices: 87.8 us -> 108 us
  waiting for transfers between devices: 77.8 us -> 91.5 us
  local copies, waits for them, and re-layouts: 15.1 us -> 12.2 us
    ppermute x12 -> x15, starting transfers between devices: 15.4 us -> 91.5 us  [across(): return lax.ppermute(array, 'orb', [(i, i ^ mask) for i in range(orb_count)])]
    ppermute x5 -> x2, starting transfers between devices: 63.5 us -> 7.71 us  [the longest x1 5.84 us: on_device(): from_end = lax.ppermute(fitted[0], 'orb', ends)]
    ppermute x12 -> x15, waiting for transfers between devices: 54.4 us -> 72.8 us  [across(): return lax.ppermute(array, 'orb', [(i, i ^ mask) for i in range(orb_count)])]
    all_to_all x2, waiting for transfers between devices: 23.3 us -> 18.6 us  [exchange(): lax.all_to_all(array[:, :, :, k * half:(k + 1) * half], 'aux', split_axis...]
    slice x6 -> x3, local copies, waits for them, and re-layouts: 5.66 us -> 2.75 us  [on_device(): mirrored.append(across(fitted[1][begin:begin + size], reverse))]
  transfers between devices with their start and end apart: 19 -> 19, of which waited for: 9 -> 10; matrix products, arithmetic and copies ran while one was open for 7% -> 4% of each run, Pallas kernels for 15% -> 12%
where the time goes in v5:
time: 264 us; the launch traced here: 263 us
  starting transfers between devices  108 us (41%)
  waiting for transfers between devices  91.5 us (35%)
  Pallas kernels  36.6 us (14%)
  local copies, waits for them, and re-layouts  12.2 us (5%)
  matrix products  10.5 us (4%)
    ppermute x15, starting transfers between devices, across(): return lax.ppermute(array, 'orb', [(i, i ^ mask) for i in range(orb_count)])  91.5 us
    ppermute x15, waiting for transfers between devices, across(): return lax.ppermute(array, 'orb', [(i, i ^ mask) for i in range(orb_count)])  72.8 us
    pallas_call x4, Pallas kernels, project(): pl.pallas_call(functools.partial(project_kernel, group, capacity, kind, t...  20.8 us
    all_to_all x2, waiting for transfers between devices, exchange(): lax.all_to_all(array[:, :, :, k * half:(k + 1) * half], 'aux', split_axis...  18.6 us
    dot_general x2, matrix products, on_device(): jnp.dot(turned, raw_parts[k], preferred_element_type=jnp.float32)  10.5 us
    all_to_all x2, starting transfers between devices, exchange(): lax.all_to_all(array[:, :, :, k * half:(k + 1) * half], 'aux', split_axis...  8.85 us
    pallas_call x3, Pallas kernels, relay(): pl.pallas_call(functools.partial(relay_kernel, inner, (span,), margin), o...  7.04 us
    ppermute x1, starting transfers between devices, on_device(): from_end = lax.ppermute(fitted[0], 'orb', ends)  5.84 us
  transfers between devices with their start and end apart: 19, of which 10 were waited for; matrix products, arithmetic and copies ran while one was open for 4% of the time, Pallas kernels for 12%

profile of v5, /device:TPU:0, one launch (start us, length us, event | category | flops | bytes accessed | tf_op | source)
XLA Modules:
  0.0 263.3 jit_solution(4129585977835301662)
XLA Ops:
  0.6 2.7 %slice.30 = bf16[4,1,256,768]{3,2,1,0:T(8,128)(2,1)} slice(bf16[4,1,256,1536]{3,2,1,0:T(8,128)(2,1)} %param.7), slice={[0:4], [0:1], [0:256], [0:768]} | slice | bytes 3145728 | tf_op jit(solution)/shard_map/slice | solution.py:351
  3.3 4.4 %all-to-all-start = ((bf16[4,1,256,768]{3,2,1,0:T(8,128)(2,1)}), bf16[4,1,256,768]{3,2,1,0:T(8,128)(2,1)S(1)}, u32[]{:S(2)}, u32[]{:S(2)}) async-start(bf16[4,1,256,768]{3,2,1,0:T(8,128)(2,1)} %slice.30), calls=%async_computation | async-start | bytes 3145728 | tf_op jit(solution)/shard_map/all_to_all | solution.py:350
  10.0 17.8 %all-to-all-done = bf16[4,1,256,768]{3,2,1,0:T(8,128)(2,1)S(1)} async-done(((bf16[4,1,256,768]{3,2,1,0:T(8,128)(2,1)}), bf16[4,1,256,768]{3,2,1,0:T(8,128)(2,1)S(1)}, u32[]{:S(2)}, u32[]{:S(2)}) %all-to-all-start) | async-done | bytes 1572896 | tf_op jit(solution)/shard_map/all_to_all | solution.py:350
  27.8 5.6 %convolution_convert_fusion.1.refs_4_ = bf16[1024,768]{1,0:T(8,128)(2,1)} fusion(bf16[1024,768]{1,0:T(8,128)(2,1)S(1)} %bitcast.15, s32[]{:T(128)S(6)} %select_n.41, bf16[1024,1024]{1,0:T(8,128)(2,1)} %bitcast.20), kind=kOutput, calls=%fused_computation.4 | convolution fusion | flops 1615593472 | bytes 5242884 | tf_op jit(solution)/shard_map/dot_general | solution.py:389
  34.6 4.5 %all-to-all-start.1 = ((bf16[4,1,256,768]{3,2,1,0:T(8,128)(2,1)}), bf16[4,1,256,768]{3,2,1,0:T(8,128)(2,1)}, u32[]{:S(2)}, u32[]{:S(2)}) async-start(bf16[4,1,256,768]{3,2,1,0:T(8,128)(2,1)} %slice.31), calls=%async_computation.1 | async-start | bytes 3145728 | tf_op jit(solution)/shard_map/all_to_all | solution.py:350
  40.4 5.4 %pack.1 = (bf16[16,32,1536]{2,1,0:T(8,128)(2,1)}, bf16[16,32,1536]{2,1,0:T(8,128)(2,1)}, bf16[16,32,1536]{2,1,0:T(8,128)(2,1)}, bf16[16,32,1536]{2,1,0:T(8,128)(2,1)}) custom-call(s32[32]{0:T(128)} %reshape.70.orbs, s32[2]{0:T(128)} %pad_add_fusion.1.place, bf16[32,32,1536]{2,1,0:T(8,128)(2,1)} %bitcast.14), custom_call_target="tpu_custom_call" | custom-call | bytes 9437184 | tf_op jit(solution)/shard_map/pack/pallas_call | solution.py:59
  45.9 2.4 collective-permute-start.1
  48.3 1.6 collective-permute-start.2
  50.4 5.8 %collective-permute-start.6 = (bf16[1024,768]{1,0:T(8,128)(2,1)}, bf16[1024,768]{1,0:T(8,128)(2,1)}, u32[]{:S(2)}, u32[]{:S(2)}) collective-permute-start(bf16[1024,768]{1,0:T(8,128)(2,1)} %convolution_convert_fusion.1.refs_4_), channel_id=1, source_target_pairs={{0,6},{1,7},{6,0},{7,1},{8,14},{9,15},{14,8},{15,9},{16,22},{17,23... | collective-permute-start | bytes 4718600 | tf_op jit(solution)/shard_map/ppermute | solution.py:393
  56.2 1.9 collective-permute-start.5
  59.2 4.9 %convolution_convert_fusion.refs_5_ = bf16[1024,768]{1,0:T(8,128)(2,1)S(1)} fusion(bf16[1024,768]{1,0:T(8,128)(2,1)} %bitcast.6, s32[]{:T(128)S(6)} %select_n.41, bf16[1024,1024]{1,0:T(8,128)(2,1)} %bitcast.21), kind=kOutput, calls=%fused_computation.3 | convolution fusion | flops 1615593472 | bytes 5242884 | tf_op jit(solution)/shard_map/dot_general | solution.py:389
  65.9 17.5 %collective-permute-done.1.refs_1_ = bf16[16,32,1536]{2,1,0:T(8,128)(2,1)S(1)} collective-permute-done((bf16[16,32,1536]{2,1,0:T(8,128)(2,1)}, bf16[16,32,1536]{2,1,0:T(8,128)(2,1)S(1)}, u32[]{:S(2)}, u32[]{:S(2)}) %collective-permute-start.1) | collective-permute-done | bytes 1572896 | tf_op jit(solution)/shard_map/ppermute | solution.py:343
  83.5 1.8 collective-permute-start
  85.8 3.6 %collective-permute-start.9 = (bf16[384,768]{1,0:T(8,128)(2,1)}, bf16[384,768]{1,0:T(8,128)(2,1)S(1)}, u32[]{:S(2)}, u32[]{:S(2)}) collective-permute-start(bf16[384,768]{1,0:T(8,128)(2,1)} %slice.43), channel_id=1, source_target_pairs={{0,6},{1,7},{2,4},{3,5},{4,2},{5,3},{6,0},{7,1},{8,14},{9,15},{10,... | collective-permute-start | bytes 1769480 | tf_op jit(solution)/shard_map/ppermute | solution.py:343
  89.4 29.3 %collective-permute-done.3.refs_3_ = bf16[16,32,1536]{2,1,0:T(8,128)(2,1)} collective-permute-done((bf16[16,32,1536]{2,1,0:T(8,128)(2,1)}, bf16[16,32,1536]{2,1,0:T(8,128)(2,1)}, u32[]{:S(2)}, u32[]{:S(2)}) %collective-permute-start.3) | collective-permute-done | bytes 1572896 | tf_op jit(solution)/shard_map/ppermute | solution.py:343
  118.7 58.4 %collective-permute-start.7 = (bf16[512,768]{1,0:T(8,128)(2,1)}, bf16[512,768]{1,0:T(8,128)(2,1)}, u32[]{:S(2)}, u32[]{:S(2)}) collective-permute-start(bf16[512,768]{1,0:T(8,128)(2,1)} %slice.42), channel_id=1, source_target_pairs={{0,6},{1,7},{2,4},{3,5},{4,2},{5,3},{6,0},{7,1},{8,14},{9,15},{10,... | collective-permute-start | bytes 2359304 | tf_op jit(solution)/shard_map/ppermute | solution.py:343
  177.0 7.9 %shard_map.86 = (bf16[16,32,1024]{2,1,0:T(8,128)(2,1)S(1)}, bf16[16,32,1024]{2,1,0:T(8,128)(2,1)}) custom-call(s32[2]{0:T(128)S(1)} %copy-done.7, bf16[16,32,1536]{2,1,0:T(8,128)(2,1)S(1)} %copy-done, bf16[16,32,1536]{2,1,0:T(8,128)(2,1)S(1)} %collective-permute-done.1.refs_1_, bf16[16,32,1536]{2,1,0:T(8,128)(2,1)} %collective-permute-done.2.refs_2_, ...), custom_call_target="tpu_custom_call" | custom-call | flops 3221225472 | bytes 3145728 | tf_op jit(solution)/shard_map/pallas_call | solution.py:137
  190.2 4.3 %shard_map.87 = (bf16[16,32,512]{2,1,0:T(8,128)(2,1)S(1)}, bf16[16,32,512]{2,1,0:T(8,128)(2,1)S(1)}) custom-call(s32[2]{0:T(128)S(1)} %copy-done.7, bf16[16,32,1536]{2,1,0:T(8,128)(2,1)S(1)} %copy-done.1, bf16[16,32,1536]{2,1,0:T(8,128)(2,1)S(1)} %copy-done.4, bf16[16,32,1536]{2,1,0:T(8,128)(2,1)} %collective-permute-done.2.refs_2_, ...), custom_call_target="tpu_custom_call" | custom-call | flops 1610612736 | bytes 3145728 | tf_op jit(solution)/shard_map/pallas_call | solution.py:137
  196.1 5.9 %collective-permute-done.4.refs_1_ = bf16[16,32,1024]{2,1,0:T(8,128)(2,1)S(1)} collective-permute-done((bf16[16,32,1024]{2,1,0:T(8,128)(2,1)}, bf16[16,32,1024]{2,1,0:T(8,128)(2,1)S(1)}, u32[]{:S(2)}, u32[]{:S(2)}) %collective-permute-start.4) | collective-permute-done | bytes 1048608 | tf_op jit(solution)/shard_map/ppermute | solution.py:343
  202.1 9.8 %collective-permute-done.8.refs_3_ = bf16[16,32,512]{2,1,0:T(8,128)(2,1)S(1)} collective-permute-done((bf16[16,32,512]{2,1,0:T(8,128)(2,1)S(1)}, bf16[16,32,512]{2,1,0:T(8,128)(2,1)S(1)}, u32[]{:S(2)}, u32[]{:S(2)}) %collective-permute-start.8) | collective-permute-done | bytes 524320 | tf_op jit(solution)/shard_map/ppermute | solution.py:343
  211.9 2.3 shard_map.88
  214.3 4.3 %shard_map.89 = (bf16[16,32,384]{2,1,0:T(8,128)(2,1)S(1)}, bf16[16,32,384]{2,1,0:T(8,128)(2,1)S(1)}) custom-call(s32[2]{0:T(128)S(1)} %copy-done.7, bf16[16,32,1536]{2,1,0:T(8,128)(2,1)S(1)} %copy-done.2, bf16[16,32,1536]{2,1,0:T(8,128)(2,1)S(1)} %copy-done.5, bf16[16,32,1536]{2,1,0:T(8,128)(2,1)} %collective-permute-done.2.refs_2_, ...), custom_call_target="tpu_custom_call" | custom-call | flops 1207959552 | bytes 3145728 | tf_op jit(solution)/shard_map/pallas_call | solution.py:137
  221.5 9.7 %collective-permute-start.14 = (bf16[16,32,512]{2,1,0:T(8,128)(2,1)S(1)}, bf16[16,32,512]{2,1,0:T(8,128)(2,1)S(1)}, u32[]{:S(2)}, u32[]{:S(2)}) collective-permute-start(bf16[16,32,512]{2,1,0:T(8,128)(2,1)S(1)} %get-tuple-element.47), channel_id=1, source_target_pairs={{0,2},{1,3},{2,0},{3,1},{4,6},{5,7},{6,4},{7,5},{8,10},{9,11},{10,... | collective-permute-start | bytes 1572872 | tf_op jit(solution)/shard_map/ppermute | solution.py:343
  231.2 4.2 %shard_map.90 = (bf16[16,32,128]{2,1,0:T(8,128)(2,1)S(1)}, bf16[16,32,128]{2,1,0:T(8,128)(2,1)S(1)}) custom-call(s32[2]{0:T(128)S(1)} %copy-done.7, bf16[16,32,1536]{2,1,0:T(8,128)(2,1)S(1)} %copy-done.2, bf16[16,32,1536]{2,1,0:T(8,128)(2,1)S(1)} %copy-done.5, bf16[16,32,1536]{2,1,0:T(8,128)(2,1)} %collective-permute-done.2.refs_2_, ...), custom_call_target="tpu_custom_call" | custom-call | flops 402653184 | bytes 3145728 | tf_op jit(solution)/shard_map/pallas_call | solution.py:137
  235.4 1.6 collective-permute-start.12
  237.0 2.5 shard_map.91
  239.6 5.2 %collective-permute-start.15 = (bf16[16,32,384]{2,1,0:T(8,128)(2,1)S(1)}, bf16[16,32,384]{2,1,0:T(8,128)(2,1)S(1)}, u32[]{:S(2)}, u32[]{:S(2)}) collective-permute-start(bf16[16,32,384]{2,1,0:T(8,128)(2,1)S(1)} %get-tuple-element.48), channel_id=1, source_target_pairs={{0,2},{1,3},{2,0},{3,1},{4,6},{5,7},{6,4},{7,5},{8,10},{9,11},{10,... | collective-permute-start | bytes 1179656 | tf_op jit(solution)/shard_map/ppermute | solution.py:343
  244.7 2.2 shard_map.92
  249.1 5.6 %collective-permute-done.15.refs_7_ = bf16[16,32,384]{2,1,0:T(8,128)(2,1)S(1)} collective-permute-done((bf16[16,32,384]{2,1,0:T(8,128)(2,1)S(1)}, bf16[16,32,384]{2,1,0:T(8,128)(2,1)S(1)}, u32[]{:S(2)}, u32[]{:S(2)}) %collective-permute-start.15) | collective-permute-done | bytes 393248 | tf_op jit(solution)/shard_map/ppermute | solution.py:343
  254.7 1.7 shard_map.93.before
  256.4 3.8 %collective-permute-done.13.there = f32[16,32,32]{2,1,0:T(8,128)S(1)} collective-permute-done((f32[16,32,32]{2,1,0:T(8,128)S(1)}, f32[16,32,32]{2,1,0:T(8,128)S(1)}, u32[]{:S(2)}, u32[]{:S(2)}) %collective-permute-start.13) | collective-permute-done | bytes 65568 | tf_op jit(solution)/shard_map/ppermute | solution.py:343
  260.2 1.7 shard_map.94
  (76 shorter events, 20.5 us)
Async XLA Ops:
  3.3 4.4 %copy-start.14 = (s32[32]{0:T(128)S(1)}, s32[32]{0:T(128)}, u32[]{:S(2)}) copy-start(s32[32]{0:T(128)} %param.13) | copy-start | bytes 388
  3.3 24.4 %all-to-all-start = ((bf16[4,1,256,768]{3,2,1,0:T(8,128)(2,1)}), bf16[4,1,256,768]{3,2,1,0:T(8,128)(2,1)S(1)}, u32[]{:S(2)}, u32[]{:S(2)}) async-start(bf16[4,1,256,768]{3,2,1,0:T(8,128)(2,1)} %slice.30), calls=%async_computation | async-start | bytes 3145728 | tf_op jit(solution)/shard_map/all_to_all | solution.py:350
  27.8 5.6 %copy-start.9 = (bf16[4,1,256,1536]{3,2,1,0:T(8,128)(2,1)S(1)}, bf16[4,1,256,1536]{3,2,1,0:T(8,128)(2,1)}, u32[]{:S(2)}) copy-start(bf16[4,1,256,1536]{3,2,1,0:T(8,128)(2,1)} %param.7) | copy-start | bytes 9437188
  34.6 5.1 %copy-start.12 = (s32[16,2]{0,1:T(2,128)S(1)}, s32[16,2]{0,1:T(2,128)}, u32[]{:S(2)}) copy-start(s32[16,2]{0,1:T(2,128)} %param.9) | copy-start | bytes 388
  34.6 24.6 %all-to-all-start.1 = ((bf16[4,1,256,768]{3,2,1,0:T(8,128)(2,1)}), bf16[4,1,256,768]{3,2,1,0:T(8,128)(2,1)}, u32[]{:S(2)}, u32[]{:S(2)}) async-start(bf16[4,1,256,768]{3,2,1,0:T(8,128)(2,1)} %slice.31), calls=%async_computation.1 | async-start | bytes 3145728 | tf_op jit(solution)/shard_map/all_to_all | solution.py:350
  39.1 10.7 %copy-start.13 = (f32[32]{0:T(128)S(1)}, f32[32]{0:T(128)}, u32[]{:S(2)}) copy-start(f32[32]{0:T(128)} %param.12) | copy-start | bytes 388
  39.1 11.2 %copy-start.10 = (f32[16,2,32]{2,1,0:T(2,128)S(1)}, f32[16,2,32]{2,1,0:T(2,128)}, u32[]{:S(2)}) copy-start(f32[16,2,32]{2,1,0:T(2,128)} %param.11) | copy-start | bytes 12292
  40.4 9.4 %copy-start.11 = (s32[32]{0:T(128)S(1)}, s32[32]{0:T(128)}, u32[]{:S(2)}) copy-start(s32[32]{0:T(128)} %reshape.70.orbs) | copy-start | bytes 388
  45.9 37.6 %collective-permute-start.1 = (bf16[16,32,1536]{2,1,0:T(8,128)(2,1)}, bf16[16,32,1536]{2,1,0:T(8,128)(2,1)S(1)}, u32[]{:S(2)}, u32[]{:S(2)}) collective-permute-start(bf16[16,32,1536]{2,1,0:T(8,128)(2,1)} %get-tuple-element.28), channel_id=1, source_target_pairs={{0,1},{1,0},{2,3},{3,2},{4,5},{5,4},{6,7},{7,6},{8,9},{9,8},{10,11... | collective-permute-start | bytes 4718600 | tf_op jit(solution)/shard_map/ppermute | solution.py:343
  48.3 37.6 %collective-permute-start.2 = (bf16[16,32,1536]{2,1,0:T(8,128)(2,1)}, bf16[16,32,1536]{2,1,0:T(8,128)(2,1)}, u32[]{:S(2)}, u32[]{:S(2)}) collective-permute-start(bf16[16,32,1536]{2,1,0:T(8,128)(2,1)} %get-tuple-element.29), channel_id=1, source_target_pairs={{0,2},{1,3},{2,0},{3,1},{4,6},{5,7},{6,4},{7,5},{8,10},{9,11},{10,... | collective-permute-start | bytes 4718600 | tf_op jit(solution)/shard_map/ppermute | solution.py:343
  49.9 68.8 %collective-permute-start.3 = (bf16[16,32,1536]{2,1,0:T(8,128)(2,1)}, bf16[16,32,1536]{2,1,0:T(8,128)(2,1)}, u32[]{:S(2)}, u32[]{:S(2)}) collective-permute-start(bf16[16,32,1536]{2,1,0:T(8,128)(2,1)} %get-tuple-element.30), channel_id=1, source_target_pairs={{0,3},{1,2},{2,1},{3,0},{4,7},{5,6},{6,5},{7,4},{8,11},{9,10},{10,... | collective-permute-start | bytes 4718600 | tf_op jit(solution)/shard_map/ppermute | solution.py:343
  50.4 136.8 %collective-permute-start.6 = (bf16[1024,768]{1,0:T(8,128)(2,1)}, bf16[1024,768]{1,0:T(8,128)(2,1)}, u32[]{:S(2)}, u32[]{:S(2)}) collective-permute-start(bf16[1024,768]{1,0:T(8,128)(2,1)} %convolution_convert_fusion.1.refs_4_), channel_id=1, source_target_pairs={{0,6},{1,7},{6,0},{7,1},{8,14},{9,15},{14,8},{15,9},{16,22},{17,23... | collective-permute-start | bytes 4718600 | tf_op jit(solution)/shard_map/ppermute | solution.py:393
  56.2 130.9 %collective-permute-start.5 = (bf16[1024,768]{1,0:T(8,128)(2,1)}, bf16[1024,768]{1,0:T(8,128)(2,1)}, u32[]{:S(2)}, u32[]{:S(2)}) collective-permute-start(bf16[1024,768]{1,0:T(8,128)(2,1)} %convolution_convert_fusion.1.refs_4_), channel_id=1, source_target_pairs={{2,4},{3,5},{4,2},{5,3},{10,12},{11,13},{12,10},{13,11},{18,20},{1... | collective-permute-start | bytes 4718600 | tf_op jit(solution)/shard_map/ppermute | solution.py:392
  59.2 117.8 %copy-start.8 = (bf16[1024,768]{1,0:T(8,128)(2,1)S(1)}, bf16[1024,768]{1,0:T(8,128)(2,1)}, u32[]{:S(2)}) copy-start(bf16[1024,768]{1,0:T(8,128)(2,1)} %convolution_convert_fusion.1.refs_4_) | copy-start | bytes 4718596
  64.1 120.9 %copy-start.6 = (bf16[1024,768]{1,0:T(8,128)(2,1)}, bf16[1024,768]{1,0:T(8,128)(2,1)S(1)}, u32[]{:S(2)}) copy-start(bf16[1024,768]{1,0:T(8,128)(2,1)S(1)} %convolution_convert_fusion.refs_5_) | copy-start | bytes 4718596
  64.1 112.9 %copy-start = (bf16[16,32,1536]{2,1,0:T(8,128)(2,1)S(1)}, bf16[16,32,1536]{2,1,0:T(8,128)(2,1)}, u32[]{:S(2)}) copy-start(bf16[16,32,1536]{2,1,0:T(8,128)(2,1)} %get-tuple-element.27.refs_0_) | copy-start | bytes 4718596
  64.1 112.9 %copy-start.7 = (s32[2]{0:T(128)S(1)}, s32[2]{0:T(128)}, u32[]{:S(2)}) copy-start(s32[2]{0:T(128)} %pad_add_fusion.1.place) | copy-start | bytes 28
  83.5 101.5 %copy-start.3 = (bf16[16,32,1536]{2,1,0:T(8,128)(2,1)}, bf16[16,32,1536]{2,1,0:T(8,128)(2,1)S(1)}, u32[]{:S(2)}) copy-start(bf16[16,32,1536]{2,1,0:T(8,128)(2,1)S(1)} %collective-permute-done.1.refs_1_) | copy-start | bytes 4718596
  83.5 101.5 %collective-permute-start = (s32[32]{0:T(128)S(1)}, s32[32]{0:T(128)S(1)}, u32[]{:S(2)}, u32[]{:S(2)}) collective-permute-start(s32[32]{0:T(128)S(1)} %copy-done.11), channel_id=1, source_target_pairs={{0,2},{1,3},{2,0},{3,1},{4,6},{5,7},{6,4},{7,5},{8,10},{9,11},{10,... | collective-permute-start | bytes 392 | tf_op jit(solution)/shard_map/ppermute | solution.py:343
  85.8 128.4 %collective-permute-start.9 = (bf16[384,768]{1,0:T(8,128)(2,1)}, bf16[384,768]{1,0:T(8,128)(2,1)S(1)}, u32[]{:S(2)}, u32[]{:S(2)}) collective-permute-start(bf16[384,768]{1,0:T(8,128)(2,1)} %slice.43), channel_id=1, source_target_pairs={{0,6},{1,7},{2,4},{3,5},{4,2},{5,3},{6,0},{7,1},{8,14},{9,15},{10,... | collective-permute-start | bytes 1769480 | tf_op jit(solution)/shard_map/ppermute | solution.py:343
  118.7 68.7 %collective-permute-start.7 = (bf16[512,768]{1,0:T(8,128)(2,1)}, bf16[512,768]{1,0:T(8,128)(2,1)}, u32[]{:S(2)}, u32[]{:S(2)}) collective-permute-start(bf16[512,768]{1,0:T(8,128)(2,1)} %slice.42), channel_id=1, source_target_pairs={{0,6},{1,7},{2,4},{3,5},{4,2},{5,3},{6,0},{7,1},{8,14},{9,15},{10,... | collective-permute-start | bytes 2359304 | tf_op jit(solution)/shard_map/ppermute | solution.py:343
  185.0 17.1 %collective-permute-start.4 = (bf16[16,32,1024]{2,1,0:T(8,128)(2,1)}, bf16[16,32,1024]{2,1,0:T(8,128)(2,1)S(1)}, u32[]{:S(2)}, u32[]{:S(2)}) collective-permute-start(bf16[16,32,1024]{2,1,0:T(8,128)(2,1)} %get-tuple-element.37), channel_id=1, source_target_pairs={{0,1},{1,0},{2,3},{3,2},{4,5},{5,4},{6,7},{7,6},{8,9},{9,8},{10,11... | collective-permute-start | bytes 3145736 | tf_op jit(solution)/shard_map/ppermute | solution.py:343
  194.5 19.7 %copy-start.2 = (bf16[16,32,1536]{2,1,0:T(8,128)(2,1)S(1)}, bf16[16,32,1536]{2,1,0:T(8,128)(2,1)}, u32[]{:S(2)}) copy-start(bf16[16,32,1536]{2,1,0:T(8,128)(2,1)} %get-tuple-element.27.refs_0_) | copy-start | bytes 4718596
  194.5 19.7 %copy-start.5 = (bf16[16,32,1536]{2,1,0:T(8,128)(2,1)S(1)}, bf16[16,32,1536]{2,1,0:T(8,128)(2,1)}, u32[]{:S(2)}) copy-start(bf16[16,32,1536]{2,1,0:T(8,128)(2,1)} %copy-done.3) | copy-start | bytes 4718596
  194.5 17.3 %collective-permute-start.8 = (bf16[16,32,512]{2,1,0:T(8,128)(2,1)S(1)}, bf16[16,32,512]{2,1,0:T(8,128)(2,1)S(1)}, u32[]{:S(2)}, u32[]{:S(2)}) collective-permute-start(bf16[16,32,512]{2,1,0:T(8,128)(2,1)S(1)} %get-tuple-element.39), channel_id=1, source_target_pairs={{0,1},{1,0},{2,3},{3,2},{4,5},{5,4},{6,7},{7,6},{8,9},{9,8},{10,11... | collective-permute-start | bytes 1572872 | tf_op jit(solution)/shard_map/ppermute | solution.py:343
  218.6 18.5 %collective-permute-start.10 = (bf16[16,32,384]{2,1,0:T(8,128)(2,1)S(1)}, bf16[16,32,384]{2,1,0:T(8,128)(2,1)S(1)}, u32[]{:S(2)}, u32[]{:S(2)}) collective-permute-start(bf16[16,32,384]{2,1,0:T(8,128)(2,1)S(1)} %get-tuple-element.42), channel_id=1, source_target_pairs={{0,1},{1,0},{2,3},{3,2},{4,5},{5,4},{6,7},{7,6},{8,9},{9,8},{10,11... | collective-permute-start | bytes 1179656 | tf_op jit(solution)/shard_map/ppermute | solution.py:343
  220.1 11.1 %collective-permute-start.11 = (bf16[128,768]{1,0:T(8,128)(2,1)S(1)}, bf16[128,768]{1,0:T(8,128)(2,1)S(1)}, u32[]{:S(2)}, u32[]{:S(2)}) collective-permute-start(bf16[128,768]{1,0:T(8,128)(2,1)S(1)} %slice.44), channel_id=1, source_target_pairs={{0,6},{1,7},{2,4},{3,5},{4,2},{5,3},{6,0},{7,1},{8,14},{9,15},{10,... | collective-permute-start | bytes 589832 | tf_op jit(solution)/shard_map/ppermute | solution.py:343
  221.5 27.7 %collective-permute-start.14 = (bf16[16,32,512]{2,1,0:T(8,128)(2,1)S(1)}, bf16[16,32,512]{2,1,0:T(8,128)(2,1)S(1)}, u32[]{:S(2)}, u32[]{:S(2)}) collective-permute-start(bf16[16,32,512]{2,1,0:T(8,128)(2,1)S(1)} %get-tuple-element.47), channel_id=1, source_target_pairs={{0,2},{1,3},{2,0},{3,1},{4,6},{5,7},{6,4},{7,5},{8,10},{9,11},{10,... | collective-permute-start | bytes 1572872 | tf_op jit(solution)/shard_map/ppermute | solution.py:343
  235.4 9.3 %collective-permute-start.12 = (bf16[16,32,128]{2,1,0:T(8,128)(2,1)S(1)}, bf16[16,32,128]{2,1,0:T(8,128)(2,1)S(1)}, u32[]{:S(2)}, u32[]{:S(2)}) collective-permute-start(bf16[16,32,128]{2,1,0:T(8,128)(2,1)S(1)} %get-tuple-element.45), channel_id=1, source_target_pairs={{0,1},{1,0},{2,3},{3,2},{4,5},{5,4},{6,7},{7,6},{8,9},{9,8},{10,11... | collective-permute-start | bytes 393224 | tf_op jit(solution)/shard_map/ppermute | solution.py:343
  239.6 15.2 %collective-permute-start.15 = (bf16[16,32,384]{2,1,0:T(8,128)(2,1)S(1)}, bf16[16,32,384]{2,1,0:T(8,128)(2,1)S(1)}, u32[]{:S(2)}, u32[]{:S(2)}) collective-permute-start(bf16[16,32,384]{2,1,0:T(8,128)(2,1)S(1)} %get-tuple-element.48), channel_id=1, source_target_pairs={{0,2},{1,3},{2,0},{3,1},{4,6},{5,7},{6,4},{7,5},{8,10},{9,11},{10,... | collective-permute-start | bytes 1179656 | tf_op jit(solution)/shard_map/ppermute | solution.py:343
  247.0 13.2 %collective-permute-start.16 = (bf16[16,32,128]{2,1,0:T(8,128)(2,1)S(1)}, bf16[16,32,128]{2,1,0:T(8,128)(2,1)S(1)}, u32[]{:S(2)}, u32[]{:S(2)}) collective-permute-start(bf16[16,32,128]{2,1,0:T(8,128)(2,1)S(1)} %get-tuple-element.49), channel_id=1, source_target_pairs={{0,2},{1,3},{2,0},{3,1},{4,6},{5,7},{6,4},{7,5},{8,10},{9,11},{10,... | collective-permute-start | bytes 393224 | tf_op jit(solution)/shard_map/ppermute | solution.py:343
  247.9 12.3 %collective-permute-start.13 = (f32[16,32,32]{2,1,0:T(8,128)S(1)}, f32[16,32,32]{2,1,0:T(8,128)S(1)}, u32[]{:S(2)}, u32[]{:S(2)}) collective-permute-start(f32[16,32,32]{2,1,0:T(8,128)S(1)} %slice_bitcast_fusion), channel_id=1, source_target_pairs={{0,2},{1,3},{2,0},{3,1},{4,6},{5,7},{6,4},{7,5},{8,10},{9,11},{10,... | collective-permute-start | bytes 196616 | tf_op jit(solution)/shard_map/ppermute | solution.py:343
  (2 other events, 2.8 us)

commit v6 on v5

--- a/solution.py
+++ b/solution.py
@@ -75,85 +75,71 @@
     )(orbs, place, coef)
 
 
-def project_kernel(group, capacity, kind, pieces, place, *refs):
+def project_kernel(group, capacity, kind, low, place, *refs):
     inner = group // 2
-    blocks, parts = refs[:group], refs[group : group + len(pieces)]
-    outs, (left, right, made, left_sem, right_sem, out_sem) = refs[-6 - inner : -6], refs[-6:]
-    row_count = right.shape[0]
-    _, pno_count, dom_count = left.shape
-    lines = 2 * capacity
+    blocks, heads = refs[:group], refs[group : -1 - inner]
+    tail, outs = refs[-1 - inner], refs[-inner:]
+    row_count, half = tail.shape
+    pno_count = outs[0].shape[1]
+    step = row_count if row_count <= 640 else 256
     plane = place[1] // inner
     at_end = (plane == 0) | (plane == 3)
-    for part, (row, column, width, end) in zip(parts, pieces):
-
-        @pl.when((plane >= 0) if end is None else (at_end == end))
-        def _(part=part, row=row, column=column, width=width):
-            copy(
-                part.at[pl.ds(row, row_count)], right.at[:, pl.ds(column, width)], right_sem
-            ).start()
-
-    for i in range(inner):
-        for j in range(2):
-            copy(
-                blocks[i + j * inner].at[pl.ds(kind * capacity, capacity)],
-                left.at[pl.ds(i * lines + j * capacity, capacity)],
-                left_sem.at[i],
-            ).start()
-    copy(right, right, right_sem).wait()
-    step = row_count if row_count <= 512 else 256
-    for i in range(inner):
-        mine = left.at[pl.ds(i * lines, lines)]
-        copy(mine, mine, left_sem.at[i]).wait()
-
-        def tile(t, carry, i=i, mine=mine):
-            at = t * step if isinstance(t, int) else pl.multiple_of(t * step, step)
-            product = lax.dot_general(
-                mine[...].reshape(lines * pno_count, dom_count),
-                right[pl.ds(at, step), :],
-                (((1,), (1,)), ((), ())),
-                preferred_element_type=jnp.float32,
-            )
-            made[i, :, :, pl.ds(at, step)] = product.astype(made.dtype).reshape(
-                lines, pno_count, step
-            )
-            return carry
-
-        if row_count == step:
-            tile(0, 0)
-        else:
-            lax.fori_loop(0, row_count // step, tile, 0)
-        copy(made.at[i], outs[i], out_sem).start()
-    for i in range(inner):
-        copy(made.at[i], outs[i], out_sem).wait()
-
-
-def project(place, blocks, kind, parts, pieces, row_count, tokens):
+
+    def tile(t, carry):
+        at = t * step if isinstance(t, int) else pl.multiple_of(t * step, step)
+        head = heads[0][pl.ds(low + at, step), :]
+        if len(heads) > 1:
+            head = jnp.where(at_end, heads[1][pl.ds(low + at, step), :], head)
+        rest = tail[pl.ds(at, step), :]
+        for i in range(inner):
+            for j in range(2):
+                lines = blocks[i + j * inner][kind * capacity : (kind + 1) * capacity]
+                lines = lines.reshape(capacity * pno_count, 2 * half)
+                product = lax.dot_general(
+                    lines[:, :half],
+                    head,
+                    (((1,), (1,)), ((), ())),
+                    preferred_element_type=jnp.float32,
+                ) + lax.dot_general(
+                    lines[:, half:],
+                    rest,
+                    (((1,), (1,)), ((), ())),
+                    preferred_element_type=jnp.float32,
+                )
+                outs[i][j * capacity : (j + 1) * capacity, :, pl.ds(at, step)] = product.astype(
+                    outs[i].dtype
+                ).reshape(capacity, pno_count, step)
+        return carry
+
+    if row_count == step:
+        tile(0, 0)
+    else:
+        lax.fori_loop(0, row_count // step, tile, 0)
+
+
+def project(place, blocks, kind, heads, tail, low, tokens):
     group = len(blocks)
     inner = group // 2
     slots, pno_count, dom_count = blocks[0].shape
     capacity = slots // 2
-    dtype = blocks[0].dtype
-    out = jax.ShapeDtypeStruct((slots, pno_count, row_count), dtype)
+    row_count = tail.shape[0]
+
+    def kernel(*refs):
+        used = 1 + group + len(heads) + 1
+        project_kernel(group, capacity, kind, low, *refs[:used], *refs[-inner:])
+
     return pl.pallas_call(
-        functools.partial(project_kernel, group, capacity, kind, tuple(pieces)),
-        out_shape=(out,) * inner,
-        in_specs=[SMEM] + [ANY] * (group + len(parts) + len(tokens)),
-        out_specs=(ANY,) * inner,
-        scratch_shapes=[
-            pltpu.VMEM((group * capacity, pno_count, dom_count), dtype),
-            pltpu.VMEM((row_count, dom_count), dtype),
-            pltpu.VMEM((inner, slots, pno_count, row_count), dtype),
-            pltpu.SemaphoreType.DMA((inner,)),
-            pltpu.SemaphoreType.DMA,
-            pltpu.SemaphoreType.DMA,
-        ],
+        kernel,
+        out_shape=(jax.ShapeDtypeStruct((slots, pno_count, row_count), blocks[0].dtype),) * inner,
+        in_specs=[SMEM] + [VMEM] * (group + len(heads) + 1) + [ANY] * len(tokens),
+        out_specs=(VMEM,) * inner,
         compiler_params=pltpu.CompilerParams(vmem_limit_bytes=24 << 20),
         cost_estimate=pl.CostEstimate(
             flops=2 * group * capacity * pno_count * dom_count * row_count,
             transcendentals=0,
             bytes_accessed=2 * group * capacity * pno_count * dom_count,
         ),
-    )(place, *blocks, *parts, *tokens)
+    )(place, *blocks, *heads, tail, *tokens)
 
 
 def gather_sides(near, far, spans, slots, held, sem):
@@ -323,7 +309,7 @@
 
 
 def chunk_spans(fit_rows):
-    sizes = (fit_rows // 2, 3 * fit_rows // 8, fit_rows // 8)
+    sizes = (5 * fit_rows // 8, fit_rows // 4, fit_rows // 8)
     return [(sum(sizes[:c]), size) for c, size in enumerate(sizes)]
 
 
@@ -401,33 +387,19 @@
         return [outs[0]] + [across(outs[i], i) for i in range(1, inner)]
 
     def project_far(c, tokens):
-        begin, size = spans[c]
-        parts = project(
-            place,
-            blocks,
-            1,
-            [from_middle, from_end, mirrored[c]],
-            [(begin, 0, half, False), (begin, 0, half, True), (0, half, half, None)],
-            size,
-            tokens,
-        )
+        parts = project(place, blocks, 1, [from_middle, from_end], mirrored[c], spans[c][0], tokens)
         return hop(parts)
 
     def pass_on(c, before, tokens):
         sent, here = relay(rows, offsets, before, near, far[c], spans[c], margin, tokens)
         return across(sent, inner), here
 
-    near = project(
-        place,
-        blocks,
-        0,
-        fitted,
-        [(0, 0, half, None), (0, half, half, None)],
-        fit_rows,
-        [denominator],
-    )
-    mate_orbs, *near = lax.optimization_barrier((mate_orbs, *near))
+    near = project(place, blocks, 0, fitted[:1], fitted[1], 0, [denominator])
     near = hop(near)
+    far, others = [None] * 3, [None] * 3
+    far[0] = project_far(0, [])
+    far[1] = project_far(1, [far[0][0]])
+    mate_orbs, far[1][0] = lax.optimization_barrier((mate_orbs, far[1][0]))
     orbs = jnp.stack([own_orbs, mate_orbs])
     differs = orbs ^ me
     other_half = (differs & group) != 0
@@ -438,11 +410,8 @@
     rows = jnp.where(there, -1, line * 2 * capacity + home * capacity + position)
     rows_home = jnp.where(there, -1, line * capacity + position)
     offsets = pick(fit_offset, orbs.reshape(2 * side_count)).reshape(2, side_count)
-    far, others = [None] * 3, [None] * 3
-    far[0] = project_far(0, [rows, rows_home, offsets])
-    others[0], here = pass_on(0, jnp.zeros((8, 128), jnp.float32), [])
-    far[1] = project_far(1, [here])
-    far[2] = project_far(2, [far[1][0]])
+    others[0], here = pass_on(0, jnp.zeros((8, 128), jnp.float32), [far[1][0]])
+    far[2] = project_far(2, [here])
     others[1], here = pass_on(1, here, [far[2][0]])
     others[2], here = pass_on(2, here, [])
     there = across(here[1], inner)

time: 264 us -> 243 us (0.920)
  starting transfers between devices: 108 us -> 51.4 us
  waiting for transfers between devices: 91.5 us -> 121 us
  local copies, waits for them, and re-layouts: 12.2 us -> 15.9 us
    ppermute x15, starting transfers between devices: 91.5 us -> 35 us  [across(): return lax.ppermute(array, 'orb', [(i, i ^ mask) for i in range(orb_count)])]
    ppermute x1, waiting for transfers between devices: 0.01 us -> 28 us  [on_device(): from_end = lax.ppermute(fitted[0], 'orb', ends)]
    unnamed x31 -> x47, local copies, waits for them, and re-layouts: 2.95 us -> 6.91 us
  transfers between devices with their start and end apart: 19 -> 19, of which waited for: 10 -> 9; matrix products, arithmetic and copies ran while one was open for 4% -> 4% of each run, Pallas kernels for 12% -> 15%
where the time goes in v6:
time: 243 us; the launch traced here: 241 us
  waiting for transfers between devices  121 us (50%)
  starting transfers between devices  51.4 us (21%)
  Pallas kernels  36.8 us (15%)
  local copies, waits for them, and re-layouts  15.9 us (7%)
  matrix products  10.5 us (4%)
  between operations  2.86 us (1%)
    ppermute x15, waiting for transfers between devices, across(): return lax.ppermute(array, 'orb', [(i, i ^ mask) for i in range(orb_count)])  74.3 us
    ppermute x15, starting transfers between devices, across(): return lax.ppermute(array, 'orb', [(i, i ^ mask) for i in range(orb_count)])  35 us
    ppermute x1, waiting for transfers between devices, on_device(): from_end = lax.ppermute(fitted[0], 'orb', ends)  28 us
    pallas_call x4, Pallas kernels, project(): pl.pallas_call(kernel, out_shape=(jax.ShapeDtypeStruct((slots, pno_count,...  21 us
    all_to_all x2, waiting for transfers between devices, exchange(): lax.all_to_all(array[:, :, :, k * half:(k + 1) * half], 'aux', split_axis...  18.9 us
    dot_general x2, matrix products, on_device(): jnp.dot(turned, raw_parts[k], preferred_element_type=jnp.float32)  10.5 us
    all_to_all x2, starting transfers between devices, exchange(): lax.all_to_all(array[:, :, :, k * half:(k + 1) * half], 'aux', split_axis...  8.72 us
    pallas_call x3, Pallas kernels, relay(): pl.pallas_call(functools.partial(relay_kernel, inner, (span,), margin), o...  7 us
  transfers between devices with their start and end apart: 19, of which 9 were waited for; matrix products, arithmetic and copies ran while one was open for 4% of the time, Pallas kernels for 15%

profile of v6, /device:TPU:0, one launch (start us, length us, event | category | flops | bytes accessed | tf_op | source)
XLA Modules:
  0.0 240.7 jit_solution(1677977053517518893)
XLA Ops:
  0.6 2.7 %slice.30 = bf16[4,1,256,768]{3,2,1,0:T(8,128)(2,1)} slice(bf16[4,1,256,1536]{3,2,1,0:T(8,128)(2,1)} %param.7), slice={[0:4], [0:1], [0:256], [0:768]} | slice | bytes 3145728 | tf_op jit(solution)/shard_map/slice | solution.py:337
  3.3 4.4 %all-to-all-start = ((bf16[4,1,256,768]{3,2,1,0:T(8,128)(2,1)}), bf16[4,1,256,768]{3,2,1,0:T(8,128)(2,1)S(1)}, u32[]{:S(2)}, u32[]{:S(2)}) async-start(bf16[4,1,256,768]{3,2,1,0:T(8,128)(2,1)} %slice.30), calls=%async_computation | async-start | bytes 3145728 | tf_op jit(solution)/shard_map/all_to_all | solution.py:336
  10.9 16.8 %all-to-all-done = bf16[4,1,256,768]{3,2,1,0:T(8,128)(2,1)S(1)} async-done(((bf16[4,1,256,768]{3,2,1,0:T(8,128)(2,1)}), bf16[4,1,256,768]{3,2,1,0:T(8,128)(2,1)S(1)}, u32[]{:S(2)}, u32[]{:S(2)}) %all-to-all-start) | async-done | bytes 1572896 | tf_op jit(solution)/shard_map/all_to_all | solution.py:336
  27.8 5.6 %convolution_convert_fusion.1.refs_5_ = bf16[1024,768]{1,0:T(8,128)(2,1)} fusion(bf16[1024,768]{1,0:T(8,128)(2,1)S(1)} %bitcast.15, s32[]{:T(128)S(6)} %select_n.41, bf16[1024,1024]{1,0:T(8,128)(2,1)} %bitcast.20), kind=kOutput, calls=%fused_computation.4 | convolution fusion | flops 1615593472 | bytes 5242884 | tf_op jit(solution)/shard_map/dot_general | solution.py:375
  34.7 4.4 %all-to-all-start.1 = ((bf16[4,1,256,768]{3,2,1,0:T(8,128)(2,1)}), bf16[4,1,256,768]{3,2,1,0:T(8,128)(2,1)}, u32[]{:S(2)}, u32[]{:S(2)}) async-start(bf16[4,1,256,768]{3,2,1,0:T(8,128)(2,1)} %slice.31), calls=%async_computation.1 | async-start | bytes 3145728 | tf_op jit(solution)/shard_map/all_to_all | solution.py:336
  39.7 5.4 %pack.1 = (bf16[16,32,1536]{2,1,0:T(8,128)(2,1)}, bf16[16,32,1536]{2,1,0:T(8,128)(2,1)}, bf16[16,32,1536]{2,1,0:T(8,128)(2,1)}, bf16[16,32,1536]{2,1,0:T(8,128)(2,1)}) custom-call(s32[32]{0:T(128)} %reshape.70.orbs, s32[2]{0:T(128)} %pad_add_fusion.1.place.refs_0_, bf16[32,32,1536]{2,1,0:T(8,128)(2,1)} %bitcast.14), custom_call_target="tpu_custom_call" | custom-call | bytes 9437184 | tf_op jit(solution)/shard_map/pack/pallas_call | solution.py:59
  45.1 2.4 collective-permute-start.1
  47.5 1.6 collective-permute-start.2
  49.1 5.8 %collective-permute-start.5 = (bf16[1024,768]{1,0:T(8,128)(2,1)}, bf16[1024,768]{1,0:T(8,128)(2,1)}, u32[]{:S(2)}, u32[]{:S(2)}) collective-permute-start(bf16[1024,768]{1,0:T(8,128)(2,1)} %convolution_convert_fusion.1.refs_5_), channel_id=1, source_target_pairs={{0,6},{1,7},{6,0},{7,1},{8,14},{9,15},{14,8},{15,9},{16,22},{17,23... | collective-permute-start | bytes 4718600 | tf_op jit(solution)/shard_map/ppermute | solution.py:379
  54.9 1.8 collective-permute-start.4
  57.0 2.1 all-to-all-done.1
  59.1 4.9 %convolution_convert_fusion.refs_6_ = bf16[1024,768]{1,0:T(8,128)(2,1)S(1)} fusion(bf16[1024,768]{1,0:T(8,128)(2,1)} %bitcast.6, s32[]{:T(128)S(6)} %select_n.41, bf16[1024,1024]{1,0:T(8,128)(2,1)} %bitcast.21), kind=kOutput, calls=%fused_computation.3 | convolution fusion | flops 1615593472 | bytes 5242884 | tf_op jit(solution)/shard_map/dot_general | solution.py:375
  64.1 18.6 %collective-permute-done.1.refs_2_ = bf16[16,32,1536]{2,1,0:T(8,128)(2,1)S(1)} collective-permute-done((bf16[16,32,1536]{2,1,0:T(8,128)(2,1)}, bf16[16,32,1536]{2,1,0:T(8,128)(2,1)S(1)}, u32[]{:S(2)}, u32[]{:S(2)}) %collective-permute-start.1) | collective-permute-done | bytes 1572896 | tf_op jit(solution)/shard_map/ppermute | solution.py:329
  82.7 3.8 %collective-permute-start.7 = (bf16[640,768]{1,0:T(8,128)(2,1)S(1)}, bf16[640,768]{1,0:T(8,128)(2,1)S(1)}, u32[]{:S(2)}, u32[]{:S(2)}) collective-permute-start(bf16[640,768]{1,0:T(8,128)(2,1)S(1)} %slice.41), channel_id=1, source_target_pairs={{0,6},{1,7},{2,4},{3,5},{4,2},{5,3},{6,0},{7,1},{8,14},{9,15},{10,... | collective-permute-start | bytes 2949128 | tf_op jit(solution)/shard_map/ppermute | solution.py:329
  88.6 29.3 %collective-permute-done.3.refs_4_ = bf16[16,32,1536]{2,1,0:T(8,128)(2,1)} collective-permute-done((bf16[16,32,1536]{2,1,0:T(8,128)(2,1)}, bf16[16,32,1536]{2,1,0:T(8,128)(2,1)}, u32[]{:S(2)}, u32[]{:S(2)}) %collective-permute-start.3) | collective-permute-done | bytes 1572896 | tf_op jit(solution)/shard_map/ppermute | solution.py:329
  117.9 6.9 %shard_map.88 = (bf16[16,32,1024]{2,1,0:T(8,128)(2,1)S(1)}, bf16[16,32,1024]{2,1,0:T(8,128)(2,1)}) custom-call(s32[2]{0:T(128)S(1)} %copy-done.13, bf16[16,32,1536]{2,1,0:T(8,128)(2,1)S(1)} %copy-done, bf16[16,32,1536]{2,1,0:T(8,128)(2,1)S(1)} %collective-permute-done.1.refs_2_, bf16[16,32,1536]{2,1,0:T(8,128)(2,1)} %collective-permute-done.2.refs_3_, ...), custom_call_target="tpu_custom_call" | custom-call | flops 3221225472 | bytes 3145728 | tf_op jit(solution)/shard_map/pallas_call | solution.py:131
  124.8 1.6 collective-permute-start.8
  126.5 28.0 %collective-permute-done.5.refs_6_ = bf16[1024,768]{1,0:T(8,128)(2,1)} collective-permute-done((bf16[1024,768]{1,0:T(8,128)(2,1)}, bf16[1024,768]{1,0:T(8,128)(2,1)}, u32[]{:S(2)}, u32[]{:S(2)}) %collective-permute-start.5) | collective-permute-done | bytes 1572896 | tf_op jit(solution)/shard_map/ppermute | solution.py:379
  154.5 21.1 %collective-permute-done.7.refs_7_ = bf16[640,768]{1,0:T(8,128)(2,1)S(1)} collective-permute-done((bf16[640,768]{1,0:T(8,128)(2,1)S(1)}, bf16[640,768]{1,0:T(8,128)(2,1)S(1)}, u32[]{:S(2)}, u32[]{:S(2)}) %collective-permute-start.7) | collective-permute-done | bytes 983072 | tf_op jit(solution)/shard_map/ppermute | solution.py:329
  176.9 6.4 %shard_map.86 = (bf16[16,32,640]{2,1,0:T(8,128)(2,1)S(1)}, bf16[16,32,640]{2,1,0:T(8,128)(2,1)}) custom-call(s32[2]{0:T(128)S(1)} %copy-done.13, bf16[16,32,1536]{2,1,0:T(8,128)(2,1)S(1)} %copy-done, bf16[16,32,1536]{2,1,0:T(8,128)(2,1)S(1)} %copy-done.4, bf16[16,32,1536]{2,1,0:T(8,128)(2,1)} %collective-permute-done.2.refs_3_, ...), custom_call_target="tpu_custom_call" | custom-call | flops 2013265920 | bytes 3145728 | tf_op jit(solution)/shard_map/pallas_call | solution.py:131
  183.9 1.6 slice.44
  185.5 17.8 %collective-permute-start.11 = (bf16[128,768]{1,0:T(8,128)(2,1)}, bf16[128,768]{1,0:T(8,128)(2,1)}, u32[]{:S(2)}, u32[]{:S(2)}) collective-permute-start(bf16[128,768]{1,0:T(8,128)(2,1)} %slice.44), channel_id=1, source_target_pairs={{0,6},{1,7},{2,4},{3,5},{4,2},{5,3},{6,0},{7,1},{8,14},{9,15},{10,... | collective-permute-start | bytes 589832 | tf_op jit(solution)/shard_map/ppermute | solution.py:329
  203.3 1.4 copy-done.1
  206.1 3.9 %shard_map.87 = (bf16[16,32,256]{2,1,0:T(8,128)(2,1)S(1)}, bf16[16,32,256]{2,1,0:T(8,128)(2,1)S(1)}) custom-call(s32[2]{0:T(128)S(1)} %copy-done.13, bf16[16,32,1536]{2,1,0:T(8,128)(2,1)S(1)} %copy-done.1, bf16[16,32,1536]{2,1,0:T(8,128)(2,1)S(1)} %copy-done.5, bf16[16,32,1536]{2,1,0:T(8,128)(2,1)} %collective-permute-done.2.refs_3_, ...), custom_call_target="tpu_custom_call" | custom-call | flops 805306368 | bytes 3145728 | tf_op jit(solution)/shard_map/pallas_call | solution.py:131
  213.1 2.8 %shard_map.89 = (bf16[16,32,640]{2,1,0:T(8,128)(2,1)S(1)}, f32[2,16,32,32]{3,2,1,0:T(8,128)S(1)}) custom-call(s32[2,32]{1,0:T(2,128)S(1)} %get-tuple-element.54.rows, s32[2,32]{1,0:T(2,128)S(1)} %reshape.72.offsets, f32[8,128]{1,0:T(8,128)S(1)} %broadcast_in_dim.60.before, bf16[16,32,1024]{2,1,0:T(8,128)(2,1)S(1)} %get-tuple-element.35.refs_0_, ...), custom_call_target="tpu_custom_call" | custom-call | tf_op jit(solution)/shard_map/pallas_call | solution.py:206
  217.1 1.5 collective-permute-start.10
  218.6 3.8 %shard_map.90 = (bf16[16,32,128]{2,1,0:T(8,128)(2,1)S(1)}, bf16[16,32,128]{2,1,0:T(8,128)(2,1)S(1)}) custom-call(s32[2]{0:T(128)S(1)} %copy-done.13, bf16[16,32,1536]{2,1,0:T(8,128)(2,1)S(1)} %copy-done.2, bf16[16,32,1536]{2,1,0:T(8,128)(2,1)S(1)} %copy-done.6, bf16[16,32,1536]{2,1,0:T(8,128)(2,1)} %collective-permute-done.2.refs_3_, ...), custom_call_target="tpu_custom_call" | custom-call | flops 402653184 | bytes 3145728 | tf_op jit(solution)/shard_map/pallas_call | solution.py:131
  223.5 2.0 shard_map.91
  227.5 2.2 shard_map.92
  231.9 1.7 shard_map.93.before
  233.6 3.9 %collective-permute-done.13.there = f32[16,32,32]{2,1,0:T(8,128)S(1)} collective-permute-done((f32[16,32,32]{2,1,0:T(8,128)S(1)}, f32[16,32,32]{2,1,0:T(8,128)S(1)}, u32[]{:S(2)}, u32[]{:S(2)}) %collective-permute-start.13) | collective-permute-done | bytes 65568 | tf_op jit(solution)/shard_map/ppermute | solution.py:329
  237.6 1.7 shard_map.94
  (92 shorter events, 20.0 us)
Async XLA Ops:
  3.3 6.9 %copy-start.20 = (s32[16,2]{0,1:T(2,128)S(1)}, s32[16,2]{0,1:T(2,128)}, u32[]{:S(2)}) copy-start(s32[16,2]{0,1:T(2,128)} %param.9) | copy-start | bytes 388
  3.3 24.4 %all-to-all-start = ((bf16[4,1,256,768]{3,2,1,0:T(8,128)(2,1)}), bf16[4,1,256,768]{3,2,1,0:T(8,128)(2,1)S(1)}, u32[]{:S(2)}, u32[]{:S(2)}) async-start(bf16[4,1,256,768]{3,2,1,0:T(8,128)(2,1)} %slice.30), calls=%async_computation | async-start | bytes 3145728 | tf_op jit(solution)/shard_map/all_to_all | solution.py:336
  34.7 24.5 %all-to-all-start.1 = ((bf16[4,1,256,768]{3,2,1,0:T(8,128)(2,1)}), bf16[4,1,256,768]{3,2,1,0:T(8,128)(2,1)}, u32[]{:S(2)}, u32[]{:S(2)}) async-start(bf16[4,1,256,768]{3,2,1,0:T(8,128)(2,1)} %slice.31), calls=%async_computation.1 | async-start | bytes 3145728 | tf_op jit(solution)/shard_map/all_to_all | solution.py:336
  39.0 17.7 %copy-start.19 = (s32[32]{0:T(128)S(1)}, s32[32]{0:T(128)}, u32[]{:S(2)}) copy-start(s32[32]{0:T(128)} %reshape.70.orbs) | copy-start | bytes 388
  39.0 17.7 %copy-start.21 = (f32[32]{0:T(128)S(1)}, f32[32]{0:T(128)}, u32[]{:S(2)}) copy-start(f32[32]{0:T(128)} %param.12) | copy-start | bytes 388
  45.1 37.6 %collective-permute-start.1 = (bf16[16,32,1536]{2,1,0:T(8,128)(2,1)}, bf16[16,32,1536]{2,1,0:T(8,128)(2,1)S(1)}, u32[]{:S(2)}, u32[]{:S(2)}) collective-permute-start(bf16[16,32,1536]{2,1,0:T(8,128)(2,1)} %get-tuple-element.27), channel_id=1, source_target_pairs={{0,1},{1,0},{2,3},{3,2},{4,5},{5,4},{6,7},{7,6},{8,9},{9,8},{10,11... | collective-permute-start | bytes 4718600 | tf_op jit(solution)/shard_map/ppermute | solution.py:329
  47.5 40.2 %collective-permute-start.2 = (bf16[16,32,1536]{2,1,0:T(8,128)(2,1)}, bf16[16,32,1536]{2,1,0:T(8,128)(2,1)}, u32[]{:S(2)}, u32[]{:S(2)}) collective-permute-start(bf16[16,32,1536]{2,1,0:T(8,128)(2,1)} %get-tuple-element.28), channel_id=1, source_target_pairs={{0,2},{1,3},{2,0},{3,1},{4,6},{5,7},{6,4},{7,5},{8,10},{9,11},{10,... | collective-permute-start | bytes 4718600 | tf_op jit(solution)/shard_map/ppermute | solution.py:329
  49.1 68.8 %collective-permute-start.3 = (bf16[16,32,1536]{2,1,0:T(8,128)(2,1)}, bf16[16,32,1536]{2,1,0:T(8,128)(2,1)}, u32[]{:S(2)}, u32[]{:S(2)}) collective-permute-start(bf16[16,32,1536]{2,1,0:T(8,128)(2,1)} %get-tuple-element.29), channel_id=1, source_target_pairs={{0,3},{1,2},{2,1},{3,0},{4,7},{5,6},{6,5},{7,4},{8,11},{9,10},{10,... | collective-permute-start | bytes 4718600 | tf_op jit(solution)/shard_map/ppermute | solution.py:329
  49.1 105.4 %collective-permute-start.5 = (bf16[1024,768]{1,0:T(8,128)(2,1)}, bf16[1024,768]{1,0:T(8,128)(2,1)}, u32[]{:S(2)}, u32[]{:S(2)}) collective-permute-start(bf16[1024,768]{1,0:T(8,128)(2,1)} %convolution_convert_fusion.1.refs_5_), channel_id=1, source_target_pairs={{0,6},{1,7},{6,0},{7,1},{8,14},{9,15},{14,8},{15,9},{16,22},{17,23... | collective-permute-start | bytes 4718600 | tf_op jit(solution)/shard_map/ppermute | solution.py:379
  54.9 99.5 %collective-permute-start.4 = (bf16[1024,768]{1,0:T(8,128)(2,1)}, bf16[1024,768]{1,0:T(8,128)(2,1)}, u32[]{:S(2)}, u32[]{:S(2)}) collective-permute-start(bf16[1024,768]{1,0:T(8,128)(2,1)} %convolution_convert_fusion.1.refs_5_), channel_id=1, source_target_pairs={{2,4},{3,5},{4,2},{5,3},{10,12},{11,13},{12,10},{13,11},{18,20},{1... | collective-permute-start | bytes 4718600 | tf_op jit(solution)/shard_map/ppermute | solution.py:378
  59.1 27.5 %copy-start.18 = (f32[16,2,32]{2,1,0:T(2,128)S(1)}, f32[16,2,32]{2,1,0:T(2,128)}, u32[]{:S(2)}) copy-start(f32[16,2,32]{2,1,0:T(2,128)} %param.11) | copy-start | bytes 12292
  59.1 58.7 %copy-start.14 = (bf16[1024,768]{1,0:T(8,128)(2,1)S(1)}, bf16[1024,768]{1,0:T(8,128)(2,1)}, u32[]{:S(2)}) copy-start(bf16[1024,768]{1,0:T(8,128)(2,1)} %convolution_convert_fusion.1.refs_5_) | copy-start | bytes 4718596
  64.0 60.8 %copy-start.10 = (bf16[1024,768]{1,0:T(8,128)(2,1)}, bf16[1024,768]{1,0:T(8,128)(2,1)S(1)}, u32[]{:S(2)}) copy-start(bf16[1024,768]{1,0:T(8,128)(2,1)S(1)} %convolution_convert_fusion.refs_6_) | copy-start | bytes 4718596
  64.0 53.9 %copy-start = (bf16[16,32,1536]{2,1,0:T(8,128)(2,1)S(1)}, bf16[16,32,1536]{2,1,0:T(8,128)(2,1)}, u32[]{:S(2)}) copy-start(bf16[16,32,1536]{2,1,0:T(8,128)(2,1)} %get-tuple-element.26.refs_1_) | copy-start | bytes 4718596
  64.0 53.9 %copy-start.13 = (s32[2]{0:T(128)S(1)}, s32[2]{0:T(128)}, u32[]{:S(2)}) copy-start(s32[2]{0:T(128)} %pad_add_fusion.1.place.refs_0_) | copy-start | bytes 28
  82.7 42.1 %copy-start.3 = (bf16[16,32,1536]{2,1,0:T(8,128)(2,1)}, bf16[16,32,1536]{2,1,0:T(8,128)(2,1)S(1)}, u32[]{:S(2)}) copy-start(bf16[16,32,1536]{2,1,0:T(8,128)(2,1)S(1)} %collective-permute-done.1.refs_2_) | copy-start | bytes 4718596
  82.7 92.8 %collective-permute-start.7 = (bf16[640,768]{1,0:T(8,128)(2,1)S(1)}, bf16[640,768]{1,0:T(8,128)(2,1)S(1)}, u32[]{:S(2)}, u32[]{:S(2)}) collective-permute-start(bf16[640,768]{1,0:T(8,128)(2,1)S(1)} %slice.41), channel_id=1, source_target_pairs={{0,6},{1,7},{2,4},{3,5},{4,2},{5,3},{6,0},{7,1},{8,14},{9,15},{10,... | collective-permute-start | bytes 2949128 | tf_op jit(solution)/shard_map/ppermute | solution.py:329
  86.9 38.0 %copy-start.11 = (f32[16,32,32]{2,1,0:T(8,128)}, f32[16,32,32]{2,1,0:T(8,128)S(1)}, u32[]{:S(2)}) copy-start(f32[16,32,32]{2,1,0:T(8,128)S(1)} %subtract_subtract_fusion.refs_7_.denominator) | copy-start | bytes 196612
  87.7 115.6 %collective-permute-start.6 = (bf16[256,768]{1,0:T(8,128)(2,1)}, bf16[256,768]{1,0:T(8,128)(2,1)}, u32[]{:S(2)}, u32[]{:S(2)}) collective-permute-start(bf16[256,768]{1,0:T(8,128)(2,1)} %slice.40), channel_id=1, source_target_pairs={{0,6},{1,7},{2,4},{3,5},{4,2},{5,3},{6,0},{7,1},{8,14},{9,15},{10,... | collective-permute-start | bytes 1179656 | tf_op jit(solution)/shard_map/ppermute | solution.py:329
  124.8 87.2 %collective-permute-start.8 = (bf16[16,32,1024]{2,1,0:T(8,128)(2,1)}, bf16[16,32,1024]{2,1,0:T(8,128)(2,1)S(1)}, u32[]{:S(2)}, u32[]{:S(2)}) collective-permute-start(bf16[16,32,1024]{2,1,0:T(8,128)(2,1)} %get-tuple-element.36), channel_id=1, source_target_pairs={{0,1},{1,0},{2,3},{3,2},{4,5},{5,4},{6,7},{7,6},{8,9},{9,8},{10,11... | collective-permute-start | bytes 3145736 | tf_op jit(solution)/shard_map/ppermute | solution.py:329
  154.5 57.0 %collective-permute-start = (s32[32]{0:T(128)S(1)}, s32[32]{0:T(128)S(1)}, u32[]{:S(2)}, u32[]{:S(2)}) collective-permute-start(s32[32]{0:T(128)S(1)} %copy-done.19), channel_id=1, source_target_pairs={{0,2},{1,3},{2,0},{3,1},{4,6},{5,7},{6,4},{7,5},{8,10},{9,11},{10,... | collective-permute-start | bytes 392 | tf_op jit(solution)/shard_map/ppermute | solution.py:329
  183.3 28.7 %collective-permute-start.9 = (bf16[16,32,640]{2,1,0:T(8,128)(2,1)}, bf16[16,32,640]{2,1,0:T(8,128)(2,1)S(1)}, u32[]{:S(2)}, u32[]{:S(2)}) collective-permute-start(bf16[16,32,640]{2,1,0:T(8,128)(2,1)} %get-tuple-element.37), channel_id=1, source_target_pairs={{0,1},{1,0},{2,3},{3,2},{4,5},{5,4},{6,7},{7,6},{8,9},{9,8},{10,11... | collective-permute-start | bytes 1966088 | tf_op jit(solution)/shard_map/ppermute | solution.py:329
  185.5 33.1 %collective-permute-start.11 = (bf16[128,768]{1,0:T(8,128)(2,1)}, bf16[128,768]{1,0:T(8,128)(2,1)}, u32[]{:S(2)}, u32[]{:S(2)}) collective-permute-start(bf16[128,768]{1,0:T(8,128)(2,1)} %slice.44), channel_id=1, source_target_pairs={{0,6},{1,7},{2,4},{3,5},{4,2},{5,3},{6,0},{7,1},{8,14},{9,15},{10,... | collective-permute-start | bytes 589832 | tf_op jit(solution)/shard_map/ppermute | solution.py:329
  212.0 6.6 %copy-start.2 = (bf16[16,32,1536]{2,1,0:T(8,128)(2,1)S(1)}, bf16[16,32,1536]{2,1,0:T(8,128)(2,1)}, u32[]{:S(2)}) copy-start(bf16[16,32,1536]{2,1,0:T(8,128)(2,1)} %get-tuple-element.26.refs_1_) | copy-start | bytes 4718596
  212.0 6.6 %copy-start.6 = (bf16[16,32,1536]{2,1,0:T(8,128)(2,1)S(1)}, bf16[16,32,1536]{2,1,0:T(8,128)(2,1)}, u32[]{:S(2)}) copy-start(bf16[16,32,1536]{2,1,0:T(8,128)(2,1)} %copy-done.3) | copy-start | bytes 4718596
  215.9 16.0 %collective-permute-start.14 = (bf16[16,32,640]{2,1,0:T(8,128)(2,1)S(1)}, bf16[16,32,640]{2,1,0:T(8,128)(2,1)S(1)}, u32[]{:S(2)}, u32[]{:S(2)}) collective-permute-start(bf16[16,32,640]{2,1,0:T(8,128)(2,1)S(1)} %get-tuple-element.45), channel_id=1, source_target_pairs={{0,2},{1,3},{2,0},{3,1},{4,6},{5,7},{6,4},{7,5},{8,10},{9,11},{10,... | collective-permute-start | bytes 1966088 | tf_op jit(solution)/shard_map/ppermute | solution.py:329
  217.1 6.4 %collective-permute-start.10 = (bf16[16,32,256]{2,1,0:T(8,128)(2,1)S(1)}, bf16[16,32,256]{2,1,0:T(8,128)(2,1)S(1)}, u32[]{:S(2)}, u32[]{:S(2)}) collective-permute-start(bf16[16,32,256]{2,1,0:T(8,128)(2,1)S(1)} %copy-done.16), channel_id=1, source_target_pairs={{0,1},{1,0},{2,3},{3,2},{4,5},{5,4},{6,7},{7,6},{8,9},{9,8},{10,11... | collective-permute-start | bytes 786440 | tf_op jit(solution)/shard_map/ppermute | solution.py:329
  222.5 5.0 %collective-permute-start.12 = (bf16[16,32,128]{2,1,0:T(8,128)(2,1)S(1)}, bf16[16,32,128]{2,1,0:T(8,128)(2,1)S(1)}, u32[]{:S(2)}, u32[]{:S(2)}) collective-permute-start(bf16[16,32,128]{2,1,0:T(8,128)(2,1)S(1)} %get-tuple-element.43), channel_id=1, source_target_pairs={{0,1},{1,0},{2,3},{3,2},{4,5},{5,4},{6,7},{7,6},{8,9},{9,8},{10,11... | collective-permute-start | bytes 393224 | tf_op jit(solution)/shard_map/ppermute | solution.py:329
  225.5 6.5 %copy-start.9 = (bf16[16,32,256]{2,1,0:T(8,128)(2,1)S(1)}, bf16[16,32,256]{2,1,0:T(8,128)(2,1)}, u32[]{:S(2)}) copy-start(bf16[16,32,256]{2,1,0:T(8,128)(2,1)} %copy-done.7) | copy-start | bytes 786436
  225.5 6.4 %collective-permute-start.15 = (bf16[16,32,256]{2,1,0:T(8,128)(2,1)S(1)}, bf16[16,32,256]{2,1,0:T(8,128)(2,1)S(1)}, u32[]{:S(2)}, u32[]{:S(2)}) collective-permute-start(bf16[16,32,256]{2,1,0:T(8,128)(2,1)S(1)} %get-tuple-element.46), channel_id=1, source_target_pairs={{0,2},{1,3},{2,0},{3,1},{4,6},{5,7},{6,4},{7,5},{8,10},{9,11},{10,... | collective-permute-start | bytes 786440 | tf_op jit(solution)/shard_map/ppermute | solution.py:329
  229.7 7.8 %collective-permute-start.16 = (bf16[16,32,128]{2,1,0:T(8,128)(2,1)S(1)}, bf16[16,32,128]{2,1,0:T(8,128)(2,1)S(1)}, u32[]{:S(2)}, u32[]{:S(2)}) collective-permute-start(bf16[16,32,128]{2,1,0:T(8,128)(2,1)S(1)} %get-tuple-element.47), channel_id=1, source_target_pairs={{0,2},{1,3},{2,0},{3,1},{4,6},{5,7},{6,4},{7,5},{8,10},{9,11},{10,... | collective-permute-start | bytes 393224 | tf_op jit(solution)/shard_map/ppermute | solution.py:329
  230.7 6.8 %collective-permute-start.13 = (f32[16,32,32]{2,1,0:T(8,128)S(1)}, f32[16,32,32]{2,1,0:T(8,128)S(1)}, u32[]{:S(2)}, u32[]{:S(2)}) collective-permute-start(f32[16,32,32]{2,1,0:T(8,128)S(1)} %slice_bitcast_fusion), channel_id=1, source_target_pairs={{0,2},{1,3},{2,0},{3,1},{4,6},{5,7},{6,4},{7,5},{8,10},{9,11},{10,... | collective-permute-start | bytes 196616 | tf_op jit(solution)/shard_map/ppermute | solution.py:329
  (10 other events, 26.4 us)

commit v7 on v6

--- a/solution.py
+++ b/solution.py
@@ -75,36 +75,27 @@
     )(orbs, place, coef)
 
 
-def project_kernel(group, capacity, kind, low, place, *refs):
+def project_kernel(group, capacity, *refs):
     inner = group // 2
-    blocks, heads = refs[:group], refs[group : -1 - inner]
-    tail, outs = refs[-1 - inner], refs[-inner:]
-    row_count, half = tail.shape
+    blocks, parts, outs = refs[:group], refs[group : group + 2], refs[-inner:]
+    row_count, half = parts[0].shape
     pno_count = outs[0].shape[1]
     step = row_count if row_count <= 640 else 256
-    plane = place[1] // inner
-    at_end = (plane == 0) | (plane == 3)
 
     def tile(t, carry):
         at = t * step if isinstance(t, int) else pl.multiple_of(t * step, step)
-        head = heads[0][pl.ds(low + at, step), :]
-        if len(heads) > 1:
-            head = jnp.where(at_end, heads[1][pl.ds(low + at, step), :], head)
-        rest = tail[pl.ds(at, step), :]
+        rows = [part[pl.ds(at, step), :] for part in parts]
         for i in range(inner):
             for j in range(2):
-                lines = blocks[i + j * inner][kind * capacity : (kind + 1) * capacity]
-                lines = lines.reshape(capacity * pno_count, 2 * half)
-                product = lax.dot_general(
-                    lines[:, :half],
-                    head,
-                    (((1,), (1,)), ((), ())),
-                    preferred_element_type=jnp.float32,
-                ) + lax.dot_general(
-                    lines[:, half:],
-                    rest,
-                    (((1,), (1,)), ((), ())),
-                    preferred_element_type=jnp.float32,
+                lines = blocks[i + j * inner][...].reshape(capacity * pno_count, 2 * half)
+                product = sum(
+                    lax.dot_general(
+                        lines[:, k * half : (k + 1) * half],
+                        rows[k],
+                        (((1,), (1,)), ((), ())),
+                        preferred_element_type=jnp.float32,
+                    )
+                    for k in range(2)
                 )
                 outs[i][j * capacity : (j + 1) * capacity, :, pl.ds(at, step)] = product.astype(
                     outs[i].dtype
@@ -117,29 +108,31 @@
         lax.fori_loop(0, row_count // step, tile, 0)
 
 
-def project(place, blocks, kind, heads, tail, low, tokens):
+def project(blocks, kind, parts, tokens):
     group = len(blocks)
     inner = group // 2
     slots, pno_count, dom_count = blocks[0].shape
     capacity = slots // 2
-    row_count = tail.shape[0]
+    row_count = parts[0].shape[0]
 
     def kernel(*refs):
-        used = 1 + group + len(heads) + 1
-        project_kernel(group, capacity, kind, low, *refs[:used], *refs[-inner:])
-
+        project_kernel(group, capacity, *refs[: group + 2], *refs[-inner:])
+
+    block = pl.BlockSpec((capacity, pno_count, dom_count), lambda i: (kind, 0, 0))
+    part = pl.BlockSpec(parts[0].shape, lambda i: (0, 0))
     return pl.pallas_call(
         kernel,
+        grid=(1,),
         out_shape=(jax.ShapeDtypeStruct((slots, pno_count, row_count), blocks[0].dtype),) * inner,
-        in_specs=[SMEM] + [VMEM] * (group + len(heads) + 1) + [ANY] * len(tokens),
-        out_specs=(VMEM,) * inner,
-        compiler_params=pltpu.CompilerParams(vmem_limit_bytes=24 << 20),
+        in_specs=[block] * group + [part] * 2 + [ANY] * len(tokens),
+        out_specs=(pl.BlockSpec((slots, pno_count, row_count), lambda i: (0, 0, 0)),) * inner,
+        compiler_params=pltpu.CompilerParams(vmem_limit_bytes=32 << 20),
         cost_estimate=pl.CostEstimate(
             flops=2 * group * capacity * pno_count * dom_count * row_count,
             transcendentals=0,
             bytes_accessed=2 * group * capacity * pno_count * dom_count,
         ),
-    )(place, *blocks, *heads, tail, *tokens)
+    )(*blocks, *parts, *tokens)
 
 
 def gather_sides(near, far, spans, slots, held, sem):
@@ -367,39 +360,40 @@
     )
     spans = chunk_spans(fit_rows)
     reverse = group + inner
-    ends = [(i, i ^ reverse) for i in range(orb_count) if i // inner in (0, 3)]
-    middles = [(i, i ^ reverse) for i in range(orb_count) if i // inner in (1, 2)]
-    fitted = []
+    fitted, mirrored = [], [[None] * 2 for _ in spans]
+
+    def mirror(c, k):
+        begin, size = spans[c]
+        mirrored[c][k] = across(fitted[k][begin : begin + size], reverse)
+
     for k in range(2):
         fitted.append(
             jnp.dot(turned, raw_parts[k], preferred_element_type=jnp.float32).astype(jnp.bfloat16)
         )
+        mirror(0, k)
         if k == 0:
-            from_middle = lax.ppermute(fitted[0], "orb", middles)
-            from_end = lax.ppermute(fitted[0], "orb", ends)
             later, fitted[0] = lax.optimization_barrier((raw_ints, fitted[0]))
             raw_parts.append(exchange(later, 1))
-    mirrored = []
-    for begin, size in spans:
-        mirrored.append(across(fitted[1][begin : begin + size], reverse))
+        mirror(1, k)
+    mirror(2, 0)
+    mirror(2, 1)
 
     def hop(outs):
         return [outs[0]] + [across(outs[i], i) for i in range(1, inner)]
 
     def project_far(c, tokens):
-        parts = project(place, blocks, 1, [from_middle, from_end], mirrored[c], spans[c][0], tokens)
+        parts = project(blocks, 1, mirrored[c], tokens)
         return hop(parts)
 
     def pass_on(c, before, tokens):
         sent, here = relay(rows, offsets, before, near, far[c], spans[c], margin, tokens)
         return across(sent, inner), here
 
-    near = project(place, blocks, 0, fitted[:1], fitted[1], 0, [denominator])
+    near = project(blocks, 0, fitted, [denominator])
     near = hop(near)
     far, others = [None] * 3, [None] * 3
     far[0] = project_far(0, [])
-    far[1] = project_far(1, [far[0][0]])
-    mate_orbs, far[1][0] = lax.optimization_barrier((mate_orbs, far[1][0]))
+    mate_orbs, far[0][0] = lax.optimization_barrier((mate_orbs, far[0][0]))
     orbs = jnp.stack([own_orbs, mate_orbs])
     differs = orbs ^ me
     other_half = (differs & group) != 0
@@ -410,8 +404,9 @@
     rows = jnp.where(there, -1, line * 2 * capacity + home * capacity + position)
     rows_home = jnp.where(there, -1, line * capacity + position)
     offsets = pick(fit_offset, orbs.reshape(2 * side_count)).reshape(2, side_count)
-    others[0], here = pass_on(0, jnp.zeros((8, 128), jnp.float32), [far[1][0]])
-    far[2] = project_far(2, [here])
+    others[0], here = pass_on(0, jnp.zeros((8, 128), jnp.float32), [])
+    far[1] = project_far(1, [here])
+    far[2] = project_far(2, [far[1][0]])
     others[1], here = pass_on(1, here, [far[2][0]])
     others[2], here = pass_on(2, here, [])
     there = across(here[1], inner)

time: 243 us -> 240 us (0.988)
  local copies, waits for them, and re-layouts: 15.9 us -> 21.1 us
  Pallas kernels: 36.8 us -> 33.5 us
    ppermute x2 -> x0, waiting for transfers between devices: 28 us -> none  [the longest x1 28 us: on_device(): from_end = lax.ppermute(fitted[0], 'orb', ends)]
    ppermute x15 -> x18, waiting for transfers between devices: 74.3 us -> 98 us  [across(): return lax.ppermute(array, 'orb', [(i, i ^ mask) for i in range(orb_count)])]
    ppermute x15 -> x18, starting transfers between devices: 35 us -> 42.9 us  [across(): return lax.ppermute(array, 'orb', [(i, i ^ mask) for i in range(orb_count)])]
    ppermute x2 -> x0, starting transfers between devices: 7.65 us -> none  [the longest x1 5.84 us: on_device(): from_end = lax.ppermute(fitted[0], 'orb', ends)]
    slice x3 -> x6, local copies, waits for them, and re-layouts: 2.52 us -> 8.85 us  [mirror(): mirrored[c][k] = across(fitted[k][begin:begin + size], reverse)]
    pallas_call x4, Pallas kernels: 21 us -> 17.8 us  [project(): pl.pallas_call(kernel, grid=(1,), out_shape=(jax.ShapeDtypeStruct((slots,...]
    all_to_all x2, waiting for transfers between devices: 18.9 us -> 21.6 us  [exchange(): lax.all_to_all(array[:, :, :, k * half:(k + 1) * half], 'aux', split_axis...]
    unnamed x47 -> x31, local copies, waits for them, and re-layouts: 6.91 us -> 5.58 us
  transfers between devices with their start and end apart: 19 -> 20, of which waited for: 9 -> 13; matrix products, arithmetic and copies ran while one was open for 4% -> 7% of each run, Pallas kernels for 15% -> 13%
where the time goes in v7:
time: 240 us; the launch traced here: 239 us
  waiting for transfers between devices  120 us (50%)
  starting transfers between devices  51.2 us (21%)
  Pallas kernels  33.5 us (14%)
  local copies, waits for them, and re-layouts  21.1 us (9%)
  matrix products  8.73 us (4%)
  between operations  2.82 us (1%)
    ppermute x18, waiting for transfers between devices, across(): return lax.ppermute(array, 'orb', [(i, i ^ mask) for i in range(orb_count)])  98 us
    ppermute x18, starting transfers between devices, across(): return lax.ppermute(array, 'orb', [(i, i ^ mask) for i in range(orb_count)])  42.9 us
    all_to_all x2, waiting for transfers between devices, exchange(): lax.all_to_all(array[:, :, :, k * half:(k + 1) * half], 'aux', split_axis...  21.6 us
    pallas_call x4, Pallas kernels, project(): pl.pallas_call(kernel, grid=(1,), out_shape=(jax.ShapeDtypeStruct((slots,...  17.8 us
    slice x6, local copies, waits for them, and re-layouts, mirror(): mirrored[c][k] = across(fitted[k][begin:begin + size], reverse)  8.85 us
    dot_general x2, matrix products, on_device(): jnp.dot(turned, raw_parts[k], preferred_element_type=jnp.float32)  8.73 us
    all_to_all x2, starting transfers between devices, exchange(): lax.all_to_all(array[:, :, :, k * half:(k + 1) * half], 'aux', split_axis...  8.24 us
    pallas_call x3, Pallas kernels, relay(): pl.pallas_call(functools.partial(relay_kernel, inner, (span,), margin), o...  7 us
  transfers between devices with their start and end apart: 20, of which 13 were waited for; matrix products, arithmetic and copies ran while one was open for 7% of the time, Pallas kernels for 13%

profile of v7, /device:TPU:0, one launch (start us, length us, event | category | flops | bytes accessed | tf_op | source)
XLA Modules:
  0.0 239.0 jit_solution(11283931554459200245)
XLA Ops:
  0.6 2.7 %slice.39 = bf16[4,1,256,768]{3,2,1,0:T(8,128)(2,1)} slice(bf16[4,1,256,1536]{3,2,1,0:T(8,128)(2,1)} %param.7), slice={[0:4], [0:1], [0:256], [0:768]} | slice | bytes 3145728 | tf_op jit(solution)/shard_map/slice | solution.py:330
  3.3 4.4 %all-to-all-start = ((bf16[4,1,256,768]{3,2,1,0:T(8,128)(2,1)}), bf16[4,1,256,768]{3,2,1,0:T(8,128)(2,1)S(1)}, u32[]{:S(2)}, u32[]{:S(2)}) async-start(bf16[4,1,256,768]{3,2,1,0:T(8,128)(2,1)} %slice.39), calls=%async_computation | async-start | bytes 3145728 | tf_op jit(solution)/shard_map/all_to_all | solution.py:329
  10.2 17.5 %all-to-all-done = bf16[4,1,256,768]{3,2,1,0:T(8,128)(2,1)S(1)} async-done(((bf16[4,1,256,768]{3,2,1,0:T(8,128)(2,1)}), bf16[4,1,256,768]{3,2,1,0:T(8,128)(2,1)S(1)}, u32[]{:S(2)}, u32[]{:S(2)}) %all-to-all-start) | async-done | bytes 1572896 | tf_op jit(solution)/shard_map/all_to_all | solution.py:329
  27.8 4.4 %convolution_convert_fusion.1.refs_4_ = bf16[1024,768]{1,0:T(8,128)(2,1)S(1)} fusion(bf16[1024,768]{1,0:T(8,128)(2,1)S(1)} %bitcast.15, s32[]{:T(128)S(6)} %select_n.41, bf16[1024,1024]{1,0:T(8,128)(2,1)} %bitcast.21), kind=kOutput, calls=%fused_computation.4 | convolution fusion | flops 1615593472 | bytes 5242884 | tf_op jit(solution)/shard_map/dot_general | solution.py:371
  33.6 3.9 %all-to-all-start.1 = ((bf16[4,1,256,768]{3,2,1,0:T(8,128)(2,1)}), bf16[4,1,256,768]{3,2,1,0:T(8,128)(2,1)S(1)}, u32[]{:S(2)}, u32[]{:S(2)}) async-start(bf16[4,1,256,768]{3,2,1,0:T(8,128)(2,1)} %slice.41), calls=%async_computation.1 | async-start | bytes 3145728 | tf_op jit(solution)/shard_map/all_to_all | solution.py:329
  38.9 5.3 %pack.1 = (bf16[16,32,1536]{2,1,0:T(8,128)(2,1)}, bf16[16,32,1536]{2,1,0:T(8,128)(2,1)}, bf16[16,32,1536]{2,1,0:T(8,128)(2,1)}, bf16[16,32,1536]{2,1,0:T(8,128)(2,1)}) custom-call(s32[32]{0:T(128)} %reshape.70.orbs, s32[2]{0:T(128)} %pad_add_fusion.1.place, bf16[32,32,1536]{2,1,0:T(8,128)(2,1)} %bitcast.14), custom_call_target="tpu_custom_call" | custom-call | bytes 9437184 | tf_op jit(solution)/shard_map/pack/pallas_call | solution.py:59
  44.2 2.4 collective-permute-start.1
  49.3 3.9 %collective-permute-start.4 = (bf16[640,768]{1,0:T(8,128)(2,1)}, bf16[640,768]{1,0:T(8,128)(2,1)}, u32[]{:S(2)}, u32[]{:S(2)}) collective-permute-start(bf16[640,768]{1,0:T(8,128)(2,1)} %slice.52), channel_id=1, source_target_pairs={{0,6},{1,7},{2,4},{3,5},{4,2},{5,3},{6,0},{7,1},{8,14},{9,15},{10,... | collective-permute-start | bytes 2949128 | tf_op jit(solution)/shard_map/ppermute | solution.py:322
  53.2 4.1 %all-to-all-done.1 = bf16[4,1,256,768]{3,2,1,0:T(8,128)(2,1)S(1)} async-done(((bf16[4,1,256,768]{3,2,1,0:T(8,128)(2,1)}), bf16[4,1,256,768]{3,2,1,0:T(8,128)(2,1)S(1)}, u32[]{:S(2)}, u32[]{:S(2)}) %all-to-all-start.1) | async-done | bytes 1572896 | tf_op jit(solution)/shard_map/all_to_all | solution.py:329
  57.4 4.3 %convolution_convert_fusion.refs_5_ = bf16[1024,768]{1,0:T(8,128)(2,1)S(1)} fusion(bf16[1024,768]{1,0:T(8,128)(2,1)S(1)} %bitcast.16, s32[]{:T(128)S(6)} %select_n.41, bf16[1024,1024]{1,0:T(8,128)(2,1)} %bitcast.22), kind=kOutput, calls=%fused_computation.3 | convolution fusion | flops 1615593472 | bytes 5242884 | tf_op jit(solution)/shard_map/dot_general | solution.py:371
  64.0 4.4 %collective-permute-start.5 = (bf16[640,768]{1,0:T(8,128)(2,1)}, bf16[640,768]{1,0:T(8,128)(2,1)}, u32[]{:S(2)}, u32[]{:S(2)}) collective-permute-start(bf16[640,768]{1,0:T(8,128)(2,1)} %slice.53), channel_id=1, source_target_pairs={{0,6},{1,7},{2,4},{3,5},{4,2},{5,3},{6,0},{7,1},{8,14},{9,15},{10,... | collective-permute-start | bytes 2949128 | tf_op jit(solution)/shard_map/ppermute | solution.py:322
  69.0 12.8 %collective-permute-done.1.refs_1_ = bf16[16,32,1536]{2,1,0:T(8,128)(2,1)} collective-permute-done((bf16[16,32,1536]{2,1,0:T(8,128)(2,1)}, bf16[16,32,1536]{2,1,0:T(8,128)(2,1)}, u32[]{:S(2)}, u32[]{:S(2)}) %collective-permute-start.1) | collective-permute-done | bytes 1572896 | tf_op jit(solution)/shard_map/ppermute | solution.py:322
  81.8 2.4 %collective-permute-done.2.refs_2_ = bf16[16,32,1536]{2,1,0:T(8,128)(2,1)} collective-permute-done((bf16[16,32,1536]{2,1,0:T(8,128)(2,1)}, bf16[16,32,1536]{2,1,0:T(8,128)(2,1)}, u32[]{:S(2)}, u32[]{:S(2)}) %collective-permute-start.2) | collective-permute-done | bytes 1572896 | tf_op jit(solution)/shard_map/ppermute | solution.py:322
  84.2 32.8 %collective-permute-done.3.refs_3_ = bf16[16,32,1536]{2,1,0:T(8,128)(2,1)} collective-permute-done((bf16[16,32,1536]{2,1,0:T(8,128)(2,1)}, bf16[16,32,1536]{2,1,0:T(8,128)(2,1)}, u32[]{:S(2)}, u32[]{:S(2)}) %collective-permute-start.3) | collective-permute-done | bytes 1572896 | tf_op jit(solution)/shard_map/ppermute | solution.py:322
  119.8 6.7 %shard_map.87 = (bf16[16,32,1024]{2,1,0:T(8,128)(2,1)S(1)}, bf16[16,32,1024]{2,1,0:T(8,128)(2,1)}) custom-call(bf16[16,32,1536]{2,1,0:T(8,128)(2,1)S(1)} %copy-done, bf16[16,32,1536]{2,1,0:T(8,128)(2,1)} %collective-permute-done.1.refs_1_, bf16[16,32,1536]{2,1,0:T(8,128)(2,1)} %collective-permute-done.2.refs_2_, ...), custom_call_target="tpu_custom_call" | custom-call | flops 3221225472 | bytes 3145728 | tf_op jit(solution)/shard_map/pallas_call | solution.py:123
  127.9 2.6 %collective-permute-start = (s32[32]{0:T(128)S(1)}, s32[32]{0:T(128)S(1)}, u32[]{:S(2)}, u32[]{:S(2)}) collective-permute-start(s32[32]{0:T(128)S(1)} %copy-done.11), channel_id=1, source_target_pairs={{0,2},{1,3},{2,0},{3,1},{4,6},{5,7},{6,4},{7,5},{8,10},{9,11},{10,... | collective-permute-start | bytes 392 | tf_op jit(solution)/shard_map/ppermute | solution.py:322
  130.5 10.4 %collective-permute-done.4.refs_4_ = bf16[640,768]{1,0:T(8,128)(2,1)} collective-permute-done((bf16[640,768]{1,0:T(8,128)(2,1)}, bf16[640,768]{1,0:T(8,128)(2,1)}, u32[]{:S(2)}, u32[]{:S(2)}) %collective-permute-start.4) | collective-permute-done | bytes 983072 | tf_op jit(solution)/shard_map/ppermute | solution.py:322
  141.0 20.2 %collective-permute-done.5.refs_5_ = bf16[640,768]{1,0:T(8,128)(2,1)} collective-permute-done((bf16[640,768]{1,0:T(8,128)(2,1)}, bf16[640,768]{1,0:T(8,128)(2,1)}, u32[]{:S(2)}, u32[]{:S(2)}) %collective-permute-start.5) | collective-permute-done | bytes 983072 | tf_op jit(solution)/shard_map/ppermute | solution.py:322
  162.6 5.7 %shard_map.86 = (bf16[16,32,640]{2,1,0:T(8,128)(2,1)S(1)}, bf16[16,32,640]{2,1,0:T(8,128)(2,1)}) custom-call(bf16[16,32,1536]{2,1,0:T(8,128)(2,1)S(1)} %copy-done.1, bf16[16,32,1536]{2,1,0:T(8,128)(2,1)} %collective-permute-done.1.refs_1_, bf16[16,32,1536]{2,1,0:T(8,128)(2,1)} %collective-permute-done.2.refs_2_, ...), custom_call_target="tpu_custom_call" | custom-call | flops 2013265920 | bytes 3145728 | tf_op jit(solution)/shard_map/pallas_call | solution.py:123
  170.4 1.8 slice.47
  172.1 12.6 %collective-permute-start.11 = (bf16[128,768]{1,0:T(8,128)(2,1)}, bf16[128,768]{1,0:T(8,128)(2,1)}, u32[]{:S(2)}, u32[]{:S(2)}) collective-permute-start(bf16[128,768]{1,0:T(8,128)(2,1)} %slice.49), channel_id=1, source_target_pairs={{0,6},{1,7},{2,4},{3,5},{4,2},{5,3},{6,0},{7,1},{8,14},{9,15},{10,... | collective-permute-start | bytes 589832 | tf_op jit(solution)/shard_map/ppermute | solution.py:322
  188.1 3.8 %collective-permute-start.9 = (bf16[256,768]{1,0:T(8,128)(2,1)}, bf16[256,768]{1,0:T(8,128)(2,1)}, u32[]{:S(2)}, u32[]{:S(2)}) collective-permute-start(bf16[256,768]{1,0:T(8,128)(2,1)} %slice.56), channel_id=1, source_target_pairs={{0,6},{1,7},{2,4},{3,5},{4,2},{5,3},{6,0},{7,1},{8,14},{9,15},{10,... | collective-permute-start | bytes 1179656 | tf_op jit(solution)/shard_map/ppermute | solution.py:322
  192.5 2.8 %shard_map.88 = (bf16[16,32,640]{2,1,0:T(8,128)(2,1)S(1)}, f32[2,16,32,32]{3,2,1,0:T(8,128)S(1)}) custom-call(s32[2,32]{1,0:T(2,128)S(1)} %get-tuple-element.54.rows, s32[2,32]{1,0:T(2,128)S(1)} %reshape.72.offsets, f32[8,128]{1,0:T(8,128)S(1)} %broadcast_in_dim.60.before, bf16[16,32,1024]{2,1,0:T(8,128)(2,1)S(1)} %get-tuple-element.34.refs_0_, ...), custom_call_target="tpu_custom_call" | custom-call | tf_op jit(solution)/shard_map/pallas_call | solution.py:199
  195.4 3.9 %collective-permute-done.8.refs_4_ = bf16[256,768]{1,0:T(8,128)(2,1)} collective-permute-done((bf16[256,768]{1,0:T(8,128)(2,1)}, bf16[256,768]{1,0:T(8,128)(2,1)}, u32[]{:S(2)}, u32[]{:S(2)}) %collective-permute-start.8) | collective-permute-done | bytes 393248 | tf_op jit(solution)/shard_map/ppermute | solution.py:322
  199.3 8.4 %collective-permute-done.9.refs_5_ = bf16[256,768]{1,0:T(8,128)(2,1)} collective-permute-done((bf16[256,768]{1,0:T(8,128)(2,1)}, bf16[256,768]{1,0:T(8,128)(2,1)}, u32[]{:S(2)}, u32[]{:S(2)}) %collective-permute-start.9) | collective-permute-done | bytes 393248 | tf_op jit(solution)/shard_map/ppermute | solution.py:322
  207.7 2.8 %shard_map.89 = (bf16[16,32,256]{2,1,0:T(8,128)(2,1)S(1)}, bf16[16,32,256]{2,1,0:T(8,128)(2,1)S(1)}) custom-call(bf16[16,32,1536]{2,1,0:T(8,128)(2,1)S(1)} %copy-done.2, bf16[16,32,1536]{2,1,0:T(8,128)(2,1)} %collective-permute-done.1.refs_1_, bf16[16,32,1536]{2,1,0:T(8,128)(2,1)} %collective-permute-done.2.refs_2_, ...), custom_call_target="tpu_custom_call" | custom-call | flops 805306368 | bytes 3145728 | tf_op jit(solution)/shard_map/pallas_call | solution.py:123
  212.1 2.7 %shard_map.90 = (bf16[16,32,128]{2,1,0:T(8,128)(2,1)S(1)}, bf16[16,32,128]{2,1,0:T(8,128)(2,1)S(1)}) custom-call(bf16[16,32,1536]{2,1,0:T(8,128)(2,1)S(1)} %copy-done.2, bf16[16,32,1536]{2,1,0:T(8,128)(2,1)} %collective-permute-done.1.refs_1_, bf16[16,32,1536]{2,1,0:T(8,128)(2,1)} %collective-permute-done.2.refs_2_, ...), custom_call_target="tpu_custom_call" | custom-call | flops 402653184 | bytes 3145728 | tf_op jit(solution)/shard_map/pallas_call | solution.py:123
  217.0 2.0 shard_map.91
  219.8 2.2 shard_map.92
  222.0 4.7 %collective-permute-start.17 = (bf16[16,32,128]{2,1,0:T(8,128)(2,1)S(1)}, bf16[16,32,128]{2,1,0:T(8,128)(2,1)S(1)}, u32[]{:S(2)}, u32[]{:S(2)}) collective-permute-start(bf16[16,32,128]{2,1,0:T(8,128)(2,1)S(1)} %get-tuple-element.47), channel_id=1, source_target_pairs={{0,2},{1,3},{2,0},{3,1},{4,6},{5,7},{6,4},{7,5},{8,10},{9,11},{10,... | collective-permute-start | bytes 393224 | tf_op jit(solution)/shard_map/ppermute | solution.py:322
  226.8 2.0 collective-permute-start.14
  228.8 4.3 %collective-permute-done.16.refs_7_ = bf16[16,32,256]{2,1,0:T(8,128)(2,1)S(1)} collective-permute-done((bf16[16,32,256]{2,1,0:T(8,128)(2,1)S(1)}, bf16[16,32,256]{2,1,0:T(8,128)(2,1)S(1)}, u32[]{:S(2)}, u32[]{:S(2)}) %collective-permute-start.16) | collective-permute-done | bytes 262176 | tf_op jit(solution)/shard_map/ppermute | solution.py:322
  (81 shorter events, 31.4 us)
Async XLA Ops:
  3.3 4.4 %copy-start.14 = (s32[32]{0:T(128)S(1)}, s32[32]{0:T(128)}, u32[]{:S(2)}) copy-start(s32[32]{0:T(128)} %param.13) | copy-start | bytes 388
  3.3 24.4 %all-to-all-start = ((bf16[4,1,256,768]{3,2,1,0:T(8,128)(2,1)}), bf16[4,1,256,768]{3,2,1,0:T(8,128)(2,1)S(1)}, u32[]{:S(2)}, u32[]{:S(2)}) async-start(bf16[4,1,256,768]{3,2,1,0:T(8,128)(2,1)} %slice.39), calls=%async_computation | async-start | bytes 3145728 | tf_op jit(solution)/shard_map/all_to_all | solution.py:329
  27.8 4.4 %copy-start.9 = (bf16[4,1,256,1536]{3,2,1,0:T(8,128)(2,1)S(1)}, bf16[4,1,256,1536]{3,2,1,0:T(8,128)(2,1)}, u32[]{:S(2)}) copy-start(bf16[4,1,256,1536]{3,2,1,0:T(8,128)(2,1)} %param.7) | copy-start | bytes 9437188
  32.2 16.1 %copy-start.3 = (bf16[1024,768]{1,0:T(8,128)(2,1)}, bf16[1024,768]{1,0:T(8,128)(2,1)S(1)}, u32[]{:S(2)}) copy-start(bf16[1024,768]{1,0:T(8,128)(2,1)S(1)} %convolution_convert_fusion.1.refs_4_) | copy-start | bytes 4718596
  33.6 3.9 %copy-start.12 = (s32[16,2]{0,1:T(2,128)S(1)}, s32[16,2]{0,1:T(2,128)}, u32[]{:S(2)}) copy-start(s32[16,2]{0,1:T(2,128)} %param.9) | copy-start | bytes 388
  33.6 23.7 %all-to-all-start.1 = ((bf16[4,1,256,768]{3,2,1,0:T(8,128)(2,1)}), bf16[4,1,256,768]{3,2,1,0:T(8,128)(2,1)S(1)}, u32[]{:S(2)}, u32[]{:S(2)}) async-start(bf16[4,1,256,768]{3,2,1,0:T(8,128)(2,1)} %slice.41), calls=%async_computation.1 | async-start | bytes 3145728 | tf_op jit(solution)/shard_map/all_to_all | solution.py:329
  37.5 10.7 %copy-start.10 = (f32[16,2,32]{2,1,0:T(2,128)S(1)}, f32[16,2,32]{2,1,0:T(2,128)}, u32[]{:S(2)}) copy-start(f32[16,2,32]{2,1,0:T(2,128)} %param.11) | copy-start | bytes 12292
  38.2 10.0 %copy-start.11 = (s32[32]{0:T(128)S(1)}, s32[32]{0:T(128)}, u32[]{:S(2)}) copy-start(s32[32]{0:T(128)} %reshape.70.orbs) | copy-start | bytes 388
  44.2 37.5 %collective-permute-start.1 = (bf16[16,32,1536]{2,1,0:T(8,128)(2,1)}, bf16[16,32,1536]{2,1,0:T(8,128)(2,1)}, u32[]{:S(2)}, u32[]{:S(2)}) collective-permute-start(bf16[16,32,1536]{2,1,0:T(8,128)(2,1)} %get-tuple-element.27), channel_id=1, source_target_pairs={{0,1},{1,0},{2,3},{3,2},{4,5},{5,4},{6,7},{7,6},{8,9},{9,8},{10,11... | collective-permute-start | bytes 4718600 | tf_op jit(solution)/shard_map/ppermute | solution.py:322
  46.6 37.6 %collective-permute-start.2 = (bf16[16,32,1536]{2,1,0:T(8,128)(2,1)}, bf16[16,32,1536]{2,1,0:T(8,128)(2,1)}, u32[]{:S(2)}, u32[]{:S(2)}) collective-permute-start(bf16[16,32,1536]{2,1,0:T(8,128)(2,1)} %get-tuple-element.28), channel_id=1, source_target_pairs={{0,2},{1,3},{2,0},{3,1},{4,6},{5,7},{6,4},{7,5},{8,10},{9,11},{10,... | collective-permute-start | bytes 4718600 | tf_op jit(solution)/shard_map/ppermute | solution.py:322
  48.2 68.8 %collective-permute-start.3 = (bf16[16,32,1536]{2,1,0:T(8,128)(2,1)}, bf16[16,32,1536]{2,1,0:T(8,128)(2,1)}, u32[]{:S(2)}, u32[]{:S(2)}) collective-permute-start(bf16[16,32,1536]{2,1,0:T(8,128)(2,1)} %get-tuple-element.29), channel_id=1, source_target_pairs={{0,3},{1,2},{2,1},{3,0},{4,7},{5,6},{6,5},{7,4},{8,11},{9,10},{10,... | collective-permute-start | bytes 4718600 | tf_op jit(solution)/shard_map/ppermute | solution.py:322
  49.3 91.7 %collective-permute-start.4 = (bf16[640,768]{1,0:T(8,128)(2,1)}, bf16[640,768]{1,0:T(8,128)(2,1)}, u32[]{:S(2)}, u32[]{:S(2)}) collective-permute-start(bf16[640,768]{1,0:T(8,128)(2,1)} %slice.52), channel_id=1, source_target_pairs={{0,6},{1,7},{2,4},{3,5},{4,2},{5,3},{6,0},{7,1},{8,14},{9,15},{10,... | collective-permute-start | bytes 2949128 | tf_op jit(solution)/shard_map/ppermute | solution.py:322
  57.4 11.0 %copy-start.13 = (f32[32]{0:T(128)S(1)}, f32[32]{0:T(128)}, u32[]{:S(2)}) copy-start(f32[32]{0:T(128)} %param.12) | copy-start | bytes 388
  61.7 55.3 %copy-start = (bf16[16,32,1536]{2,1,0:T(8,128)(2,1)S(1)}, bf16[16,32,1536]{2,1,0:T(8,128)(2,1)}, u32[]{:S(2)}) copy-start(bf16[16,32,1536]{2,1,0:T(8,128)(2,1)} %get-tuple-element.26.refs_0_) | copy-start | bytes 4718596
  64.0 97.2 %collective-permute-start.5 = (bf16[640,768]{1,0:T(8,128)(2,1)}, bf16[640,768]{1,0:T(8,128)(2,1)}, u32[]{:S(2)}, u32[]{:S(2)}) collective-permute-start(bf16[640,768]{1,0:T(8,128)(2,1)} %slice.53), channel_id=1, source_target_pairs={{0,6},{1,7},{2,4},{3,5},{4,2},{5,3},{6,0},{7,1},{8,14},{9,15},{10,... | collective-permute-start | bytes 2949128 | tf_op jit(solution)/shard_map/ppermute | solution.py:322
  69.0 57.5 %copy-start.7 = (f32[16,32,32]{2,1,0:T(8,128)}, f32[16,32,32]{2,1,0:T(8,128)S(1)}, u32[]{:S(2)}) copy-start(f32[16,32,32]{2,1,0:T(8,128)S(1)} %subtract_subtract_fusion.refs_6_.denominator) | copy-start | bytes 196612
  117.0 1.4 copy-start.4
  126.5 65.8 %collective-permute-start.6 = (bf16[16,32,1024]{2,1,0:T(8,128)(2,1)}, bf16[16,32,1024]{2,1,0:T(8,128)(2,1)S(1)}, u32[]{:S(2)}, u32[]{:S(2)}) collective-permute-start(bf16[16,32,1024]{2,1,0:T(8,128)(2,1)} %get-tuple-element.35), channel_id=1, source_target_pairs={{0,1},{1,0},{2,3},{3,2},{4,5},{5,4},{6,7},{7,6},{8,9},{9,8},{10,11... | collective-permute-start | bytes 3145736 | tf_op jit(solution)/shard_map/ppermute | solution.py:322
  127.9 60.2 %collective-permute-start = (s32[32]{0:T(128)S(1)}, s32[32]{0:T(128)S(1)}, u32[]{:S(2)}, u32[]{:S(2)}) collective-permute-start(s32[32]{0:T(128)S(1)} %copy-done.11), channel_id=1, source_target_pairs={{0,2},{1,3},{2,0},{3,1},{4,6},{5,7},{6,4},{7,5},{8,10},{9,11},{10,... | collective-permute-start | bytes 392 | tf_op jit(solution)/shard_map/ppermute | solution.py:322
  168.2 24.2 %collective-permute-start.7 = (bf16[16,32,640]{2,1,0:T(8,128)(2,1)}, bf16[16,32,640]{2,1,0:T(8,128)(2,1)S(1)}, u32[]{:S(2)}, u32[]{:S(2)}) collective-permute-start(bf16[16,32,640]{2,1,0:T(8,128)(2,1)} %get-tuple-element.37), channel_id=1, source_target_pairs={{0,1},{1,0},{2,3},{3,2},{4,5},{5,4},{6,7},{7,6},{8,9},{9,8},{10,11... | collective-permute-start | bytes 1966088 | tf_op jit(solution)/shard_map/ppermute | solution.py:322
  172.1 39.9 %collective-permute-start.11 = (bf16[128,768]{1,0:T(8,128)(2,1)}, bf16[128,768]{1,0:T(8,128)(2,1)}, u32[]{:S(2)}, u32[]{:S(2)}) collective-permute-start(bf16[128,768]{1,0:T(8,128)(2,1)} %slice.49), channel_id=1, source_target_pairs={{0,6},{1,7},{2,4},{3,5},{4,2},{5,3},{6,0},{7,1},{8,14},{9,15},{10,... | collective-permute-start | bytes 589832 | tf_op jit(solution)/shard_map/ppermute | solution.py:322
  184.7 14.6 %collective-permute-start.8 = (bf16[256,768]{1,0:T(8,128)(2,1)}, bf16[256,768]{1,0:T(8,128)(2,1)}, u32[]{:S(2)}, u32[]{:S(2)}) collective-permute-start(bf16[256,768]{1,0:T(8,128)(2,1)} %slice.47), channel_id=1, source_target_pairs={{0,6},{1,7},{2,4},{3,5},{4,2},{5,3},{6,0},{7,1},{8,14},{9,15},{10,... | collective-permute-start | bytes 1179656 | tf_op jit(solution)/shard_map/ppermute | solution.py:322
  188.1 19.6 %collective-permute-start.9 = (bf16[256,768]{1,0:T(8,128)(2,1)}, bf16[256,768]{1,0:T(8,128)(2,1)}, u32[]{:S(2)}, u32[]{:S(2)}) collective-permute-start(bf16[256,768]{1,0:T(8,128)(2,1)} %slice.56), channel_id=1, source_target_pairs={{0,6},{1,7},{2,4},{3,5},{4,2},{5,3},{6,0},{7,1},{8,14},{9,15},{10,... | collective-permute-start | bytes 1179656 | tf_op jit(solution)/shard_map/ppermute | solution.py:322
  192.3 19.8 %collective-permute-start.12 = (bf16[128,768]{1,0:T(8,128)(2,1)}, bf16[128,768]{1,0:T(8,128)(2,1)}, u32[]{:S(2)}, u32[]{:S(2)}) collective-permute-start(bf16[128,768]{1,0:T(8,128)(2,1)} %slice.57), channel_id=1, source_target_pairs={{0,6},{1,7},{2,4},{3,5},{4,2},{5,3},{6,0},{7,1},{8,14},{9,15},{10,... | collective-permute-start | bytes 589832 | tf_op jit(solution)/shard_map/ppermute | solution.py:322
  192.5 15.2 %copy-start.2 = (bf16[16,32,1536]{2,1,0:T(8,128)(2,1)S(1)}, bf16[16,32,1536]{2,1,0:T(8,128)(2,1)}, u32[]{:S(2)}) copy-start(bf16[16,32,1536]{2,1,0:T(8,128)(2,1)} %get-tuple-element.26.refs_0_) | copy-start | bytes 4718596
  195.3 37.8 %collective-permute-start.15 = (bf16[16,32,640]{2,1,0:T(8,128)(2,1)S(1)}, bf16[16,32,640]{2,1,0:T(8,128)(2,1)S(1)}, u32[]{:S(2)}, u32[]{:S(2)}) collective-permute-start(bf16[16,32,640]{2,1,0:T(8,128)(2,1)S(1)} %get-tuple-element.45), channel_id=1, source_target_pairs={{0,2},{1,3},{2,0},{3,1},{4,6},{5,7},{6,4},{7,5},{8,10},{9,11},{10,... | collective-permute-start | bytes 1966088 | tf_op jit(solution)/shard_map/ppermute | solution.py:322
  210.5 6.4 %collective-permute-start.10 = (bf16[16,32,256]{2,1,0:T(8,128)(2,1)S(1)}, bf16[16,32,256]{2,1,0:T(8,128)(2,1)S(1)}, u32[]{:S(2)}, u32[]{:S(2)}) collective-permute-start(bf16[16,32,256]{2,1,0:T(8,128)(2,1)S(1)} %get-tuple-element.40), channel_id=1, source_target_pairs={{0,1},{1,0},{2,3},{3,2},{4,5},{5,4},{6,7},{7,6},{8,9},{9,8},{10,11... | collective-permute-start | bytes 786440 | tf_op jit(solution)/shard_map/ppermute | solution.py:322
  214.8 5.0 %collective-permute-start.13 = (bf16[16,32,128]{2,1,0:T(8,128)(2,1)S(1)}, bf16[16,32,128]{2,1,0:T(8,128)(2,1)S(1)}, u32[]{:S(2)}, u32[]{:S(2)}) collective-permute-start(bf16[16,32,128]{2,1,0:T(8,128)(2,1)S(1)} %get-tuple-element.43), channel_id=1, source_target_pairs={{0,1},{1,0},{2,3},{3,2},{4,5},{5,4},{6,7},{7,6},{8,9},{9,8},{10,11... | collective-permute-start | bytes 393224 | tf_op jit(solution)/shard_map/ppermute | solution.py:322
  222.0 13.9 %collective-permute-start.17 = (bf16[16,32,128]{2,1,0:T(8,128)(2,1)S(1)}, bf16[16,32,128]{2,1,0:T(8,128)(2,1)S(1)}, u32[]{:S(2)}, u32[]{:S(2)}) collective-permute-start(bf16[16,32,128]{2,1,0:T(8,128)(2,1)S(1)} %get-tuple-element.47), channel_id=1, source_target_pairs={{0,2},{1,3},{2,0},{3,1},{4,6},{5,7},{6,4},{7,5},{8,10},{9,11},{10,... | collective-permute-start | bytes 393224 | tf_op jit(solution)/shard_map/ppermute | solution.py:322
  226.7 6.4 %collective-permute-start.16 = (bf16[16,32,256]{2,1,0:T(8,128)(2,1)S(1)}, bf16[16,32,256]{2,1,0:T(8,128)(2,1)S(1)}, u32[]{:S(2)}, u32[]{:S(2)}) collective-permute-start(bf16[16,32,256]{2,1,0:T(8,128)(2,1)S(1)} %get-tuple-element.46), channel_id=1, source_target_pairs={{0,2},{1,3},{2,0},{3,1},{4,6},{5,7},{6,4},{7,5},{8,10},{9,11},{10,... | collective-permute-start | bytes 786440 | tf_op jit(solution)/shard_map/ppermute | solution.py:322
  226.8 9.1 %collective-permute-start.14 = (f32[16,32,32]{2,1,0:T(8,128)S(1)}, f32[16,32,32]{2,1,0:T(8,128)S(1)}, u32[]{:S(2)}, u32[]{:S(2)}) collective-permute-start(f32[16,32,32]{2,1,0:T(8,128)S(1)} %slice_bitcast_fusion), channel_id=1, source_target_pairs={{0,2},{1,3},{2,0},{3,1},{4,6},{5,7},{6,4},{7,5},{8,10},{9,11},{10,... | collective-permute-start | bytes 196616 | tf_op jit(solution)/shard_map/ppermute | solution.py:322
  233.1 2.8 %copy-start.8 = (f32[16,32,32]{2,1,0:T(8,128)S(1)}, f32[16,32,32]{2,1,0:T(8,128)}, u32[]{:S(2)}) copy-start(f32[16,32,32]{2,1,0:T(8,128)} %copy-done.7) | copy-start | bytes 196612
  (3 other events, 4.0 us)

commit v8 on v7

--- a/solution.py
+++ b/solution.py
@@ -75,9 +75,9 @@
     )(orbs, place, coef)
 
 
-def project_kernel(group, capacity, *refs):
+def project_kernel(group, capacity, direct, *refs):
     inner = group // 2
-    blocks, parts, outs = refs[:group], refs[group : group + 2], refs[-inner:]
+    blocks, parts, outs = refs[:group], refs[group : group + 2], refs[group + 2 :]
     row_count, half = parts[0].shape
     pno_count = outs[0].shape[1]
     step = row_count if row_count <= 640 else 256
@@ -97,8 +97,9 @@
                     )
                     for k in range(2)
                 )
-                outs[i][j * capacity : (j + 1) * capacity, :, pl.ds(at, step)] = product.astype(
-                    outs[i].dtype
+                out, first = (outs[i + j * inner], 0) if direct else (outs[i], j * capacity)
+                out[first : first + capacity, :, pl.ds(at, step)] = product.astype(
+                    out.dtype
                 ).reshape(capacity, pno_count, step)
         return carry
 
@@ -108,24 +109,25 @@
         lax.fori_loop(0, row_count // step, tile, 0)
 
 
-def project(blocks, kind, parts, tokens):
+def project(blocks, kind, parts, tokens, direct):
     group = len(blocks)
     inner = group // 2
     slots, pno_count, dom_count = blocks[0].shape
     capacity = slots // 2
     row_count = parts[0].shape[0]
+    count, lines = (group, capacity) if direct else (inner, slots)
 
     def kernel(*refs):
-        project_kernel(group, capacity, *refs[: group + 2], *refs[-inner:])
+        project_kernel(group, capacity, direct, *refs[: group + 2], *refs[-count:])
 
     block = pl.BlockSpec((capacity, pno_count, dom_count), lambda i: (kind, 0, 0))
     part = pl.BlockSpec(parts[0].shape, lambda i: (0, 0))
     return pl.pallas_call(
         kernel,
         grid=(1,),
-        out_shape=(jax.ShapeDtypeStruct((slots, pno_count, row_count), blocks[0].dtype),) * inner,
+        out_shape=(jax.ShapeDtypeStruct((lines, pno_count, row_count), blocks[0].dtype),) * count,
         in_specs=[block] * group + [part] * 2 + [ANY] * len(tokens),
-        out_specs=(pl.BlockSpec((slots, pno_count, row_count), lambda i: (0, 0, 0)),) * inner,
+        out_specs=(pl.BlockSpec((lines, pno_count, row_count), lambda i: (0, 0, 0)),) * count,
         compiler_params=pltpu.CompilerParams(vmem_limit_bytes=32 << 20),
         cost_estimate=pl.CostEstimate(
             flops=2 * group * capacity * pno_count * dom_count * row_count,
@@ -250,16 +252,37 @@
     mixed_pairs(inner, spans, margin, rows, offsets, near, far, others, held, sem, write)
 
 
-def finish_kernel(inner, spans, margin, rows, offsets, here, there, before, denominator, *refs):
-    near, refs = refs[:inner], refs[inner:]
-    far, refs = refs[: inner * len(spans)], refs[inner * len(spans) :]
-    others = refs[: len(spans)]
+def finish_kernel(group, sizes, rows, here, there, before, denominator, *refs):
+    inner = group // 2
+    near, straight, far = refs[:inner], refs[inner:group], refs[group : group + group * len(sizes)]
     amplitude, energy, coupling, held, sem = refs[-5:]
-
-    def write(n, product):
-        coupling[n] = product
-
-    mixed_pairs(inner, spans, margin, rows, offsets, near, far, others, held, sem, write)
+    capacity, _, width = straight[0].shape
+    low = near[0].shape[2] - width
+    for m in range(group):
+        source = straight[m - inner]
+        if m < inner:
+            source = near[m].at[pl.ds(0, capacity), :, pl.ds(low, width)]
+        copy(source, held.at[pl.ds(m * capacity, capacity)], sem).start()
+        at = 0
+        for c, size in enumerate(sizes):
+            copy(
+                far[c * group + m],
+                held.at[pl.ds((group + m) * capacity, capacity), :, pl.ds(at, size)],
+                sem,
+            ).start()
+            at += size
+    copy(held, held, sem).wait()
+
+    def one_pair(n, carry):
+        coupling[n] = lax.dot_general(
+            held[rows[2 * n]],
+            held[rows[2 * n + 1]],
+            (((1,), (1,)), ((), ())),
+            preferred_element_type=jnp.float32,
+        )
+        return carry
+
+    lax.fori_loop(0, coupling.shape[0], one_pair, 0, unroll=4)
     total = coupling[...] + before[...] + here[0] + there[...]
     result = -total / denominator[...]
     amplitude[...] = result
@@ -267,31 +290,42 @@
     energy[...] = jnp.sum(jnp.sum(parts, axis=1), axis=1, keepdims=True)
 
 
-def mixed(rows, offsets, near, far, others, spans, margin, tokens, finals):
+def finish(rows, finals, near, straight, far, sizes):
+    group = 2 * len(near)
+    capacity, pno_count, width = straight[0].shape
+    pair_count = rows.shape[0] // 2
+    square = jax.ShapeDtypeStruct((pair_count, pno_count, pno_count), jnp.float32)
+    return pl.pallas_call(
+        functools.partial(finish_kernel, group, sizes),
+        out_shape=(square, jax.ShapeDtypeStruct((pair_count, 1), jnp.float32)),
+        in_specs=[SMEM] + [VMEM] * len(finals) + [ANY] * (len(near) + len(straight) + len(far)),
+        out_specs=(VMEM, VMEM),
+        scratch_shapes=[
+            pltpu.VMEM(square.shape, jnp.float32),
+            pltpu.VMEM((2 * group * capacity, pno_count, width), near[0].dtype),
+            pltpu.SemaphoreType.DMA,
+        ],
+        compiler_params=pltpu.CompilerParams(vmem_limit_bytes=24 << 20),
+        name="finish",
+    )(rows, *finals, *near, *straight, *far)
+
+
+def mixed(rows, offsets, near, far, others, spans, margin, tokens):
     inner = len(near)
     slots, pno_count, _ = near[0].shape
     pair_count = rows.shape[1] // 2
     width = sum(size for _, size in spans)
-    square = jax.ShapeDtypeStruct((pair_count, pno_count, pno_count), jnp.float32)
-    line = jax.ShapeDtypeStruct((pair_count, 1), jnp.float32)
-    scratch = [
-        pltpu.VMEM((inner * slots + pair_count, pno_count, width), near[0].dtype),
-        pltpu.SemaphoreType.DMA,
-    ]
-    if finals:
-        scratch = [pltpu.VMEM(square.shape, jnp.float32)] + scratch
     return pl.pallas_call(
-        functools.partial(
-            finish_kernel if finals else mixed_kernel, inner, tuple(spans), margin
-        ),
-        out_shape=(square, line) if finals else square,
-        in_specs=[SMEM] * 2
-        + [VMEM] * len(finals)
-        + [ANY] * (len(near) + len(far) + len(others) + len(tokens)),
-        out_specs=(VMEM, VMEM) if finals else VMEM,
-        scratch_shapes=scratch,
+        functools.partial(mixed_kernel, inner, tuple(spans), margin),
+        out_shape=jax.ShapeDtypeStruct((pair_count, pno_count, pno_count), jnp.float32),
+        in_specs=[SMEM] * 2 + [ANY] * (len(near) + len(far) + len(others) + len(tokens)),
+        out_specs=VMEM,
+        scratch_shapes=[
+            pltpu.VMEM((inner * slots + pair_count, pno_count, width), near[0].dtype),
+            pltpu.SemaphoreType.DMA,
+        ],
         compiler_params=pltpu.CompilerParams(vmem_limit_bytes=24 << 20),
-    )(rows, offsets, *finals, *near, *far, *others, *tokens)
+    )(rows, offsets, *near, *far, *others, *tokens)
 
 
 def slots_of(orbs):
@@ -302,7 +336,7 @@
 
 
 def chunk_spans(fit_rows):
-    sizes = (5 * fit_rows // 8, fit_rows // 4, fit_rows // 8)
+    sizes = (fit_rows // 2, fit_rows // 4, fit_rows // 8, fit_rows // 8)
     return [(sum(sizes[:c]), size) for c, size in enumerate(sizes)]
 
 
@@ -339,6 +373,8 @@
     packed = pack(
         own_orbs, place, pno_coef.reshape(side_count, pno_count, dom_count), group, capacity
     )
+    later, packed = lax.optimization_barrier((raw_ints, packed))
+    raw_parts.append(exchange(later, 1))
     blocks = [packed[0]]
     for m in range(1, group):
         blocks.append(across(packed[m], m))
@@ -351,47 +387,47 @@
         selector = (region * orb_count + chosen)[:, None] == jnp.arange(orb_total, dtype=jnp.int32)
         return jnp.sum(jnp.where(selector, values[None, :], 0), axis=1)
 
-    occupied = pick(occ_energy, own_orbs).reshape(pair_count, 2)
+    spans = chunk_spans(fit_rows)
+    reverse = group + inner
+    fitted, mirrored = [], [[None] * 2 for _ in spans]
+
+    def mirror(c, k):
+        begin, size = spans[c]
+        mirrored[c][k] = across(fitted[k][begin : begin + size], reverse)
+
+    for k in range(2):
+        product = jnp.dot(turned, raw_parts[k], preferred_element_type=jnp.float32)
+        fitted.append(product.astype(jnp.bfloat16))
+        mirror(0, k)
+    for c in range(1, len(spans)):
+        mirror(c, 0)
+        mirror(c, 1)
+
+    energies, fitted[1] = lax.optimization_barrier((occ_energy, fitted[1]))
+    occupied = pick(energies, own_orbs).reshape(pair_count, 2)
     denominator = (
         pno_energy[:, 0, :, None]
         + pno_energy[:, 1, None, :]
         - occupied[:, 0, None, None]
         - occupied[:, 1, None, None]
     )
-    spans = chunk_spans(fit_rows)
-    reverse = group + inner
-    fitted, mirrored = [], [[None] * 2 for _ in spans]
-
-    def mirror(c, k):
-        begin, size = spans[c]
-        mirrored[c][k] = across(fitted[k][begin : begin + size], reverse)
-
-    for k in range(2):
-        fitted.append(
-            jnp.dot(turned, raw_parts[k], preferred_element_type=jnp.float32).astype(jnp.bfloat16)
-        )
-        mirror(0, k)
-        if k == 0:
-            later, fitted[0] = lax.optimization_barrier((raw_ints, fitted[0]))
-            raw_parts.append(exchange(later, 1))
-        mirror(1, k)
-    mirror(2, 0)
-    mirror(2, 1)
 
     def hop(outs):
         return [outs[0]] + [across(outs[i], i) for i in range(1, inner)]
 
     def project_far(c, tokens):
-        parts = project(blocks, 1, mirrored[c], tokens)
-        return hop(parts)
+        parts = project(blocks, 1, mirrored[c], tokens, c > 1)
+        return hop(parts) if c < 2 else [parts[0]] + [across(parts[m], m) for m in range(1, group)]
 
     def pass_on(c, before, tokens):
         sent, here = relay(rows, offsets, before, near, far[c], spans[c], margin, tokens)
         return across(sent, inner), here
 
-    near = project(blocks, 0, fitted, [denominator])
+    near = project(blocks, 0, fitted, [denominator], False)
+    last = spans[2][0]
+    straight = [across(near[i][capacity:, :, last:], i + inner) for i in range(inner)]
     near = hop(near)
-    far, others = [None] * 3, [None] * 3
+    far, others = [None] * 4, [None] * 2
     far[0] = project_far(0, [])
     mate_orbs, far[0][0] = lax.optimization_barrier((mate_orbs, far[0][0]))
     orbs = jnp.stack([own_orbs, mate_orbs])
@@ -403,26 +439,25 @@
     there = ((differs & inner) != 0) != other_half
     rows = jnp.where(there, -1, line * 2 * capacity + home * capacity + position)
     rows_home = jnp.where(there, -1, line * capacity + position)
+    place_of = (differs[0] ^ jnp.where(other_half[0], reverse, 0)) + jnp.where(
+        other_half[0], group, 0
+    )
+    rows_all = place_of * capacity + position[0]
     offsets = pick(fit_offset, orbs.reshape(2 * side_count)).reshape(2, side_count)
     others[0], here = pass_on(0, jnp.zeros((8, 128), jnp.float32), [])
     far[1] = project_far(1, [here])
     far[2] = project_far(2, [far[1][0]])
     others[1], here = pass_on(1, here, [far[2][0]])
-    others[2], here = pass_on(2, here, [])
     there = across(here[1], inner)
-    body = mixed(
-        rows_home, offsets, near, far[0] + far[1], others[:2], spans[:2], margin, [here], []
-    )
-    amplitude, energy = mixed(
-        rows_home,
-        offsets,
+    far[3] = project_far(3, [here])
+    body = mixed(rows_home, offsets, near, far[0] + far[1], others, spans[:2], margin, [far[3][0]])
+    amplitude, energy = finish(
+        rows_all,
+        [here, there, body, denominator],
         near,
-        far[2],
-        others[2:],
-        spans[2:],
-        margin,
-        [],
-        [here, there, body, denominator],
+        straight,
+        far[2] + far[3],
+        tuple(size for _, size in spans[2:]),
     )
     return (amplitude.reshape(pair_count, pno_count * pno_count), energy.reshape(pair_count))
 

time: 240 us -> 239 us (level)
  waiting for transfers between devices: 120 us -> 67.9 us
  starting transfers between devices: 51.2 us -> 92.3 us
  other arithmetic: 2.02 us -> 6.21 us
  local copies, waits for them, and re-layouts: 21.1 us -> 25.2 us
    ppermute x18 -> x26, waiting for transfers between devices: 98 us -> 55.3 us  [across(): return lax.ppermute(array, 'orb', [(i, i ^ mask) for i in range(orb_count)])]
    ppermute x18 -> x26, starting transfers between devices: 42.9 us -> 83.6 us  [across(): return lax.ppermute(array, 'orb', [(i, i ^ mask) for i in range(orb_count)])]
    all_to_all x2, waiting for transfers between devices: 21.6 us -> 12.6 us  [exchange(): lax.all_to_all(array[:, :, :, k * half:(k + 1) * half], 'aux', split_axis...]
    slice x6, local copies, waits for them, and re-layouts: 8.85 us -> 6.09 us  [mirror(): mirrored[c][k] = across(fitted[k][begin:begin + size], reverse)]
    unnamed x31 -> x37, local copies, waits for them, and re-layouts: 5.58 us -> 8.34 us
    pallas_call x6 -> x7, Pallas kernels: 21.2 us -> 23 us  [the longest x5 18.2 us: project(): pl.pallas_call(kernel, grid=(1,), out_shape=(jax.ShapeDtypeStruct((lines,...]
    pallas_call x3 -> x2, Pallas kernels: 7 us -> 6.24 us  [relay(): pl.pallas_call(functools.partial(relay_kernel, inner, (span,), margin), o...]
  transfers between devices with their start and end apart: 20 -> 28, of which waited for: 13 -> 11; matrix products, arithmetic and copies ran while one was open for 7% -> 12% of each run, Pallas kernels for 13% -> 14%
where the time goes in v8:
time: 239 us; the launch traced here: 238 us
  starting transfers between devices  92.3 us (39%)
  waiting for transfers between devices  67.9 us (28%)
  Pallas kernels  34.5 us (14%)
  local copies, waits for them, and re-layouts  25.2 us (11%)
  matrix products  9.07 us (4%)
  other arithmetic  6.21 us (3%)
  between operations  2.85 us (1%)
    ppermute x26, starting transfers between devices, across(): return lax.ppermute(array, 'orb', [(i, i ^ mask) for i in range(orb_count)])  83.6 us
    ppermute x26, waiting for transfers between devices, across(): return lax.ppermute(array, 'orb', [(i, i ^ mask) for i in range(orb_count)])  55.3 us
    pallas_call x5, Pallas kernels, project(): pl.pallas_call(kernel, grid=(1,), out_shape=(jax.ShapeDtypeStruct((lines,...  18.2 us
    all_to_all x2, waiting for transfers between devices, exchange(): lax.all_to_all(array[:, :, :, k * half:(k + 1) * half], 'aux', split_axis...  12.6 us
    dot_general x2, matrix products, on_device(): product = jnp.dot(turned, raw_parts[k], preferred_element_type=jnp.float32)  9.07 us
    all_to_all x2, starting transfers between devices, exchange(): lax.all_to_all(array[:, :, :, k * half:(k + 1) * half], 'aux', split_axis...  8.74 us
    unnamed x37, local copies, waits for them, and re-layouts  8.34 us
    pallas_call x2, Pallas kernels, relay(): pl.pallas_call(functools.partial(relay_kernel, inner, (span,), margin), o...  6.24 us
  transfers between devices with their start and end apart: 28, of which 11 were waited for; matrix products, arithmetic and copies ran while one was open for 12% of the time, Pallas kernels for 14%

profile of v8, /device:TPU:0, one launch (start us, length us, event | category | flops | bytes accessed | tf_op | source)
XLA Modules:
  0.0 238.0 jit_solution(2769261128327236523)
XLA Ops:
  0.6 2.7 %slice.61 = bf16[4,1,256,768]{3,2,1,0:T(8,128)(2,1)} slice(bf16[4,1,256,1536]{3,2,1,0:T(8,128)(2,1)} %param.7), slice={[0:4], [0:1], [0:256], [0:768]} | slice | bytes 3145728 | tf_op jit(solution)/shard_map/slice | solution.py:364
  3.3 4.4 %all-to-all-start = ((bf16[4,1,256,768]{3,2,1,0:T(8,128)(2,1)}), bf16[4,1,256,768]{3,2,1,0:T(8,128)(2,1)S(1)}, u32[]{:S(2)}, u32[]{:S(2)}) async-start(bf16[4,1,256,768]{3,2,1,0:T(8,128)(2,1)} %slice.61), calls=%async_computation | async-start | bytes 3145728 | tf_op jit(solution)/shard_map/all_to_all | solution.py:363
  8.9 5.2 %pack.1 = (bf16[16,32,1536]{2,1,0:T(8,128)(2,1)}, bf16[16,32,1536]{2,1,0:T(8,128)(2,1)}, bf16[16,32,1536]{2,1,0:T(8,128)(2,1)}, bf16[16,32,1536]{2,1,0:T(8,128)(2,1)}) custom-call(s32[32]{0:T(128)} %reshape.80.orbs, s32[2]{0:T(128)} %pad_add_fusion.1.place, bf16[32,32,1536]{2,1,0:T(8,128)(2,1)} %bitcast.16), custom_call_target="tpu_custom_call" | custom-call | bytes 9437184 | tf_op jit(solution)/shard_map/pack/pallas_call | solution.py:59
  14.2 2.7 %slice.63 = bf16[4,1,256,768]{3,2,1,0:T(8,128)(2,1)} slice(bf16[4,1,256,1536]{3,2,1,0:T(8,128)(2,1)} %param.7), slice={[0:4], [0:1], [0:256], [768:1536]} | slice | bytes 3145728 | tf_op jit(solution)/shard_map/slice | solution.py:364
  16.9 10.8 %all-to-all-done = bf16[4,1,256,768]{3,2,1,0:T(8,128)(2,1)S(1)} async-done(((bf16[4,1,256,768]{3,2,1,0:T(8,128)(2,1)}), bf16[4,1,256,768]{3,2,1,0:T(8,128)(2,1)S(1)}, u32[]{:S(2)}, u32[]{:S(2)}) %all-to-all-start) | async-done | bytes 1572896 | tf_op jit(solution)/shard_map/all_to_all | solution.py:363
  27.7 4.4 %all-to-all-start.1 = ((bf16[4,1,256,768]{3,2,1,0:T(8,128)(2,1)}), bf16[4,1,256,768]{3,2,1,0:T(8,128)(2,1)}, u32[]{:S(2)}, u32[]{:S(2)}) async-start(bf16[4,1,256,768]{3,2,1,0:T(8,128)(2,1)} %slice.63), calls=%async_computation.1 | async-start | bytes 3145728 | tf_op jit(solution)/shard_map/all_to_all | solution.py:363
  32.1 2.4 collective-permute-start.1
  40.0 4.3 %convolution_convert_fusion.1.refs_4_ = bf16[1024,768]{1,0:T(8,128)(2,1)S(1)} fusion(bf16[1024,768]{1,0:T(8,128)(2,1)S(1)} %bitcast.17, s32[]{:T(128)S(6)} %select_n.50, bf16[1024,1024]{1,0:T(8,128)(2,1)} %bitcast.22), kind=kOutput, calls=%fused_computation.4 | convolution fusion | flops 1615593472 | bytes 5242884 | tf_op jit(solution)/shard_map/dot_general | solution.py:399
  46.4 4.0 %collective-permute-start.4 = (bf16[512,768]{1,0:T(8,128)(2,1)}, bf16[512,768]{1,0:T(8,128)(2,1)}, u32[]{:S(2)}, u32[]{:S(2)}) collective-permute-start(bf16[512,768]{1,0:T(8,128)(2,1)} %slice.81), channel_id=1, source_target_pairs={{0,6},{1,7},{2,4},{3,5},{4,2},{5,3},{6,0},{7,1},{8,14},{9,15},{10,... | collective-permute-start | bytes 2359304 | tf_op jit(solution)/shard_map/ppermute | solution.py:356
  52.2 4.8 %convolution_convert_fusion.refs_5_ = bf16[1024,768]{1,0:T(8,128)(2,1)S(1)} fusion(bf16[1024,768]{1,0:T(8,128)(2,1)} %bitcast.6, s32[]{:T(128)S(6)} %select_n.50, bf16[1024,1024]{1,0:T(8,128)(2,1)} %bitcast.23), kind=kOutput, calls=%fused_computation.3 | convolution fusion | flops 1615593472 | bytes 5242884 | tf_op jit(solution)/shard_map/dot_general | solution.py:399
  59.4 4.4 %collective-permute-start.5 = (bf16[512,768]{1,0:T(8,128)(2,1)}, bf16[512,768]{1,0:T(8,128)(2,1)S(1)}, u32[]{:S(2)}, u32[]{:S(2)}) collective-permute-start(bf16[512,768]{1,0:T(8,128)(2,1)} %slice.82), channel_id=1, source_target_pairs={{0,6},{1,7},{2,4},{3,5},{4,2},{5,3},{6,0},{7,1},{8,14},{9,15},{10,... | collective-permute-start | bytes 2359304 | tf_op jit(solution)/shard_map/ppermute | solution.py:356
  66.0 3.6 %collective-permute-done.1.refs_1_ = bf16[16,32,1536]{2,1,0:T(8,128)(2,1)S(1)} collective-permute-done((bf16[16,32,1536]{2,1,0:T(8,128)(2,1)}, bf16[16,32,1536]{2,1,0:T(8,128)(2,1)S(1)}, u32[]{:S(2)}, u32[]{:S(2)}) %collective-permute-start.1) | collective-permute-done | bytes 1572896 | tf_op jit(solution)/shard_map/ppermute | solution.py:356
  72.0 32.8 %collective-permute-done.3.refs_3_ = bf16[16,32,1536]{2,1,0:T(8,128)(2,1)} collective-permute-done((bf16[16,32,1536]{2,1,0:T(8,128)(2,1)}, bf16[16,32,1536]{2,1,0:T(8,128)(2,1)}, u32[]{:S(2)}, u32[]{:S(2)}) %collective-permute-start.3) | collective-permute-done | bytes 1572896 | tf_op jit(solution)/shard_map/ppermute | solution.py:356
  107.7 6.4 %shard_map.87 = (bf16[16,32,1024]{2,1,0:T(8,128)(2,1)S(1)}, bf16[16,32,1024]{2,1,0:T(8,128)(2,1)}) custom-call(bf16[16,32,1536]{2,1,0:T(8,128)(2,1)S(1)} %copy-done, bf16[16,32,1536]{2,1,0:T(8,128)(2,1)S(1)} %collective-permute-done.1.refs_1_, bf16[16,32,1536]{2,1,0:T(8,128)(2,1)} %collective-permute-done.2.refs_2_, ...), custom_call_target="tpu_custom_call" | custom-call | flops 3221225472 | bytes 3145728 | tf_op jit(solution)/shard_map/pallas_call | solution.py:125
  117.9 47.9 %collective-permute-start.11 = (bf16[128,768]{1,0:T(8,128)(2,1)}, bf16[128,768]{1,0:T(8,128)(2,1)}, u32[]{:S(2)}, u32[]{:S(2)}) collective-permute-start(bf16[128,768]{1,0:T(8,128)(2,1)} %get-tuple-element.75), channel_id=1, source_target_pairs={{0,6},{1,7},{2,4},{3,5},{4,2},{5,3},{6,0},{7,1},{8,14},{9,15},{10,... | collective-permute-start | bytes 589832 | tf_op jit(solution)/shard_map/ppermute | solution.py:356
  167.5 3.8 %collective-permute-start.9 = (bf16[256,768]{1,0:T(8,128)(2,1)}, bf16[256,768]{1,0:T(8,128)(2,1)}, u32[]{:S(2)}, u32[]{:S(2)}) collective-permute-start(bf16[256,768]{1,0:T(8,128)(2,1)} %slice.86), channel_id=1, source_target_pairs={{0,6},{1,7},{2,4},{3,5},{4,2},{5,3},{6,0},{7,1},{8,14},{9,15},{10,... | collective-permute-start | bytes 1179656 | tf_op jit(solution)/shard_map/ppermute | solution.py:356
  171.3 4.3 %shard_map.86 = (bf16[16,32,512]{2,1,0:T(8,128)(2,1)S(1)}, bf16[16,32,512]{2,1,0:T(8,128)(2,1)}) custom-call(bf16[16,32,1536]{2,1,0:T(8,128)(2,1)S(1)} %copy-done, bf16[16,32,1536]{2,1,0:T(8,128)(2,1)S(1)} %collective-permute-done.1.refs_1_, bf16[16,32,1536]{2,1,0:T(8,128)(2,1)} %collective-permute-done.2.refs_2_, ...), custom_call_target="tpu_custom_call" | custom-call | flops 1610612736 | bytes 3145728 | tf_op jit(solution)/shard_map/pallas_call | solution.py:125
  181.0 4.9 %collective-permute-done.7.refs_3_ = bf16[16,32,512]{2,1,0:T(8,128)(2,1)} collective-permute-done((bf16[16,32,512]{2,1,0:T(8,128)(2,1)}, bf16[16,32,512]{2,1,0:T(8,128)(2,1)}, u32[]{:S(2)}, u32[]{:S(2)}) %collective-permute-start.7) | collective-permute-done | bytes 524320 | tf_op jit(solution)/shard_map/ppermute | solution.py:356
  186.7 3.8 %collective-permute-start.16 = (bf16[128,768]{1,0:T(8,128)(2,1)}, bf16[128,768]{1,0:T(8,128)(2,1)S(1)}, u32[]{:S(2)}, u32[]{:S(2)}) collective-permute-start(bf16[128,768]{1,0:T(8,128)(2,1)} %get-tuple-element.74), channel_id=1, source_target_pairs={{0,6},{1,7},{2,4},{3,5},{4,2},{5,3},{6,0},{7,1},{8,14},{9,15},{10,... | collective-permute-start | bytes 589832 | tf_op jit(solution)/shard_map/ppermute | solution.py:356
  192.7 3.4 %shard_map.88 = (bf16[16,32,512]{2,1,0:T(8,128)(2,1)S(1)}, f32[2,16,32,32]{3,2,1,0:T(8,128)S(1)}) custom-call(s32[2,32]{1,0:T(2,128)S(1)} %add_select_fusion.1.rows, s32[2,32]{1,0:T(2,128)S(1)} %reshape.82.offsets, f32[8,128]{1,0:T(8,128)S(1)} %broadcast_in_dim.75.before, bf16[16,32,1024]{2,1,0:T(8,128)(2,1)S(1)} %copy-done.2, ...), custom_call_target="tpu_custom_call" | custom-call | tf_op jit(solution)/shard_map/pallas_call | solution.py:201
  196.3 2.6 %shard_map.89 = (bf16[16,32,256]{2,1,0:T(8,128)(2,1)S(1)}, bf16[16,32,256]{2,1,0:T(8,128)(2,1)S(1)}) custom-call(bf16[16,32,1536]{2,1,0:T(8,128)(2,1)S(1)} %copy-done, bf16[16,32,1536]{2,1,0:T(8,128)(2,1)S(1)} %collective-permute-done.1.refs_1_, bf16[16,32,1536]{2,1,0:T(8,128)(2,1)} %collective-permute-done.2.refs_2_, ...), custom_call_target="tpu_custom_call" | custom-call | flops 805306368 | bytes 3145728 | tf_op jit(solution)/shard_map/pallas_call | solution.py:125
  200.1 2.0 collective-permute-start.14
  202.2 2.5 %shard_map.90 = (bf16[8,32,128]{2,1,0:T(8,128)(2,1)S(1)}, bf16[8,32,128]{2,1,0:T(8,128)(2,1)S(1)}, bf16[8,32,128]{2,1,0:T(8,128)(2,1)S(1)}, bf16[8,32,128]{2,1,0:T(8,128)(2,1)S(1)}) custom-call(bf16[16,32,1536]{2,1,0:T(8,128)(2,1)S(1)} %copy-done, bf16[16,32,1536]{2,1,0:T(8,128)(2,1)S(1)} %collective-permute-done.1.refs_1_, ...), custom_call_target="tpu_custom_call" | custom-call | flops 402653184 | bytes 3145728 | tf_op jit(solution)/shard_map/pallas_call | solution.py:125
  205.4 2.8 %shard_map.91 = (bf16[16,32,256]{2,1,0:T(8,128)(2,1)S(1)}, f32[2,16,32,32]{3,2,1,0:T(8,128)S(1)}) custom-call(s32[2,32]{1,0:T(2,128)S(1)} %add_select_fusion.1.rows, s32[2,32]{1,0:T(2,128)S(1)} %reshape.82.offsets, f32[2,16,32,32]{3,2,1,0:T(8,128)S(1)} %get-tuple-element.52.refs_6_.before, bf16[16,32,1024]{2,1,0:T(8,128)(2,1)S(1)} %copy-done.3, ...), custom_call_target="tpu_custom_call" | custom-call | tf_op jit(solution)/shard_map/pallas_call | solution.py:201
  209.4 2.3 collective-permute-start.21
  211.9 2.4 %shard_map.92 = (bf16[8,32,128]{2,1,0:T(8,128)(2,1)S(1)}, bf16[8,32,128]{2,1,0:T(8,128)(2,1)S(1)}, bf16[8,32,128]{2,1,0:T(8,128)(2,1)S(1)}, bf16[8,32,128]{2,1,0:T(8,128)(2,1)S(1)}) custom-call(bf16[16,32,1536]{2,1,0:T(8,128)(2,1)S(1)} %copy-done, bf16[16,32,1536]{2,1,0:T(8,128)(2,1)S(1)} %collective-permute-done.1.refs_1_, ...), custom_call_target="tpu_custom_call" | custom-call | flops 402653184 | bytes 3145728 | tf_op jit(solution)/shard_map/pallas_call | solution.py:125
  214.3 7.0 %collective-permute-done.19.refs_3_ = bf16[8,32,256]{2,1,0:T(8,128)(2,1)S(1)} collective-permute-done((bf16[8,32,256]{2,1,0:T(8,128)(2,1)S(1)}, bf16[8,32,256]{2,1,0:T(8,128)(2,1)S(1)}, u32[]{:S(2)}, u32[]{:S(2)}) %collective-permute-start.19) | collective-permute-done | bytes 131104 | tf_op jit(solution)/shard_map/ppermute | solution.py:356
  222.8 1.9 collective-permute-start.24
  224.7 2.3 collective-permute-done.15.refs_7_
  228.3 2.5 %shard_map.93.before = f32[16,32,32]{2,1,0:T(8,128)S(1)} custom-call(s32[2,32]{1,0:T(2,128)S(1)} %get-tuple-element.70.rows, s32[2,32]{1,0:T(2,128)S(1)} %reshape.82.offsets, bf16[16,32,1024]{2,1,0:T(8,128)(2,1)S(1)} %copy-done.3, bf16[16,32,1024]{2,1,0:T(8,128)(2,1)} %collective-permute-done.6.refs_1_, bf16[16,32,512]{2,1,0:T(8,128)(2,1)S(1)} %copy-done.6, ...), custom_call_target="tpu_custom_call" | custom-call | tf_op jit(solution)/shard_map/pallas_call | solution.py:318
  232.2 2.1 collective-permute-done.13.there
  234.3 2.3 finish.1
  (108 shorter events, 41.6 us)
Async XLA Ops:
  3.3 24.4 %all-to-all-start = ((bf16[4,1,256,768]{3,2,1,0:T(8,128)(2,1)}), bf16[4,1,256,768]{3,2,1,0:T(8,128)(2,1)S(1)}, u32[]{:S(2)}, u32[]{:S(2)}) async-start(bf16[4,1,256,768]{3,2,1,0:T(8,128)(2,1)} %slice.61), calls=%async_computation | async-start | bytes 3145728 | tf_op jit(solution)/shard_map/all_to_all | solution.py:363
  16.9 23.0 %copy-start.13 = (f32[16,2,32]{2,1,0:T(2,128)S(1)}, f32[16,2,32]{2,1,0:T(2,128)}, u32[]{:S(2)}) copy-start(f32[16,2,32]{2,1,0:T(2,128)} %param.11) | copy-start | bytes 12292
  27.7 24.5 %all-to-all-start.1 = ((bf16[4,1,256,768]{3,2,1,0:T(8,128)(2,1)}), bf16[4,1,256,768]{3,2,1,0:T(8,128)(2,1)}, u32[]{:S(2)}, u32[]{:S(2)}) async-start(bf16[4,1,256,768]{3,2,1,0:T(8,128)(2,1)} %slice.63), calls=%async_computation.1 | async-start | bytes 3145728 | tf_op jit(solution)/shard_map/all_to_all | solution.py:363
  32.1 37.5 %collective-permute-start.1 = (bf16[16,32,1536]{2,1,0:T(8,128)(2,1)}, bf16[16,32,1536]{2,1,0:T(8,128)(2,1)S(1)}, u32[]{:S(2)}, u32[]{:S(2)}) collective-permute-start(bf16[16,32,1536]{2,1,0:T(8,128)(2,1)} %get-tuple-element.40), channel_id=1, source_target_pairs={{0,1},{1,0},{2,3},{3,2},{4,5},{5,4},{6,7},{7,6},{8,9},{9,8},{10,11... | collective-permute-start | bytes 4718600 | tf_op jit(solution)/shard_map/ppermute | solution.py:356
  34.4 37.6 %collective-permute-start.2 = (bf16[16,32,1536]{2,1,0:T(8,128)(2,1)}, bf16[16,32,1536]{2,1,0:T(8,128)(2,1)}, u32[]{:S(2)}, u32[]{:S(2)}) collective-permute-start(bf16[16,32,1536]{2,1,0:T(8,128)(2,1)} %get-tuple-element.41), channel_id=1, source_target_pairs={{0,2},{1,3},{2,0},{3,1},{4,6},{5,7},{6,4},{7,5},{8,10},{9,11},{10,... | collective-permute-start | bytes 4718600 | tf_op jit(solution)/shard_map/ppermute | solution.py:356
  36.0 68.8 %collective-permute-start.3 = (bf16[16,32,1536]{2,1,0:T(8,128)(2,1)}, bf16[16,32,1536]{2,1,0:T(8,128)(2,1)}, u32[]{:S(2)}, u32[]{:S(2)}) collective-permute-start(bf16[16,32,1536]{2,1,0:T(8,128)(2,1)} %get-tuple-element.42), channel_id=1, source_target_pairs={{0,3},{1,2},{2,1},{3,0},{4,7},{5,6},{6,5},{7,4},{8,11},{9,10},{10,... | collective-permute-start | bytes 4718600 | tf_op jit(solution)/shard_map/ppermute | solution.py:356
  38.7 138.2 %copy-start.14 = (s32[1,32]{1,0:T(1,128)}, s32[1,32]{1,0:T(1,128)S(1)}, u32[]{:S(2)}) copy-start(s32[1,32]{1,0:T(1,128)S(1)} %stack_reshape.3) | copy-start | bytes 388
  46.4 121.1 %collective-permute-start.4 = (bf16[512,768]{1,0:T(8,128)(2,1)}, bf16[512,768]{1,0:T(8,128)(2,1)}, u32[]{:S(2)}, u32[]{:S(2)}) collective-permute-start(bf16[512,768]{1,0:T(8,128)(2,1)} %slice.81), channel_id=1, source_target_pairs={{0,6},{1,7},{2,4},{3,5},{4,2},{5,3},{6,0},{7,1},{8,14},{9,15},{10,... | collective-permute-start | bytes 2359304 | tf_op jit(solution)/shard_map/ppermute | solution.py:356
  57.0 47.9 %copy-start = (bf16[16,32,1536]{2,1,0:T(8,128)(2,1)S(1)}, bf16[16,32,1536]{2,1,0:T(8,128)(2,1)}, u32[]{:S(2)}) copy-start(bf16[16,32,1536]{2,1,0:T(8,128)(2,1)} %get-tuple-element.39.refs_0_) | copy-start | bytes 4718596
  59.4 108.1 %collective-permute-start.5 = (bf16[512,768]{1,0:T(8,128)(2,1)}, bf16[512,768]{1,0:T(8,128)(2,1)S(1)}, u32[]{:S(2)}, u32[]{:S(2)}) collective-permute-start(bf16[512,768]{1,0:T(8,128)(2,1)} %slice.82), channel_id=1, source_target_pairs={{0,6},{1,7},{2,4},{3,5},{4,2},{5,3},{6,0},{7,1},{8,14},{9,15},{10,... | collective-permute-start | bytes 2359304 | tf_op jit(solution)/shard_map/ppermute | solution.py:356
  69.6 106.8 %collective-permute-start = (s32[32]{0:T(128)}, s32[32]{0:T(128)S(1)}, u32[]{:S(2)}, u32[]{:S(2)}) collective-permute-start(s32[32]{0:T(128)} %reshape.80.orbs), channel_id=1, source_target_pairs={{0,2},{1,3},{2,0},{3,1},{4,6},{5,7},{6,4},{7,5},{8,10},{9,11},{10,... | collective-permute-start | bytes 392 | tf_op jit(solution)/shard_map/ppermute | solution.py:356
  114.1 61.5 %copy-start.1 = (bf16[16,32,1024]{2,1,0:T(8,128)(2,1)}, bf16[16,32,1024]{2,1,0:T(8,128)(2,1)S(1)}, u32[]{:S(2)}) copy-start(bf16[16,32,1024]{2,1,0:T(8,128)(2,1)S(1)} %get-tuple-element.48.refs_0_) | copy-start | bytes 3145732
  114.1 72.6 %collective-permute-start.6 = (bf16[16,32,1024]{2,1,0:T(8,128)(2,1)}, bf16[16,32,1024]{2,1,0:T(8,128)(2,1)}, u32[]{:S(2)}, u32[]{:S(2)}) collective-permute-start(bf16[16,32,1024]{2,1,0:T(8,128)(2,1)} %get-tuple-element.49), channel_id=1, source_target_pairs={{0,1},{1,0},{2,3},{3,2},{4,5},{5,4},{6,7},{7,6},{8,9},{9,8},{10,11... | collective-permute-start | bytes 3145736 | tf_op jit(solution)/shard_map/ppermute | solution.py:356
  117.9 82.2 %collective-permute-start.11 = (bf16[128,768]{1,0:T(8,128)(2,1)}, bf16[128,768]{1,0:T(8,128)(2,1)}, u32[]{:S(2)}, u32[]{:S(2)}) collective-permute-start(bf16[128,768]{1,0:T(8,128)(2,1)} %get-tuple-element.75), channel_id=1, source_target_pairs={{0,6},{1,7},{2,4},{3,5},{4,2},{5,3},{6,0},{7,1},{8,14},{9,15},{10,... | collective-permute-start | bytes 589832 | tf_op jit(solution)/shard_map/ppermute | solution.py:356
  167.5 28.6 %collective-permute-start.8 = (bf16[256,768]{1,0:T(8,128)(2,1)}, bf16[256,768]{1,0:T(8,128)(2,1)}, u32[]{:S(2)}, u32[]{:S(2)}) collective-permute-start(bf16[256,768]{1,0:T(8,128)(2,1)} %slice.85), channel_id=1, source_target_pairs={{0,6},{1,7},{2,4},{3,5},{4,2},{5,3},{6,0},{7,1},{8,14},{9,15},{10,... | collective-permute-start | bytes 1179656 | tf_op jit(solution)/shard_map/ppermute | solution.py:356
  167.5 28.8 %collective-permute-start.9 = (bf16[256,768]{1,0:T(8,128)(2,1)}, bf16[256,768]{1,0:T(8,128)(2,1)}, u32[]{:S(2)}, u32[]{:S(2)}) collective-permute-start(bf16[256,768]{1,0:T(8,128)(2,1)} %slice.86), channel_id=1, source_target_pairs={{0,6},{1,7},{2,4},{3,5},{4,2},{5,3},{6,0},{7,1},{8,14},{9,15},{10,... | collective-permute-start | bytes 1179656 | tf_op jit(solution)/shard_map/ppermute | solution.py:356
  176.4 9.5 %collective-permute-start.7 = (bf16[16,32,512]{2,1,0:T(8,128)(2,1)}, bf16[16,32,512]{2,1,0:T(8,128)(2,1)}, u32[]{:S(2)}, u32[]{:S(2)}) collective-permute-start(bf16[16,32,512]{2,1,0:T(8,128)(2,1)} %get-tuple-element.51), channel_id=1, source_target_pairs={{0,1},{1,0},{2,3},{3,2},{4,5},{5,4},{6,7},{7,6},{8,9},{9,8},{10,11... | collective-permute-start | bytes 1572872 | tf_op jit(solution)/shard_map/ppermute | solution.py:356
  185.9 14.3 %collective-permute-start.12 = (bf16[128,768]{1,0:T(8,128)(2,1)}, bf16[128,768]{1,0:T(8,128)(2,1)S(1)}, u32[]{:S(2)}, u32[]{:S(2)}) collective-permute-start(bf16[128,768]{1,0:T(8,128)(2,1)} %get-tuple-element.73), channel_id=1, source_target_pairs={{0,6},{1,7},{2,4},{3,5},{4,2},{5,3},{6,0},{7,1},{8,14},{9,15},{10,... | collective-permute-start | bytes 589832 | tf_op jit(solution)/shard_map/ppermute | solution.py:356
  186.7 21.5 %collective-permute-start.16 = (bf16[128,768]{1,0:T(8,128)(2,1)}, bf16[128,768]{1,0:T(8,128)(2,1)S(1)}, u32[]{:S(2)}, u32[]{:S(2)}) collective-permute-start(bf16[128,768]{1,0:T(8,128)(2,1)} %get-tuple-element.74), channel_id=1, source_target_pairs={{0,6},{1,7},{2,4},{3,5},{4,2},{5,3},{6,0},{7,1},{8,14},{9,15},{10,... | collective-permute-start | bytes 589832 | tf_op jit(solution)/shard_map/ppermute | solution.py:356
  196.1 13.3 %collective-permute-start.17 = (bf16[128,768]{1,0:T(8,128)(2,1)S(1)}, bf16[128,768]{1,0:T(8,128)(2,1)S(1)}, u32[]{:S(2)}, u32[]{:S(2)}) collective-permute-start(bf16[128,768]{1,0:T(8,128)(2,1)S(1)} %copy-done.11), channel_id=1, source_target_pairs={{0,6},{1,7},{2,4},{3,5},{4,2},{5,3},{6,0},{7,1},{8,14},{9,15},{10,... | collective-permute-start | bytes 589832 | tf_op jit(solution)/shard_map/ppermute | solution.py:356
  198.9 6.4 %collective-permute-start.10 = (bf16[16,32,256]{2,1,0:T(8,128)(2,1)S(1)}, bf16[16,32,256]{2,1,0:T(8,128)(2,1)S(1)}, u32[]{:S(2)}, u32[]{:S(2)}) collective-permute-start(bf16[16,32,256]{2,1,0:T(8,128)(2,1)S(1)} %get-tuple-element.54), channel_id=1, source_target_pairs={{0,1},{1,0},{2,3},{3,2},{4,5},{5,4},{6,7},{7,6},{8,9},{9,8},{10,11... | collective-permute-start | bytes 786440 | tf_op jit(solution)/shard_map/ppermute | solution.py:356
  200.1 11.6 %collective-permute-start.18 = (bf16[8,32,256]{2,1,0:T(8,128)(2,1)S(1)}, bf16[8,32,256]{2,1,0:T(8,128)(2,1)S(1)}, u32[]{:S(2)}, u32[]{:S(2)}) collective-permute-start(bf16[8,32,256]{2,1,0:T(8,128)(2,1)S(1)} %copy-done.12), channel_id=1, source_target_pairs={{0,2},{1,3},{2,0},{3,1},{4,6},{5,7},{6,4},{7,5},{8,10},{9,11},{10,... | collective-permute-start | bytes 393224 | tf_op jit(solution)/shard_map/ppermute | solution.py:356
  200.1 27.8 %collective-permute-start.14 = (bf16[16,32,512]{2,1,0:T(8,128)(2,1)S(1)}, bf16[16,32,512]{2,1,0:T(8,128)(2,1)S(1)}, u32[]{:S(2)}, u32[]{:S(2)}) collective-permute-start(bf16[16,32,512]{2,1,0:T(8,128)(2,1)S(1)} %get-tuple-element.57), channel_id=1, source_target_pairs={{0,2},{1,3},{2,0},{3,1},{4,6},{5,7},{6,4},{7,5},{8,10},{9,11},{10,... | collective-permute-start | bytes 1572872 | tf_op jit(solution)/shard_map/ppermute | solution.py:356
  205.3 15.9 %collective-permute-start.19 = (bf16[8,32,256]{2,1,0:T(8,128)(2,1)S(1)}, bf16[8,32,256]{2,1,0:T(8,128)(2,1)S(1)}, u32[]{:S(2)}, u32[]{:S(2)}) collective-permute-start(bf16[8,32,256]{2,1,0:T(8,128)(2,1)S(1)} %slice.80), channel_id=1, source_target_pairs={{0,3},{1,2},{2,1},{3,0},{4,7},{5,6},{6,5},{7,4},{8,11},{9,10},{10,... | collective-permute-start | bytes 393224 | tf_op jit(solution)/shard_map/ppermute | solution.py:356
  208.2 13.2 %collective-permute-start.20 = (bf16[8,32,128]{2,1,0:T(8,128)(2,1)S(1)}, bf16[8,32,128]{2,1,0:T(8,128)(2,1)S(1)}, u32[]{:S(2)}, u32[]{:S(2)}) collective-permute-start(bf16[8,32,128]{2,1,0:T(8,128)(2,1)S(1)} %get-tuple-element.60), channel_id=1, source_target_pairs={{0,1},{1,0},{2,3},{3,2},{4,5},{5,4},{6,7},{7,6},{8,9},{9,8},{10,11... | collective-permute-start | bytes 196616 | tf_op jit(solution)/shard_map/ppermute | solution.py:356
  209.4 13.4 %collective-permute-start.21 = (bf16[8,32,128]{2,1,0:T(8,128)(2,1)S(1)}, bf16[8,32,128]{2,1,0:T(8,128)(2,1)S(1)}, u32[]{:S(2)}, u32[]{:S(2)}) collective-permute-start(bf16[8,32,128]{2,1,0:T(8,128)(2,1)S(1)} %get-tuple-element.61), channel_id=1, source_target_pairs={{0,2},{1,3},{2,0},{3,1},{4,6},{5,7},{6,4},{7,5},{8,10},{9,11},{10,... | collective-permute-start | bytes 196616 | tf_op jit(solution)/shard_map/ppermute | solution.py:356
  211.8 15.2 %collective-permute-start.15 = (bf16[16,32,256]{2,1,0:T(8,128)(2,1)S(1)}, bf16[16,32,256]{2,1,0:T(8,128)(2,1)S(1)}, u32[]{:S(2)}, u32[]{:S(2)}) collective-permute-start(bf16[16,32,256]{2,1,0:T(8,128)(2,1)S(1)} %get-tuple-element.58), channel_id=1, source_target_pairs={{0,2},{1,3},{2,0},{3,1},{4,6},{5,7},{6,4},{7,5},{8,10},{9,11},{10,... | collective-permute-start | bytes 786440 | tf_op jit(solution)/shard_map/ppermute | solution.py:356
  221.2 9.6 %collective-permute-start.22 = (bf16[8,32,128]{2,1,0:T(8,128)(2,1)S(1)}, bf16[8,32,128]{2,1,0:T(8,128)(2,1)S(1)}, u32[]{:S(2)}, u32[]{:S(2)}) collective-permute-start(bf16[8,32,128]{2,1,0:T(8,128)(2,1)S(1)} %get-tuple-element.62), channel_id=1, source_target_pairs={{0,3},{1,2},{2,1},{3,0},{4,7},{5,6},{6,5},{7,4},{8,11},{9,10},{10,... | collective-permute-start | bytes 196616 | tf_op jit(solution)/shard_map/ppermute | solution.py:356
  221.4 9.4 %collective-permute-start.23 = (bf16[8,32,128]{2,1,0:T(8,128)(2,1)S(1)}, bf16[8,32,128]{2,1,0:T(8,128)(2,1)S(1)}, u32[]{:S(2)}, u32[]{:S(2)}) collective-permute-start(bf16[8,32,128]{2,1,0:T(8,128)(2,1)S(1)} %get-tuple-element.63), channel_id=1, source_target_pairs={{0,1},{1,0},{2,3},{3,2},{4,5},{5,4},{6,7},{7,6},{8,9},{9,8},{10,11... | collective-permute-start | bytes 196616 | tf_op jit(solution)/shard_map/ppermute | solution.py:356
  222.8 8.0 %collective-permute-start.24 = (bf16[8,32,128]{2,1,0:T(8,128)(2,1)S(1)}, bf16[8,32,128]{2,1,0:T(8,128)(2,1)S(1)}, u32[]{:S(2)}, u32[]{:S(2)}) collective-permute-start(bf16[8,32,128]{2,1,0:T(8,128)(2,1)S(1)} %get-tuple-element.64), channel_id=1, source_target_pairs={{0,2},{1,3},{2,0},{3,1},{4,6},{5,7},{6,4},{7,5},{8,10},{9,11},{10,... | collective-permute-start | bytes 196616 | tf_op jit(solution)/shard_map/ppermute | solution.py:356
  227.0 5.2 %collective-permute-start.25 = (bf16[8,32,128]{2,1,0:T(8,128)(2,1)S(1)}, bf16[8,32,128]{2,1,0:T(8,128)(2,1)S(1)}, u32[]{:S(2)}, u32[]{:S(2)}) collective-permute-start(bf16[8,32,128]{2,1,0:T(8,128)(2,1)S(1)} %get-tuple-element.65), channel_id=1, source_target_pairs={{0,3},{1,2},{2,1},{3,0},{4,7},{5,6},{6,5},{7,4},{8,11},{9,10},{10,... | collective-permute-start | bytes 196616 | tf_op jit(solution)/shard_map/ppermute | solution.py:356
  227.9 6.4 %collective-permute-start.13 = (f32[16,32,32]{2,1,0:T(8,128)S(1)}, f32[16,32,32]{2,1,0:T(8,128)S(1)}, u32[]{:S(2)}, u32[]{:S(2)}) collective-permute-start(f32[16,32,32]{2,1,0:T(8,128)S(1)} %slice_bitcast_fusion), channel_id=1, source_target_pairs={{0,2},{1,3},{2,0},{3,1},{4,6},{5,7},{6,4},{7,5},{8,10},{9,11},{10,... | collective-permute-start | bytes 196616 | tf_op jit(solution)/shard_map/ppermute | solution.py:356
  (14 other events, 65.6 us)

commit v9 on v8

--- a/solution.py
+++ b/solution.py
@@ -336,7 +336,7 @@
 
 
 def chunk_spans(fit_rows):
-    sizes = (fit_rows // 2, fit_rows // 4, fit_rows // 8, fit_rows // 8)
+    sizes = (fit_rows // 2, fit_rows // 8, fit_rows // 4, fit_rows // 8)
     return [(sum(sizes[:c]), size) for c, size in enumerate(sizes)]
 
 
@@ -378,6 +378,8 @@
     blocks = [packed[0]]
     for m in range(1, group):
         blocks.append(across(packed[m], m))
+    pairs = [(i, i ^ inner) for i in range(orb_count) if i // inner in (0, 3)]
+    guard = lax.ppermute(packed[0][:2], "orb", pairs)
     own_offset = fit_offset[region * orb_count + me]
     turned = jnp.roll(fit_inverse[0], own_offset, axis=0)
     mate_orbs = across(own_orbs, inner)
@@ -423,7 +425,7 @@
         sent, here = relay(rows, offsets, before, near, far[c], spans[c], margin, tokens)
         return across(sent, inner), here
 
-    near = project(blocks, 0, fitted, [denominator], False)
+    near = project(blocks, 0, fitted, [denominator, guard], False)
     last = spans[2][0]
     straight = [across(near[i][capacity:, :, last:], i + inner) for i in range(inner)]
     near = hop(near)

time: 239 us -> 249 us (1.042)
  waiting for transfers between devices: 67.9 us -> 97.3 us
  starting transfers between devices: 92.3 us -> 77 us
  other arithmetic: 6.21 us -> 1.97 us
    ppermute x26, waiting for transfers between devices: 55.3 us -> 84.4 us  [across(): return lax.ppermute(array, 'orb', [(i, i ^ mask) for i in range(orb_count)])]
    ppermute x26, starting transfers between devices: 83.6 us -> 63.8 us  [across(): return lax.ppermute(array, 'orb', [(i, i ^ mask) for i in range(orb_count)])]
    ppermute x0 -> x1, starting transfers between devices: none -> 4.29 us  [on_device(): guard = lax.ppermute(packed[0][:2], 'orb', pairs)]
    unnamed x37 -> x45, local copies, waits for them, and re-layouts: 8.34 us -> 9.96 us
  transfers between devices with their start and end apart: 28 -> 29, of which waited for: 11 -> 13; matrix products, arithmetic and copies ran while one was open for 12% -> 9% of each run, Pallas kernels for 14% -> 13%
where the time goes in v9:
time: 249 us
  waiting for transfers between devices  97.3 us (39%)
  starting transfers between devices  77 us (31%)
  Pallas kernels  34.4 us (14%)
  local copies, waits for them, and re-layouts  25.5 us (10%)
  matrix products  9.53 us (4%)
  between operations  2.88 us (1%)
    ppermute x26, waiting for transfers between devices, across(): return lax.ppermute(array, 'orb', [(i, i ^ mask) for i in range(orb_count)])  84.4 us
    ppermute x26, starting transfers between devices, across(): return lax.ppermute(array, 'orb', [(i, i ^ mask) for i in range(orb_count)])  63.8 us
    pallas_call x5, Pallas kernels, project(): pl.pallas_call(kernel, grid=(1,), out_shape=(jax.ShapeDtypeStruct((lines,...  18.1 us
    all_to_all x2, waiting for transfers between devices, exchange(): lax.all_to_all(array[:, :, :, k * half:(k + 1) * half], 'aux', split_axis...  13 us
    unnamed x45, local copies, waits for them, and re-layouts  9.96 us
    dot_general x2, matrix products, on_device(): product = jnp.dot(turned, raw_parts[k], preferred_element_type=jnp.float32)  9.53 us
    all_to_all x2, starting transfers between devices, exchange(): lax.all_to_all(array[:, :, :, k * half:(k + 1) * half], 'aux', split_axis...  8.85 us
    pallas_call x2, Pallas kernels, relay(): pl.pallas_call(functools.partial(relay_kernel, inner, (span,), margin), o...  6.24 us
  transfers between devices with their start and end apart: 29, of which 13 were waited for; matrix products, arithmetic and copies ran while one was open for 9% of the time, Pallas kernels for 13%

profile of v9, /device:TPU:0, one launch (start us, length us, event | category | flops | bytes accessed | tf_op | source)
XLA Modules:
  0.0 248.7 jit_solution(18002631701823389876)
XLA Ops:
  0.6 2.7 %slice.64 = bf16[4,1,256,768]{3,2,1,0:T(8,128)(2,1)} slice(bf16[4,1,256,1536]{3,2,1,0:T(8,128)(2,1)} %param.7), slice={[0:4], [0:1], [0:256], [0:768]} | slice | bytes 3145728 | tf_op jit(solution)/shard_map/slice | solution.py:364
  3.3 4.5 %all-to-all-start = ((bf16[4,1,256,768]{3,2,1,0:T(8,128)(2,1)}), bf16[4,1,256,768]{3,2,1,0:T(8,128)(2,1)}, u32[]{:S(2)}, u32[]{:S(2)}) async-start(bf16[4,1,256,768]{3,2,1,0:T(8,128)(2,1)} %slice.64), calls=%async_computation | async-start | bytes 3145728 | tf_op jit(solution)/shard_map/all_to_all | solution.py:363
  9.1 5.2 %pack.1 = (bf16[16,32,1536]{2,1,0:T(8,128)(2,1)}, bf16[16,32,1536]{2,1,0:T(8,128)(2,1)}, bf16[16,32,1536]{2,1,0:T(8,128)(2,1)}, bf16[16,32,1536]{2,1,0:T(8,128)(2,1)}) custom-call(s32[32]{0:T(128)} %reshape.80.orbs, s32[2]{0:T(128)} %pad_add_fusion.1.place, bf16[32,32,1536]{2,1,0:T(8,128)(2,1)} %bitcast.16), custom_call_target="tpu_custom_call" | custom-call | bytes 9437184 | tf_op jit(solution)/shard_map/pack/pallas_call | solution.py:59
  15.6 13.0 %all-to-all-done = bf16[4,1,256,768]{3,2,1,0:T(8,128)(2,1)} async-done(((bf16[4,1,256,768]{3,2,1,0:T(8,128)(2,1)}), bf16[4,1,256,768]{3,2,1,0:T(8,128)(2,1)}, u32[]{:S(2)}, u32[]{:S(2)}) %all-to-all-start) | async-done | bytes 1572896 | tf_op jit(solution)/shard_map/all_to_all | solution.py:363
  28.6 4.3 %all-to-all-start.1 = ((bf16[4,1,256,768]{3,2,1,0:T(8,128)(2,1)}), bf16[4,1,256,768]{3,2,1,0:T(8,128)(2,1)}, u32[]{:S(2)}, u32[]{:S(2)}) async-start(bf16[4,1,256,768]{3,2,1,0:T(8,128)(2,1)} %slice.66), calls=%async_computation.1 | async-start | bytes 3145728 | tf_op jit(solution)/shard_map/all_to_all | solution.py:363
  33.7 4.3 %collective-permute-start.6 = (bf16[2,32,1536]{2,1,0:T(8,128)(2,1)}, bf16[2,32,1536]{2,1,0:T(8,128)(2,1)S(1)}, u32[]{:S(2)}, u32[]{:S(2)}) collective-permute-start(bf16[2,32,1536]{2,1,0:T(8,128)(2,1)} %slice.75), channel_id=1, source_target_pairs={{0,2},{1,3},{6,4},{7,5},{8,10},{9,11},{14,12},{15,13},{16,18},{17,... | collective-permute-start | bytes 589832 | tf_op jit(solution)/shard_map/ppermute | solution.py:382
  39.6 2.0 collective-permute-start.3
  44.2 4.8 %convolution_convert_fusion.1.refs_4_ = bf16[1024,768]{1,0:T(8,128)(2,1)S(1)} fusion(bf16[1024,768]{1,0:T(8,128)(2,1)} %bitcast.5, s32[]{:T(128)S(6)} %select_n.50, bf16[1024,1024]{1,0:T(8,128)(2,1)} %bitcast.21), kind=kOutput, calls=%fused_computation.4 | convolution fusion | flops 1615593472 | bytes 5242884 | tf_op jit(solution)/shard_map/dot_general | solution.py:401
  51.1 2.5 collective-permute-start.4
  53.6 4.8 %convolution_convert_fusion.refs_5_ = bf16[1024,768]{1,0:T(8,128)(2,1)S(1)} fusion(bf16[1024,768]{1,0:T(8,128)(2,1)} %bitcast.6, s32[]{:T(128)S(6)} %select_n.50, bf16[1024,1024]{1,0:T(8,128)(2,1)} %bitcast.22), kind=kOutput, calls=%fused_computation.3 | convolution fusion | flops 1615593472 | bytes 5242884 | tf_op jit(solution)/shard_map/dot_general | solution.py:401
  61.6 3.9 %collective-permute-start.5 = (bf16[512,768]{1,0:T(8,128)(2,1)}, bf16[512,768]{1,0:T(8,128)(2,1)S(1)}, u32[]{:S(2)}, u32[]{:S(2)}) collective-permute-start(bf16[512,768]{1,0:T(8,128)(2,1)} %slice.86), channel_id=1, source_target_pairs={{0,6},{1,7},{2,4},{3,5},{4,2},{5,3},{6,0},{7,1},{8,14},{9,15},{10,... | collective-permute-start | bytes 2359304 | tf_op jit(solution)/shard_map/ppermute | solution.py:356
  67.5 7.2 %collective-permute-done.1.refs_1_ = bf16[16,32,1536]{2,1,0:T(8,128)(2,1)S(1)} collective-permute-done((bf16[16,32,1536]{2,1,0:T(8,128)(2,1)}, bf16[16,32,1536]{2,1,0:T(8,128)(2,1)S(1)}, u32[]{:S(2)}, u32[]{:S(2)}) %collective-permute-start.1) | collective-permute-done | bytes 1572896 | tf_op jit(solution)/shard_map/ppermute | solution.py:356
  74.7 2.5 %collective-permute-done.2.refs_2_ = bf16[16,32,1536]{2,1,0:T(8,128)(2,1)} collective-permute-done((bf16[16,32,1536]{2,1,0:T(8,128)(2,1)}, bf16[16,32,1536]{2,1,0:T(8,128)(2,1)}, u32[]{:S(2)}, u32[]{:S(2)}) %collective-permute-start.2) | collective-permute-done | bytes 1572896 | tf_op jit(solution)/shard_map/ppermute | solution.py:356
  77.3 33.7 %collective-permute-done.3.refs_3_ = bf16[16,32,1536]{2,1,0:T(8,128)(2,1)} collective-permute-done((bf16[16,32,1536]{2,1,0:T(8,128)(2,1)}, bf16[16,32,1536]{2,1,0:T(8,128)(2,1)}, u32[]{:S(2)}, u32[]{:S(2)}) %collective-permute-start.3) | collective-permute-done | bytes 1572896 | tf_op jit(solution)/shard_map/ppermute | solution.py:356
  114.7 6.4 %shard_map.87 = (bf16[16,32,1024]{2,1,0:T(8,128)(2,1)S(1)}, bf16[16,32,1024]{2,1,0:T(8,128)(2,1)}) custom-call(bf16[16,32,1536]{2,1,0:T(8,128)(2,1)S(1)} %copy-done, bf16[16,32,1536]{2,1,0:T(8,128)(2,1)S(1)} %collective-permute-done.1.refs_1_, bf16[16,32,1536]{2,1,0:T(8,128)(2,1)} %collective-permute-done.2.refs_2_, ...), custom_call_target="tpu_custom_call" | custom-call | flops 3221225472 | bytes 3145728 | tf_op jit(solution)/shard_map/pallas_call | solution.py:125
  125.0 2.5 collective-permute-start.9
  132.2 15.4 %collective-permute-done.5.refs_5_ = bf16[512,768]{1,0:T(8,128)(2,1)S(1)} collective-permute-done((bf16[512,768]{1,0:T(8,128)(2,1)}, bf16[512,768]{1,0:T(8,128)(2,1)S(1)}, u32[]{:S(2)}, u32[]{:S(2)}) %collective-permute-start.5) | collective-permute-done | bytes 786464 | tf_op jit(solution)/shard_map/ppermute | solution.py:356
  148.9 4.3 %shard_map.86 = (bf16[16,32,512]{2,1,0:T(8,128)(2,1)S(1)}, bf16[16,32,512]{2,1,0:T(8,128)(2,1)}) custom-call(bf16[16,32,1536]{2,1,0:T(8,128)(2,1)S(1)} %copy-done, bf16[16,32,1536]{2,1,0:T(8,128)(2,1)S(1)} %collective-permute-done.1.refs_1_, bf16[16,32,1536]{2,1,0:T(8,128)(2,1)} %collective-permute-done.2.refs_2_, ...), custom_call_target="tpu_custom_call" | custom-call | flops 1610612736 | bytes 3145728 | tf_op jit(solution)/shard_map/pallas_call | solution.py:125
  156.0 10.9 %collective-permute-done.8.refs_3_ = bf16[16,32,512]{2,1,0:T(8,128)(2,1)} collective-permute-done((bf16[16,32,512]{2,1,0:T(8,128)(2,1)}, bf16[16,32,512]{2,1,0:T(8,128)(2,1)}, u32[]{:S(2)}, u32[]{:S(2)}) %collective-permute-start.8) | collective-permute-done | bytes 524320 | tf_op jit(solution)/shard_map/ppermute | solution.py:356
  166.9 2.5 collective-permute-start.10
  173.1 3.4 %shard_map.88 = (bf16[16,32,512]{2,1,0:T(8,128)(2,1)S(1)}, f32[2,16,32,32]{3,2,1,0:T(8,128)S(1)}) custom-call(s32[2,32]{1,0:T(2,128)S(1)} %add_select_fusion.1.rows, s32[2,32]{1,0:T(2,128)S(1)} %reshape.82.offsets, f32[8,128]{1,0:T(8,128)S(1)} %broadcast_in_dim.75.before, bf16[16,32,1024]{2,1,0:T(8,128)(2,1)S(1)} %copy-done.2, ...), custom_call_target="tpu_custom_call" | custom-call | tf_op jit(solution)/shard_map/pallas_call | solution.py:201
  176.5 2.5 %collective-permute-start.18 = (bf16[128,768]{1,0:T(8,128)(2,1)S(1)}, bf16[128,768]{1,0:T(8,128)(2,1)S(1)}, u32[]{:S(2)}, u32[]{:S(2)}) collective-permute-start(bf16[128,768]{1,0:T(8,128)(2,1)S(1)} %copy-done.16), channel_id=1, source_target_pairs={{0,6},{1,7},{2,4},{3,5},{4,2},{5,3},{6,0},{7,1},{8,14},{9,15},{10,... | collective-permute-start | bytes 589832 | tf_op jit(solution)/shard_map/ppermute | solution.py:356
  179.0 27.6 %collective-permute-start.19 = (bf16[8,32,384]{2,1,0:T(8,128)(2,1)S(1)}, bf16[8,32,384]{2,1,0:T(8,128)(2,1)S(1)}, u32[]{:S(2)}, u32[]{:S(2)}) collective-permute-start(bf16[8,32,384]{2,1,0:T(8,128)(2,1)S(1)} %copy-done.15), channel_id=1, source_target_pairs={{0,2},{1,3},{2,0},{3,1},{4,6},{5,7},{6,4},{7,5},{8,10},{9,11},{10,... | collective-permute-start | bytes 589832 | tf_op jit(solution)/shard_map/ppermute | solution.py:356
  206.6 2.4 shard_map.89
  210.6 2.7 %shard_map.90 = (bf16[8,32,256]{2,1,0:T(8,128)(2,1)S(1)}, bf16[8,32,256]{2,1,0:T(8,128)(2,1)S(1)}, bf16[8,32,256]{2,1,0:T(8,128)(2,1)S(1)}, bf16[8,32,256]{2,1,0:T(8,128)(2,1)S(1)}) custom-call(bf16[16,32,1536]{2,1,0:T(8,128)(2,1)S(1)} %copy-done, bf16[16,32,1536]{2,1,0:T(8,128)(2,1)S(1)} %collective-permute-done.1.refs_1_, ...), custom_call_target="tpu_custom_call" | custom-call | flops 805306368 | bytes 3145728 | tf_op jit(solution)/shard_map/pallas_call | solution.py:125
  215.4 2.8 %shard_map.91 = (bf16[16,32,128]{2,1,0:T(8,128)(2,1)S(1)}, f32[2,16,32,32]{3,2,1,0:T(8,128)S(1)}) custom-call(s32[2,32]{1,0:T(2,128)S(1)} %add_select_fusion.1.rows, s32[2,32]{1,0:T(2,128)S(1)} %reshape.82.offsets, f32[2,16,32,32]{3,2,1,0:T(8,128)S(1)} %get-tuple-element.52.refs_6_.before, bf16[16,32,1024]{2,1,0:T(8,128)(2,1)S(1)} %copy-done.3, ...), custom_call_target="tpu_custom_call" | custom-call | tf_op jit(solution)/shard_map/pallas_call | solution.py:201
  221.9 2.4 shard_map.92
  224.3 5.3 %collective-permute-done.20.refs_3_ = bf16[8,32,384]{2,1,0:T(8,128)(2,1)S(1)} collective-permute-done((bf16[8,32,384]{2,1,0:T(8,128)(2,1)S(1)}, bf16[8,32,384]{2,1,0:T(8,128)(2,1)S(1)}, u32[]{:S(2)}, u32[]{:S(2)}) %collective-permute-start.20) | collective-permute-done | bytes 196640 | tf_op jit(solution)/shard_map/ppermute | solution.py:356
  233.0 2.2 collective-permute-done.16.refs_7_
  237.2 2.5 shard_map.93.before
  241.1 3.8 %collective-permute-done.14.there = f32[16,32,32]{2,1,0:T(8,128)S(1)} collective-permute-done((f32[16,32,32]{2,1,0:T(8,128)S(1)}, f32[16,32,32]{2,1,0:T(8,128)S(1)}, u32[]{:S(2)}, u32[]{:S(2)}) %collective-permute-start.14) | collective-permute-done | bytes 65568 | tf_op jit(solution)/shard_map/ppermute | solution.py:356
  244.8 2.4 finish.1
  (119 shorter events, 48.7 us)
Async XLA Ops:
  3.3 25.3 %all-to-all-start = ((bf16[4,1,256,768]{3,2,1,0:T(8,128)(2,1)}), bf16[4,1,256,768]{3,2,1,0:T(8,128)(2,1)}, u32[]{:S(2)}, u32[]{:S(2)}) async-start(bf16[4,1,256,768]{3,2,1,0:T(8,128)(2,1)} %slice.64), calls=%async_computation | async-start | bytes 3145728 | tf_op jit(solution)/shard_map/all_to_all | solution.py:363
  15.6 28.5 %copy-start.18 = (s32[32]{0:T(128)S(1)}, s32[32]{0:T(128)}, u32[]{:S(2)}) copy-start(s32[32]{0:T(128)} %reshape.80.orbs) | copy-start | bytes 388
  15.6 28.5 %copy-start.17 = (f32[16,2,32]{2,1,0:T(2,128)S(1)}, f32[16,2,32]{2,1,0:T(2,128)}, u32[]{:S(2)}) copy-start(f32[16,2,32]{2,1,0:T(2,128)} %param.11) | copy-start | bytes 12292
  28.6 25.0 %all-to-all-start.1 = ((bf16[4,1,256,768]{3,2,1,0:T(8,128)(2,1)}), bf16[4,1,256,768]{3,2,1,0:T(8,128)(2,1)}, u32[]{:S(2)}, u32[]{:S(2)}) async-start(bf16[4,1,256,768]{3,2,1,0:T(8,128)(2,1)} %slice.66), calls=%async_computation.1 | async-start | bytes 3145728 | tf_op jit(solution)/shard_map/all_to_all | solution.py:363
  33.7 27.3 %collective-permute-start.6 = (bf16[2,32,1536]{2,1,0:T(8,128)(2,1)}, bf16[2,32,1536]{2,1,0:T(8,128)(2,1)S(1)}, u32[]{:S(2)}, u32[]{:S(2)}) collective-permute-start(bf16[2,32,1536]{2,1,0:T(8,128)(2,1)} %slice.75), channel_id=1, source_target_pairs={{0,2},{1,3},{6,4},{7,5},{8,10},{9,11},{14,12},{15,13},{16,18},{17,... | collective-permute-start | bytes 589832 | tf_op jit(solution)/shard_map/ppermute | solution.py:382
  38.0 36.7 %collective-permute-start.1 = (bf16[16,32,1536]{2,1,0:T(8,128)(2,1)}, bf16[16,32,1536]{2,1,0:T(8,128)(2,1)S(1)}, u32[]{:S(2)}, u32[]{:S(2)}) collective-permute-start(bf16[16,32,1536]{2,1,0:T(8,128)(2,1)} %get-tuple-element.40), channel_id=1, source_target_pairs={{0,1},{1,0},{2,3},{3,2},{4,5},{5,4},{6,7},{7,6},{8,9},{9,8},{10,11... | collective-permute-start | bytes 4718600 | tf_op jit(solution)/shard_map/ppermute | solution.py:356
  39.6 37.7 %collective-permute-start.2 = (bf16[16,32,1536]{2,1,0:T(8,128)(2,1)}, bf16[16,32,1536]{2,1,0:T(8,128)(2,1)}, u32[]{:S(2)}, u32[]{:S(2)}) collective-permute-start(bf16[16,32,1536]{2,1,0:T(8,128)(2,1)} %get-tuple-element.41), channel_id=1, source_target_pairs={{0,2},{1,3},{2,0},{3,1},{4,6},{5,7},{6,4},{7,5},{8,10},{9,11},{10,... | collective-permute-start | bytes 4718600 | tf_op jit(solution)/shard_map/ppermute | solution.py:356
  39.6 71.4 %collective-permute-start.3 = (bf16[16,32,1536]{2,1,0:T(8,128)(2,1)}, bf16[16,32,1536]{2,1,0:T(8,128)(2,1)}, u32[]{:S(2)}, u32[]{:S(2)}) collective-permute-start(bf16[16,32,1536]{2,1,0:T(8,128)(2,1)} %get-tuple-element.42), channel_id=1, source_target_pairs={{0,3},{1,2},{2,1},{3,0},{4,7},{5,6},{6,5},{7,4},{8,11},{9,10},{10,... | collective-permute-start | bytes 4718600 | tf_op jit(solution)/shard_map/ppermute | solution.py:356
  51.1 79.7 %collective-permute-start.4 = (bf16[512,768]{1,0:T(8,128)(2,1)}, bf16[512,768]{1,0:T(8,128)(2,1)}, u32[]{:S(2)}, u32[]{:S(2)}) collective-permute-start(bf16[512,768]{1,0:T(8,128)(2,1)} %slice.85), channel_id=1, source_target_pairs={{0,6},{1,7},{2,4},{3,5},{4,2},{5,3},{6,0},{7,1},{8,14},{9,15},{10,... | collective-permute-start | bytes 2359304 | tf_op jit(solution)/shard_map/ppermute | solution.py:356
  61.6 85.9 %collective-permute-start.5 = (bf16[512,768]{1,0:T(8,128)(2,1)}, bf16[512,768]{1,0:T(8,128)(2,1)S(1)}, u32[]{:S(2)}, u32[]{:S(2)}) collective-permute-start(bf16[512,768]{1,0:T(8,128)(2,1)} %slice.86), channel_id=1, source_target_pairs={{0,6},{1,7},{2,4},{3,5},{4,2},{5,3},{6,0},{7,1},{8,14},{9,15},{10,... | collective-permute-start | bytes 2359304 | tf_op jit(solution)/shard_map/ppermute | solution.py:356
  74.7 79.3 %collective-permute-start = (s32[32]{0:T(128)S(1)}, s32[32]{0:T(128)S(1)}, u32[]{:S(2)}, u32[]{:S(2)}) collective-permute-start(s32[32]{0:T(128)S(1)} %copy-done.18), channel_id=1, source_target_pairs={{0,2},{1,3},{2,0},{3,1},{4,6},{5,7},{6,4},{7,5},{8,10},{9,11},{10,... | collective-permute-start | bytes 392 | tf_op jit(solution)/shard_map/ppermute | solution.py:356
  121.1 32.1 %copy-start.1 = (bf16[16,32,1024]{2,1,0:T(8,128)(2,1)}, bf16[16,32,1024]{2,1,0:T(8,128)(2,1)S(1)}, u32[]{:S(2)}) copy-start(bf16[16,32,1024]{2,1,0:T(8,128)(2,1)S(1)} %get-tuple-element.48.refs_0_) | copy-start | bytes 3145732
  121.1 48.3 %collective-permute-start.7 = (bf16[16,32,1024]{2,1,0:T(8,128)(2,1)}, bf16[16,32,1024]{2,1,0:T(8,128)(2,1)}, u32[]{:S(2)}, u32[]{:S(2)}) collective-permute-start(bf16[16,32,1024]{2,1,0:T(8,128)(2,1)} %get-tuple-element.49), channel_id=1, source_target_pairs={{0,1},{1,0},{2,3},{3,2},{4,5},{5,4},{6,7},{7,6},{8,9},{9,8},{10,11... | collective-permute-start | bytes 3145736 | tf_op jit(solution)/shard_map/ppermute | solution.py:356
  125.0 51.5 %collective-permute-start.9 = (bf16[128,768]{1,0:T(8,128)(2,1)}, bf16[128,768]{1,0:T(8,128)(2,1)}, u32[]{:S(2)}, u32[]{:S(2)}) collective-permute-start(bf16[128,768]{1,0:T(8,128)(2,1)} %get-tuple-element.75), channel_id=1, source_target_pairs={{0,6},{1,7},{2,4},{3,5},{4,2},{5,3},{6,0},{7,1},{8,14},{9,15},{10,... | collective-permute-start | bytes 589832 | tf_op jit(solution)/shard_map/ppermute | solution.py:356
  130.8 78.2 %collective-permute-start.12 = (bf16[256,768]{1,0:T(8,128)(2,1)}, bf16[256,768]{1,0:T(8,128)(2,1)}, u32[]{:S(2)}, u32[]{:S(2)}) collective-permute-start(bf16[256,768]{1,0:T(8,128)(2,1)} %slice.91), channel_id=1, source_target_pairs={{0,6},{1,7},{2,4},{3,5},{4,2},{5,3},{6,0},{7,1},{8,14},{9,15},{10,... | collective-permute-start | bytes 1179656 | tf_op jit(solution)/shard_map/ppermute | solution.py:356
  147.6 63.0 %collective-permute-start.13 = (bf16[256,768]{1,0:T(8,128)(2,1)}, bf16[256,768]{1,0:T(8,128)(2,1)}, u32[]{:S(2)}, u32[]{:S(2)}) collective-permute-start(bf16[256,768]{1,0:T(8,128)(2,1)} %slice.92), channel_id=1, source_target_pairs={{0,6},{1,7},{2,4},{3,5},{4,2},{5,3},{6,0},{7,1},{8,14},{9,15},{10,... | collective-permute-start | bytes 1179656 | tf_op jit(solution)/shard_map/ppermute | solution.py:356
  154.0 12.9 %collective-permute-start.8 = (bf16[16,32,512]{2,1,0:T(8,128)(2,1)}, bf16[16,32,512]{2,1,0:T(8,128)(2,1)}, u32[]{:S(2)}, u32[]{:S(2)}) collective-permute-start(bf16[16,32,512]{2,1,0:T(8,128)(2,1)} %get-tuple-element.51), channel_id=1, source_target_pairs={{0,1},{1,0},{2,3},{3,2},{4,5},{5,4},{6,7},{7,6},{8,9},{9,8},{10,11... | collective-permute-start | bytes 1572872 | tf_op jit(solution)/shard_map/ppermute | solution.py:356
  166.9 12.1 %collective-permute-start.10 = (bf16[128,768]{1,0:T(8,128)(2,1)}, bf16[128,768]{1,0:T(8,128)(2,1)S(1)}, u32[]{:S(2)}, u32[]{:S(2)}) collective-permute-start(bf16[128,768]{1,0:T(8,128)(2,1)} %get-tuple-element.73), channel_id=1, source_target_pairs={{0,6},{1,7},{2,4},{3,5},{4,2},{5,3},{6,0},{7,1},{8,14},{9,15},{10,... | collective-permute-start | bytes 589832 | tf_op jit(solution)/shard_map/ppermute | solution.py:356
  169.4 48.8 %collective-permute-start.17 = (bf16[128,768]{1,0:T(8,128)(2,1)}, bf16[128,768]{1,0:T(8,128)(2,1)S(1)}, u32[]{:S(2)}, u32[]{:S(2)}) collective-permute-start(bf16[128,768]{1,0:T(8,128)(2,1)} %get-tuple-element.74), channel_id=1, source_target_pairs={{0,6},{1,7},{2,4},{3,5},{4,2},{5,3},{6,0},{7,1},{8,14},{9,15},{10,... | collective-permute-start | bytes 589832 | tf_op jit(solution)/shard_map/ppermute | solution.py:356
  176.5 43.3 %collective-permute-start.18 = (bf16[128,768]{1,0:T(8,128)(2,1)S(1)}, bf16[128,768]{1,0:T(8,128)(2,1)S(1)}, u32[]{:S(2)}, u32[]{:S(2)}) collective-permute-start(bf16[128,768]{1,0:T(8,128)(2,1)S(1)} %copy-done.16), channel_id=1, source_target_pairs={{0,6},{1,7},{2,4},{3,5},{4,2},{5,3},{6,0},{7,1},{8,14},{9,15},{10,... | collective-permute-start | bytes 589832 | tf_op jit(solution)/shard_map/ppermute | solution.py:356
  179.0 41.5 %collective-permute-start.19 = (bf16[8,32,384]{2,1,0:T(8,128)(2,1)S(1)}, bf16[8,32,384]{2,1,0:T(8,128)(2,1)S(1)}, u32[]{:S(2)}, u32[]{:S(2)}) collective-permute-start(bf16[8,32,384]{2,1,0:T(8,128)(2,1)S(1)} %copy-done.15), channel_id=1, source_target_pairs={{0,2},{1,3},{2,0},{3,1},{4,6},{5,7},{6,4},{7,5},{8,10},{9,11},{10,... | collective-permute-start | bytes 589832 | tf_op jit(solution)/shard_map/ppermute | solution.py:356
  209.0 5.1 %collective-permute-start.11 = (bf16[16,32,128]{2,1,0:T(8,128)(2,1)S(1)}, bf16[16,32,128]{2,1,0:T(8,128)(2,1)S(1)}, u32[]{:S(2)}, u32[]{:S(2)}) collective-permute-start(bf16[16,32,128]{2,1,0:T(8,128)(2,1)S(1)} %get-tuple-element.54), channel_id=1, source_target_pairs={{0,1},{1,0},{2,3},{3,2},{4,5},{5,4},{6,7},{7,6},{8,9},{9,8},{10,11... | collective-permute-start | bytes 393224 | tf_op jit(solution)/shard_map/ppermute | solution.py:356
  210.6 25.8 %collective-permute-start.15 = (bf16[16,32,512]{2,1,0:T(8,128)(2,1)S(1)}, bf16[16,32,512]{2,1,0:T(8,128)(2,1)S(1)}, u32[]{:S(2)}, u32[]{:S(2)}) collective-permute-start(bf16[16,32,512]{2,1,0:T(8,128)(2,1)S(1)} %get-tuple-element.57), channel_id=1, source_target_pairs={{0,2},{1,3},{2,0},{3,1},{4,6},{5,7},{6,4},{7,5},{8,10},{9,11},{10,... | collective-permute-start | bytes 1572872 | tf_op jit(solution)/shard_map/ppermute | solution.py:356
  214.1 15.4 %collective-permute-start.20 = (bf16[8,32,384]{2,1,0:T(8,128)(2,1)S(1)}, bf16[8,32,384]{2,1,0:T(8,128)(2,1)S(1)}, u32[]{:S(2)}, u32[]{:S(2)}) collective-permute-start(bf16[8,32,384]{2,1,0:T(8,128)(2,1)S(1)} %copy-done.14), channel_id=1, source_target_pairs={{0,3},{1,2},{2,1},{3,0},{4,7},{5,6},{6,5},{7,4},{8,11},{9,10},{10,... | collective-permute-start | bytes 589832 | tf_op jit(solution)/shard_map/ppermute | solution.py:356
  218.2 12.3 %collective-permute-start.21 = (bf16[8,32,256]{2,1,0:T(8,128)(2,1)S(1)}, bf16[8,32,256]{2,1,0:T(8,128)(2,1)S(1)}, u32[]{:S(2)}, u32[]{:S(2)}) collective-permute-start(bf16[8,32,256]{2,1,0:T(8,128)(2,1)S(1)} %get-tuple-element.60), channel_id=1, source_target_pairs={{0,1},{1,0},{2,3},{3,2},{4,5},{5,4},{6,7},{7,6},{8,9},{9,8},{10,11... | collective-permute-start | bytes 393224 | tf_op jit(solution)/shard_map/ppermute | solution.py:356
  219.8 12.6 %collective-permute-start.22 = (bf16[8,32,256]{2,1,0:T(8,128)(2,1)S(1)}, bf16[8,32,256]{2,1,0:T(8,128)(2,1)S(1)}, u32[]{:S(2)}, u32[]{:S(2)}) collective-permute-start(bf16[8,32,256]{2,1,0:T(8,128)(2,1)S(1)} %get-tuple-element.61), channel_id=1, source_target_pairs={{0,2},{1,3},{2,0},{3,1},{4,6},{5,7},{6,4},{7,5},{8,10},{9,11},{10,... | collective-permute-start | bytes 393224 | tf_op jit(solution)/shard_map/ppermute | solution.py:356
  220.5 14.7 %collective-permute-start.16 = (bf16[16,32,128]{2,1,0:T(8,128)(2,1)S(1)}, bf16[16,32,128]{2,1,0:T(8,128)(2,1)S(1)}, u32[]{:S(2)}, u32[]{:S(2)}) collective-permute-start(bf16[16,32,128]{2,1,0:T(8,128)(2,1)S(1)} %get-tuple-element.58), channel_id=1, source_target_pairs={{0,2},{1,3},{2,0},{3,1},{4,6},{5,7},{6,4},{7,5},{8,10},{9,11},{10,... | collective-permute-start | bytes 393224 | tf_op jit(solution)/shard_map/ppermute | solution.py:356
  229.5 10.1 %collective-permute-start.23 = (bf16[8,32,256]{2,1,0:T(8,128)(2,1)S(1)}, bf16[8,32,256]{2,1,0:T(8,128)(2,1)S(1)}, u32[]{:S(2)}, u32[]{:S(2)}) collective-permute-start(bf16[8,32,256]{2,1,0:T(8,128)(2,1)S(1)} %get-tuple-element.62), channel_id=1, source_target_pairs={{0,3},{1,2},{2,1},{3,0},{4,7},{5,6},{6,5},{7,4},{8,11},{9,10},{10,... | collective-permute-start | bytes 393224 | tf_op jit(solution)/shard_map/ppermute | solution.py:356
  230.5 9.2 %collective-permute-start.24 = (bf16[8,32,128]{2,1,0:T(8,128)(2,1)S(1)}, bf16[8,32,128]{2,1,0:T(8,128)(2,1)S(1)}, u32[]{:S(2)}, u32[]{:S(2)}) collective-permute-start(bf16[8,32,128]{2,1,0:T(8,128)(2,1)S(1)} %get-tuple-element.63), channel_id=1, source_target_pairs={{0,1},{1,0},{2,3},{3,2},{4,5},{5,4},{6,7},{7,6},{8,9},{9,8},{10,11... | collective-permute-start | bytes 196616 | tf_op jit(solution)/shard_map/ppermute | solution.py:356
  232.4 7.3 %collective-permute-start.25 = (bf16[8,32,128]{2,1,0:T(8,128)(2,1)S(1)}, bf16[8,32,128]{2,1,0:T(8,128)(2,1)S(1)}, u32[]{:S(2)}, u32[]{:S(2)}) collective-permute-start(bf16[8,32,128]{2,1,0:T(8,128)(2,1)S(1)} %get-tuple-element.64), channel_id=1, source_target_pairs={{0,2},{1,3},{2,0},{3,1},{4,6},{5,7},{6,4},{7,5},{8,10},{9,11},{10,... | collective-permute-start | bytes 196616 | tf_op jit(solution)/shard_map/ppermute | solution.py:356
  235.2 5.9 %collective-permute-start.26 = (bf16[8,32,128]{2,1,0:T(8,128)(2,1)S(1)}, bf16[8,32,128]{2,1,0:T(8,128)(2,1)S(1)}, u32[]{:S(2)}, u32[]{:S(2)}) collective-permute-start(bf16[8,32,128]{2,1,0:T(8,128)(2,1)S(1)} %get-tuple-element.65), channel_id=1, source_target_pairs={{0,3},{1,2},{2,1},{3,0},{4,7},{5,6},{6,5},{7,4},{8,11},{9,10},{10,... | collective-permute-start | bytes 196616 | tf_op jit(solution)/shard_map/ppermute | solution.py:356
  236.4 8.4 %collective-permute-start.14 = (f32[16,32,32]{2,1,0:T(8,128)S(1)}, f32[16,32,32]{2,1,0:T(8,128)S(1)}, u32[]{:S(2)}, u32[]{:S(2)}) collective-permute-start(f32[16,32,32]{2,1,0:T(8,128)S(1)} %slice_bitcast_fusion), channel_id=1, source_target_pairs={{0,2},{1,3},{2,0},{3,1},{4,6},{5,7},{6,4},{7,5},{8,10},{9,11},{10,... | collective-permute-start | bytes 196616 | tf_op jit(solution)/shard_map/ppermute | solution.py:356
  (19 other events, 104.0 us)

commit v10 on v9

--- a/solution.py
+++ b/solution.py
@@ -16,7 +16,7 @@
     return pltpu.make_async_copy(source, target, sem)
 
 
-def pack_kernel(group, capacity, orbs, place, coef, *refs):
+def pack_kernel(group, capacity, masks, orbs, place, coef, *refs):
     outs, (held, count, holder, load_sem, store_sem) = refs[:-5], refs[-5:]
     load = copy(coef, held, load_sem)
     load.start()
@@ -40,38 +40,37 @@
     lax.fori_loop(0, 2 * group, clear_count, 0)
     lax.fori_loop(0, held.shape[0], assign, 0)
     load.wait()
-    for mask, out in enumerate(outs):
+    for at, (mask, out) in enumerate(zip(masks, outs)):
         for kind in range(2):
             orb = place[1] ^ mask ^ (kind * (group + group // 2))
 
-            def send(k, carry, orb=orb, kind=kind, out=out, sem=store_sem.at[mask]):
+            def send(k, carry, orb=orb, kind=kind, out=out, sem=store_sem.at[at]):
                 copy(held.at[holder[orb * capacity + k]], out.at[kind * capacity + k], sem).start()
                 return carry
 
             lax.fori_loop(0, capacity, send, 0)
-    for mask, out in enumerate(outs):
-        copy(held.at[pl.ds(0, 2 * capacity)], out, store_sem.at[mask]).wait()
-
-
-def pack(orbs, place, coef, group, capacity):
+    for at, out in enumerate(outs):
+        copy(held.at[pl.ds(0, 2 * capacity)], out, store_sem.at[at]).wait()
+
+
+def pack(orbs, place, coef, group, capacity, masks):
     side_count, pno_count, dom_count = coef.shape
     block = jax.ShapeDtypeStruct((2 * capacity, pno_count, dom_count), coef.dtype)
     return pl.pallas_call(
-        functools.partial(pack_kernel, group, capacity),
-        out_shape=(block,) * group,
+        functools.partial(pack_kernel, group, capacity, masks),
+        out_shape=(block,) * len(masks),
         in_specs=[SMEM, SMEM, ANY],
-        out_specs=(ANY,) * group,
+        out_specs=(ANY,) * len(masks),
         scratch_shapes=[
             pltpu.VMEM(coef.shape, coef.dtype),
             pltpu.SMEM((2 * group,), jnp.int32),
             pltpu.SMEM((2 * group * capacity,), jnp.int32),
             pltpu.SemaphoreType.DMA,
-            pltpu.SemaphoreType.DMA((group,)),
+            pltpu.SemaphoreType.DMA((len(masks),)),
         ],
         cost_estimate=pl.CostEstimate(
             flops=0, transcendentals=0, bytes_accessed=6 * side_count * pno_count * dom_count
         ),
-        name="pack",
     )(orbs, place, coef)
 
 
@@ -285,9 +284,11 @@
     lax.fori_loop(0, coupling.shape[0], one_pair, 0, unroll=4)
     total = coupling[...] + before[...] + here[0] + there[...]
     result = -total / denominator[...]
-    amplitude[...] = result
+    count = result.shape[1]
+    for p in range(count):
+        amplitude[:, p * count : (p + 1) * count] = result[:, p, :]
     parts = total * (2.0 * result - jnp.swapaxes(result, 1, 2))
-    energy[...] = jnp.sum(jnp.sum(parts, axis=1), axis=1, keepdims=True)
+    energy[...] = jnp.sum(jnp.sum(parts, axis=1), axis=1)
 
 
 def finish(rows, finals, near, straight, far, sizes):
@@ -297,7 +298,10 @@
     square = jax.ShapeDtypeStruct((pair_count, pno_count, pno_count), jnp.float32)
     return pl.pallas_call(
         functools.partial(finish_kernel, group, sizes),
-        out_shape=(square, jax.ShapeDtypeStruct((pair_count, 1), jnp.float32)),
+        out_shape=(
+            jax.ShapeDtypeStruct((pair_count, pno_count * pno_count), jnp.float32),
+            jax.ShapeDtypeStruct((pair_count,), jnp.float32),
+        ),
         in_specs=[SMEM] + [VMEM] * len(finals) + [ANY] * (len(near) + len(straight) + len(far)),
         out_specs=(VMEM, VMEM),
         scratch_shapes=[
@@ -370,16 +374,19 @@
         return part[0, 0]
 
     raw_parts = [exchange(raw_ints, 0)]
-    packed = pack(
-        own_orbs, place, pno_coef.reshape(side_count, pno_count, dom_count), group, capacity
-    )
-    later, packed = lax.optimization_barrier((raw_ints, packed))
+    coef = pno_coef.reshape(side_count, pno_count, dom_count)
+    blocks = [None] * group
+    packed = pack(own_orbs, place, coef, group, capacity, tuple(range(inner, group)))
+    for m in range(inner, group):
+        blocks[m] = across(packed[m - inner], m)
+    pairs = [(i, i ^ inner) for i in range(orb_count) if i // inner in (0, 3)]
+    guard = lax.ppermute(packed[0][:1], "orb", pairs)
+    packed = pack(own_orbs, place, coef, group, capacity, tuple(range(inner)))
+    blocks[0] = packed[0]
+    for m in range(1, inner):
+        blocks[m] = across(packed[m], m)
+    later, blocks[0] = lax.optimization_barrier((raw_ints, blocks[0]))
     raw_parts.append(exchange(later, 1))
-    blocks = [packed[0]]
-    for m in range(1, group):
-        blocks.append(across(packed[m], m))
-    pairs = [(i, i ^ inner) for i in range(orb_count) if i // inner in (0, 3)]
-    guard = lax.ppermute(packed[0][:2], "orb", pairs)
     own_offset = fit_offset[region * orb_count + me]
     turned = jnp.roll(fit_inverse[0], own_offset, axis=0)
     mate_orbs = across(own_orbs, inner)
@@ -405,11 +412,13 @@
         mirror(c, 0)
         mirror(c, 1)
 
-    energies, fitted[1] = lax.optimization_barrier((occ_energy, fitted[1]))
-    occupied = pick(energies, own_orbs).reshape(pair_count, 2)
+    energies, levels, named, fitted[1] = lax.optimization_barrier(
+        (occ_energy, pno_energy, own_orbs, fitted[1])
+    )
+    occupied = pick(energies, named).reshape(pair_count, 2)
     denominator = (
-        pno_energy[:, 0, :, None]
-        + pno_energy[:, 1, None, :]
+        levels[:, 0, :, None]
+        + levels[:, 1, None, :]
         - occupied[:, 0, None, None]
         - occupied[:, 1, None, None]
     )
@@ -461,7 +470,7 @@
         far[2] + far[3],
         tuple(size for _, size in spans[2:]),
     )
-    return (amplitude.reshape(pair_count, pno_count * pno_count), energy.reshape(pair_count))
+    return amplitude, energy
 
 
 def solution(mesh):

time: 249 us -> 248 us (level)
  waiting for transfers between devices: 97.3 us -> 92.4 us
  Pallas kernels: 34.4 us -> 38.6 us
    ppermute x26, waiting for transfers between devices: 84.4 us -> 68.5 us  [across(): return lax.ppermute(array, 'orb', [(i, i ^ mask) for i in range(orb_count)])]
    ppermute x1, waiting for transfers between devices: 0.01 us -> 12.1 us  [on_device(): guard = lax.ppermute(packed[0][:1], 'orb', pairs)]
    pallas_call x1 -> x2, Pallas kernels: 5.2 us -> 8.69 us  [pack(): pl.pallas_call(functools.partial(pack_kernel, group, capacity, masks), ou...]
    ppermute x26, starting transfers between devices: 63.8 us -> 67.2 us  [across(): return lax.ppermute(array, 'orb', [(i, i ^ mask) for i in range(orb_count)])]
    unnamed x45 -> x39, local copies, waits for them, and re-layouts: 9.96 us -> 8.3 us
  transfers between devices with their start and end apart: 29 -> 29, of which waited for: 13 -> 11; matrix products, arithmetic and copies ran while one was open for 9% -> 10% of each run, Pallas kernels for 13% -> 14%
where the time goes in v10:
time: 248 us; the launch traced here: 247 us
  waiting for transfers between devices  92.4 us (37%)
  starting transfers between devices  77.8 us (31%)
  Pallas kernels  38.6 us (16%)
  local copies, waits for them, and re-layouts  24.8 us (10%)
  matrix products  9.09 us (4%)
  between operations  2.99 us (1%)
    ppermute x26, waiting for transfers between devices, across(): return lax.ppermute(array, 'orb', [(i, i ^ mask) for i in range(orb_count)])  68.5 us
    ppermute x26, starting transfers between devices, across(): return lax.ppermute(array, 'orb', [(i, i ^ mask) for i in range(orb_count)])  67.2 us
    pallas_call x5, Pallas kernels, project(): pl.pallas_call(kernel, grid=(1,), out_shape=(jax.ShapeDtypeStruct((lines,...  18.1 us
    ppermute x1, waiting for transfers between devices, on_device(): guard = lax.ppermute(packed[0][:1], 'orb', pairs)  12.1 us
    all_to_all x2, waiting for transfers between devices, exchange(): lax.all_to_all(array[:, :, :, k * half:(k + 1) * half], 'aux', split_axis...  11.8 us
    dot_general x2, matrix products, on_device(): product = jnp.dot(turned, raw_parts[k], preferred_element_type=jnp.float32)  9.09 us
    all_to_all x2, starting transfers between devices, exchange(): lax.all_to_all(array[:, :, :, k * half:(k + 1) * half], 'aux', split_axis...  8.71 us
    pallas_call x2, Pallas kernels, pack(): pl.pallas_call(functools.partial(pack_kernel, group, capacity, masks), ou...  8.69 us
  transfers between devices with their start and end apart: 29, of which 11 were waited for; matrix products, arithmetic and copies ran while one was open for 10% of the time, Pallas kernels for 14%

profile of v10, /device:TPU:0, one launch (start us, length us, event | category | flops | bytes accessed | tf_op | source)
XLA Modules:
  0.0 247.1 jit_solution(2776938186864840993)
XLA Ops:
  0.6 2.7 %slice.64 = bf16[4,1,256,768]{3,2,1,0:T(8,128)(2,1)} slice(bf16[4,1,256,1536]{3,2,1,0:T(8,128)(2,1)} %param.7), slice={[0:4], [0:1], [0:256], [0:768]} | slice | bytes 3145728 | tf_op jit(solution)/shard_map/slice | solution.py:368
  3.3 4.4 %all-to-all-start = ((bf16[4,1,256,768]{3,2,1,0:T(8,128)(2,1)}), bf16[4,1,256,768]{3,2,1,0:T(8,128)(2,1)S(1)}, u32[]{:S(2)}, u32[]{:S(2)}) async-start(bf16[4,1,256,768]{3,2,1,0:T(8,128)(2,1)} %slice.64), calls=%async_computation | async-start | bytes 3145728 | tf_op jit(solution)/shard_map/all_to_all | solution.py:367
  9.0 4.3 %shard_map.86 = (bf16[16,32,1536]{2,1,0:T(8,128)(2,1)}, bf16[16,32,1536]{2,1,0:T(8,128)(2,1)}) custom-call(s32[32]{0:T(128)} %reshape.70.orbs, s32[2]{0:T(128)} %pad_add_fusion.1.place, bf16[32,32,1536]{2,1,0:T(8,128)(2,1)} %bitcast.16), custom_call_target="tpu_custom_call" | custom-call | bytes 9437184 | tf_op jit(solution)/shard_map/pallas_call | solution.py:59
  13.3 2.7 %slice.66 = bf16[4,1,256,768]{3,2,1,0:T(8,128)(2,1)} slice(bf16[4,1,256,1536]{3,2,1,0:T(8,128)(2,1)} %param.7), slice={[0:4], [0:1], [0:256], [768:1536]} | slice | bytes 3145728 | tf_op jit(solution)/shard_map/slice | solution.py:368
  16.0 11.8 %all-to-all-done = bf16[4,1,256,768]{3,2,1,0:T(8,128)(2,1)S(1)} async-done(((bf16[4,1,256,768]{3,2,1,0:T(8,128)(2,1)}), bf16[4,1,256,768]{3,2,1,0:T(8,128)(2,1)S(1)}, u32[]{:S(2)}, u32[]{:S(2)}) %all-to-all-start) | async-done | bytes 1572896 | tf_op jit(solution)/shard_map/all_to_all | solution.py:367
  27.7 4.3 %all-to-all-start.1 = ((bf16[4,1,256,768]{3,2,1,0:T(8,128)(2,1)}), bf16[4,1,256,768]{3,2,1,0:T(8,128)(2,1)}, u32[]{:S(2)}, u32[]{:S(2)}) async-start(bf16[4,1,256,768]{3,2,1,0:T(8,128)(2,1)} %slice.66), calls=%async_computation.1 | async-start | bytes 3145728 | tf_op jit(solution)/shard_map/all_to_all | solution.py:367
  32.1 4.4 %shard_map.87 = (bf16[16,32,1536]{2,1,0:T(8,128)(2,1)}, bf16[16,32,1536]{2,1,0:T(8,128)(2,1)}) custom-call(s32[32]{0:T(128)} %reshape.70.orbs, s32[2]{0:T(128)} %pad_add_fusion.1.place, bf16[32,32,1536]{2,1,0:T(8,128)(2,1)} %bitcast.17), custom_call_target="tpu_custom_call" | custom-call | bytes 9437184 | tf_op jit(solution)/shard_map/pallas_call | solution.py:59
  36.6 2.4 collective-permute-start.2
  46.6 4.3 %convolution_convert_fusion.1.refs_4_ = bf16[1024,768]{1,0:T(8,128)(2,1)S(1)} fusion(bf16[1024,768]{1,0:T(8,128)(2,1)S(1)} %bitcast.18, s32[]{:T(128)S(6)} %select_n.50, bf16[1024,1024]{1,0:T(8,128)(2,1)} %bitcast.23), kind=kOutput, calls=%fused_computation.4 | convolution fusion | flops 1615593472 | bytes 5242884 | tf_op jit(solution)/shard_map/dot_general | solution.py:408
  53.0 3.6 %collective-permute-start.4 = (bf16[512,768]{1,0:T(8,128)(2,1)}, bf16[512,768]{1,0:T(8,128)(2,1)}, u32[]{:S(2)}, u32[]{:S(2)}) collective-permute-start(bf16[512,768]{1,0:T(8,128)(2,1)} %slice.85), channel_id=1, source_target_pairs={{0,6},{1,7},{2,4},{3,5},{4,2},{5,3},{6,0},{7,1},{8,14},{9,15},{10,... | collective-permute-start | bytes 2359304 | tf_op jit(solution)/shard_map/ppermute | solution.py:360
  56.6 4.8 %convolution_convert_fusion.refs_5_ = bf16[1024,768]{1,0:T(8,128)(2,1)S(1)} fusion(bf16[1024,768]{1,0:T(8,128)(2,1)} %bitcast.6, s32[]{:T(128)S(6)} %select_n.50, bf16[1024,1024]{1,0:T(8,128)(2,1)} %bitcast.24), kind=kOutput, calls=%fused_computation.3 | convolution fusion | flops 1615593472 | bytes 5242884 | tf_op jit(solution)/shard_map/dot_general | solution.py:408
  64.0 12.1 %collective-permute-done.6.refs_7_ = bf16[1,32,1536]{2,1,0:T(8,128)(2,1)S(1)} collective-permute-done((bf16[1,32,1536]{2,1,0:T(8,128)(2,1)S(1)}, bf16[1,32,1536]{2,1,0:T(8,128)(2,1)S(1)}, u32[]{:S(2)}, u32[]{:S(2)}) %collective-permute-start.6) | collective-permute-done | bytes 98336 | tf_op jit(solution)/shard_map/ppermute | solution.py:383
  76.1 2.5 %collective-permute-start.5 = (bf16[512,768]{1,0:T(8,128)(2,1)}, bf16[512,768]{1,0:T(8,128)(2,1)S(1)}, u32[]{:S(2)}, u32[]{:S(2)}) collective-permute-start(bf16[512,768]{1,0:T(8,128)(2,1)} %slice.86), channel_id=1, source_target_pairs={{0,6},{1,7},{2,4},{3,5},{4,2},{5,3},{6,0},{7,1},{8,14},{9,15},{10,... | collective-permute-start | bytes 2359304 | tf_op jit(solution)/shard_map/ppermute | solution.py:360
  80.5 29.4 %collective-permute-done.3.refs_3_ = bf16[16,32,1536]{2,1,0:T(8,128)(2,1)} collective-permute-done((bf16[16,32,1536]{2,1,0:T(8,128)(2,1)}, bf16[16,32,1536]{2,1,0:T(8,128)(2,1)}, u32[]{:S(2)}, u32[]{:S(2)}) %collective-permute-start.3) | collective-permute-done | bytes 1572896 | tf_op jit(solution)/shard_map/ppermute | solution.py:360
  109.9 3.4 %collective-permute-start = (s32[32]{0:T(128)S(1)}, s32[32]{0:T(128)S(1)}, u32[]{:S(2)}, u32[]{:S(2)}) collective-permute-start(s32[32]{0:T(128)S(1)} %copy-done.15), channel_id=1, source_target_pairs={{0,2},{1,3},{2,0},{3,1},{4,6},{5,7},{6,4},{7,5},{8,10},{9,11},{10,... | collective-permute-start | bytes 392 | tf_op jit(solution)/shard_map/ppermute | solution.py:360
  116.2 6.4 %shard_map.89 = (bf16[16,32,1024]{2,1,0:T(8,128)(2,1)S(1)}, bf16[16,32,1024]{2,1,0:T(8,128)(2,1)}) custom-call(bf16[16,32,1536]{2,1,0:T(8,128)(2,1)S(1)} %copy-done, bf16[16,32,1536]{2,1,0:T(8,128)(2,1)} %collective-permute-done.1.refs_1_, bf16[16,32,1536]{2,1,0:T(8,128)(2,1)S(1)} %collective-permute-done.2.refs_2_, ...), custom_call_target="tpu_custom_call" | custom-call | flops 3221225472 | bytes 3145728 | tf_op jit(solution)/shard_map/pallas_call | solution.py:124
  125.7 3.6 %collective-permute-start.9 = (bf16[128,768]{1,0:T(8,128)(2,1)}, bf16[128,768]{1,0:T(8,128)(2,1)}, u32[]{:S(2)}, u32[]{:S(2)}) collective-permute-start(bf16[128,768]{1,0:T(8,128)(2,1)} %get-tuple-element.69), channel_id=1, source_target_pairs={{0,6},{1,7},{2,4},{3,5},{4,2},{5,3},{6,0},{7,1},{8,14},{9,15},{10,... | collective-permute-start | bytes 589832 | tf_op jit(solution)/shard_map/ppermute | solution.py:360
  131.9 14.7 %collective-permute-done.5.refs_5_ = bf16[512,768]{1,0:T(8,128)(2,1)S(1)} collective-permute-done((bf16[512,768]{1,0:T(8,128)(2,1)}, bf16[512,768]{1,0:T(8,128)(2,1)S(1)}, u32[]{:S(2)}, u32[]{:S(2)}) %collective-permute-start.5) | collective-permute-done | bytes 786464 | tf_op jit(solution)/shard_map/ppermute | solution.py:360
  147.9 4.3 %shard_map.88 = (bf16[16,32,512]{2,1,0:T(8,128)(2,1)S(1)}, bf16[16,32,512]{2,1,0:T(8,128)(2,1)}) custom-call(bf16[16,32,1536]{2,1,0:T(8,128)(2,1)S(1)} %copy-done, bf16[16,32,1536]{2,1,0:T(8,128)(2,1)} %collective-permute-done.1.refs_1_, bf16[16,32,1536]{2,1,0:T(8,128)(2,1)S(1)} %collective-permute-done.2.refs_2_, ...), custom_call_target="tpu_custom_call" | custom-call | flops 1610612736 | bytes 3145728 | tf_op jit(solution)/shard_map/pallas_call | solution.py:124
  155.0 10.9 %collective-permute-done.8.refs_3_ = bf16[16,32,512]{2,1,0:T(8,128)(2,1)} collective-permute-done((bf16[16,32,512]{2,1,0:T(8,128)(2,1)}, bf16[16,32,512]{2,1,0:T(8,128)(2,1)}, u32[]{:S(2)}, u32[]{:S(2)}) %collective-permute-start.8) | collective-permute-done | bytes 524320 | tf_op jit(solution)/shard_map/ppermute | solution.py:360
  165.8 2.5 %collective-permute-start.10 = (bf16[128,768]{1,0:T(8,128)(2,1)}, bf16[128,768]{1,0:T(8,128)(2,1)S(1)}, u32[]{:S(2)}, u32[]{:S(2)}) collective-permute-start(bf16[128,768]{1,0:T(8,128)(2,1)} %get-tuple-element.67), channel_id=1, source_target_pairs={{0,6},{1,7},{2,4},{3,5},{4,2},{5,3},{6,0},{7,1},{8,14},{9,15},{10,... | collective-permute-start | bytes 589832 | tf_op jit(solution)/shard_map/ppermute | solution.py:360
  172.0 3.4 %shard_map.90 = (bf16[16,32,512]{2,1,0:T(8,128)(2,1)S(1)}, f32[2,16,32,32]{3,2,1,0:T(8,128)S(1)}) custom-call(s32[2,32]{1,0:T(2,128)S(1)} %add_select_fusion.1.rows, s32[2,32]{1,0:T(2,128)S(1)} %reshape.72.offsets, f32[8,128]{1,0:T(8,128)S(1)} %broadcast_in_dim.75.before, bf16[16,32,1024]{2,1,0:T(8,128)(2,1)S(1)} %copy-done.2, ...), custom_call_target="tpu_custom_call" | custom-call | tf_op jit(solution)/shard_map/pallas_call | solution.py:200
  175.4 2.5 %collective-permute-start.18 = (bf16[128,768]{1,0:T(8,128)(2,1)S(1)}, bf16[128,768]{1,0:T(8,128)(2,1)S(1)}, u32[]{:S(2)}, u32[]{:S(2)}) collective-permute-start(bf16[128,768]{1,0:T(8,128)(2,1)S(1)} %copy-done.13), channel_id=1, source_target_pairs={{0,6},{1,7},{2,4},{3,5},{4,2},{5,3},{6,0},{7,1},{8,14},{9,15},{10,... | collective-permute-start | bytes 589832 | tf_op jit(solution)/shard_map/ppermute | solution.py:360
  178.0 27.6 %collective-permute-start.19 = (bf16[8,32,384]{2,1,0:T(8,128)(2,1)S(1)}, bf16[8,32,384]{2,1,0:T(8,128)(2,1)S(1)}, u32[]{:S(2)}, u32[]{:S(2)}) collective-permute-start(bf16[8,32,384]{2,1,0:T(8,128)(2,1)S(1)} %copy-done.12), channel_id=1, source_target_pairs={{0,2},{1,3},{2,0},{3,1},{4,6},{5,7},{6,4},{7,5},{8,10},{9,11},{10,... | collective-permute-start | bytes 589832 | tf_op jit(solution)/shard_map/ppermute | solution.py:360
  205.6 2.4 shard_map.91
  209.6 2.7 %shard_map.92 = (bf16[8,32,256]{2,1,0:T(8,128)(2,1)S(1)}, bf16[8,32,256]{2,1,0:T(8,128)(2,1)S(1)}, bf16[8,32,256]{2,1,0:T(8,128)(2,1)S(1)}, bf16[8,32,256]{2,1,0:T(8,128)(2,1)S(1)}) custom-call(bf16[16,32,1536]{2,1,0:T(8,128)(2,1)S(1)} %copy-done, bf16[16,32,1536]{2,1,0:T(8,128)(2,1)} %collective-permute-done.1.refs_1_, ...), custom_call_target="tpu_custom_call" | custom-call | flops 805306368 | bytes 3145728 | tf_op jit(solution)/shard_map/pallas_call | solution.py:124
  214.3 2.8 %shard_map.93 = (bf16[16,32,128]{2,1,0:T(8,128)(2,1)S(1)}, f32[2,16,32,32]{3,2,1,0:T(8,128)S(1)}) custom-call(s32[2,32]{1,0:T(2,128)S(1)} %add_select_fusion.1.rows, s32[2,32]{1,0:T(2,128)S(1)} %reshape.72.offsets, f32[2,16,32,32]{3,2,1,0:T(8,128)S(1)} %get-tuple-element.48.refs_6_.before, bf16[16,32,1024]{2,1,0:T(8,128)(2,1)S(1)} %copy-done.3, ...), custom_call_target="tpu_custom_call" | custom-call | tf_op jit(solution)/shard_map/pallas_call | solution.py:200
  220.8 2.4 shard_map.94
  223.2 5.3 %collective-permute-done.20.refs_3_ = bf16[8,32,384]{2,1,0:T(8,128)(2,1)S(1)} collective-permute-done((bf16[8,32,384]{2,1,0:T(8,128)(2,1)S(1)}, bf16[8,32,384]{2,1,0:T(8,128)(2,1)S(1)}, u32[]{:S(2)}, u32[]{:S(2)}) %collective-permute-start.20) | collective-permute-done | bytes 196640 | tf_op jit(solution)/shard_map/ppermute | solution.py:360
  236.2 2.5 shard_map.95.before
  240.1 3.8 %collective-permute-done.14.there = f32[16,32,32]{2,1,0:T(8,128)S(1)} collective-permute-done((f32[16,32,32]{2,1,0:T(8,128)S(1)}, f32[16,32,32]{2,1,0:T(8,128)S(1)}, u32[]{:S(2)}, u32[]{:S(2)}) %collective-permute-start.14) | collective-permute-done | bytes 65568 | tf_op jit(solution)/shard_map/ppermute | solution.py:360
  243.8 3.1 %finish.1 = (f32[16,1024]{1,0:T(8,128)}, f32[16]{0:T(128)}) custom-call(s32[32]{0:T(128)S(1)} %add_bitcast_fusion.rows, f32[2,16,32,32]{3,2,1,0:T(8,128)S(1)} %get-tuple-element.52.refs_6_.here, f32[16,32,32]{2,1,0:T(8,128)S(1)} %collective-permute-done.14.there, f32[16,32,32]{2,1,0:T(8,128)S(1)} %shard_map.95.before, ...), custom_call_target="tpu_custom_call" | custom-call | tf_op jit(solution)/shard_map/finish/pallas_call | solution.py:299
  (112 shorter events, 46.4 us)
Async XLA Ops:
  3.3 24.4 %all-to-all-start = ((bf16[4,1,256,768]{3,2,1,0:T(8,128)(2,1)}), bf16[4,1,256,768]{3,2,1,0:T(8,128)(2,1)S(1)}, u32[]{:S(2)}, u32[]{:S(2)}) async-start(bf16[4,1,256,768]{3,2,1,0:T(8,128)(2,1)} %slice.64), calls=%async_computation | async-start | bytes 3145728 | tf_op jit(solution)/shard_map/all_to_all | solution.py:367
  27.7 28.8 %all-to-all-start.1 = ((bf16[4,1,256,768]{3,2,1,0:T(8,128)(2,1)}), bf16[4,1,256,768]{3,2,1,0:T(8,128)(2,1)}, u32[]{:S(2)}, u32[]{:S(2)}) async-start(bf16[4,1,256,768]{3,2,1,0:T(8,128)(2,1)} %slice.66), calls=%async_computation.1 | async-start | bytes 3145728 | tf_op jit(solution)/shard_map/all_to_all | solution.py:367
  36.6 76.8 %collective-permute-start.2 = (bf16[16,32,1536]{2,1,0:T(8,128)(2,1)}, bf16[16,32,1536]{2,1,0:T(8,128)(2,1)S(1)}, u32[]{:S(2)}, u32[]{:S(2)}) collective-permute-start(bf16[16,32,1536]{2,1,0:T(8,128)(2,1)} %get-tuple-element.35), channel_id=1, source_target_pairs={{0,2},{1,3},{2,0},{3,1},{4,6},{5,7},{6,4},{7,5},{8,10},{9,11},{10,... | collective-permute-start | bytes 4718600 | tf_op jit(solution)/shard_map/ppermute | solution.py:360
  39.9 36.2 %collective-permute-start.6 = (bf16[1,32,1536]{2,1,0:T(8,128)(2,1)S(1)}, bf16[1,32,1536]{2,1,0:T(8,128)(2,1)S(1)}, u32[]{:S(2)}, u32[]{:S(2)}) collective-permute-start(bf16[1,32,1536]{2,1,0:T(8,128)(2,1)S(1)} %slice.75), channel_id=1, source_target_pairs={{0,2},{1,3},{6,4},{7,5},{8,10},{9,11},{14,12},{15,13},{16,18},{17,... | collective-permute-start | bytes 294920 | tf_op jit(solution)/shard_map/ppermute | solution.py:383
  41.8 68.1 %collective-permute-start.3 = (bf16[16,32,1536]{2,1,0:T(8,128)(2,1)}, bf16[16,32,1536]{2,1,0:T(8,128)(2,1)}, u32[]{:S(2)}, u32[]{:S(2)}) collective-permute-start(bf16[16,32,1536]{2,1,0:T(8,128)(2,1)} %get-tuple-element.36), channel_id=1, source_target_pairs={{0,3},{1,2},{2,1},{3,0},{4,7},{5,6},{6,5},{7,4},{8,11},{9,10},{10,... | collective-permute-start | bytes 4718600 | tf_op jit(solution)/shard_map/ppermute | solution.py:360
  42.7 70.7 %collective-permute-start.1 = (bf16[16,32,1536]{2,1,0:T(8,128)(2,1)}, bf16[16,32,1536]{2,1,0:T(8,128)(2,1)}, u32[]{:S(2)}, u32[]{:S(2)}) collective-permute-start(bf16[16,32,1536]{2,1,0:T(8,128)(2,1)} %get-tuple-element.34), channel_id=1, source_target_pairs={{0,1},{1,0},{2,3},{3,2},{4,5},{5,4},{6,7},{7,6},{8,9},{9,8},{10,11... | collective-permute-start | bytes 4718600 | tf_op jit(solution)/shard_map/ppermute | solution.py:360
  53.0 78.6 %collective-permute-start.4 = (bf16[512,768]{1,0:T(8,128)(2,1)}, bf16[512,768]{1,0:T(8,128)(2,1)}, u32[]{:S(2)}, u32[]{:S(2)}) collective-permute-start(bf16[512,768]{1,0:T(8,128)(2,1)} %slice.85), channel_id=1, source_target_pairs={{0,6},{1,7},{2,4},{3,5},{4,2},{5,3},{6,0},{7,1},{8,14},{9,15},{10,... | collective-permute-start | bytes 2359304 | tf_op jit(solution)/shard_map/ppermute | solution.py:360
  61.4 52.0 %copy-start = (bf16[16,32,1536]{2,1,0:T(8,128)(2,1)S(1)}, bf16[16,32,1536]{2,1,0:T(8,128)(2,1)}, u32[]{:S(2)}) copy-start(bf16[16,32,1536]{2,1,0:T(8,128)(2,1)} %get-tuple-element.33.refs_0_) | copy-start | bytes 4718596
  76.1 70.5 %collective-permute-start.5 = (bf16[512,768]{1,0:T(8,128)(2,1)}, bf16[512,768]{1,0:T(8,128)(2,1)S(1)}, u32[]{:S(2)}, u32[]{:S(2)}) collective-permute-start(bf16[512,768]{1,0:T(8,128)(2,1)} %slice.86), channel_id=1, source_target_pairs={{0,6},{1,7},{2,4},{3,5},{4,2},{5,3},{6,0},{7,1},{8,14},{9,15},{10,... | collective-permute-start | bytes 2359304 | tf_op jit(solution)/shard_map/ppermute | solution.py:360
  109.9 43.0 %collective-permute-start = (s32[32]{0:T(128)S(1)}, s32[32]{0:T(128)S(1)}, u32[]{:S(2)}, u32[]{:S(2)}) collective-permute-start(s32[32]{0:T(128)S(1)} %copy-done.15), channel_id=1, source_target_pairs={{0,2},{1,3},{2,0},{3,1},{4,6},{5,7},{6,4},{7,5},{8,10},{9,11},{10,... | collective-permute-start | bytes 392 | tf_op jit(solution)/shard_map/ppermute | solution.py:360
  122.6 29.6 %copy-start.1 = (bf16[16,32,1024]{2,1,0:T(8,128)(2,1)}, bf16[16,32,1024]{2,1,0:T(8,128)(2,1)S(1)}, u32[]{:S(2)}) copy-start(bf16[16,32,1024]{2,1,0:T(8,128)(2,1)S(1)} %get-tuple-element.44.refs_0_) | copy-start | bytes 3145732
  122.6 45.8 %collective-permute-start.7 = (bf16[16,32,1024]{2,1,0:T(8,128)(2,1)}, bf16[16,32,1024]{2,1,0:T(8,128)(2,1)}, u32[]{:S(2)}, u32[]{:S(2)}) collective-permute-start(bf16[16,32,1024]{2,1,0:T(8,128)(2,1)} %get-tuple-element.45), channel_id=1, source_target_pairs={{0,1},{1,0},{2,3},{3,2},{4,5},{5,4},{6,7},{7,6},{8,9},{9,8},{10,11... | collective-permute-start | bytes 3145736 | tf_op jit(solution)/shard_map/ppermute | solution.py:360
  125.7 49.7 %collective-permute-start.9 = (bf16[128,768]{1,0:T(8,128)(2,1)}, bf16[128,768]{1,0:T(8,128)(2,1)}, u32[]{:S(2)}, u32[]{:S(2)}) collective-permute-start(bf16[128,768]{1,0:T(8,128)(2,1)} %get-tuple-element.69), channel_id=1, source_target_pairs={{0,6},{1,7},{2,4},{3,5},{4,2},{5,3},{6,0},{7,1},{8,14},{9,15},{10,... | collective-permute-start | bytes 589832 | tf_op jit(solution)/shard_map/ppermute | solution.py:360
  131.6 76.3 %collective-permute-start.12 = (bf16[256,768]{1,0:T(8,128)(2,1)}, bf16[256,768]{1,0:T(8,128)(2,1)}, u32[]{:S(2)}, u32[]{:S(2)}) collective-permute-start(bf16[256,768]{1,0:T(8,128)(2,1)} %slice.91), channel_id=1, source_target_pairs={{0,6},{1,7},{2,4},{3,5},{4,2},{5,3},{6,0},{7,1},{8,14},{9,15},{10,... | collective-permute-start | bytes 1179656 | tf_op jit(solution)/shard_map/ppermute | solution.py:360
  146.5 63.0 %collective-permute-start.13 = (bf16[256,768]{1,0:T(8,128)(2,1)}, bf16[256,768]{1,0:T(8,128)(2,1)}, u32[]{:S(2)}, u32[]{:S(2)}) collective-permute-start(bf16[256,768]{1,0:T(8,128)(2,1)} %slice.92), channel_id=1, source_target_pairs={{0,6},{1,7},{2,4},{3,5},{4,2},{5,3},{6,0},{7,1},{8,14},{9,15},{10,... | collective-permute-start | bytes 1179656 | tf_op jit(solution)/shard_map/ppermute | solution.py:360
  153.0 12.9 %collective-permute-start.8 = (bf16[16,32,512]{2,1,0:T(8,128)(2,1)}, bf16[16,32,512]{2,1,0:T(8,128)(2,1)}, u32[]{:S(2)}, u32[]{:S(2)}) collective-permute-start(bf16[16,32,512]{2,1,0:T(8,128)(2,1)} %get-tuple-element.47), channel_id=1, source_target_pairs={{0,1},{1,0},{2,3},{3,2},{4,5},{5,4},{6,7},{7,6},{8,9},{9,8},{10,11... | collective-permute-start | bytes 1572872 | tf_op jit(solution)/shard_map/ppermute | solution.py:360
  165.8 12.1 %collective-permute-start.10 = (bf16[128,768]{1,0:T(8,128)(2,1)}, bf16[128,768]{1,0:T(8,128)(2,1)S(1)}, u32[]{:S(2)}, u32[]{:S(2)}) collective-permute-start(bf16[128,768]{1,0:T(8,128)(2,1)} %get-tuple-element.67), channel_id=1, source_target_pairs={{0,6},{1,7},{2,4},{3,5},{4,2},{5,3},{6,0},{7,1},{8,14},{9,15},{10,... | collective-permute-start | bytes 589832 | tf_op jit(solution)/shard_map/ppermute | solution.py:360
  168.4 48.8 %collective-permute-start.17 = (bf16[128,768]{1,0:T(8,128)(2,1)}, bf16[128,768]{1,0:T(8,128)(2,1)S(1)}, u32[]{:S(2)}, u32[]{:S(2)}) collective-permute-start(bf16[128,768]{1,0:T(8,128)(2,1)} %get-tuple-element.68), channel_id=1, source_target_pairs={{0,6},{1,7},{2,4},{3,5},{4,2},{5,3},{6,0},{7,1},{8,14},{9,15},{10,... | collective-permute-start | bytes 589832 | tf_op jit(solution)/shard_map/ppermute | solution.py:360
  175.4 43.3 %collective-permute-start.18 = (bf16[128,768]{1,0:T(8,128)(2,1)S(1)}, bf16[128,768]{1,0:T(8,128)(2,1)S(1)}, u32[]{:S(2)}, u32[]{:S(2)}) collective-permute-start(bf16[128,768]{1,0:T(8,128)(2,1)S(1)} %copy-done.13), channel_id=1, source_target_pairs={{0,6},{1,7},{2,4},{3,5},{4,2},{5,3},{6,0},{7,1},{8,14},{9,15},{10,... | collective-permute-start | bytes 589832 | tf_op jit(solution)/shard_map/ppermute | solution.py:360
  178.0 41.5 %collective-permute-start.19 = (bf16[8,32,384]{2,1,0:T(8,128)(2,1)S(1)}, bf16[8,32,384]{2,1,0:T(8,128)(2,1)S(1)}, u32[]{:S(2)}, u32[]{:S(2)}) collective-permute-start(bf16[8,32,384]{2,1,0:T(8,128)(2,1)S(1)} %copy-done.12), channel_id=1, source_target_pairs={{0,2},{1,3},{2,0},{3,1},{4,6},{5,7},{6,4},{7,5},{8,10},{9,11},{10,... | collective-permute-start | bytes 589832 | tf_op jit(solution)/shard_map/ppermute | solution.py:360
  208.0 5.1 %collective-permute-start.11 = (bf16[16,32,128]{2,1,0:T(8,128)(2,1)S(1)}, bf16[16,32,128]{2,1,0:T(8,128)(2,1)S(1)}, u32[]{:S(2)}, u32[]{:S(2)}) collective-permute-start(bf16[16,32,128]{2,1,0:T(8,128)(2,1)S(1)} %get-tuple-element.50), channel_id=1, source_target_pairs={{0,1},{1,0},{2,3},{3,2},{4,5},{5,4},{6,7},{7,6},{8,9},{9,8},{10,11... | collective-permute-start | bytes 393224 | tf_op jit(solution)/shard_map/ppermute | solution.py:360
  209.6 25.8 %collective-permute-start.15 = (bf16[16,32,512]{2,1,0:T(8,128)(2,1)S(1)}, bf16[16,32,512]{2,1,0:T(8,128)(2,1)S(1)}, u32[]{:S(2)}, u32[]{:S(2)}) collective-permute-start(bf16[16,32,512]{2,1,0:T(8,128)(2,1)S(1)} %get-tuple-element.53), channel_id=1, source_target_pairs={{0,2},{1,3},{2,0},{3,1},{4,6},{5,7},{6,4},{7,5},{8,10},{9,11},{10,... | collective-permute-start | bytes 1572872 | tf_op jit(solution)/shard_map/ppermute | solution.py:360
  213.1 15.4 %collective-permute-start.20 = (bf16[8,32,384]{2,1,0:T(8,128)(2,1)S(1)}, bf16[8,32,384]{2,1,0:T(8,128)(2,1)S(1)}, u32[]{:S(2)}, u32[]{:S(2)}) collective-permute-start(bf16[8,32,384]{2,1,0:T(8,128)(2,1)S(1)} %copy-done.11), channel_id=1, source_target_pairs={{0,3},{1,2},{2,1},{3,0},{4,7},{5,6},{6,5},{7,4},{8,11},{9,10},{10,... | collective-permute-start | bytes 589832 | tf_op jit(solution)/shard_map/ppermute | solution.py:360
  217.2 12.3 %collective-permute-start.21 = (bf16[8,32,256]{2,1,0:T(8,128)(2,1)S(1)}, bf16[8,32,256]{2,1,0:T(8,128)(2,1)S(1)}, u32[]{:S(2)}, u32[]{:S(2)}) collective-permute-start(bf16[8,32,256]{2,1,0:T(8,128)(2,1)S(1)} %get-tuple-element.56), channel_id=1, source_target_pairs={{0,1},{1,0},{2,3},{3,2},{4,5},{5,4},{6,7},{7,6},{8,9},{9,8},{10,11... | collective-permute-start | bytes 393224 | tf_op jit(solution)/shard_map/ppermute | solution.py:360
  218.8 12.6 %collective-permute-start.22 = (bf16[8,32,256]{2,1,0:T(8,128)(2,1)S(1)}, bf16[8,32,256]{2,1,0:T(8,128)(2,1)S(1)}, u32[]{:S(2)}, u32[]{:S(2)}) collective-permute-start(bf16[8,32,256]{2,1,0:T(8,128)(2,1)S(1)} %get-tuple-element.57), channel_id=1, source_target_pairs={{0,2},{1,3},{2,0},{3,1},{4,6},{5,7},{6,4},{7,5},{8,10},{9,11},{10,... | collective-permute-start | bytes 393224 | tf_op jit(solution)/shard_map/ppermute | solution.py:360
  219.5 14.7 %collective-permute-start.16 = (bf16[16,32,128]{2,1,0:T(8,128)(2,1)S(1)}, bf16[16,32,128]{2,1,0:T(8,128)(2,1)S(1)}, u32[]{:S(2)}, u32[]{:S(2)}) collective-permute-start(bf16[16,32,128]{2,1,0:T(8,128)(2,1)S(1)} %get-tuple-element.54), channel_id=1, source_target_pairs={{0,2},{1,3},{2,0},{3,1},{4,6},{5,7},{6,4},{7,5},{8,10},{9,11},{10,... | collective-permute-start | bytes 393224 | tf_op jit(solution)/shard_map/ppermute | solution.py:360
  220.8 15.3 %copy-start.6 = (bf16[16,32,512]{2,1,0:T(8,128)(2,1)S(1)}, bf16[16,32,512]{2,1,0:T(8,128)(2,1)}, u32[]{:S(2)}) copy-start(bf16[16,32,512]{2,1,0:T(8,128)(2,1)} %copy-done.4) | copy-start | bytes 1572868
  228.5 10.1 %collective-permute-start.23 = (bf16[8,32,256]{2,1,0:T(8,128)(2,1)S(1)}, bf16[8,32,256]{2,1,0:T(8,128)(2,1)S(1)}, u32[]{:S(2)}, u32[]{:S(2)}) collective-permute-start(bf16[8,32,256]{2,1,0:T(8,128)(2,1)S(1)} %get-tuple-element.58), channel_id=1, source_target_pairs={{0,3},{1,2},{2,1},{3,0},{4,7},{5,6},{6,5},{7,4},{8,11},{9,10},{10,... | collective-permute-start | bytes 393224 | tf_op jit(solution)/shard_map/ppermute | solution.py:360
  229.5 9.2 %collective-permute-start.24 = (bf16[8,32,128]{2,1,0:T(8,128)(2,1)S(1)}, bf16[8,32,128]{2,1,0:T(8,128)(2,1)S(1)}, u32[]{:S(2)}, u32[]{:S(2)}) collective-permute-start(bf16[8,32,128]{2,1,0:T(8,128)(2,1)S(1)} %get-tuple-element.59), channel_id=1, source_target_pairs={{0,1},{1,0},{2,3},{3,2},{4,5},{5,4},{6,7},{7,6},{8,9},{9,8},{10,11... | collective-permute-start | bytes 196616 | tf_op jit(solution)/shard_map/ppermute | solution.py:360
  231.4 7.3 %collective-permute-start.25 = (bf16[8,32,128]{2,1,0:T(8,128)(2,1)S(1)}, bf16[8,32,128]{2,1,0:T(8,128)(2,1)S(1)}, u32[]{:S(2)}, u32[]{:S(2)}) collective-permute-start(bf16[8,32,128]{2,1,0:T(8,128)(2,1)S(1)} %get-tuple-element.60), channel_id=1, source_target_pairs={{0,2},{1,3},{2,0},{3,1},{4,6},{5,7},{6,4},{7,5},{8,10},{9,11},{10,... | collective-permute-start | bytes 196616 | tf_op jit(solution)/shard_map/ppermute | solution.py:360
  234.2 5.9 %collective-permute-start.26 = (bf16[8,32,128]{2,1,0:T(8,128)(2,1)S(1)}, bf16[8,32,128]{2,1,0:T(8,128)(2,1)S(1)}, u32[]{:S(2)}, u32[]{:S(2)}) collective-permute-start(bf16[8,32,128]{2,1,0:T(8,128)(2,1)S(1)} %get-tuple-element.61), channel_id=1, source_target_pairs={{0,3},{1,2},{2,1},{3,0},{4,7},{5,6},{6,5},{7,4},{8,11},{9,10},{10,... | collective-permute-start | bytes 196616 | tf_op jit(solution)/shard_map/ppermute | solution.py:360
  235.4 8.4 %collective-permute-start.14 = (f32[16,32,32]{2,1,0:T(8,128)S(1)}, f32[16,32,32]{2,1,0:T(8,128)S(1)}, u32[]{:S(2)}, u32[]{:S(2)}) collective-permute-start(f32[16,32,32]{2,1,0:T(8,128)S(1)} %slice_bitcast_fusion), channel_id=1, source_target_pairs={{0,2},{1,3},{2,0},{3,1},{4,6},{5,7},{6,4},{7,5},{8,10},{9,11},{10,... | collective-permute-start | bytes 196616 | tf_op jit(solution)/shard_map/ppermute | solution.py:360
  (16 other events, 63.1 us)

commit v11 on v10

--- a/solution.py
+++ b/solution.py
@@ -340,7 +340,7 @@
 
 
 def chunk_spans(fit_rows):
-    sizes = (fit_rows // 2, fit_rows // 8, fit_rows // 4, fit_rows // 8)
+    sizes = (fit_rows // 2, fit_rows // 4, fit_rows // 8, fit_rows // 8)
     return [(sum(sizes[:c]), size) for c, size in enumerate(sizes)]
 
 
@@ -377,18 +377,22 @@
     coef = pno_coef.reshape(side_count, pno_count, dom_count)
     blocks = [None] * group
     packed = pack(own_orbs, place, coef, group, capacity, tuple(range(inner, group)))
+    own = (region * orb_count + me).astype(jnp.uint32)
+    own_offset = lax.dynamic_slice_in_dim(fit_offset, own, 1)[0]
+    first_row = (fit_rows - own_offset).astype(jnp.uint32)
+    later, *packed = lax.optimization_barrier((raw_ints, *packed))
     for m in range(inner, group):
         blocks[m] = across(packed[m - inner], m)
     pairs = [(i, i ^ inner) for i in range(orb_count) if i // inner in (0, 3)]
     guard = lax.ppermute(packed[0][:1], "orb", pairs)
+    twice = jnp.concatenate([fit_inverse[0], fit_inverse[0]])
+    turned = lax.dynamic_slice_in_dim(twice, first_row, fit_rows)
+    raw_parts.append(exchange(later, 1))
     packed = pack(own_orbs, place, coef, group, capacity, tuple(range(inner)))
     blocks[0] = packed[0]
     for m in range(1, inner):
         blocks[m] = across(packed[m], m)
-    later, blocks[0] = lax.optimization_barrier((raw_ints, blocks[0]))
     raw_parts.append(exchange(later, 1))
-    own_offset = fit_offset[region * orb_count + me]
-    turned = jnp.roll(fit_inverse[0], own_offset, axis=0)
     mate_orbs = across(own_orbs, inner)
     orb_total = occ_energy.shape[0]
 
@@ -408,9 +412,10 @@
         product = jnp.dot(turned, raw_parts[k], preferred_element_type=jnp.float32)
         fitted.append(product.astype(jnp.bfloat16))
         mirror(0, k)
-    for c in range(1, len(spans)):
-        mirror(c, 0)
-        mirror(c, 1)
+        mirror(1, k)
+        mirror(2, k)
+    for k in range(2):
+        mirror(3, k)
 
     energies, levels, named, fitted[1] = lax.optimization_barrier(
         (occ_energy, pno_energy, own_orbs, fitted[1])
@@ -457,10 +462,10 @@
     offsets = pick(fit_offset, orbs.reshape(2 * side_count)).reshape(2, side_count)
     others[0], here = pass_on(0, jnp.zeros((8, 128), jnp.float32), [])
     far[1] = project_far(1, [here])
-    far[2] = project_far(2, [far[1][0]])
-    others[1], here = pass_on(1, here, [far[2][0]])
+    others[1], here = pass_on(1, here, [])
     there = across(here[1], inner)
-    far[3] = project_far(3, [here])
+    far[2] = project_far(2, [here])
+    far[3] = project_far(3, [far[2][0]])
     body = mixed(rows_home, offsets, near, far[0] + far[1], others, spans[:2], margin, [far[3][0]])
     amplitude, energy = finish(
         rows_all,

time: 248 us -> 243 us (0.980)
  waiting for transfers between devices: 92.4 us -> 89.5 us
    ppermute x1, waiting for transfers between devices: 12.1 us -> 9.04 us  [on_device(): guard = lax.ppermute(packed[0][:1], 'orb', pairs)]
    unnamed x39 -> x37, local copies, waits for them, and re-layouts: 8.3 us -> 9.77 us
  transfers between devices with their start and end apart: 29 -> 29, of which waited for: 11 -> 10; matrix products, arithmetic and copies ran while one was open for 10% -> 9% of each run, Pallas kernels for 14% -> 13%
where the time goes in v11:
time: 243 us; the launch traced here: 242 us
  waiting for transfers between devices  89.5 us (37%)
  starting transfers between devices  80 us (33%)
  Pallas kernels  37.4 us (15%)
  local copies, waits for them, and re-layouts  22.9 us (9%)
  matrix products  9.55 us (4%)
    ppermute x26, starting transfers between devices, across(): return lax.ppermute(array, 'orb', [(i, i ^ mask) for i in range(orb_count)])  69.2 us
    ppermute x26, waiting for transfers between devices, across(): return lax.ppermute(array, 'orb', [(i, i ^ mask) for i in range(orb_count)])  66.5 us
    pallas_call x5, Pallas kernels, project(): pl.pallas_call(kernel, grid=(1,), out_shape=(jax.ShapeDtypeStruct((lines,...  17.1 us
    all_to_all x2, waiting for transfers between devices, exchange(): lax.all_to_all(array[:, :, :, k * half:(k + 1) * half], 'aux', split_axis...  13.9 us
    unnamed x37, local copies, waits for them, and re-layouts  9.77 us
    dot_general x2, matrix products, on_device(): product = jnp.dot(turned, raw_parts[k], preferred_element_type=jnp.float32)  9.55 us
    ppermute x1, waiting for transfers between devices, on_device(): guard = lax.ppermute(packed[0][:1], 'orb', pairs)  9.04 us
    all_to_all x2, starting transfers between devices, exchange(): lax.all_to_all(array[:, :, :, k * half:(k + 1) * half], 'aux', split_axis...  8.83 us
  transfers between devices with their start and end apart: 29, of which 10 were waited for; matrix products, arithmetic and copies ran while one was open for 9% of the time, Pallas kernels for 13%

profile of v11, /device:TPU:0, one launch (start us, length us, event | category | flops | bytes accessed | tf_op | source)
XLA Modules:
  0.0 242.3 jit_solution(17677495651455347662)
XLA Ops:
  0.6 2.7 %slice.64 = bf16[4,1,256,768]{3,2,1,0:T(8,128)(2,1)} slice(bf16[4,1,256,1536]{3,2,1,0:T(8,128)(2,1)} %param.7), slice={[0:4], [0:1], [0:256], [0:768]} | slice | bytes 3145728 | tf_op jit(solution)/shard_map/slice | solution.py:368
  3.3 4.5 %all-to-all-start = ((bf16[4,1,256,768]{3,2,1,0:T(8,128)(2,1)}), bf16[4,1,256,768]{3,2,1,0:T(8,128)(2,1)}, u32[]{:S(2)}, u32[]{:S(2)}) async-start(bf16[4,1,256,768]{3,2,1,0:T(8,128)(2,1)} %slice.64), calls=%async_computation | async-start | bytes 3145728 | tf_op jit(solution)/shard_map/all_to_all | solution.py:367
  9.1 4.3 %shard_map.87 = (bf16[16,32,1536]{2,1,0:T(8,128)(2,1)}, bf16[16,32,1536]{2,1,0:T(8,128)(2,1)}) custom-call(s32[32]{0:T(128)} %reshape.73.orbs, s32[2]{0:T(128)} %pad_add_fusion.1.place, bf16[32,32,1536]{2,1,0:T(8,128)(2,1)} %bitcast.16), custom_call_target="tpu_custom_call" | custom-call | bytes 9437184 | tf_op jit(solution)/shard_map/pallas_call | solution.py:59
  14.7 13.9 %all-to-all-done = bf16[4,1,256,768]{3,2,1,0:T(8,128)(2,1)} async-done(((bf16[4,1,256,768]{3,2,1,0:T(8,128)(2,1)}), bf16[4,1,256,768]{3,2,1,0:T(8,128)(2,1)}, u32[]{:S(2)}, u32[]{:S(2)}) %all-to-all-start) | async-done | bytes 1572896 | tf_op jit(solution)/shard_map/all_to_all | solution.py:367
  28.6 4.4 %all-to-all-start.1 = ((bf16[4,1,256,768]{3,2,1,0:T(8,128)(2,1)}), bf16[4,1,256,768]{3,2,1,0:T(8,128)(2,1)}, u32[]{:S(2)}, u32[]{:S(2)}) async-start(bf16[4,1,256,768]{3,2,1,0:T(8,128)(2,1)} %slice.66), calls=%async_computation.1 | async-start | bytes 3145728 | tf_op jit(solution)/shard_map/all_to_all | solution.py:367
  32.9 2.4 %collective-permute-start.2 = (bf16[16,32,1536]{2,1,0:T(8,128)(2,1)}, bf16[16,32,1536]{2,1,0:T(8,128)(2,1)S(1)}, u32[]{:S(2)}, u32[]{:S(2)}) collective-permute-start(bf16[16,32,1536]{2,1,0:T(8,128)(2,1)} %get-tuple-element.37), channel_id=1, source_target_pairs={{0,2},{1,3},{2,0},{3,1},{4,6},{5,7},{6,4},{7,5},{8,10},{9,11},{10,... | collective-permute-start | bytes 4718600 | tf_op jit(solution)/shard_map/ppermute | solution.py:360
  39.1 4.3 %shard_map.86 = (bf16[16,32,1536]{2,1,0:T(8,128)(2,1)}, bf16[16,32,1536]{2,1,0:T(8,128)(2,1)}) custom-call(s32[32]{0:T(128)} %reshape.73.orbs, s32[2]{0:T(128)} %pad_add_fusion.1.place, bf16[32,32,1536]{2,1,0:T(8,128)(2,1)} %bitcast.17), custom_call_target="tpu_custom_call" | custom-call | bytes 9437184 | tf_op jit(solution)/shard_map/pallas_call | solution.py:59
  46.0 4.8 %convolution_convert_fusion.1.refs_4_ = bf16[1024,768]{1,0:T(8,128)(2,1)S(1)} fusion(bf16[1024,768]{1,0:T(8,128)(2,1)} %bitcast.5, u32[]{:T(128)} %bitcast.4, bf16[1024,1024]{1,0:T(8,128)(2,1)} %bitcast.22), kind=kOutput, calls=%fused_computation.4 | convolution fusion | flops 1615593472 | bytes 5242884 | tf_op jit(solution)/shard_map/dot_general | solution.py:412
  52.9 3.6 %collective-permute-start.4 = (bf16[512,768]{1,0:T(8,128)(2,1)}, bf16[512,768]{1,0:T(8,128)(2,1)}, u32[]{:S(2)}, u32[]{:S(2)}) collective-permute-start(bf16[512,768]{1,0:T(8,128)(2,1)} %slice.85), channel_id=1, source_target_pairs={{0,6},{1,7},{2,4},{3,5},{4,2},{5,3},{6,0},{7,1},{8,14},{9,15},{10,... | collective-permute-start | bytes 2359304 | tf_op jit(solution)/shard_map/ppermute | solution.py:360
  56.5 4.8 %convolution_convert_fusion.refs_5_ = bf16[1024,768]{1,0:T(8,128)(2,1)S(1)} fusion(bf16[1024,768]{1,0:T(8,128)(2,1)} %bitcast.6, u32[]{:T(128)} %bitcast.4, bf16[1024,1024]{1,0:T(8,128)(2,1)} %bitcast.23), kind=kOutput, calls=%fused_computation.3 | convolution fusion | flops 1615593472 | bytes 5242884 | tf_op jit(solution)/shard_map/dot_general | solution.py:412
  63.4 9.0 %collective-permute-done.6.refs_7_ = bf16[1,32,1536]{2,1,0:T(8,128)(2,1)S(1)} collective-permute-done((bf16[1,32,1536]{2,1,0:T(8,128)(2,1)S(1)}, bf16[1,32,1536]{2,1,0:T(8,128)(2,1)S(1)}, u32[]{:S(2)}, u32[]{:S(2)}) %collective-permute-start.6) | collective-permute-done | bytes 98336 | tf_op jit(solution)/shard_map/ppermute | solution.py:387
  72.5 2.5 %collective-permute-start.5 = (bf16[512,768]{1,0:T(8,128)(2,1)}, bf16[512,768]{1,0:T(8,128)(2,1)}, u32[]{:S(2)}, u32[]{:S(2)}) collective-permute-start(bf16[512,768]{1,0:T(8,128)(2,1)} %slice.86), channel_id=1, source_target_pairs={{0,6},{1,7},{2,4},{3,5},{4,2},{5,3},{6,0},{7,1},{8,14},{9,15},{10,... | collective-permute-start | bytes 2359304 | tf_op jit(solution)/shard_map/ppermute | solution.py:360
  75.6 30.7 %collective-permute-done.3.refs_3_ = bf16[16,32,1536]{2,1,0:T(8,128)(2,1)S(1)} collective-permute-done((bf16[16,32,1536]{2,1,0:T(8,128)(2,1)}, bf16[16,32,1536]{2,1,0:T(8,128)(2,1)S(1)}, u32[]{:S(2)}, u32[]{:S(2)}) %collective-permute-start.3) | collective-permute-done | bytes 1572896 | tf_op jit(solution)/shard_map/ppermute | solution.py:360
  106.3 3.3 %collective-permute-start = (s32[32]{0:T(128)S(1)}, s32[32]{0:T(128)S(1)}, u32[]{:S(2)}, u32[]{:S(2)}) collective-permute-start(s32[32]{0:T(128)S(1)} %copy-done.14), channel_id=1, source_target_pairs={{0,2},{1,3},{2,0},{3,1},{4,6},{5,7},{6,4},{7,5},{8,10},{9,11},{10,... | collective-permute-start | bytes 392 | tf_op jit(solution)/shard_map/ppermute | solution.py:360
  109.7 3.9 %collective-permute-done.1.refs_1_ = bf16[16,32,1536]{2,1,0:T(8,128)(2,1)} collective-permute-done((bf16[16,32,1536]{2,1,0:T(8,128)(2,1)}, bf16[16,32,1536]{2,1,0:T(8,128)(2,1)}, u32[]{:S(2)}, u32[]{:S(2)}) %collective-permute-start.1) | collective-permute-done | bytes 1572896 | tf_op jit(solution)/shard_map/ppermute | solution.py:360
  117.8 6.2 %shard_map.89 = (bf16[16,32,1024]{2,1,0:T(8,128)(2,1)S(1)}, bf16[16,32,1024]{2,1,0:T(8,128)(2,1)}) custom-call(bf16[16,32,1536]{2,1,0:T(8,128)(2,1)S(1)} %copy-done, bf16[16,32,1536]{2,1,0:T(8,128)(2,1)} %collective-permute-done.1.refs_1_, bf16[16,32,1536]{2,1,0:T(8,128)(2,1)S(1)} %collective-permute-done.2.refs_2_, ...), custom_call_target="tpu_custom_call" | custom-call | flops 3221225472 | bytes 3145728 | tf_op jit(solution)/shard_map/pallas_call | solution.py:124
  126.7 3.6 %collective-permute-start.9 = (bf16[256,768]{1,0:T(8,128)(2,1)}, bf16[256,768]{1,0:T(8,128)(2,1)}, u32[]{:S(2)}, u32[]{:S(2)}) collective-permute-start(bf16[256,768]{1,0:T(8,128)(2,1)} %slice.89), channel_id=1, source_target_pairs={{0,6},{1,7},{2,4},{3,5},{4,2},{5,3},{6,0},{7,1},{8,14},{9,15},{10,... | collective-permute-start | bytes 1179656 | tf_op jit(solution)/shard_map/ppermute | solution.py:360
  130.6 12.5 %collective-permute-done.5.refs_5_ = bf16[512,768]{1,0:T(8,128)(2,1)} collective-permute-done((bf16[512,768]{1,0:T(8,128)(2,1)}, bf16[512,768]{1,0:T(8,128)(2,1)}, u32[]{:S(2)}, u32[]{:S(2)}) %collective-permute-start.5) | collective-permute-done | bytes 786464 | tf_op jit(solution)/shard_map/ppermute | solution.py:360
  143.1 4.2 %shard_map.88 = (bf16[16,32,512]{2,1,0:T(8,128)(2,1)S(1)}, bf16[16,32,512]{2,1,0:T(8,128)(2,1)}) custom-call(bf16[16,32,1536]{2,1,0:T(8,128)(2,1)S(1)} %copy-done, bf16[16,32,1536]{2,1,0:T(8,128)(2,1)} %collective-permute-done.1.refs_1_, bf16[16,32,1536]{2,1,0:T(8,128)(2,1)S(1)} %collective-permute-done.2.refs_2_, ...), custom_call_target="tpu_custom_call" | custom-call | flops 1610612736 | bytes 3145728 | tf_op jit(solution)/shard_map/pallas_call | solution.py:124
  150.2 11.0 %collective-permute-done.8.refs_3_ = bf16[16,32,512]{2,1,0:T(8,128)(2,1)} collective-permute-done((bf16[16,32,512]{2,1,0:T(8,128)(2,1)}, bf16[16,32,512]{2,1,0:T(8,128)(2,1)}, u32[]{:S(2)}, u32[]{:S(2)}) %collective-permute-start.8) | collective-permute-done | bytes 524320 | tf_op jit(solution)/shard_map/ppermute | solution.py:360
  163.4 3.4 %shard_map.90 = (bf16[16,32,512]{2,1,0:T(8,128)(2,1)S(1)}, f32[2,16,32,32]{3,2,1,0:T(8,128)S(1)}) custom-call(s32[2,32]{1,0:T(2,128)S(1)} %add_select_fusion.1.rows, s32[2,32]{1,0:T(2,128)S(1)} %reshape.75.offsets, f32[8,128]{1,0:T(8,128)S(1)} %broadcast_in_dim.75.before, bf16[16,32,1024]{2,1,0:T(8,128)(2,1)S(1)} %copy-done.3, ...), custom_call_target="tpu_custom_call" | custom-call | tf_op jit(solution)/shard_map/pallas_call | solution.py:200
  166.9 2.4 %shard_map.91 = (bf16[16,32,256]{2,1,0:T(8,128)(2,1)S(1)}, bf16[16,32,256]{2,1,0:T(8,128)(2,1)S(1)}) custom-call(bf16[16,32,1536]{2,1,0:T(8,128)(2,1)S(1)} %copy-done.1, bf16[16,32,1536]{2,1,0:T(8,128)(2,1)} %collective-permute-done.1.refs_1_, bf16[16,32,1536]{2,1,0:T(8,128)(2,1)S(1)} %collective-permute-done.2.refs_2_, ...), custom_call_target="tpu_custom_call" | custom-call | flops 805306368 | bytes 3145728 | tf_op jit(solution)/shard_map/pallas_call | solution.py:124
  173.7 2.1 collective-permute-start.15
  181.8 24.7 %collective-permute-start.19 = (bf16[8,32,256]{2,1,0:T(8,128)(2,1)S(1)}, bf16[8,32,256]{2,1,0:T(8,128)(2,1)S(1)}, u32[]{:S(2)}, u32[]{:S(2)}) collective-permute-start(bf16[8,32,256]{2,1,0:T(8,128)(2,1)S(1)} %slice.83), channel_id=1, source_target_pairs={{0,2},{1,3},{2,0},{3,1},{4,6},{5,7},{6,4},{7,5},{8,10},{9,11},{10,... | collective-permute-start | bytes 393224 | tf_op jit(solution)/shard_map/ppermute | solution.py:360
  206.5 2.8 %shard_map.92 = (bf16[16,32,256]{2,1,0:T(8,128)(2,1)S(1)}, f32[2,16,32,32]{3,2,1,0:T(8,128)S(1)}) custom-call(s32[2,32]{1,0:T(2,128)S(1)} %add_select_fusion.1.rows, s32[2,32]{1,0:T(2,128)S(1)} %reshape.75.offsets, f32[2,16,32,32]{3,2,1,0:T(8,128)S(1)} %get-tuple-element.50.refs_6_.before, bf16[16,32,1024]{2,1,0:T(8,128)(2,1)S(1)} %copy-done.4, ...), custom_call_target="tpu_custom_call" | custom-call | tf_op jit(solution)/shard_map/pallas_call | solution.py:200
  209.3 5.5 %collective-permute-start.20 = (bf16[8,32,256]{2,1,0:T(8,128)(2,1)S(1)}, bf16[8,32,256]{2,1,0:T(8,128)(2,1)S(1)}, u32[]{:S(2)}, u32[]{:S(2)}) collective-permute-start(bf16[8,32,256]{2,1,0:T(8,128)(2,1)S(1)} %slice.84), channel_id=1, source_target_pairs={{0,3},{1,2},{2,1},{3,0},{4,7},{5,6},{6,5},{7,4},{8,11},{9,10},{10,... | collective-permute-start | bytes 393224 | tf_op jit(solution)/shard_map/ppermute | solution.py:360
  220.6 2.2 shard_map.94
  224.8 3.0 %collective-permute-start.23 = (bf16[8,32,128]{2,1,0:T(8,128)(2,1)S(1)}, bf16[8,32,128]{2,1,0:T(8,128)(2,1)S(1)}, u32[]{:S(2)}, u32[]{:S(2)}) collective-permute-start(bf16[8,32,128]{2,1,0:T(8,128)(2,1)S(1)} %get-tuple-element.60), channel_id=1, source_target_pairs={{0,3},{1,2},{2,1},{3,0},{4,7},{5,6},{6,5},{7,4},{8,11},{9,10},{10,... | collective-permute-start | bytes 196616 | tf_op jit(solution)/shard_map/ppermute | solution.py:360
  228.3 3.5 %collective-permute-done.14.refs_7_ = bf16[16,32,256]{2,1,0:T(8,128)(2,1)S(1)} collective-permute-done((bf16[16,32,256]{2,1,0:T(8,128)(2,1)S(1)}, bf16[16,32,256]{2,1,0:T(8,128)(2,1)S(1)}, u32[]{:S(2)}, u32[]{:S(2)}) %collective-permute-start.14) | collective-permute-done | bytes 262176 | tf_op jit(solution)/shard_map/ppermute | solution.py:360
  233.9 2.5 %shard_map.95.before = f32[16,32,32]{2,1,0:T(8,128)S(1)} custom-call(s32[2,32]{1,0:T(2,128)S(1)} %get-tuple-element.66.rows, s32[2,32]{1,0:T(2,128)S(1)} %reshape.75.offsets, bf16[16,32,1024]{2,1,0:T(8,128)(2,1)S(1)} %copy-done.4, bf16[16,32,1024]{2,1,0:T(8,128)(2,1)} %collective-permute-done.7.refs_1_, bf16[16,32,512]{2,1,0:T(8,128)(2,1)S(1)} %copy-done.7, ...), custom_call_target="tpu_custom_call" | custom-call | tf_op jit(solution)/shard_map/pallas_call | solution.py:322
  237.0 2.3 collective-permute-done.12.there
  239.3 3.0 %finish.1 = (f32[16,1024]{1,0:T(8,128)}, f32[16]{0:T(128)}) custom-call(s32[32]{0:T(128)S(1)} %add_bitcast_fusion.rows, f32[2,16,32,32]{3,2,1,0:T(8,128)S(1)} %get-tuple-element.53.refs_6_.here, f32[16,32,32]{2,1,0:T(8,128)S(1)} %collective-permute-done.12.there, f32[16,32,32]{2,1,0:T(8,128)S(1)} %shard_map.95.before, ...), custom_call_target="tpu_custom_call" | custom-call | tf_op jit(solution)/shard_map/finish/pallas_call | solution.py:299
  (110 shorter events, 46.8 us)
Async XLA Ops:
  3.3 25.3 %all-to-all-start = ((bf16[4,1,256,768]{3,2,1,0:T(8,128)(2,1)}), bf16[4,1,256,768]{3,2,1,0:T(8,128)(2,1)}, u32[]{:S(2)}, u32[]{:S(2)}) async-start(bf16[4,1,256,768]{3,2,1,0:T(8,128)(2,1)} %slice.64), calls=%async_computation | async-start | bytes 3145728 | tf_op jit(solution)/shard_map/all_to_all | solution.py:367
  28.6 27.9 %all-to-all-start.1 = ((bf16[4,1,256,768]{3,2,1,0:T(8,128)(2,1)}), bf16[4,1,256,768]{3,2,1,0:T(8,128)(2,1)}, u32[]{:S(2)}, u32[]{:S(2)}) async-start(bf16[4,1,256,768]{3,2,1,0:T(8,128)(2,1)} %slice.66), calls=%async_computation.1 | async-start | bytes 3145728 | tf_op jit(solution)/shard_map/all_to_all | solution.py:367
  32.9 76.7 %collective-permute-start.2 = (bf16[16,32,1536]{2,1,0:T(8,128)(2,1)}, bf16[16,32,1536]{2,1,0:T(8,128)(2,1)S(1)}, u32[]{:S(2)}, u32[]{:S(2)}) collective-permute-start(bf16[16,32,1536]{2,1,0:T(8,128)(2,1)} %get-tuple-element.37), channel_id=1, source_target_pairs={{0,2},{1,3},{2,0},{3,1},{4,6},{5,7},{6,4},{7,5},{8,10},{9,11},{10,... | collective-permute-start | bytes 4718600 | tf_op jit(solution)/shard_map/ppermute | solution.py:360
  36.3 36.2 %collective-permute-start.6 = (bf16[1,32,1536]{2,1,0:T(8,128)(2,1)S(1)}, bf16[1,32,1536]{2,1,0:T(8,128)(2,1)S(1)}, u32[]{:S(2)}, u32[]{:S(2)}) collective-permute-start(bf16[1,32,1536]{2,1,0:T(8,128)(2,1)S(1)} %slice.75), channel_id=1, source_target_pairs={{0,2},{1,3},{6,4},{7,5},{8,10},{9,11},{14,12},{15,13},{16,18},{17,... | collective-permute-start | bytes 294920 | tf_op jit(solution)/shard_map/ppermute | solution.py:387
  38.2 68.1 %collective-permute-start.3 = (bf16[16,32,1536]{2,1,0:T(8,128)(2,1)}, bf16[16,32,1536]{2,1,0:T(8,128)(2,1)S(1)}, u32[]{:S(2)}, u32[]{:S(2)}) collective-permute-start(bf16[16,32,1536]{2,1,0:T(8,128)(2,1)} %get-tuple-element.38), channel_id=1, source_target_pairs={{0,3},{1,2},{2,1},{3,0},{4,7},{5,6},{6,5},{7,4},{8,11},{9,10},{10,... | collective-permute-start | bytes 4718600 | tf_op jit(solution)/shard_map/ppermute | solution.py:360
  43.3 70.2 %collective-permute-start.1 = (bf16[16,32,1536]{2,1,0:T(8,128)(2,1)}, bf16[16,32,1536]{2,1,0:T(8,128)(2,1)}, u32[]{:S(2)}, u32[]{:S(2)}) collective-permute-start(bf16[16,32,1536]{2,1,0:T(8,128)(2,1)} %get-tuple-element.34), channel_id=1, source_target_pairs={{0,1},{1,0},{2,3},{3,2},{4,5},{5,4},{6,7},{7,6},{8,9},{9,8},{10,11... | collective-permute-start | bytes 4718600 | tf_op jit(solution)/shard_map/ppermute | solution.py:360
  52.9 77.5 %collective-permute-start.4 = (bf16[512,768]{1,0:T(8,128)(2,1)}, bf16[512,768]{1,0:T(8,128)(2,1)}, u32[]{:S(2)}, u32[]{:S(2)}) collective-permute-start(bf16[512,768]{1,0:T(8,128)(2,1)} %slice.85), channel_id=1, source_target_pairs={{0,6},{1,7},{2,4},{3,5},{4,2},{5,3},{6,0},{7,1},{8,14},{9,15},{10,... | collective-permute-start | bytes 2359304 | tf_op jit(solution)/shard_map/ppermute | solution.py:360
  56.5 18.5 %copy-start.16 = (f32[32]{0:T(128)S(1)}, f32[32]{0:T(128)}, u32[]{:S(2)}) copy-start(f32[32]{0:T(128)} %param.12) | copy-start | bytes 388
  72.5 70.6 %collective-permute-start.5 = (bf16[512,768]{1,0:T(8,128)(2,1)}, bf16[512,768]{1,0:T(8,128)(2,1)}, u32[]{:S(2)}, u32[]{:S(2)}) collective-permute-start(bf16[512,768]{1,0:T(8,128)(2,1)} %slice.86), channel_id=1, source_target_pairs={{0,6},{1,7},{2,4},{3,5},{4,2},{5,3},{6,0},{7,1},{8,14},{9,15},{10,... | collective-permute-start | bytes 2359304 | tf_op jit(solution)/shard_map/ppermute | solution.py:360
  106.3 41.8 %collective-permute-start = (s32[32]{0:T(128)S(1)}, s32[32]{0:T(128)S(1)}, u32[]{:S(2)}, u32[]{:S(2)}) collective-permute-start(s32[32]{0:T(128)S(1)} %copy-done.14), channel_id=1, source_target_pairs={{0,2},{1,3},{2,0},{3,1},{4,6},{5,7},{6,4},{7,5},{8,10},{9,11},{10,... | collective-permute-start | bytes 392 | tf_op jit(solution)/shard_map/ppermute | solution.py:360
  124.0 23.3 %copy-start.2 = (bf16[16,32,1024]{2,1,0:T(8,128)(2,1)}, bf16[16,32,1024]{2,1,0:T(8,128)(2,1)S(1)}, u32[]{:S(2)}) copy-start(bf16[16,32,1024]{2,1,0:T(8,128)(2,1)S(1)} %get-tuple-element.46.refs_0_) | copy-start | bytes 3145732
  124.0 37.2 %collective-permute-start.7 = (bf16[16,32,1024]{2,1,0:T(8,128)(2,1)}, bf16[16,32,1024]{2,1,0:T(8,128)(2,1)}, u32[]{:S(2)}, u32[]{:S(2)}) collective-permute-start(bf16[16,32,1024]{2,1,0:T(8,128)(2,1)} %get-tuple-element.47), channel_id=1, source_target_pairs={{0,1},{1,0},{2,3},{3,2},{4,5},{5,4},{6,7},{7,6},{8,9},{9,8},{10,11... | collective-permute-start | bytes 3145736 | tf_op jit(solution)/shard_map/ppermute | solution.py:360
  126.7 40.1 %collective-permute-start.9 = (bf16[256,768]{1,0:T(8,128)(2,1)}, bf16[256,768]{1,0:T(8,128)(2,1)}, u32[]{:S(2)}, u32[]{:S(2)}) collective-permute-start(bf16[256,768]{1,0:T(8,128)(2,1)} %slice.89), channel_id=1, source_target_pairs={{0,6},{1,7},{2,4},{3,5},{4,2},{5,3},{6,0},{7,1},{8,14},{9,15},{10,... | collective-permute-start | bytes 1179656 | tf_op jit(solution)/shard_map/ppermute | solution.py:360
  130.4 36.5 %collective-permute-start.10 = (bf16[256,768]{1,0:T(8,128)(2,1)}, bf16[256,768]{1,0:T(8,128)(2,1)}, u32[]{:S(2)}, u32[]{:S(2)}) collective-permute-start(bf16[256,768]{1,0:T(8,128)(2,1)} %slice.90), channel_id=1, source_target_pairs={{0,6},{1,7},{2,4},{3,5},{4,2},{5,3},{6,0},{7,1},{8,14},{9,15},{10,... | collective-permute-start | bytes 1179656 | tf_op jit(solution)/shard_map/ppermute | solution.py:360
  148.1 13.0 %collective-permute-start.8 = (bf16[16,32,512]{2,1,0:T(8,128)(2,1)}, bf16[16,32,512]{2,1,0:T(8,128)(2,1)}, u32[]{:S(2)}, u32[]{:S(2)}) collective-permute-start(bf16[16,32,512]{2,1,0:T(8,128)(2,1)} %get-tuple-element.49), channel_id=1, source_target_pairs={{0,1},{1,0},{2,3},{3,2},{4,5},{5,4},{6,7},{7,6},{8,9},{9,8},{10,11... | collective-permute-start | bytes 1572872 | tf_op jit(solution)/shard_map/ppermute | solution.py:360
  150.1 16.7 %copy-start.1 = (bf16[16,32,1536]{2,1,0:T(8,128)(2,1)S(1)}, bf16[16,32,1536]{2,1,0:T(8,128)(2,1)}, u32[]{:S(2)}) copy-start(bf16[16,32,1536]{2,1,0:T(8,128)(2,1)} %get-tuple-element.33.refs_0_) | copy-start | bytes 4718596
  169.3 37.1 %collective-permute-start.11 = (bf16[16,32,256]{2,1,0:T(8,128)(2,1)S(1)}, bf16[16,32,256]{2,1,0:T(8,128)(2,1)S(1)}, u32[]{:S(2)}, u32[]{:S(2)}) collective-permute-start(bf16[16,32,256]{2,1,0:T(8,128)(2,1)S(1)} %get-tuple-element.52), channel_id=1, source_target_pairs={{0,1},{1,0},{2,3},{3,2},{4,5},{5,4},{6,7},{7,6},{8,9},{9,8},{10,11... | collective-permute-start | bytes 786440 | tf_op jit(solution)/shard_map/ppermute | solution.py:360
  172.0 9.8 %collective-permute-start.17 = (bf16[128,768]{1,0:T(8,128)(2,1)S(1)}, bf16[128,768]{1,0:T(8,128)(2,1)S(1)}, u32[]{:S(2)}, u32[]{:S(2)}) collective-permute-start(bf16[128,768]{1,0:T(8,128)(2,1)S(1)} %get-tuple-element.70), channel_id=1, source_target_pairs={{0,6},{1,7},{2,4},{3,5},{4,2},{5,3},{6,0},{7,1},{8,14},{9,15},{10,... | collective-permute-start | bytes 589832 | tf_op jit(solution)/shard_map/ppermute | solution.py:360
  173.7 43.2 %collective-permute-start.15 = (bf16[128,768]{1,0:T(8,128)(2,1)S(1)}, bf16[128,768]{1,0:T(8,128)(2,1)S(1)}, u32[]{:S(2)}, u32[]{:S(2)}) collective-permute-start(bf16[128,768]{1,0:T(8,128)(2,1)S(1)} %get-tuple-element.71), channel_id=1, source_target_pairs={{0,6},{1,7},{2,4},{3,5},{4,2},{5,3},{6,0},{7,1},{8,14},{9,15},{10,... | collective-permute-start | bytes 589832 | tf_op jit(solution)/shard_map/ppermute | solution.py:360
  176.9 32.4 %collective-permute-start.18 = (bf16[128,768]{1,0:T(8,128)(2,1)S(1)}, bf16[128,768]{1,0:T(8,128)(2,1)S(1)}, u32[]{:S(2)}, u32[]{:S(2)}) collective-permute-start(bf16[128,768]{1,0:T(8,128)(2,1)S(1)} %get-tuple-element.68), channel_id=1, source_target_pairs={{0,6},{1,7},{2,4},{3,5},{4,2},{5,3},{6,0},{7,1},{8,14},{9,15},{10,... | collective-permute-start | bytes 589832 | tf_op jit(solution)/shard_map/ppermute | solution.py:360
  178.7 39.9 %collective-permute-start.16 = (bf16[128,768]{1,0:T(8,128)(2,1)S(1)}, bf16[128,768]{1,0:T(8,128)(2,1)S(1)}, u32[]{:S(2)}, u32[]{:S(2)}) collective-permute-start(bf16[128,768]{1,0:T(8,128)(2,1)S(1)} %get-tuple-element.69), channel_id=1, source_target_pairs={{0,6},{1,7},{2,4},{3,5},{4,2},{5,3},{6,0},{7,1},{8,14},{9,15},{10,... | collective-permute-start | bytes 589832 | tf_op jit(solution)/shard_map/ppermute | solution.py:360
  181.8 36.8 %collective-permute-start.19 = (bf16[8,32,256]{2,1,0:T(8,128)(2,1)S(1)}, bf16[8,32,256]{2,1,0:T(8,128)(2,1)S(1)}, u32[]{:S(2)}, u32[]{:S(2)}) collective-permute-start(bf16[8,32,256]{2,1,0:T(8,128)(2,1)S(1)} %slice.83), channel_id=1, source_target_pairs={{0,2},{1,3},{2,0},{3,1},{4,6},{5,7},{6,4},{7,5},{8,10},{9,11},{10,... | collective-permute-start | bytes 393224 | tf_op jit(solution)/shard_map/ppermute | solution.py:360
  206.5 26.5 %collective-permute-start.13 = (bf16[16,32,512]{2,1,0:T(8,128)(2,1)S(1)}, bf16[16,32,512]{2,1,0:T(8,128)(2,1)S(1)}, u32[]{:S(2)}, u32[]{:S(2)}) collective-permute-start(bf16[16,32,512]{2,1,0:T(8,128)(2,1)S(1)} %get-tuple-element.54), channel_id=1, source_target_pairs={{0,2},{1,3},{2,0},{3,1},{4,6},{5,7},{6,4},{7,5},{8,10},{9,11},{10,... | collective-permute-start | bytes 1572872 | tf_op jit(solution)/shard_map/ppermute | solution.py:360
  209.3 15.4 %collective-permute-start.20 = (bf16[8,32,256]{2,1,0:T(8,128)(2,1)S(1)}, bf16[8,32,256]{2,1,0:T(8,128)(2,1)S(1)}, u32[]{:S(2)}, u32[]{:S(2)}) collective-permute-start(bf16[8,32,256]{2,1,0:T(8,128)(2,1)S(1)} %slice.84), channel_id=1, source_target_pairs={{0,3},{1,2},{2,1},{3,0},{4,7},{5,6},{6,5},{7,4},{8,11},{9,10},{10,... | collective-permute-start | bytes 393224 | tf_op jit(solution)/shard_map/ppermute | solution.py:360
  216.9 10.8 %collective-permute-start.21 = (bf16[8,32,128]{2,1,0:T(8,128)(2,1)S(1)}, bf16[8,32,128]{2,1,0:T(8,128)(2,1)S(1)}, u32[]{:S(2)}, u32[]{:S(2)}) collective-permute-start(bf16[8,32,128]{2,1,0:T(8,128)(2,1)S(1)} %get-tuple-element.58), channel_id=1, source_target_pairs={{0,1},{1,0},{2,3},{3,2},{4,5},{5,4},{6,7},{7,6},{8,9},{9,8},{10,11... | collective-permute-start | bytes 196616 | tf_op jit(solution)/shard_map/ppermute | solution.py:360
  218.5 9.7 %collective-permute-start.22 = (bf16[8,32,128]{2,1,0:T(8,128)(2,1)S(1)}, bf16[8,32,128]{2,1,0:T(8,128)(2,1)S(1)}, u32[]{:S(2)}, u32[]{:S(2)}) collective-permute-start(bf16[8,32,128]{2,1,0:T(8,128)(2,1)S(1)} %get-tuple-element.59), channel_id=1, source_target_pairs={{0,2},{1,3},{2,0},{3,1},{4,6},{5,7},{6,4},{7,5},{8,10},{9,11},{10,... | collective-permute-start | bytes 196616 | tf_op jit(solution)/shard_map/ppermute | solution.py:360
  218.5 13.3 %collective-permute-start.14 = (bf16[16,32,256]{2,1,0:T(8,128)(2,1)S(1)}, bf16[16,32,256]{2,1,0:T(8,128)(2,1)S(1)}, u32[]{:S(2)}, u32[]{:S(2)}) collective-permute-start(bf16[16,32,256]{2,1,0:T(8,128)(2,1)S(1)} %get-tuple-element.55), channel_id=1, source_target_pairs={{0,2},{1,3},{2,0},{3,1},{4,6},{5,7},{6,4},{7,5},{8,10},{9,11},{10,... | collective-permute-start | bytes 786440 | tf_op jit(solution)/shard_map/ppermute | solution.py:360
  224.8 11.7 %collective-permute-start.23 = (bf16[8,32,128]{2,1,0:T(8,128)(2,1)S(1)}, bf16[8,32,128]{2,1,0:T(8,128)(2,1)S(1)}, u32[]{:S(2)}, u32[]{:S(2)}) collective-permute-start(bf16[8,32,128]{2,1,0:T(8,128)(2,1)S(1)} %get-tuple-element.60), channel_id=1, source_target_pairs={{0,3},{1,2},{2,1},{3,0},{4,7},{5,6},{6,5},{7,4},{8,11},{9,10},{10,... | collective-permute-start | bytes 196616 | tf_op jit(solution)/shard_map/ppermute | solution.py:360
  227.8 8.7 %collective-permute-start.24 = (bf16[8,32,128]{2,1,0:T(8,128)(2,1)S(1)}, bf16[8,32,128]{2,1,0:T(8,128)(2,1)S(1)}, u32[]{:S(2)}, u32[]{:S(2)}) collective-permute-start(bf16[8,32,128]{2,1,0:T(8,128)(2,1)S(1)} %get-tuple-element.61), channel_id=1, source_target_pairs={{0,1},{1,0},{2,3},{3,2},{4,5},{5,4},{6,7},{7,6},{8,9},{9,8},{10,11... | collective-permute-start | bytes 196616 | tf_op jit(solution)/shard_map/ppermute | solution.py:360
  228.3 8.2 %collective-permute-start.25 = (bf16[8,32,128]{2,1,0:T(8,128)(2,1)S(1)}, bf16[8,32,128]{2,1,0:T(8,128)(2,1)S(1)}, u32[]{:S(2)}, u32[]{:S(2)}) collective-permute-start(bf16[8,32,128]{2,1,0:T(8,128)(2,1)S(1)} %get-tuple-element.62), channel_id=1, source_target_pairs={{0,2},{1,3},{2,0},{3,1},{4,6},{5,7},{6,4},{7,5},{8,10},{9,11},{10,... | collective-permute-start | bytes 196616 | tf_op jit(solution)/shard_map/ppermute | solution.py:360
  231.9 5.2 %collective-permute-start.26 = (bf16[8,32,128]{2,1,0:T(8,128)(2,1)S(1)}, bf16[8,32,128]{2,1,0:T(8,128)(2,1)S(1)}, u32[]{:S(2)}, u32[]{:S(2)}) collective-permute-start(bf16[8,32,128]{2,1,0:T(8,128)(2,1)S(1)} %get-tuple-element.63), channel_id=1, source_target_pairs={{0,3},{1,2},{2,1},{3,0},{4,7},{5,6},{6,5},{7,4},{8,11},{9,10},{10,... | collective-permute-start | bytes 196616 | tf_op jit(solution)/shard_map/ppermute | solution.py:360
  233.0 6.4 %collective-permute-start.12 = (f32[16,32,32]{2,1,0:T(8,128)S(1)}, f32[16,32,32]{2,1,0:T(8,128)S(1)}, u32[]{:S(2)}, u32[]{:S(2)}) collective-permute-start(f32[16,32,32]{2,1,0:T(8,128)S(1)} %slice_bitcast_fusion), channel_id=1, source_target_pairs={{0,2},{1,3},{2,0},{3,1},{4,6},{5,7},{6,4},{7,5},{8,10},{9,11},{10,... | collective-permute-start | bytes 196616 | tf_op jit(solution)/shard_map/ppermute | solution.py:360
  (15 other events, 69.3 us)

commit v12 on v11

--- a/solution.py
+++ b/solution.py
@@ -77,7 +77,9 @@
 def project_kernel(group, capacity, direct, *refs):
     inner = group // 2
     blocks, parts, outs = refs[:group], refs[group : group + 2], refs[group + 2 :]
-    row_count, half = parts[0].shape
+    row_count, cut = parts[0].shape
+    dom_count = cut + parts[1].shape[1]
+    columns = (slice(0, cut), slice(cut, dom_count))
     pno_count = outs[0].shape[1]
     step = row_count if row_count <= 640 else 256
 
@@ -86,10 +88,10 @@
         rows = [part[pl.ds(at, step), :] for part in parts]
         for i in range(inner):
             for j in range(2):
-                lines = blocks[i + j * inner][...].reshape(capacity * pno_count, 2 * half)
+                lines = blocks[i + j * inner][...].reshape(capacity * pno_count, dom_count)
                 product = sum(
                     lax.dot_general(
-                        lines[:, k * half : (k + 1) * half],
+                        lines[:, columns[k]],
                         rows[k],
                         (((1,), (1,)), ((), ())),
                         preferred_element_type=jnp.float32,
@@ -120,12 +122,12 @@
         project_kernel(group, capacity, direct, *refs[: group + 2], *refs[-count:])
 
     block = pl.BlockSpec((capacity, pno_count, dom_count), lambda i: (kind, 0, 0))
-    part = pl.BlockSpec(parts[0].shape, lambda i: (0, 0))
+    rows = [pl.BlockSpec(part.shape, lambda i: (0, 0)) for part in parts]
     return pl.pallas_call(
         kernel,
         grid=(1,),
         out_shape=(jax.ShapeDtypeStruct((lines, pno_count, row_count), blocks[0].dtype),) * count,
-        in_specs=[block] * group + [part] * 2 + [ANY] * len(tokens),
+        in_specs=[block] * group + rows + [ANY] * len(tokens),
         out_specs=(pl.BlockSpec((lines, pno_count, row_count), lambda i: (0, 0, 0)),) * count,
         compiler_params=pltpu.CompilerParams(vmem_limit_bytes=32 << 20),
         cost_estimate=pl.CostEstimate(
@@ -361,11 +363,11 @@
 
     own_orbs = pair_orbs.reshape(side_count)
     place = jnp.stack([region, me]).astype(jnp.int32)
-    half = dom_count // 2
+    cuts = (0, 7 * dom_count // 12 // 128 * 128, dom_count)
 
     def exchange(array, k):
         part = lax.all_to_all(
-            array[:, :, :, k * half : (k + 1) * half],
+            array[:, :, :, cuts[k] : cuts[k + 1]],
             "aux",
             split_axis=0,
             concat_axis=2,

time: 243 us -> 245 us (level)
    all_to_all x2, waiting for transfers between devices: 13.9 us -> 20.5 us  [exchange(): lax.all_to_all(array[:, :, :, cuts[k]:cuts[k + 1]], 'aux', split_axis=0,...]
    ppermute x1, waiting for transfers between devices: 9.04 us -> 3.79 us  [on_device(): guard = lax.ppermute(packed[0][:1], 'orb', pairs)]
    unnamed x37 -> x35, local copies, waits for them, and re-layouts: 9.77 us -> 9.52 us
  transfers between devices with their start and end apart: 29 -> 29, of which waited for: 10 -> 11; matrix products, arithmetic and copies ran while one was open for 9% -> 9% of each run, Pallas kernels for 13% -> 12%
where the time goes in v12:
time: 245 us; the launch traced here: 244 us
  waiting for transfers between devices  91.8 us (37%)
  starting transfers between devices  78.2 us (32%)
  Pallas kernels  38.5 us (16%)
  local copies, waits for them, and re-layouts  21.4 us (9%)
  matrix products  10.8 us (4%)
    ppermute x26, starting transfers between devices, across(): return lax.ppermute(array, 'orb', [(i, i ^ mask) for i in range(orb_count)])  67.6 us
    ppermute x26, waiting for transfers between devices, across(): return lax.ppermute(array, 'orb', [(i, i ^ mask) for i in range(orb_count)])  67.5 us
    all_to_all x2, waiting for transfers between devices, exchange(): lax.all_to_all(array[:, :, :, cuts[k]:cuts[k + 1]], 'aux', split_axis=0,...  20.5 us
    pallas_call x5, Pallas kernels, project(): pl.pallas_call(kernel, grid=(1,), out_shape=(jax.ShapeDtypeStruct((lines,...  18 us
    dot_general x2, matrix products, on_device(): product = jnp.dot(turned, raw_parts[k], preferred_element_type=jnp.float32)  10.8 us
    unnamed x35, local copies, waits for them, and re-layouts  9.52 us
    all_to_all x2, starting transfers between devices, exchange(): lax.all_to_all(array[:, :, :, cuts[k]:cuts[k + 1]], 'aux', split_axis=0,...  8.69 us
    pallas_call x2, Pallas kernels, pack(): pl.pallas_call(functools.partial(pack_kernel, group, capacity, masks), ou...  8.58 us
  transfers between devices with their start and end apart: 29, of which 11 were waited for; matrix products, arithmetic and copies ran while one was open for 9% of the time, Pallas kernels for 12%

profile of v12, /device:TPU:0, one launch (start us, length us, event | category | flops | bytes accessed | tf_op | source)
XLA Modules:
  0.0 243.9 jit_solution(7079271002676838597)
XLA Ops:
  2.8 4.3 %shard_map.87 = (bf16[16,32,1536]{2,1,0:T(8,128)(2,1)}, bf16[16,32,1536]{2,1,0:T(8,128)(2,1)}) custom-call(s32[32]{0:T(128)} %reshape.73.orbs, s32[2]{0:T(128)} %pad_add_fusion.1.place, bf16[32,32,1536]{2,1,0:T(8,128)(2,1)} %bitcast.16), custom_call_target="tpu_custom_call" | custom-call | bytes 9437184 | tf_op jit(solution)/shard_map/pallas_call | solution.py:59
  8.3 4.3 %all-to-all-start.1 = ((bf16[4,1,256,640]{3,2,1,0:T(8,128)(2,1)}), bf16[4,1,256,640]{3,2,1,0:T(8,128)(2,1)}, u32[]{:S(2)}, u32[]{:S(2)}) async-start(bf16[4,1,256,640]{3,2,1,0:T(8,128)(2,1)} %slice.66), calls=%async_computation.1 | async-start | bytes 2621440 | tf_op jit(solution)/shard_map/all_to_all | solution.py:369
  14.0 16.5 %all-to-all-done.1 = bf16[4,1,256,640]{3,2,1,0:T(8,128)(2,1)} async-done(((bf16[4,1,256,640]{3,2,1,0:T(8,128)(2,1)}), bf16[4,1,256,640]{3,2,1,0:T(8,128)(2,1)}, u32[]{:S(2)}, u32[]{:S(2)}) %all-to-all-start.1) | async-done | bytes 1310752 | tf_op jit(solution)/shard_map/all_to_all | solution.py:369
  30.6 4.4 %all-to-all-start = ((bf16[4,1,256,896]{3,2,1,0:T(8,128)(2,1)}), bf16[4,1,256,896]{3,2,1,0:T(8,128)(2,1)}, u32[]{:S(2)}, u32[]{:S(2)}) async-start(bf16[4,1,256,896]{3,2,1,0:T(8,128)(2,1)} %slice.64), calls=%async_computation | async-start | bytes 3670016 | tf_op jit(solution)/shard_map/all_to_all | solution.py:369
  35.0 2.4 collective-permute-start.2
  41.1 4.3 %shard_map.86 = (bf16[16,32,1536]{2,1,0:T(8,128)(2,1)}, bf16[16,32,1536]{2,1,0:T(8,128)(2,1)}) custom-call(s32[32]{0:T(128)} %reshape.73.orbs, s32[2]{0:T(128)} %pad_add_fusion.1.place, bf16[32,32,1536]{2,1,0:T(8,128)(2,1)} %bitcast.17), custom_call_target="tpu_custom_call" | custom-call | bytes 9437184 | tf_op jit(solution)/shard_map/pallas_call | solution.py:59
  48.1 5.8 %convolution_convert_fusion.1.refs_5_ = bf16[1024,640]{1,0:T(8,128)(2,1)} fusion(bf16[1024,640]{1,0:T(8,128)(2,1)} %bitcast.6, u32[]{:T(128)} %bitcast.4, bf16[1024,1024]{1,0:T(8,128)(2,1)} %bitcast.22), kind=kOutput, calls=%fused_computation.4 | convolution fusion | flops 1347026944 | bytes 4718596 | tf_op jit(solution)/shard_map/dot_general | solution.py:414
  53.9 4.0 %all-to-all-done = bf16[4,1,256,896]{3,2,1,0:T(8,128)(2,1)} async-done(((bf16[4,1,256,896]{3,2,1,0:T(8,128)(2,1)}), bf16[4,1,256,896]{3,2,1,0:T(8,128)(2,1)}, u32[]{:S(2)}, u32[]{:S(2)}) %all-to-all-start) | async-done | bytes 1835040 | tf_op jit(solution)/shard_map/all_to_all | solution.py:369
  57.9 5.0 %convolution_convert_fusion.refs_4_ = bf16[1024,896]{1,0:T(8,128)(2,1)S(1)} fusion(bf16[1024,896]{1,0:T(8,128)(2,1)} %bitcast.5, u32[]{:T(128)} %bitcast.4, bf16[1024,1024]{1,0:T(8,128)(2,1)} %bitcast.23), kind=kOutput, calls=%fused_computation.3 | convolution fusion | flops 1884160000 | bytes 5767172 | tf_op jit(solution)/shard_map/dot_general | solution.py:414
  65.2 4.4 %collective-permute-start.4 = (bf16[512,896]{1,0:T(8,128)(2,1)}, bf16[512,896]{1,0:T(8,128)(2,1)}, u32[]{:S(2)}, u32[]{:S(2)}) collective-permute-start(bf16[512,896]{1,0:T(8,128)(2,1)} %slice.85), channel_id=1, source_target_pairs={{0,6},{1,7},{2,4},{3,5},{4,2},{5,3},{6,0},{7,1},{8,14},{9,15},{10,... | collective-permute-start | bytes 2752520 | tf_op jit(solution)/shard_map/ppermute | solution.py:362
  70.7 3.8 %collective-permute-done.6.refs_7_ = bf16[1,32,1536]{2,1,0:T(8,128)(2,1)S(1)} collective-permute-done((bf16[1,32,1536]{2,1,0:T(8,128)(2,1)S(1)}, bf16[1,32,1536]{2,1,0:T(8,128)(2,1)S(1)}, u32[]{:S(2)}, u32[]{:S(2)}) %collective-permute-start.6) | collective-permute-done | bytes 98336 | tf_op jit(solution)/shard_map/ppermute | solution.py:389
  74.5 2.5 %collective-permute-start.5 = (bf16[512,640]{1,0:T(8,128)(2,1)}, bf16[512,640]{1,0:T(8,128)(2,1)S(1)}, u32[]{:S(2)}, u32[]{:S(2)}) collective-permute-start(bf16[512,640]{1,0:T(8,128)(2,1)} %slice.86), channel_id=1, source_target_pairs={{0,6},{1,7},{2,4},{3,5},{4,2},{5,3},{6,0},{7,1},{8,14},{9,15},{10,... | collective-permute-start | bytes 1966088 | tf_op jit(solution)/shard_map/ppermute | solution.py:362
  77.4 31.0 %collective-permute-done.3.refs_3_ = bf16[16,32,1536]{2,1,0:T(8,128)(2,1)S(1)} collective-permute-done((bf16[16,32,1536]{2,1,0:T(8,128)(2,1)}, bf16[16,32,1536]{2,1,0:T(8,128)(2,1)S(1)}, u32[]{:S(2)}, u32[]{:S(2)}) %collective-permute-start.3) | collective-permute-done | bytes 1572896 | tf_op jit(solution)/shard_map/ppermute | solution.py:362
  108.4 3.3 %collective-permute-start = (s32[32]{0:T(128)S(1)}, s32[32]{0:T(128)S(1)}, u32[]{:S(2)}, u32[]{:S(2)}) collective-permute-start(s32[32]{0:T(128)S(1)} %copy-done.14), channel_id=1, source_target_pairs={{0,2},{1,3},{2,0},{3,1},{4,6},{5,7},{6,4},{7,5},{8,10},{9,11},{10,... | collective-permute-start | bytes 392 | tf_op jit(solution)/shard_map/ppermute | solution.py:362
  111.7 3.9 %collective-permute-done.1.refs_1_ = bf16[16,32,1536]{2,1,0:T(8,128)(2,1)} collective-permute-done((bf16[16,32,1536]{2,1,0:T(8,128)(2,1)}, bf16[16,32,1536]{2,1,0:T(8,128)(2,1)}, u32[]{:S(2)}, u32[]{:S(2)}) %collective-permute-start.1) | collective-permute-done | bytes 1572896 | tf_op jit(solution)/shard_map/ppermute | solution.py:362
  119.8 6.8 %shard_map.89 = (bf16[16,32,1024]{2,1,0:T(8,128)(2,1)S(1)}, bf16[16,32,1024]{2,1,0:T(8,128)(2,1)}) custom-call(bf16[16,32,1536]{2,1,0:T(8,128)(2,1)S(1)} %copy-done, bf16[16,32,1536]{2,1,0:T(8,128)(2,1)} %collective-permute-done.1.refs_1_, bf16[16,32,1536]{2,1,0:T(8,128)(2,1)S(1)} %collective-permute-done.2.refs_2_, ...), custom_call_target="tpu_custom_call" | custom-call | flops 3221225472 | bytes 3145728 | tf_op jit(solution)/shard_map/pallas_call | solution.py:126
  128.6 3.6 %collective-permute-start.10 = (bf16[256,640]{1,0:T(8,128)(2,1)}, bf16[256,640]{1,0:T(8,128)(2,1)}, u32[]{:S(2)}, u32[]{:S(2)}) collective-permute-start(bf16[256,640]{1,0:T(8,128)(2,1)} %slice.90), channel_id=1, source_target_pairs={{0,6},{1,7},{2,4},{3,5},{4,2},{5,3},{6,0},{7,1},{8,14},{9,15},{10,... | collective-permute-start | bytes 983048 | tf_op jit(solution)/shard_map/ppermute | solution.py:362
  133.0 12.0 %collective-permute-done.5.refs_5_ = bf16[512,640]{1,0:T(8,128)(2,1)S(1)} collective-permute-done((bf16[512,640]{1,0:T(8,128)(2,1)}, bf16[512,640]{1,0:T(8,128)(2,1)S(1)}, u32[]{:S(2)}, u32[]{:S(2)}) %collective-permute-start.5) | collective-permute-done | bytes 655392 | tf_op jit(solution)/shard_map/ppermute | solution.py:362
  146.4 4.3 %shard_map.88 = (bf16[16,32,512]{2,1,0:T(8,128)(2,1)S(1)}, bf16[16,32,512]{2,1,0:T(8,128)(2,1)}) custom-call(bf16[16,32,1536]{2,1,0:T(8,128)(2,1)S(1)} %copy-done, bf16[16,32,1536]{2,1,0:T(8,128)(2,1)} %collective-permute-done.1.refs_1_, bf16[16,32,1536]{2,1,0:T(8,128)(2,1)S(1)} %collective-permute-done.2.refs_2_, ...), custom_call_target="tpu_custom_call" | custom-call | flops 1610612736 | bytes 3145728 | tf_op jit(solution)/shard_map/pallas_call | solution.py:126
  153.5 10.7 %collective-permute-done.8.refs_3_ = bf16[16,32,512]{2,1,0:T(8,128)(2,1)} collective-permute-done((bf16[16,32,512]{2,1,0:T(8,128)(2,1)}, bf16[16,32,512]{2,1,0:T(8,128)(2,1)}, u32[]{:S(2)}, u32[]{:S(2)}) %collective-permute-start.8) | collective-permute-done | bytes 524320 | tf_op jit(solution)/shard_map/ppermute | solution.py:362
  166.5 3.4 %shard_map.90 = (bf16[16,32,512]{2,1,0:T(8,128)(2,1)S(1)}, f32[2,16,32,32]{3,2,1,0:T(8,128)S(1)}) custom-call(s32[2,32]{1,0:T(2,128)S(1)} %add_select_fusion.1.rows, s32[2,32]{1,0:T(2,128)S(1)} %reshape.75.offsets, f32[8,128]{1,0:T(8,128)S(1)} %broadcast_in_dim.75.before, bf16[16,32,1024]{2,1,0:T(8,128)(2,1)S(1)} %copy-done.3, ...), custom_call_target="tpu_custom_call" | custom-call | tf_op jit(solution)/shard_map/pallas_call | solution.py:202
  170.0 2.6 %shard_map.91 = (bf16[16,32,256]{2,1,0:T(8,128)(2,1)S(1)}, bf16[16,32,256]{2,1,0:T(8,128)(2,1)S(1)}) custom-call(bf16[16,32,1536]{2,1,0:T(8,128)(2,1)S(1)} %copy-done.1, bf16[16,32,1536]{2,1,0:T(8,128)(2,1)} %collective-permute-done.1.refs_1_, bf16[16,32,1536]{2,1,0:T(8,128)(2,1)S(1)} %collective-permute-done.2.refs_2_, ...), custom_call_target="tpu_custom_call" | custom-call | flops 805306368 | bytes 3145728 | tf_op jit(solution)/shard_map/pallas_call | solution.py:126
  175.2 2.5 %collective-permute-start.18 = (bf16[128,640]{1,0:T(8,128)(2,1)S(1)}, bf16[128,640]{1,0:T(8,128)(2,1)S(1)}, u32[]{:S(2)}, u32[]{:S(2)}) collective-permute-start(bf16[128,640]{1,0:T(8,128)(2,1)S(1)} %get-tuple-element.70), channel_id=1, source_target_pairs={{0,6},{1,7},{2,4},{3,5},{4,2},{5,3},{6,0},{7,1},{8,14},{9,15},{10,... | collective-permute-start | bytes 491528 | tf_op jit(solution)/shard_map/ppermute | solution.py:362
  180.2 2.5 %collective-permute-start.16 = (bf16[128,640]{1,0:T(8,128)(2,1)S(1)}, bf16[128,640]{1,0:T(8,128)(2,1)S(1)}, u32[]{:S(2)}, u32[]{:S(2)}) collective-permute-start(bf16[128,640]{1,0:T(8,128)(2,1)S(1)} %get-tuple-element.71), channel_id=1, source_target_pairs={{0,6},{1,7},{2,4},{3,5},{4,2},{5,3},{6,0},{7,1},{8,14},{9,15},{10,... | collective-permute-start | bytes 491528 | tf_op jit(solution)/shard_map/ppermute | solution.py:362
  185.0 22.9 %collective-permute-start.19 = (bf16[8,32,256]{2,1,0:T(8,128)(2,1)S(1)}, bf16[8,32,256]{2,1,0:T(8,128)(2,1)S(1)}, u32[]{:S(2)}, u32[]{:S(2)}) collective-permute-start(bf16[8,32,256]{2,1,0:T(8,128)(2,1)S(1)} %slice.83), channel_id=1, source_target_pairs={{0,2},{1,3},{2,0},{3,1},{4,6},{5,7},{6,4},{7,5},{8,10},{9,11},{10,... | collective-permute-start | bytes 393224 | tf_op jit(solution)/shard_map/ppermute | solution.py:362
  207.9 3.0 %shard_map.92 = (bf16[16,32,256]{2,1,0:T(8,128)(2,1)S(1)}, f32[2,16,32,32]{3,2,1,0:T(8,128)S(1)}) custom-call(s32[2,32]{1,0:T(2,128)S(1)} %add_select_fusion.1.rows, s32[2,32]{1,0:T(2,128)S(1)} %reshape.75.offsets, f32[2,16,32,32]{3,2,1,0:T(8,128)S(1)} %get-tuple-element.50.refs_6_.before, bf16[16,32,1024]{2,1,0:T(8,128)(2,1)S(1)} %copy-done.4, ...), custom_call_target="tpu_custom_call" | custom-call | tf_op jit(solution)/shard_map/pallas_call | solution.py:202
  216.7 3.3 %collective-permute-start.22 = (bf16[8,32,128]{2,1,0:T(8,128)(2,1)S(1)}, bf16[8,32,128]{2,1,0:T(8,128)(2,1)S(1)}, u32[]{:S(2)}, u32[]{:S(2)}) collective-permute-start(bf16[8,32,128]{2,1,0:T(8,128)(2,1)S(1)} %get-tuple-element.59), channel_id=1, source_target_pairs={{0,2},{1,3},{2,0},{3,1},{4,6},{5,7},{6,4},{7,5},{8,10},{9,11},{10,... | collective-permute-start | bytes 196616 | tf_op jit(solution)/shard_map/ppermute | solution.py:362
  222.3 3.6 %collective-permute-done.20.refs_3_ = bf16[8,32,256]{2,1,0:T(8,128)(2,1)S(1)} collective-permute-done((bf16[8,32,256]{2,1,0:T(8,128)(2,1)S(1)}, bf16[8,32,256]{2,1,0:T(8,128)(2,1)S(1)}, u32[]{:S(2)}, u32[]{:S(2)}) %collective-permute-start.20) | collective-permute-done | bytes 131104 | tf_op jit(solution)/shard_map/ppermute | solution.py:362
  225.8 3.4 %collective-permute-start.23 = (bf16[8,32,128]{2,1,0:T(8,128)(2,1)S(1)}, bf16[8,32,128]{2,1,0:T(8,128)(2,1)S(1)}, u32[]{:S(2)}, u32[]{:S(2)}) collective-permute-start(bf16[8,32,128]{2,1,0:T(8,128)(2,1)S(1)} %get-tuple-element.60), channel_id=1, source_target_pairs={{0,3},{1,2},{2,1},{3,0},{4,7},{5,6},{6,5},{7,4},{8,11},{9,10},{10,... | collective-permute-start | bytes 196616 | tf_op jit(solution)/shard_map/ppermute | solution.py:362
  229.8 3.3 %collective-permute-done.14.refs_7_ = bf16[16,32,256]{2,1,0:T(8,128)(2,1)S(1)} collective-permute-done((bf16[16,32,256]{2,1,0:T(8,128)(2,1)S(1)}, bf16[16,32,256]{2,1,0:T(8,128)(2,1)S(1)}, u32[]{:S(2)}, u32[]{:S(2)}) %collective-permute-start.14) | collective-permute-done | bytes 262176 | tf_op jit(solution)/shard_map/ppermute | solution.py:362
  235.1 2.5 %shard_map.95.before = f32[16,32,32]{2,1,0:T(8,128)S(1)} custom-call(s32[2,32]{1,0:T(2,128)S(1)} %get-tuple-element.66.rows, s32[2,32]{1,0:T(2,128)S(1)} %reshape.75.offsets, bf16[16,32,1024]{2,1,0:T(8,128)(2,1)S(1)} %copy-done.4, bf16[16,32,1024]{2,1,0:T(8,128)(2,1)} %collective-permute-done.7.refs_1_, bf16[16,32,512]{2,1,0:T(8,128)(2,1)S(1)} %copy-done.7, ...), custom_call_target="tpu_custom_call" | custom-call | tf_op jit(solution)/shard_map/pallas_call | solution.py:324
  240.7 3.0 %finish.1 = (f32[16,1024]{1,0:T(8,128)}, f32[16]{0:T(128)}) custom-call(s32[32]{0:T(128)S(1)} %add_bitcast_fusion.rows, f32[2,16,32,32]{3,2,1,0:T(8,128)S(1)} %get-tuple-element.53.refs_6_.here, f32[16,32,32]{2,1,0:T(8,128)S(1)} %collective-permute-done.12.there, f32[16,32,32]{2,1,0:T(8,128)S(1)} %shard_map.95.before, ...), custom_call_target="tpu_custom_call" | custom-call | tf_op jit(solution)/shard_map/finish/pallas_call | solution.py:301
  (108 shorter events, 48.9 us)
Async XLA Ops:
  8.3 22.3 %all-to-all-start.1 = ((bf16[4,1,256,640]{3,2,1,0:T(8,128)(2,1)}), bf16[4,1,256,640]{3,2,1,0:T(8,128)(2,1)}, u32[]{:S(2)}, u32[]{:S(2)}) async-start(bf16[4,1,256,640]{3,2,1,0:T(8,128)(2,1)} %slice.66), calls=%async_computation.1 | async-start | bytes 2621440 | tf_op jit(solution)/shard_map/all_to_all | solution.py:369
  30.6 27.3 %all-to-all-start = ((bf16[4,1,256,896]{3,2,1,0:T(8,128)(2,1)}), bf16[4,1,256,896]{3,2,1,0:T(8,128)(2,1)}, u32[]{:S(2)}, u32[]{:S(2)}) async-start(bf16[4,1,256,896]{3,2,1,0:T(8,128)(2,1)} %slice.64), calls=%async_computation | async-start | bytes 3670016 | tf_op jit(solution)/shard_map/all_to_all | solution.py:369
  35.0 76.7 %collective-permute-start.2 = (bf16[16,32,1536]{2,1,0:T(8,128)(2,1)}, bf16[16,32,1536]{2,1,0:T(8,128)(2,1)S(1)}, u32[]{:S(2)}, u32[]{:S(2)}) collective-permute-start(bf16[16,32,1536]{2,1,0:T(8,128)(2,1)} %get-tuple-element.37), channel_id=1, source_target_pairs={{0,2},{1,3},{2,0},{3,1},{4,6},{5,7},{6,4},{7,5},{8,10},{9,11},{10,... | collective-permute-start | bytes 4718600 | tf_op jit(solution)/shard_map/ppermute | solution.py:362
  38.4 36.2 %collective-permute-start.6 = (bf16[1,32,1536]{2,1,0:T(8,128)(2,1)S(1)}, bf16[1,32,1536]{2,1,0:T(8,128)(2,1)S(1)}, u32[]{:S(2)}, u32[]{:S(2)}) collective-permute-start(bf16[1,32,1536]{2,1,0:T(8,128)(2,1)S(1)} %slice.75), channel_id=1, source_target_pairs={{0,2},{1,3},{6,4},{7,5},{8,10},{9,11},{14,12},{15,13},{16,18},{17,... | collective-permute-start | bytes 294920 | tf_op jit(solution)/shard_map/ppermute | solution.py:389
  40.3 68.1 %collective-permute-start.3 = (bf16[16,32,1536]{2,1,0:T(8,128)(2,1)}, bf16[16,32,1536]{2,1,0:T(8,128)(2,1)S(1)}, u32[]{:S(2)}, u32[]{:S(2)}) collective-permute-start(bf16[16,32,1536]{2,1,0:T(8,128)(2,1)} %get-tuple-element.38), channel_id=1, source_target_pairs={{0,3},{1,2},{2,1},{3,0},{4,7},{5,6},{6,5},{7,4},{8,11},{9,10},{10,... | collective-permute-start | bytes 4718600 | tf_op jit(solution)/shard_map/ppermute | solution.py:362
  45.4 70.2 %collective-permute-start.1 = (bf16[16,32,1536]{2,1,0:T(8,128)(2,1)}, bf16[16,32,1536]{2,1,0:T(8,128)(2,1)}, u32[]{:S(2)}, u32[]{:S(2)}) collective-permute-start(bf16[16,32,1536]{2,1,0:T(8,128)(2,1)} %get-tuple-element.34), channel_id=1, source_target_pairs={{0,1},{1,0},{2,3},{3,2},{4,5},{5,4},{6,7},{7,6},{8,9},{9,8},{10,11... | collective-permute-start | bytes 4718600 | tf_op jit(solution)/shard_map/ppermute | solution.py:362
  65.2 81.2 %collective-permute-start.4 = (bf16[512,896]{1,0:T(8,128)(2,1)}, bf16[512,896]{1,0:T(8,128)(2,1)}, u32[]{:S(2)}, u32[]{:S(2)}) collective-permute-start(bf16[512,896]{1,0:T(8,128)(2,1)} %slice.85), channel_id=1, source_target_pairs={{0,6},{1,7},{2,4},{3,5},{4,2},{5,3},{6,0},{7,1},{8,14},{9,15},{10,... | collective-permute-start | bytes 2752520 | tf_op jit(solution)/shard_map/ppermute | solution.py:362
  74.5 70.5 %collective-permute-start.5 = (bf16[512,640]{1,0:T(8,128)(2,1)}, bf16[512,640]{1,0:T(8,128)(2,1)S(1)}, u32[]{:S(2)}, u32[]{:S(2)}) collective-permute-start(bf16[512,640]{1,0:T(8,128)(2,1)} %slice.86), channel_id=1, source_target_pairs={{0,6},{1,7},{2,4},{3,5},{4,2},{5,3},{6,0},{7,1},{8,14},{9,15},{10,... | collective-permute-start | bytes 1966088 | tf_op jit(solution)/shard_map/ppermute | solution.py:362
  108.4 43.1 %collective-permute-start = (s32[32]{0:T(128)S(1)}, s32[32]{0:T(128)S(1)}, u32[]{:S(2)}, u32[]{:S(2)}) collective-permute-start(s32[32]{0:T(128)S(1)} %copy-done.14), channel_id=1, source_target_pairs={{0,2},{1,3},{2,0},{3,1},{4,6},{5,7},{6,4},{7,5},{8,10},{9,11},{10,... | collective-permute-start | bytes 392 | tf_op jit(solution)/shard_map/ppermute | solution.py:362
  126.6 24.0 %copy-start.2 = (bf16[16,32,1024]{2,1,0:T(8,128)(2,1)}, bf16[16,32,1024]{2,1,0:T(8,128)(2,1)S(1)}, u32[]{:S(2)}) copy-start(bf16[16,32,1024]{2,1,0:T(8,128)(2,1)S(1)} %get-tuple-element.46.refs_0_) | copy-start | bytes 3145732
  126.6 26.9 %collective-permute-start.7 = (bf16[16,32,1024]{2,1,0:T(8,128)(2,1)}, bf16[16,32,1024]{2,1,0:T(8,128)(2,1)}, u32[]{:S(2)}, u32[]{:S(2)}) collective-permute-start(bf16[16,32,1024]{2,1,0:T(8,128)(2,1)} %get-tuple-element.47), channel_id=1, source_target_pairs={{0,1},{1,0},{2,3},{3,2},{4,5},{5,4},{6,7},{7,6},{8,9},{9,8},{10,11... | collective-permute-start | bytes 3145736 | tf_op jit(solution)/shard_map/ppermute | solution.py:362
  128.6 41.3 %collective-permute-start.10 = (bf16[256,640]{1,0:T(8,128)(2,1)}, bf16[256,640]{1,0:T(8,128)(2,1)}, u32[]{:S(2)}, u32[]{:S(2)}) collective-permute-start(bf16[256,640]{1,0:T(8,128)(2,1)} %slice.90), channel_id=1, source_target_pairs={{0,6},{1,7},{2,4},{3,5},{4,2},{5,3},{6,0},{7,1},{8,14},{9,15},{10,... | collective-permute-start | bytes 983048 | tf_op jit(solution)/shard_map/ppermute | solution.py:362
  145.0 24.9 %collective-permute-start.9 = (bf16[256,896]{1,0:T(8,128)(2,1)}, bf16[256,896]{1,0:T(8,128)(2,1)}, u32[]{:S(2)}, u32[]{:S(2)}) collective-permute-start(bf16[256,896]{1,0:T(8,128)(2,1)} %slice.89), channel_id=1, source_target_pairs={{0,6},{1,7},{2,4},{3,5},{4,2},{5,3},{6,0},{7,1},{8,14},{9,15},{10,... | collective-permute-start | bytes 1376264 | tf_op jit(solution)/shard_map/ppermute | solution.py:362
  151.5 12.8 %collective-permute-start.8 = (bf16[16,32,512]{2,1,0:T(8,128)(2,1)}, bf16[16,32,512]{2,1,0:T(8,128)(2,1)}, u32[]{:S(2)}, u32[]{:S(2)}) collective-permute-start(bf16[16,32,512]{2,1,0:T(8,128)(2,1)} %get-tuple-element.49), channel_id=1, source_target_pairs={{0,1},{1,0},{2,3},{3,2},{4,5},{5,4},{6,7},{7,6},{8,9},{9,8},{10,11... | collective-permute-start | bytes 1572872 | tf_op jit(solution)/shard_map/ppermute | solution.py:362
  153.5 16.5 %copy-start.1 = (bf16[16,32,1536]{2,1,0:T(8,128)(2,1)S(1)}, bf16[16,32,1536]{2,1,0:T(8,128)(2,1)}, u32[]{:S(2)}) copy-start(bf16[16,32,1536]{2,1,0:T(8,128)(2,1)} %get-tuple-element.33.refs_0_) | copy-start | bytes 4718596
  172.5 35.4 %collective-permute-start.11 = (bf16[16,32,256]{2,1,0:T(8,128)(2,1)S(1)}, bf16[16,32,256]{2,1,0:T(8,128)(2,1)S(1)}, u32[]{:S(2)}, u32[]{:S(2)}) collective-permute-start(bf16[16,32,256]{2,1,0:T(8,128)(2,1)S(1)} %get-tuple-element.52), channel_id=1, source_target_pairs={{0,1},{1,0},{2,3},{3,2},{4,5},{5,4},{6,7},{7,6},{8,9},{9,8},{10,11... | collective-permute-start | bytes 786440 | tf_op jit(solution)/shard_map/ppermute | solution.py:362
  175.2 9.8 %collective-permute-start.18 = (bf16[128,640]{1,0:T(8,128)(2,1)S(1)}, bf16[128,640]{1,0:T(8,128)(2,1)S(1)}, u32[]{:S(2)}, u32[]{:S(2)}) collective-permute-start(bf16[128,640]{1,0:T(8,128)(2,1)S(1)} %get-tuple-element.70), channel_id=1, source_target_pairs={{0,6},{1,7},{2,4},{3,5},{4,2},{5,3},{6,0},{7,1},{8,14},{9,15},{10,... | collective-permute-start | bytes 491528 | tf_op jit(solution)/shard_map/ppermute | solution.py:362
  178.8 32.2 %collective-permute-start.17 = (bf16[128,896]{1,0:T(8,128)(2,1)S(1)}, bf16[128,896]{1,0:T(8,128)(2,1)S(1)}, u32[]{:S(2)}, u32[]{:S(2)}) collective-permute-start(bf16[128,896]{1,0:T(8,128)(2,1)S(1)} %get-tuple-element.68), channel_id=1, source_target_pairs={{0,6},{1,7},{2,4},{3,5},{4,2},{5,3},{6,0},{7,1},{8,14},{9,15},{10,... | collective-permute-start | bytes 688136 | tf_op jit(solution)/shard_map/ppermute | solution.py:362
  180.2 34.4 %collective-permute-start.16 = (bf16[128,640]{1,0:T(8,128)(2,1)S(1)}, bf16[128,640]{1,0:T(8,128)(2,1)S(1)}, u32[]{:S(2)}, u32[]{:S(2)}) collective-permute-start(bf16[128,640]{1,0:T(8,128)(2,1)S(1)} %get-tuple-element.71), channel_id=1, source_target_pairs={{0,6},{1,7},{2,4},{3,5},{4,2},{5,3},{6,0},{7,1},{8,14},{9,15},{10,... | collective-permute-start | bytes 491528 | tf_op jit(solution)/shard_map/ppermute | solution.py:362
  182.7 34.0 %collective-permute-start.15 = (bf16[128,896]{1,0:T(8,128)(2,1)S(1)}, bf16[128,896]{1,0:T(8,128)(2,1)S(1)}, u32[]{:S(2)}, u32[]{:S(2)}) collective-permute-start(bf16[128,896]{1,0:T(8,128)(2,1)S(1)} %get-tuple-element.69), channel_id=1, source_target_pairs={{0,6},{1,7},{2,4},{3,5},{4,2},{5,3},{6,0},{7,1},{8,14},{9,15},{10,... | collective-permute-start | bytes 688136 | tf_op jit(solution)/shard_map/ppermute | solution.py:362
  185.0 35.0 %collective-permute-start.19 = (bf16[8,32,256]{2,1,0:T(8,128)(2,1)S(1)}, bf16[8,32,256]{2,1,0:T(8,128)(2,1)S(1)}, u32[]{:S(2)}, u32[]{:S(2)}) collective-permute-start(bf16[8,32,256]{2,1,0:T(8,128)(2,1)S(1)} %slice.83), channel_id=1, source_target_pairs={{0,2},{1,3},{2,0},{3,1},{4,6},{5,7},{6,4},{7,5},{8,10},{9,11},{10,... | collective-permute-start | bytes 393224 | tf_op jit(solution)/shard_map/ppermute | solution.py:362
  207.9 26.4 %collective-permute-start.13 = (bf16[16,32,512]{2,1,0:T(8,128)(2,1)S(1)}, bf16[16,32,512]{2,1,0:T(8,128)(2,1)S(1)}, u32[]{:S(2)}, u32[]{:S(2)}) collective-permute-start(bf16[16,32,512]{2,1,0:T(8,128)(2,1)S(1)} %get-tuple-element.54), channel_id=1, source_target_pairs={{0,2},{1,3},{2,0},{3,1},{4,6},{5,7},{6,4},{7,5},{8,10},{9,11},{10,... | collective-permute-start | bytes 1572872 | tf_op jit(solution)/shard_map/ppermute | solution.py:362
  211.0 14.9 %collective-permute-start.20 = (bf16[8,32,256]{2,1,0:T(8,128)(2,1)S(1)}, bf16[8,32,256]{2,1,0:T(8,128)(2,1)S(1)}, u32[]{:S(2)}, u32[]{:S(2)}) collective-permute-start(bf16[8,32,256]{2,1,0:T(8,128)(2,1)S(1)} %slice.84), channel_id=1, source_target_pairs={{0,3},{1,2},{2,1},{3,0},{4,7},{5,6},{6,5},{7,4},{8,11},{9,10},{10,... | collective-permute-start | bytes 393224 | tf_op jit(solution)/shard_map/ppermute | solution.py:362
  214.6 14.6 %collective-permute-start.21 = (bf16[8,32,128]{2,1,0:T(8,128)(2,1)S(1)}, bf16[8,32,128]{2,1,0:T(8,128)(2,1)S(1)}, u32[]{:S(2)}, u32[]{:S(2)}) collective-permute-start(bf16[8,32,128]{2,1,0:T(8,128)(2,1)S(1)} %get-tuple-element.58), channel_id=1, source_target_pairs={{0,1},{1,0},{2,3},{3,2},{4,5},{5,4},{6,7},{7,6},{8,9},{9,8},{10,11... | collective-permute-start | bytes 196616 | tf_op jit(solution)/shard_map/ppermute | solution.py:362
  216.7 12.5 %collective-permute-start.22 = (bf16[8,32,128]{2,1,0:T(8,128)(2,1)S(1)}, bf16[8,32,128]{2,1,0:T(8,128)(2,1)S(1)}, u32[]{:S(2)}, u32[]{:S(2)}) collective-permute-start(bf16[8,32,128]{2,1,0:T(8,128)(2,1)S(1)} %get-tuple-element.59), channel_id=1, source_target_pairs={{0,2},{1,3},{2,0},{3,1},{4,6},{5,7},{6,4},{7,5},{8,10},{9,11},{10,... | collective-permute-start | bytes 196616 | tf_op jit(solution)/shard_map/ppermute | solution.py:362
  220.0 13.1 %collective-permute-start.14 = (bf16[16,32,256]{2,1,0:T(8,128)(2,1)S(1)}, bf16[16,32,256]{2,1,0:T(8,128)(2,1)S(1)}, u32[]{:S(2)}, u32[]{:S(2)}) collective-permute-start(bf16[16,32,256]{2,1,0:T(8,128)(2,1)S(1)} %get-tuple-element.55), channel_id=1, source_target_pairs={{0,2},{1,3},{2,0},{3,1},{4,6},{5,7},{6,4},{7,5},{8,10},{9,11},{10,... | collective-permute-start | bytes 786440 | tf_op jit(solution)/shard_map/ppermute | solution.py:362
  220.1 15.1 %copy-start.7 = (bf16[16,32,512]{2,1,0:T(8,128)(2,1)S(1)}, bf16[16,32,512]{2,1,0:T(8,128)(2,1)}, u32[]{:S(2)}) copy-start(bf16[16,32,512]{2,1,0:T(8,128)(2,1)} %copy-done.5) | copy-start | bytes 1572868
  225.8 11.8 %collective-permute-start.23 = (bf16[8,32,128]{2,1,0:T(8,128)(2,1)S(1)}, bf16[8,32,128]{2,1,0:T(8,128)(2,1)S(1)}, u32[]{:S(2)}, u32[]{:S(2)}) collective-permute-start(bf16[8,32,128]{2,1,0:T(8,128)(2,1)S(1)} %get-tuple-element.60), channel_id=1, source_target_pairs={{0,3},{1,2},{2,1},{3,0},{4,7},{5,6},{6,5},{7,4},{8,11},{9,10},{10,... | collective-permute-start | bytes 196616 | tf_op jit(solution)/shard_map/ppermute | solution.py:362
  229.2 8.5 %collective-permute-start.24 = (bf16[8,32,128]{2,1,0:T(8,128)(2,1)S(1)}, bf16[8,32,128]{2,1,0:T(8,128)(2,1)S(1)}, u32[]{:S(2)}, u32[]{:S(2)}) collective-permute-start(bf16[8,32,128]{2,1,0:T(8,128)(2,1)S(1)} %get-tuple-element.61), channel_id=1, source_target_pairs={{0,1},{1,0},{2,3},{3,2},{4,5},{5,4},{6,7},{7,6},{8,9},{9,8},{10,11... | collective-permute-start | bytes 196616 | tf_op jit(solution)/shard_map/ppermute | solution.py:362
  229.2 8.4 %collective-permute-start.25 = (bf16[8,32,128]{2,1,0:T(8,128)(2,1)S(1)}, bf16[8,32,128]{2,1,0:T(8,128)(2,1)S(1)}, u32[]{:S(2)}, u32[]{:S(2)}) collective-permute-start(bf16[8,32,128]{2,1,0:T(8,128)(2,1)S(1)} %get-tuple-element.62), channel_id=1, source_target_pairs={{0,2},{1,3},{2,0},{3,1},{4,6},{5,7},{6,4},{7,5},{8,10},{9,11},{10,... | collective-permute-start | bytes 196616 | tf_op jit(solution)/shard_map/ppermute | solution.py:362
  233.1 5.2 %collective-permute-start.26 = (bf16[8,32,128]{2,1,0:T(8,128)(2,1)S(1)}, bf16[8,32,128]{2,1,0:T(8,128)(2,1)S(1)}, u32[]{:S(2)}, u32[]{:S(2)}) collective-permute-start(bf16[8,32,128]{2,1,0:T(8,128)(2,1)S(1)} %get-tuple-element.63), channel_id=1, source_target_pairs={{0,3},{1,2},{2,1},{3,0},{4,7},{5,6},{6,5},{7,4},{8,11},{9,10},{10,... | collective-permute-start | bytes 196616 | tf_op jit(solution)/shard_map/ppermute | solution.py:362
  234.3 6.4 %collective-permute-start.12 = (f32[16,32,32]{2,1,0:T(8,128)S(1)}, f32[16,32,32]{2,1,0:T(8,128)S(1)}, u32[]{:S(2)}, u32[]{:S(2)}) collective-permute-start(f32[16,32,32]{2,1,0:T(8,128)S(1)} %slice_bitcast_fusion), channel_id=1, source_target_pairs={{0,2},{1,3},{2,0},{3,1},{4,6},{5,7},{6,4},{7,5},{8,10},{9,11},{10,... | collective-permute-start | bytes 196616 | tf_op jit(solution)/shard_map/ppermute | solution.py:362
  (14 other events, 73.6 us)

commit v13 on v11

--- a/solution.py
+++ b/solution.py
@@ -340,7 +340,7 @@
 
 
 def chunk_spans(fit_rows):
-    sizes = (fit_rows // 2, fit_rows // 4, fit_rows // 8, fit_rows // 8)
+    sizes = (fit_rows // 2, fit_rows // 8, fit_rows // 4, fit_rows // 8)
     return [(sum(sizes[:c]), size) for c, size in enumerate(sizes)]
 
 
@@ -412,10 +412,10 @@
         product = jnp.dot(turned, raw_parts[k], preferred_element_type=jnp.float32)
         fitted.append(product.astype(jnp.bfloat16))
         mirror(0, k)
-        mirror(1, k)
-        mirror(2, k)
-    for k in range(2):
-        mirror(3, k)
+    fitted = list(lax.optimization_barrier(tuple(fitted)))
+    for c in range(1, len(spans)):
+        mirror(c, 0)
+        mirror(c, 1)
 
     energies, levels, named, fitted[1] = lax.optimization_barrier(
         (occ_energy, pno_energy, own_orbs, fitted[1])

time: 243 us -> 236 us (0.971)
  starting transfers between devices: 80 us -> 74.4 us
    ppermute x26, starting transfers between devices: 69.2 us -> 63.7 us  [across(): return lax.ppermute(array, 'orb', [(i, i ^ mask) for i in range(orb_count)])]
    unnamed x37 -> x41, local copies, waits for them, and re-layouts: 9.77 us -> 9.78 us
  transfers between devices with their start and end apart: 29 -> 29, of which waited for: 10 -> 10; matrix products, arithmetic and copies ran while one was open for 9% -> 9% of each run, Pallas kernels for 13% -> 15%
where the time goes in v13:
time: 236 us; the launch traced here: 235 us
  waiting for transfers between devices  87.1 us (37%)
  starting transfers between devices  74.4 us (32%)
  Pallas kernels  37.2 us (16%)
  local copies, waits for them, and re-layouts  23.5 us (10%)
  matrix products  9.55 us (4%)
    ppermute x26, waiting for transfers between devices, across(): return lax.ppermute(array, 'orb', [(i, i ^ mask) for i in range(orb_count)])  65.5 us
    ppermute x26, starting transfers between devices, across(): return lax.ppermute(array, 'orb', [(i, i ^ mask) for i in range(orb_count)])  63.7 us
    pallas_call x5, Pallas kernels, project(): pl.pallas_call(kernel, grid=(1,), out_shape=(jax.ShapeDtypeStruct((lines,...  16.9 us
    all_to_all x2, waiting for transfers between devices, exchange(): lax.all_to_all(array[:, :, :, k * half:(k + 1) * half], 'aux', split_axis...  14 us
    unnamed x41, local copies, waits for them, and re-layouts  9.78 us
    dot_general x2, matrix products, on_device(): product = jnp.dot(turned, raw_parts[k], preferred_element_type=jnp.float32)  9.55 us
    all_to_all x2, starting transfers between devices, exchange(): lax.all_to_all(array[:, :, :, k * half:(k + 1) * half], 'aux', split_axis...  8.84 us
    pallas_call x2, Pallas kernels, pack(): pl.pallas_call(functools.partial(pack_kernel, group, capacity, masks), ou...  8.51 us
  transfers between devices with their start and end apart: 29, of which 10 were waited for; matrix products, arithmetic and copies ran while one was open for 9% of the time, Pallas kernels for 15%

profile of v13, /device:TPU:0, one launch (start us, length us, event | category | flops | bytes accessed | tf_op | source)
XLA Modules:
  0.0 234.9 jit_solution(14512247107889614269)
XLA Ops:
  0.6 2.7 %slice.64 = bf16[4,1,256,768]{3,2,1,0:T(8,128)(2,1)} slice(bf16[4,1,256,1536]{3,2,1,0:T(8,128)(2,1)} %param.7), slice={[0:4], [0:1], [0:256], [0:768]} | slice | bytes 3145728 | tf_op jit(solution)/shard_map/slice | solution.py:368
  3.3 4.5 %all-to-all-start = ((bf16[4,1,256,768]{3,2,1,0:T(8,128)(2,1)}), bf16[4,1,256,768]{3,2,1,0:T(8,128)(2,1)}, u32[]{:S(2)}, u32[]{:S(2)}) async-start(bf16[4,1,256,768]{3,2,1,0:T(8,128)(2,1)} %slice.64), calls=%async_computation | async-start | bytes 3145728 | tf_op jit(solution)/shard_map/all_to_all | solution.py:367
  9.2 4.3 %shard_map.87 = (bf16[16,32,1536]{2,1,0:T(8,128)(2,1)}, bf16[16,32,1536]{2,1,0:T(8,128)(2,1)}) custom-call(s32[32]{0:T(128)} %reshape.73.orbs, s32[2]{0:T(128)} %pad_add_fusion.1.place, bf16[32,32,1536]{2,1,0:T(8,128)(2,1)} %bitcast.16), custom_call_target="tpu_custom_call" | custom-call | bytes 9437184 | tf_op jit(solution)/shard_map/pallas_call | solution.py:59
  14.7 13.9 %all-to-all-done = bf16[4,1,256,768]{3,2,1,0:T(8,128)(2,1)} async-done(((bf16[4,1,256,768]{3,2,1,0:T(8,128)(2,1)}), bf16[4,1,256,768]{3,2,1,0:T(8,128)(2,1)}, u32[]{:S(2)}, u32[]{:S(2)}) %all-to-all-start) | async-done | bytes 1572896 | tf_op jit(solution)/shard_map/all_to_all | solution.py:367
  28.6 4.3 %all-to-all-start.1 = ((bf16[4,1,256,768]{3,2,1,0:T(8,128)(2,1)}), bf16[4,1,256,768]{3,2,1,0:T(8,128)(2,1)}, u32[]{:S(2)}, u32[]{:S(2)}) async-start(bf16[4,1,256,768]{3,2,1,0:T(8,128)(2,1)} %slice.66), calls=%async_computation.1 | async-start | bytes 3145728 | tf_op jit(solution)/shard_map/all_to_all | solution.py:367
  33.0 2.5 %collective-permute-start.2 = (bf16[16,32,1536]{2,1,0:T(8,128)(2,1)}, bf16[16,32,1536]{2,1,0:T(8,128)(2,1)S(1)}, u32[]{:S(2)}, u32[]{:S(2)}) collective-permute-start(bf16[16,32,1536]{2,1,0:T(8,128)(2,1)} %get-tuple-element.39), channel_id=1, source_target_pairs={{0,2},{1,3},{2,0},{3,1},{4,6},{5,7},{6,4},{7,5},{8,10},{9,11},{10,... | collective-permute-start | bytes 4718600 | tf_op jit(solution)/shard_map/ppermute | solution.py:360
  39.1 4.3 %shard_map.86 = (bf16[16,32,1536]{2,1,0:T(8,128)(2,1)}, bf16[16,32,1536]{2,1,0:T(8,128)(2,1)}) custom-call(s32[32]{0:T(128)} %reshape.73.orbs, s32[2]{0:T(128)} %pad_add_fusion.1.place, bf16[32,32,1536]{2,1,0:T(8,128)(2,1)} %bitcast.17), custom_call_target="tpu_custom_call" | custom-call | bytes 9437184 | tf_op jit(solution)/shard_map/pallas_call | solution.py:59
  46.1 4.8 %convolution_convert_fusion.1.refs_4_ = bf16[1024,768]{1,0:T(8,128)(2,1)S(1)} fusion(bf16[1024,768]{1,0:T(8,128)(2,1)} %bitcast.5, u32[]{:T(128)} %bitcast.4, bf16[1024,1024]{1,0:T(8,128)(2,1)} %bitcast.22), kind=kOutput, calls=%fused_computation.4 | convolution fusion | flops 1615593472 | bytes 5242884 | tf_op jit(solution)/shard_map/dot_general | solution.py:412
  53.1 4.8 %convolution_convert_fusion.refs_5_ = bf16[1024,768]{1,0:T(8,128)(2,1)S(1)} fusion(bf16[1024,768]{1,0:T(8,128)(2,1)} %bitcast.6, u32[]{:T(128)} %bitcast.4, bf16[1024,1024]{1,0:T(8,128)(2,1)} %bitcast.23), kind=kOutput, calls=%fused_computation.3 | convolution fusion | flops 1615593472 | bytes 5242884 | tf_op jit(solution)/shard_map/dot_general | solution.py:412
  60.0 4.4 %collective-permute-start.4 = (bf16[512,768]{1,0:T(8,128)(2,1)}, bf16[512,768]{1,0:T(8,128)(2,1)}, u32[]{:S(2)}, u32[]{:S(2)}) collective-permute-start(bf16[512,768]{1,0:T(8,128)(2,1)} %slice.85), channel_id=1, source_target_pairs={{0,6},{1,7},{2,4},{3,5},{4,2},{5,3},{6,0},{7,1},{8,14},{9,15},{10,... | collective-permute-start | bytes 2359304 | tf_op jit(solution)/shard_map/ppermute | solution.py:360
  64.9 7.6 %collective-permute-done.6.refs_7_ = bf16[1,32,1536]{2,1,0:T(8,128)(2,1)S(1)} collective-permute-done((bf16[1,32,1536]{2,1,0:T(8,128)(2,1)S(1)}, bf16[1,32,1536]{2,1,0:T(8,128)(2,1)S(1)}, u32[]{:S(2)}, u32[]{:S(2)}) %collective-permute-start.6) | collective-permute-done | bytes 98336 | tf_op jit(solution)/shard_map/ppermute | solution.py:387
  72.5 2.5 %collective-permute-start.5 = (bf16[512,768]{1,0:T(8,128)(2,1)}, bf16[512,768]{1,0:T(8,128)(2,1)S(1)}, u32[]{:S(2)}, u32[]{:S(2)}) collective-permute-start(bf16[512,768]{1,0:T(8,128)(2,1)} %slice.86), channel_id=1, source_target_pairs={{0,6},{1,7},{2,4},{3,5},{4,2},{5,3},{6,0},{7,1},{8,14},{9,15},{10,... | collective-permute-start | bytes 2359304 | tf_op jit(solution)/shard_map/ppermute | solution.py:360
  77.0 29.4 %collective-permute-done.3.refs_3_ = bf16[16,32,1536]{2,1,0:T(8,128)(2,1)S(1)} collective-permute-done((bf16[16,32,1536]{2,1,0:T(8,128)(2,1)}, bf16[16,32,1536]{2,1,0:T(8,128)(2,1)S(1)}, u32[]{:S(2)}, u32[]{:S(2)}) %collective-permute-start.3) | collective-permute-done | bytes 1572896 | tf_op jit(solution)/shard_map/ppermute | solution.py:360
  106.4 3.3 %collective-permute-start = (s32[32]{0:T(128)S(1)}, s32[32]{0:T(128)S(1)}, u32[]{:S(2)}, u32[]{:S(2)}) collective-permute-start(s32[32]{0:T(128)S(1)} %copy-done.16), channel_id=1, source_target_pairs={{0,2},{1,3},{2,0},{3,1},{4,6},{5,7},{6,4},{7,5},{8,10},{9,11},{10,... | collective-permute-start | bytes 392 | tf_op jit(solution)/shard_map/ppermute | solution.py:360
  109.7 3.9 %collective-permute-done.1.refs_1_ = bf16[16,32,1536]{2,1,0:T(8,128)(2,1)} collective-permute-done((bf16[16,32,1536]{2,1,0:T(8,128)(2,1)}, bf16[16,32,1536]{2,1,0:T(8,128)(2,1)}, u32[]{:S(2)}, u32[]{:S(2)}) %collective-permute-start.1) | collective-permute-done | bytes 1572896 | tf_op jit(solution)/shard_map/ppermute | solution.py:360
  117.8 6.2 %shard_map.89 = (bf16[16,32,1024]{2,1,0:T(8,128)(2,1)S(1)}, bf16[16,32,1024]{2,1,0:T(8,128)(2,1)}) custom-call(bf16[16,32,1536]{2,1,0:T(8,128)(2,1)S(1)} %copy-done, bf16[16,32,1536]{2,1,0:T(8,128)(2,1)} %collective-permute-done.1.refs_1_, bf16[16,32,1536]{2,1,0:T(8,128)(2,1)S(1)} %collective-permute-done.2.refs_2_, ...), custom_call_target="tpu_custom_call" | custom-call | flops 3221225472 | bytes 3145728 | tf_op jit(solution)/shard_map/pallas_call | solution.py:124
  127.6 3.6 %collective-permute-start.9 = (bf16[128,768]{1,0:T(8,128)(2,1)}, bf16[128,768]{1,0:T(8,128)(2,1)}, u32[]{:S(2)}, u32[]{:S(2)}) collective-permute-start(bf16[128,768]{1,0:T(8,128)(2,1)} %get-tuple-element.75), channel_id=1, source_target_pairs={{0,6},{1,7},{2,4},{3,5},{4,2},{5,3},{6,0},{7,1},{8,14},{9,15},{10,... | collective-permute-start | bytes 589832 | tf_op jit(solution)/shard_map/ppermute | solution.py:360
  131.4 11.6 %collective-permute-done.5.refs_5_ = bf16[512,768]{1,0:T(8,128)(2,1)S(1)} collective-permute-done((bf16[512,768]{1,0:T(8,128)(2,1)}, bf16[512,768]{1,0:T(8,128)(2,1)S(1)}, u32[]{:S(2)}, u32[]{:S(2)}) %collective-permute-start.5) | collective-permute-done | bytes 786464 | tf_op jit(solution)/shard_map/ppermute | solution.py:360
  144.4 4.0 %shard_map.88 = (bf16[16,32,512]{2,1,0:T(8,128)(2,1)S(1)}, bf16[16,32,512]{2,1,0:T(8,128)(2,1)}) custom-call(bf16[16,32,1536]{2,1,0:T(8,128)(2,1)S(1)} %copy-done, bf16[16,32,1536]{2,1,0:T(8,128)(2,1)} %collective-permute-done.1.refs_1_, bf16[16,32,1536]{2,1,0:T(8,128)(2,1)S(1)} %collective-permute-done.2.refs_2_, ...), custom_call_target="tpu_custom_call" | custom-call | flops 1610612736 | bytes 3145728 | tf_op jit(solution)/shard_map/pallas_call | solution.py:124
  151.3 10.7 %collective-permute-done.8.refs_3_ = bf16[16,32,512]{2,1,0:T(8,128)(2,1)} collective-permute-done((bf16[16,32,512]{2,1,0:T(8,128)(2,1)}, bf16[16,32,512]{2,1,0:T(8,128)(2,1)}, u32[]{:S(2)}, u32[]{:S(2)}) %collective-permute-start.8) | collective-permute-done | bytes 524320 | tf_op jit(solution)/shard_map/ppermute | solution.py:360
  162.0 2.5 %collective-permute-start.17 = (bf16[256,768]{1,0:T(8,128)(2,1)}, bf16[256,768]{1,0:T(8,128)(2,1)S(1)}, u32[]{:S(2)}, u32[]{:S(2)}) collective-permute-start(bf16[256,768]{1,0:T(8,128)(2,1)} %slice.81), channel_id=1, source_target_pairs={{0,6},{1,7},{2,4},{3,5},{4,2},{5,3},{6,0},{7,1},{8,14},{9,15},{10,... | collective-permute-start | bytes 1179656 | tf_op jit(solution)/shard_map/ppermute | solution.py:360
  166.7 3.4 %shard_map.90 = (bf16[16,32,512]{2,1,0:T(8,128)(2,1)S(1)}, f32[2,16,32,32]{3,2,1,0:T(8,128)S(1)}) custom-call(s32[2,32]{1,0:T(2,128)S(1)} %add_select_fusion.1.rows, s32[2,32]{1,0:T(2,128)S(1)} %reshape.75.offsets, f32[8,128]{1,0:T(8,128)S(1)} %broadcast_in_dim.75.before, bf16[16,32,1024]{2,1,0:T(8,128)(2,1)S(1)} %copy-done.3, ...), custom_call_target="tpu_custom_call" | custom-call | tf_op jit(solution)/shard_map/pallas_call | solution.py:200
  170.2 2.3 shard_map.91
  175.5 2.5 %collective-permute-start.16 = (bf16[128,768]{1,0:T(8,128)(2,1)S(1)}, bf16[128,768]{1,0:T(8,128)(2,1)S(1)}, u32[]{:S(2)}, u32[]{:S(2)}) collective-permute-start(bf16[128,768]{1,0:T(8,128)(2,1)S(1)} %copy-done.14), channel_id=1, source_target_pairs={{0,6},{1,7},{2,4},{3,5},{4,2},{5,3},{6,0},{7,1},{8,14},{9,15},{10,... | collective-permute-start | bytes 589832 | tf_op jit(solution)/shard_map/ppermute | solution.py:360
  178.9 14.7 %collective-permute-start.19 = (bf16[8,32,384]{2,1,0:T(8,128)(2,1)S(1)}, bf16[8,32,384]{2,1,0:T(8,128)(2,1)S(1)}, u32[]{:S(2)}, u32[]{:S(2)}) collective-permute-start(bf16[8,32,384]{2,1,0:T(8,128)(2,1)S(1)} %slice.83), channel_id=1, source_target_pairs={{0,2},{1,3},{2,0},{3,1},{4,6},{5,7},{6,4},{7,5},{8,10},{9,11},{10,... | collective-permute-start | bytes 589832 | tf_op jit(solution)/shard_map/ppermute | solution.py:360
  193.7 2.8 %shard_map.92 = (bf16[16,32,128]{2,1,0:T(8,128)(2,1)S(1)}, f32[2,16,32,32]{3,2,1,0:T(8,128)S(1)}) custom-call(s32[2,32]{1,0:T(2,128)S(1)} %add_select_fusion.1.rows, s32[2,32]{1,0:T(2,128)S(1)} %reshape.75.offsets, f32[2,16,32,32]{3,2,1,0:T(8,128)S(1)} %get-tuple-element.54.refs_6_.before, bf16[16,32,1024]{2,1,0:T(8,128)(2,1)S(1)} %copy-done.4, ...), custom_call_target="tpu_custom_call" | custom-call | tf_op jit(solution)/shard_map/pallas_call | solution.py:200
  196.6 6.4 %collective-permute-start.20 = (bf16[8,32,384]{2,1,0:T(8,128)(2,1)S(1)}, bf16[8,32,384]{2,1,0:T(8,128)(2,1)S(1)}, u32[]{:S(2)}, u32[]{:S(2)}) collective-permute-start(bf16[8,32,384]{2,1,0:T(8,128)(2,1)S(1)} %slice.84), channel_id=1, source_target_pairs={{0,3},{1,2},{2,1},{3,0},{4,7},{5,6},{6,5},{7,4},{8,11},{9,10},{10,... | collective-permute-start | bytes 589832 | tf_op jit(solution)/shard_map/ppermute | solution.py:360
  202.9 2.2 shard_map.93
  208.0 6.1 %collective-permute-start.25 = (bf16[8,32,128]{2,1,0:T(8,128)(2,1)S(1)}, bf16[8,32,128]{2,1,0:T(8,128)(2,1)S(1)}, u32[]{:S(2)}, u32[]{:S(2)}) collective-permute-start(bf16[8,32,128]{2,1,0:T(8,128)(2,1)S(1)} %get-tuple-element.66), channel_id=1, source_target_pairs={{0,2},{1,3},{2,0},{3,1},{4,6},{5,7},{6,4},{7,5},{8,10},{9,11},{10,... | collective-permute-start | bytes 196616 | tf_op jit(solution)/shard_map/ppermute | solution.py:360
  222.1 2.5 %shard_map.95.before = f32[16,32,32]{2,1,0:T(8,128)S(1)} custom-call(s32[2,32]{1,0:T(2,128)S(1)} %get-tuple-element.70.rows, s32[2,32]{1,0:T(2,128)S(1)} %reshape.75.offsets, bf16[16,32,1024]{2,1,0:T(8,128)(2,1)S(1)} %copy-done.4, bf16[16,32,1024]{2,1,0:T(8,128)(2,1)} %collective-permute-done.7.refs_1_, bf16[16,32,512]{2,1,0:T(8,128)(2,1)S(1)} %copy-done.7, ...), custom_call_target="tpu_custom_call" | custom-call | tf_op jit(solution)/shard_map/pallas_call | solution.py:322
  224.5 7.2 %collective-permute-done.12.there = f32[16,32,32]{2,1,0:T(8,128)S(1)} collective-permute-done((f32[16,32,32]{2,1,0:T(8,128)S(1)}, f32[16,32,32]{2,1,0:T(8,128)S(1)}, u32[]{:S(2)}, u32[]{:S(2)}) %collective-permute-start.12) | collective-permute-done | bytes 65568 | tf_op jit(solution)/shard_map/ppermute | solution.py:360
  231.8 3.1 %finish.1 = (f32[16,1024]{1,0:T(8,128)}, f32[16]{0:T(128)}) custom-call(s32[32]{0:T(128)S(1)} %add_bitcast_fusion.rows, f32[2,16,32,32]{3,2,1,0:T(8,128)S(1)} %get-tuple-element.57.refs_6_.here, f32[16,32,32]{2,1,0:T(8,128)S(1)} %collective-permute-done.12.there, f32[16,32,32]{2,1,0:T(8,128)S(1)} %shard_map.95.before, ...), custom_call_target="tpu_custom_call" | custom-call | tf_op jit(solution)/shard_map/finish/pallas_call | solution.py:299
  (114 shorter events, 44.3 us)
Async XLA Ops:
  3.3 25.3 %all-to-all-start = ((bf16[4,1,256,768]{3,2,1,0:T(8,128)(2,1)}), bf16[4,1,256,768]{3,2,1,0:T(8,128)(2,1)}, u32[]{:S(2)}, u32[]{:S(2)}) async-start(bf16[4,1,256,768]{3,2,1,0:T(8,128)(2,1)} %slice.64), calls=%async_computation | async-start | bytes 3145728 | tf_op jit(solution)/shard_map/all_to_all | solution.py:367
  28.6 24.5 %all-to-all-start.1 = ((bf16[4,1,256,768]{3,2,1,0:T(8,128)(2,1)}), bf16[4,1,256,768]{3,2,1,0:T(8,128)(2,1)}, u32[]{:S(2)}, u32[]{:S(2)}) async-start(bf16[4,1,256,768]{3,2,1,0:T(8,128)(2,1)} %slice.66), calls=%async_computation.1 | async-start | bytes 3145728 | tf_op jit(solution)/shard_map/all_to_all | solution.py:367
  33.0 76.8 %collective-permute-start.2 = (bf16[16,32,1536]{2,1,0:T(8,128)(2,1)}, bf16[16,32,1536]{2,1,0:T(8,128)(2,1)S(1)}, u32[]{:S(2)}, u32[]{:S(2)}) collective-permute-start(bf16[16,32,1536]{2,1,0:T(8,128)(2,1)} %get-tuple-element.39), channel_id=1, source_target_pairs={{0,2},{1,3},{2,0},{3,1},{4,6},{5,7},{6,4},{7,5},{8,10},{9,11},{10,... | collective-permute-start | bytes 4718600 | tf_op jit(solution)/shard_map/ppermute | solution.py:360
  36.4 36.2 %collective-permute-start.6 = (bf16[1,32,1536]{2,1,0:T(8,128)(2,1)S(1)}, bf16[1,32,1536]{2,1,0:T(8,128)(2,1)S(1)}, u32[]{:S(2)}, u32[]{:S(2)}) collective-permute-start(bf16[1,32,1536]{2,1,0:T(8,128)(2,1)S(1)} %slice.75), channel_id=1, source_target_pairs={{0,2},{1,3},{6,4},{7,5},{8,10},{9,11},{14,12},{15,13},{16,18},{17,... | collective-permute-start | bytes 294920 | tf_op jit(solution)/shard_map/ppermute | solution.py:387
  38.3 68.1 %collective-permute-start.3 = (bf16[16,32,1536]{2,1,0:T(8,128)(2,1)}, bf16[16,32,1536]{2,1,0:T(8,128)(2,1)S(1)}, u32[]{:S(2)}, u32[]{:S(2)}) collective-permute-start(bf16[16,32,1536]{2,1,0:T(8,128)(2,1)} %get-tuple-element.40), channel_id=1, source_target_pairs={{0,3},{1,2},{2,1},{3,0},{4,7},{5,6},{6,5},{7,4},{8,11},{9,10},{10,... | collective-permute-start | bytes 4718600 | tf_op jit(solution)/shard_map/ppermute | solution.py:360
  43.4 70.2 %collective-permute-start.1 = (bf16[16,32,1536]{2,1,0:T(8,128)(2,1)}, bf16[16,32,1536]{2,1,0:T(8,128)(2,1)}, u32[]{:S(2)}, u32[]{:S(2)}) collective-permute-start(bf16[16,32,1536]{2,1,0:T(8,128)(2,1)} %get-tuple-element.36), channel_id=1, source_target_pairs={{0,1},{1,0},{2,3},{3,2},{4,5},{5,4},{6,7},{7,6},{8,9},{9,8},{10,11... | collective-permute-start | bytes 4718600 | tf_op jit(solution)/shard_map/ppermute | solution.py:360
  60.0 71.2 %collective-permute-start.4 = (bf16[512,768]{1,0:T(8,128)(2,1)}, bf16[512,768]{1,0:T(8,128)(2,1)}, u32[]{:S(2)}, u32[]{:S(2)}) collective-permute-start(bf16[512,768]{1,0:T(8,128)(2,1)} %slice.85), channel_id=1, source_target_pairs={{0,6},{1,7},{2,4},{3,5},{4,2},{5,3},{6,0},{7,1},{8,14},{9,15},{10,... | collective-permute-start | bytes 2359304 | tf_op jit(solution)/shard_map/ppermute | solution.py:360
  72.5 70.5 %collective-permute-start.5 = (bf16[512,768]{1,0:T(8,128)(2,1)}, bf16[512,768]{1,0:T(8,128)(2,1)S(1)}, u32[]{:S(2)}, u32[]{:S(2)}) collective-permute-start(bf16[512,768]{1,0:T(8,128)(2,1)} %slice.86), channel_id=1, source_target_pairs={{0,6},{1,7},{2,4},{3,5},{4,2},{5,3},{6,0},{7,1},{8,14},{9,15},{10,... | collective-permute-start | bytes 2359304 | tf_op jit(solution)/shard_map/ppermute | solution.py:360
  106.4 42.8 %collective-permute-start = (s32[32]{0:T(128)S(1)}, s32[32]{0:T(128)S(1)}, u32[]{:S(2)}, u32[]{:S(2)}) collective-permute-start(s32[32]{0:T(128)S(1)} %copy-done.16), channel_id=1, source_target_pairs={{0,2},{1,3},{2,0},{3,1},{4,6},{5,7},{6,4},{7,5},{8,10},{9,11},{10,... | collective-permute-start | bytes 392 | tf_op jit(solution)/shard_map/ppermute | solution.py:360
  124.0 24.4 %copy-start.2 = (bf16[16,32,1024]{2,1,0:T(8,128)(2,1)}, bf16[16,32,1024]{2,1,0:T(8,128)(2,1)S(1)}, u32[]{:S(2)}) copy-start(bf16[16,32,1024]{2,1,0:T(8,128)(2,1)S(1)} %get-tuple-element.50.refs_0_) | copy-start | bytes 3145732
  124.0 40.4 %collective-permute-start.7 = (bf16[16,32,1024]{2,1,0:T(8,128)(2,1)}, bf16[16,32,1024]{2,1,0:T(8,128)(2,1)}, u32[]{:S(2)}, u32[]{:S(2)}) collective-permute-start(bf16[16,32,1024]{2,1,0:T(8,128)(2,1)} %get-tuple-element.51), channel_id=1, source_target_pairs={{0,1},{1,0},{2,3},{3,2},{4,5},{5,4},{6,7},{7,6},{8,9},{9,8},{10,11... | collective-permute-start | bytes 3145736 | tf_op jit(solution)/shard_map/ppermute | solution.py:360
  127.6 42.5 %collective-permute-start.9 = (bf16[128,768]{1,0:T(8,128)(2,1)}, bf16[128,768]{1,0:T(8,128)(2,1)}, u32[]{:S(2)}, u32[]{:S(2)}) collective-permute-start(bf16[128,768]{1,0:T(8,128)(2,1)} %get-tuple-element.75), channel_id=1, source_target_pairs={{0,6},{1,7},{2,4},{3,5},{4,2},{5,3},{6,0},{7,1},{8,14},{9,15},{10,... | collective-permute-start | bytes 589832 | tf_op jit(solution)/shard_map/ppermute | solution.py:360
  131.2 38.9 %collective-permute-start.10 = (bf16[128,768]{1,0:T(8,128)(2,1)}, bf16[128,768]{1,0:T(8,128)(2,1)}, u32[]{:S(2)}, u32[]{:S(2)}) collective-permute-start(bf16[128,768]{1,0:T(8,128)(2,1)} %get-tuple-element.73), channel_id=1, source_target_pairs={{0,6},{1,7},{2,4},{3,5},{4,2},{5,3},{6,0},{7,1},{8,14},{9,15},{10,... | collective-permute-start | bytes 589832 | tf_op jit(solution)/shard_map/ppermute | solution.py:360
  143.0 35.9 %collective-permute-start.18 = (bf16[256,768]{1,0:T(8,128)(2,1)}, bf16[256,768]{1,0:T(8,128)(2,1)}, u32[]{:S(2)}, u32[]{:S(2)}) collective-permute-start(bf16[256,768]{1,0:T(8,128)(2,1)} %slice.82), channel_id=1, source_target_pairs={{0,6},{1,7},{2,4},{3,5},{4,2},{5,3},{6,0},{7,1},{8,14},{9,15},{10,... | collective-permute-start | bytes 1179656 | tf_op jit(solution)/shard_map/ppermute | solution.py:360
  149.2 12.8 %collective-permute-start.8 = (bf16[16,32,512]{2,1,0:T(8,128)(2,1)}, bf16[16,32,512]{2,1,0:T(8,128)(2,1)}, u32[]{:S(2)}, u32[]{:S(2)}) collective-permute-start(bf16[16,32,512]{2,1,0:T(8,128)(2,1)} %get-tuple-element.53), channel_id=1, source_target_pairs={{0,1},{1,0},{2,3},{3,2},{4,5},{5,4},{6,7},{7,6},{8,9},{9,8},{10,11... | collective-permute-start | bytes 1572872 | tf_op jit(solution)/shard_map/ppermute | solution.py:360
  151.2 18.9 %copy-start.1 = (bf16[16,32,1536]{2,1,0:T(8,128)(2,1)S(1)}, bf16[16,32,1536]{2,1,0:T(8,128)(2,1)}, u32[]{:S(2)}) copy-start(bf16[16,32,1536]{2,1,0:T(8,128)(2,1)} %get-tuple-element.35.refs_0_) | copy-start | bytes 4718596
  162.0 34.6 %collective-permute-start.17 = (bf16[256,768]{1,0:T(8,128)(2,1)}, bf16[256,768]{1,0:T(8,128)(2,1)S(1)}, u32[]{:S(2)}, u32[]{:S(2)}) collective-permute-start(bf16[256,768]{1,0:T(8,128)(2,1)} %slice.81), channel_id=1, source_target_pairs={{0,6},{1,7},{2,4},{3,5},{4,2},{5,3},{6,0},{7,1},{8,14},{9,15},{10,... | collective-permute-start | bytes 1179656 | tf_op jit(solution)/shard_map/ppermute | solution.py:360
  172.5 21.2 %collective-permute-start.11 = (bf16[16,32,128]{2,1,0:T(8,128)(2,1)S(1)}, bf16[16,32,128]{2,1,0:T(8,128)(2,1)S(1)}, u32[]{:S(2)}, u32[]{:S(2)}) collective-permute-start(bf16[16,32,128]{2,1,0:T(8,128)(2,1)S(1)} %get-tuple-element.56), channel_id=1, source_target_pairs={{0,1},{1,0},{2,3},{3,2},{4,5},{5,4},{6,7},{7,6},{8,9},{9,8},{10,11... | collective-permute-start | bytes 393224 | tf_op jit(solution)/shard_map/ppermute | solution.py:360
  174.1 31.1 %collective-permute-start.15 = (bf16[128,768]{1,0:T(8,128)(2,1)S(1)}, bf16[128,768]{1,0:T(8,128)(2,1)S(1)}, u32[]{:S(2)}, u32[]{:S(2)}) collective-permute-start(bf16[128,768]{1,0:T(8,128)(2,1)S(1)} %copy-done.13), channel_id=1, source_target_pairs={{0,6},{1,7},{2,4},{3,5},{4,2},{5,3},{6,0},{7,1},{8,14},{9,15},{10,... | collective-permute-start | bytes 589832 | tf_op jit(solution)/shard_map/ppermute | solution.py:360
  175.5 29.7 %collective-permute-start.16 = (bf16[128,768]{1,0:T(8,128)(2,1)S(1)}, bf16[128,768]{1,0:T(8,128)(2,1)S(1)}, u32[]{:S(2)}, u32[]{:S(2)}) collective-permute-start(bf16[128,768]{1,0:T(8,128)(2,1)S(1)} %copy-done.14), channel_id=1, source_target_pairs={{0,6},{1,7},{2,4},{3,5},{4,2},{5,3},{6,0},{7,1},{8,14},{9,15},{10,... | collective-permute-start | bytes 589832 | tf_op jit(solution)/shard_map/ppermute | solution.py:360
  178.9 35.1 %collective-permute-start.19 = (bf16[8,32,384]{2,1,0:T(8,128)(2,1)S(1)}, bf16[8,32,384]{2,1,0:T(8,128)(2,1)S(1)}, u32[]{:S(2)}, u32[]{:S(2)}) collective-permute-start(bf16[8,32,384]{2,1,0:T(8,128)(2,1)S(1)} %slice.83), channel_id=1, source_target_pairs={{0,2},{1,3},{2,0},{3,1},{4,6},{5,7},{6,4},{7,5},{8,10},{9,11},{10,... | collective-permute-start | bytes 589832 | tf_op jit(solution)/shard_map/ppermute | solution.py:360
  193.7 28.1 %collective-permute-start.13 = (bf16[16,32,512]{2,1,0:T(8,128)(2,1)S(1)}, bf16[16,32,512]{2,1,0:T(8,128)(2,1)S(1)}, u32[]{:S(2)}, u32[]{:S(2)}) collective-permute-start(bf16[16,32,512]{2,1,0:T(8,128)(2,1)S(1)} %get-tuple-element.58), channel_id=1, source_target_pairs={{0,2},{1,3},{2,0},{3,1},{4,6},{5,7},{6,4},{7,5},{8,10},{9,11},{10,... | collective-permute-start | bytes 1572872 | tf_op jit(solution)/shard_map/ppermute | solution.py:360
  196.6 19.0 %collective-permute-start.20 = (bf16[8,32,384]{2,1,0:T(8,128)(2,1)S(1)}, bf16[8,32,384]{2,1,0:T(8,128)(2,1)S(1)}, u32[]{:S(2)}, u32[]{:S(2)}) collective-permute-start(bf16[8,32,384]{2,1,0:T(8,128)(2,1)S(1)} %slice.84), channel_id=1, source_target_pairs={{0,3},{1,2},{2,1},{3,0},{4,7},{5,6},{6,5},{7,4},{8,11},{9,10},{10,... | collective-permute-start | bytes 589832 | tf_op jit(solution)/shard_map/ppermute | solution.py:360
  205.2 16.9 %copy-start.7 = (bf16[16,32,512]{2,1,0:T(8,128)(2,1)S(1)}, bf16[16,32,512]{2,1,0:T(8,128)(2,1)}, u32[]{:S(2)}) copy-start(bf16[16,32,512]{2,1,0:T(8,128)(2,1)} %copy-done.5) | copy-start | bytes 1572868
  207.4 9.4 %collective-permute-start.24 = (bf16[8,32,128]{2,1,0:T(8,128)(2,1)S(1)}, bf16[8,32,128]{2,1,0:T(8,128)(2,1)S(1)}, u32[]{:S(2)}, u32[]{:S(2)}) collective-permute-start(bf16[8,32,128]{2,1,0:T(8,128)(2,1)S(1)} %get-tuple-element.65), channel_id=1, source_target_pairs={{0,1},{1,0},{2,3},{3,2},{4,5},{5,4},{6,7},{7,6},{8,9},{9,8},{10,11... | collective-permute-start | bytes 196616 | tf_op jit(solution)/shard_map/ppermute | solution.py:360
  208.0 10.8 %collective-permute-start.25 = (bf16[8,32,128]{2,1,0:T(8,128)(2,1)S(1)}, bf16[8,32,128]{2,1,0:T(8,128)(2,1)S(1)}, u32[]{:S(2)}, u32[]{:S(2)}) collective-permute-start(bf16[8,32,128]{2,1,0:T(8,128)(2,1)S(1)} %get-tuple-element.66), channel_id=1, source_target_pairs={{0,2},{1,3},{2,0},{3,1},{4,6},{5,7},{6,4},{7,5},{8,10},{9,11},{10,... | collective-permute-start | bytes 196616 | tf_op jit(solution)/shard_map/ppermute | solution.py:360
  214.1 6.2 %collective-permute-start.14 = (bf16[16,32,128]{2,1,0:T(8,128)(2,1)S(1)}, bf16[16,32,128]{2,1,0:T(8,128)(2,1)S(1)}, u32[]{:S(2)}, u32[]{:S(2)}) collective-permute-start(bf16[16,32,128]{2,1,0:T(8,128)(2,1)S(1)} %get-tuple-element.59), channel_id=1, source_target_pairs={{0,2},{1,3},{2,0},{3,1},{4,6},{5,7},{6,4},{7,5},{8,10},{9,11},{10,... | collective-permute-start | bytes 393224 | tf_op jit(solution)/shard_map/ppermute | solution.py:360
  215.6 8.9 %collective-permute-start.26 = (bf16[8,32,128]{2,1,0:T(8,128)(2,1)S(1)}, bf16[8,32,128]{2,1,0:T(8,128)(2,1)S(1)}, u32[]{:S(2)}, u32[]{:S(2)}) collective-permute-start(bf16[8,32,128]{2,1,0:T(8,128)(2,1)S(1)} %get-tuple-element.67), channel_id=1, source_target_pairs={{0,3},{1,2},{2,1},{3,0},{4,7},{5,6},{6,5},{7,4},{8,11},{9,10},{10,... | collective-permute-start | bytes 196616 | tf_op jit(solution)/shard_map/ppermute | solution.py:360
  216.8 15.0 %collective-permute-start.21 = (bf16[8,32,256]{2,1,0:T(8,128)(2,1)S(1)}, bf16[8,32,256]{2,1,0:T(8,128)(2,1)S(1)}, u32[]{:S(2)}, u32[]{:S(2)}) collective-permute-start(bf16[8,32,256]{2,1,0:T(8,128)(2,1)S(1)} %get-tuple-element.62), channel_id=1, source_target_pairs={{0,1},{1,0},{2,3},{3,2},{4,5},{5,4},{6,7},{7,6},{8,9},{9,8},{10,11... | collective-permute-start | bytes 393224 | tf_op jit(solution)/shard_map/ppermute | solution.py:360
  218.7 13.0 %collective-permute-start.22 = (bf16[8,32,256]{2,1,0:T(8,128)(2,1)S(1)}, bf16[8,32,256]{2,1,0:T(8,128)(2,1)S(1)}, u32[]{:S(2)}, u32[]{:S(2)}) collective-permute-start(bf16[8,32,256]{2,1,0:T(8,128)(2,1)S(1)} %get-tuple-element.63), channel_id=1, source_target_pairs={{0,2},{1,3},{2,0},{3,1},{4,6},{5,7},{6,4},{7,5},{8,10},{9,11},{10,... | collective-permute-start | bytes 393224 | tf_op jit(solution)/shard_map/ppermute | solution.py:360
  220.3 11.5 %collective-permute-start.23 = (bf16[8,32,256]{2,1,0:T(8,128)(2,1)S(1)}, bf16[8,32,256]{2,1,0:T(8,128)(2,1)S(1)}, u32[]{:S(2)}, u32[]{:S(2)}) collective-permute-start(bf16[8,32,256]{2,1,0:T(8,128)(2,1)S(1)} %get-tuple-element.64), channel_id=1, source_target_pairs={{0,3},{1,2},{2,1},{3,0},{4,7},{5,6},{6,5},{7,4},{8,11},{9,10},{10,... | collective-permute-start | bytes 393224 | tf_op jit(solution)/shard_map/ppermute | solution.py:360
  221.7 10.0 %collective-permute-start.12 = (f32[16,32,32]{2,1,0:T(8,128)S(1)}, f32[16,32,32]{2,1,0:T(8,128)S(1)}, u32[]{:S(2)}, u32[]{:S(2)}) collective-permute-start(f32[16,32,32]{2,1,0:T(8,128)S(1)} %slice_bitcast_fusion), channel_id=1, source_target_pairs={{0,2},{1,3},{2,0},{3,1},{4,6},{5,7},{6,4},{7,5},{8,10},{9,11},{10,... | collective-permute-start | bytes 196616 | tf_op jit(solution)/shard_map/ppermute | solution.py:360
  (17 other events, 83.9 us)
